TPU v7x, 32 devices: a whole 2x2x4 slice. The times are simulated.
32 devices in a mesh: dp: 4 (over x, core), group: 4 (over z), tensor: 2 (over y).
Axes of the slice: x: 2, y: 2, z: 4, core: 2. Of those that a mesh axis runs over, the one named last changes fastest.
Arguments:
- residual_in: bfloat16 [32, 1024, 767], P(('dp', 'group'), 'tensor'), may hold values from -6 to 6
- piece_ids: int32 [32, 1024], P(('dp', 'group')), may hold values from -1 to 3, as said below
- norm_gains: bfloat16 [2, 768], replicated, may hold values from 0.25 to 1.75
- qkv_weight: bfloat16 [3, 768, 768], P(None, None, 'tensor'), may hold values from -0.21875 to 0.21875
- qv_bias: bfloat16 [2, 768], P(None, 'tensor'), may hold values from -3 to 3
- out_weight: bfloat16 [768, 767], P('tensor'), may hold values from -0.875 to 0.875
- fc_weight: bfloat16 [768, 3072], P(None, 'tensor'), may hold values from -0.21875 to 0.21875
- fc_bias: bfloat16 [3072], P('tensor'), may hold values from -3 to 3
- proj_weight: bfloat16 [3072, 767], P('tensor'), may hold values from -0.109375 to 0.109375
- out_biases: bfloat16 [2, 767], replicated, may hold values from -2 to 2
- cotangent: bfloat16 [32, 1024, 767], P(('dp', 'group'), 'tensor'), may hold values from -6 to 6
Outputs:
- block_out: bfloat16 [32, 1024, 767], P(('dp', 'group'), 'tensor')
- grad_input: bfloat16 [32, 1024, 767], P(('dp', 'group'), 'tensor')
- grad_gains: float32 [2, 768], replicated
- grad_qkv: float32 [3, 768, 768], P(None, 'dp', 'tensor')
- grad_qv_bias: float32 [2, 768], P(None, ('tensor', 'dp'))
- grad_out_weight: float32 [768, 767], P(('tensor', 'dp'))
- grad_fc_weight: float32 [768, 3072], P('dp', 'tensor')
- grad_fc_bias: float32 [3072], P(('tensor', 'dp'))
- grad_proj_weight: float32 [3072, 767], P(('tensor', 'dp'))
- grad_out_biases: float32 [2, 767], replicated
Inputs may be any that keep to these rules, and one draw needn't show every extreme that they name: `piece_ids`: each aligned block of 256 positions of a sequence carries one id: -1 (text) or the block's own number (a picture piece). The first block of every sequence is text and the last one a picture piece.
All inputs are finite; a program needn't handle non-finite values.
Results may differ from a plain program's by a relative error of at most 0.02.
Values may be sent and summed in bfloat16 or wider, within the bound.
No kernel may reach another device: no remote copies, remote signals or barrier semaphores. Data moves between devices by JAX's collectives and lax.ppermute only.
A program may use at most 192 MiB of HBM per device.

v0:
```python
import jax
import jax.numpy as jnp
from jax import lax
from jax.sharding import PartitionSpec as P

D = 768
HD = 64


EPSILON = 1e-05
MASKED = -1e30


def decompress(compact):
    return jnp.concatenate([compact, -jnp.sum(compact, axis=-1, keepdims=True)], axis=-1)


def crms_gain(compact, gain):
    full_rows = decompress(compact)
    factor = lax.rsqrt(jnp.mean(full_rows * full_rows, axis=-1, keepdims=True) + EPSILON)
    return full_rows * factor * gain


def gelu_tanh(values):
    return jax.nn.gelu(values, approximate=True)


def visible_mask(labels, row_start, row_count):
    query_pos = row_start + jnp.arange(row_count)
    key_pos = jnp.arange(labels.shape[0])
    row_labels = labels[row_start : row_start + row_count]
    causal = key_pos[None, :] <= query_pos[:, None]
    inside = (row_labels[:, None] == labels[None, :]) & (row_labels[:, None] >= 0)
    return causal | inside


def block_scores(row_query, key_rows, labels, row_start, row_block):
    scores = jnp.einsum(
        "qhd,khd->hqk", row_query, key_rows, preferred_element_type=jnp.float32
    ) * HD ** (-0.5)
    return jnp.where(visible_mask(labels, row_start, row_block)[None], scores, MASKED)


def attend_forward(inputs):
    queries, key_rows, value_rows, labels = inputs
    length = key_rows.shape[0]
    row_block = min(512, length)
    outputs = []
    log_parts = []
    for row_start in range(0, length, row_block):
        scores = block_scores(
            queries[row_start : row_start + row_block], key_rows, labels, row_start, row_block
        )
        highest = jnp.max(scores, axis=-1, keepdims=True)
        weights = jnp.exp(scores - highest)
        weight_sum = jnp.sum(weights, axis=-1, keepdims=True)
        prob_low = (weights / weight_sum).astype(jnp.bfloat16)
        outputs.append(
            jnp.einsum(
                "hqk,khd->qhd", prob_low, value_rows, preferred_element_type=jnp.float32
            ).astype(jnp.bfloat16)
        )
        log_parts.append((highest + jnp.log(weight_sum))[..., 0])
    return (jnp.concatenate(outputs, 0), jnp.concatenate(log_parts, 1))


def attend_backward(inputs):
    queries, key_rows, value_rows, labels, upstream, log_sums = inputs
    length = key_rows.shape[0]
    row_block = min(512, length)
    score_scale = HD ** (-0.5)
    grad_keys = jnp.zeros(key_rows.shape, jnp.float32)
    grad_values = jnp.zeros(value_rows.shape, jnp.float32)
    query_grads = []
    for row_start in range(0, length, row_block):
        row_query = queries[row_start : row_start + row_block]
        row_up = upstream[row_start : row_start + row_block]
        scores = block_scores(row_query, key_rows, labels, row_start, row_block)
        probs = jnp.exp(scores - log_sums[:, row_start : row_start + row_block, None])
        along = jnp.einsum("qhd,khd->hqk", row_up, value_rows, preferred_element_type=jnp.float32)
        inner = jnp.sum(along * probs, axis=-1, keepdims=True)
        score_grad = (probs * (along - inner)).astype(jnp.bfloat16)
        query_grads.append(
            jnp.einsum("hqk,khd->qhd", score_grad, key_rows, preferred_element_type=jnp.float32)
            * score_scale
        )
        grad_keys = (
            grad_keys
            + jnp.einsum("hqk,qhd->khd", score_grad, row_query, preferred_element_type=jnp.float32)
            * score_scale
        )
        grad_values = grad_values + jnp.einsum(
            "hqk,qhd->khd", probs.astype(jnp.bfloat16), row_up, preferred_element_type=jnp.float32
        )
    return (jnp.concatenate(query_grads, 0), grad_keys, grad_values)


def on_device(
    residual_in,
    piece_ids,
    norm_gains,
    qkv_weight,
    qv_bias,
    out_weight,
    fc_weight,
    fc_bias,
    proj_weight,
    out_biases,
    cotangent,
):
    residual_rows, upstream_rows, labels_all = (residual_in, cotangent, piece_ids)
    qkv_w, qv_b, out_w, fc_w, fc_b, proj_w = (
        qkv_weight,
        qv_bias,
        out_weight,
        fc_weight,
        fc_bias,
        proj_weight,
    )
    seq_count, local_len, compact_width = residual_rows.shape
    local_rows = seq_count * local_len
    local_width = qkv_w.shape[2]
    head_count = local_width // HD
    gain_values = norm_gains.astype(jnp.float32)
    bias_values = qv_b.astype(jnp.float32)
    end_biases = out_biases.astype(jnp.float32)
    inputs_flat = residual_rows.reshape(local_rows, compact_width).astype(jnp.float32)
    normed_one, norm_one_back = jax.vjp(crms_gain, inputs_flat, gain_values[0])
    one_low = normed_one.astype(jnp.bfloat16).reshape(seq_count, local_len, D)
    full_one = lax.all_gather(one_low, "tensor", axis=1, tiled=True)
    seq_len = full_one.shape[1]
    token_count = seq_count * seq_len
    flat_one = full_one.reshape(token_count, D)
    projected = jnp.einsum("td,cde->cte", flat_one, qkv_w, preferred_element_type=jnp.float32)
    queries = (
        (projected[0] + bias_values[0])
        .astype(jnp.bfloat16)
        .reshape(seq_count, seq_len, head_count, HD)
    )
    key_rows = projected[1].astype(jnp.bfloat16).reshape(seq_count, seq_len, head_count, HD)
    value_rows = (
        (projected[2] + bias_values[1])
        .astype(jnp.bfloat16)
        .reshape(seq_count, seq_len, head_count, HD)
    )
    attended, log_sums = lax.map(attend_forward, (queries, key_rows, value_rows, labels_all))
    attended_flat = attended.reshape(token_count, local_width)
    branch_part = jnp.dot(attended_flat, out_w, preferred_element_type=jnp.float32).reshape(
        seq_count, seq_len, compact_width
    )
    branch_sum = lax.psum_scatter(
        branch_part.astype(jnp.bfloat16), "tensor", scatter_dimension=1, tiled=True
    ).astype(jnp.float32)
    middle = inputs_flat + branch_sum.reshape(local_rows, compact_width) + end_biases[0]
    normed_two, norm_two_back = jax.vjp(crms_gain, middle, gain_values[1])
    two_low = normed_two.astype(jnp.bfloat16).reshape(seq_count, local_len, D)
    full_two = lax.all_gather(two_low, "tensor", axis=1, tiled=True).reshape(token_count, D)
    hidden_pre = jnp.dot(full_two, fc_w, preferred_element_type=jnp.float32) + fc_b.astype(
        jnp.float32
    )
    active_full, gelu_back = jax.vjp(gelu_tanh, hidden_pre)
    active = active_full.astype(jnp.bfloat16)
    mlp_part = jnp.dot(active, proj_w, preferred_element_type=jnp.float32).reshape(
        seq_count, seq_len, compact_width
    )
    mlp_sum = lax.psum_scatter(
        mlp_part.astype(jnp.bfloat16), "tensor", scatter_dimension=1, tiled=True
    ).astype(jnp.float32)
    block_out = (
        (middle + mlp_sum.reshape(local_rows, compact_width) + end_biases[1])
        .astype(jnp.bfloat16)
        .reshape(seq_count, local_len, compact_width)
    )
    upstream_full = lax.all_gather(upstream_rows, "tensor", axis=1, tiled=True).reshape(
        token_count, compact_width
    )
    upstream_flat = upstream_rows.reshape(local_rows, compact_width).astype(jnp.float32)
    grad_proj_weight = jnp.dot(active.T, upstream_full, preferred_element_type=jnp.float32)
    hidden_grad = gelu_back(jnp.dot(upstream_full, proj_w.T, preferred_element_type=jnp.float32))[
        0
    ].astype(jnp.bfloat16)
    grad_fc_weight = jnp.dot(full_two.T, hidden_grad, preferred_element_type=jnp.float32)
    grad_fc_bias = jnp.sum(hidden_grad.astype(jnp.float32), axis=0)
    two_part = jnp.dot(hidden_grad, fc_w.T, preferred_element_type=jnp.float32).reshape(
        seq_count, seq_len, D
    )
    two_grad = (
        lax.psum_scatter(two_part.astype(jnp.bfloat16), "tensor", scatter_dimension=1, tiled=True)
        .astype(jnp.float32)
        .reshape(local_rows, D)
    )
    middle_norm_grad, gain_two_grad = norm_two_back(two_grad)
    middle_grad = upstream_flat + middle_norm_grad
    branch_low = middle_grad.astype(jnp.bfloat16)
    branch_seq = branch_low.reshape(seq_count, local_len, compact_width)
    branch_full = lax.all_gather(branch_seq, "tensor", axis=1, tiled=True).reshape(
        token_count, compact_width
    )
    grad_out_weight = jnp.dot(attended_flat.T, branch_full, preferred_element_type=jnp.float32)
    attended_grad = (
        jnp.dot(branch_full, out_w.T, preferred_element_type=jnp.float32)
        .astype(jnp.bfloat16)
        .reshape(seq_count, seq_len, head_count, HD)
    )
    query_grad, key_grad, value_grad = lax.map(
        attend_backward, (queries, key_rows, value_rows, labels_all, attended_grad, log_sums)
    )
    stacked = (
        jnp.stack([query_grad, key_grad, value_grad])
        .astype(jnp.bfloat16)
        .reshape(3, token_count, local_width)
    )
    grad_qkv = jnp.einsum("td,cte->cde", flat_one, stacked, preferred_element_type=jnp.float32)
    grad_qv_bias = jnp.stack(
        [
            jnp.sum(stacked[0].astype(jnp.float32), axis=0),
            jnp.sum(stacked[2].astype(jnp.float32), axis=0),
        ]
    )
    one_part = jnp.einsum(
        "cte,cde->td", stacked, qkv_w, preferred_element_type=jnp.float32
    ).reshape(seq_count, seq_len, D)
    one_grad = (
        lax.psum_scatter(one_part.astype(jnp.bfloat16), "tensor", scatter_dimension=1, tiled=True)
        .astype(jnp.float32)
        .reshape(local_rows, D)
    )
    input_norm_grad, gain_one_grad = norm_one_back(one_grad)
    grad_input = (
        (middle_grad + input_norm_grad)
        .astype(jnp.bfloat16)
        .reshape(seq_count, local_len, compact_width)
    )
    gain_terms = jnp.stack([gain_one_grad, gain_two_grad])
    bias_terms = jnp.stack(
        [jnp.sum(branch_low.astype(jnp.float32), axis=0), jnp.sum(upstream_flat, axis=0)]
    )
    grad_gains, grad_out_biases = lax.psum((gain_terms, bias_terms), ("dp", "group", "tensor"))
    weight_grads = (
        grad_qkv,
        grad_qv_bias,
        grad_out_weight,
        grad_fc_weight,
        grad_fc_bias,
        grad_proj_weight,
    )
    shards = (
        lax.psum_scatter(
            weight_grads[0].astype(jnp.bfloat16), "dp", scatter_dimension=1, tiled=True
        ).astype(jnp.float32),
        lax.psum_scatter(
            weight_grads[1].astype(jnp.bfloat16), "dp", scatter_dimension=1, tiled=True
        ).astype(jnp.float32),
        lax.psum_scatter(
            weight_grads[2].astype(jnp.bfloat16), "dp", scatter_dimension=0, tiled=True
        ).astype(jnp.float32),
        lax.psum_scatter(
            weight_grads[3].astype(jnp.bfloat16), "dp", scatter_dimension=0, tiled=True
        ).astype(jnp.float32),
        lax.psum_scatter(
            weight_grads[4].astype(jnp.bfloat16), "dp", scatter_dimension=0, tiled=True
        ).astype(jnp.float32),
        lax.psum_scatter(
            weight_grads[5].astype(jnp.bfloat16), "dp", scatter_dimension=0, tiled=True
        ).astype(jnp.float32),
    )
    reduced = (
        lax.psum(shards[0].astype(jnp.bfloat16), "group").astype(jnp.float32),
        lax.psum(shards[1].astype(jnp.bfloat16), "group").astype(jnp.float32),
        lax.psum(shards[2].astype(jnp.bfloat16), "group").astype(jnp.float32),
        lax.psum(shards[3].astype(jnp.bfloat16), "group").astype(jnp.float32),
        lax.psum(shards[4].astype(jnp.bfloat16), "group").astype(jnp.float32),
        lax.psum(shards[5].astype(jnp.bfloat16), "group").astype(jnp.float32),
    )
    return (
        block_out,
        grad_input,
        grad_gains,
        reduced[0],
        reduced[1],
        reduced[2],
        reduced[3],
        reduced[4],
        reduced[5],
        grad_out_biases,
    )


def solution(mesh):
    in_specs = (
        P(("dp", "group"), "tensor", None),
        P(("dp", "group"), None),
        P(),
        P(None, None, "tensor"),
        P(None, "tensor"),
        P("tensor", None),
        P(None, "tensor"),
        P("tensor"),
        P("tensor", None),
        P(),
        P(("dp", "group"), "tensor", None),
    )
    out_specs = (
        P(("dp", "group"), "tensor", None),
        P(("dp", "group"), "tensor", None),
        P(),
        P(None, "dp", "tensor"),
        P(None, ("tensor", "dp")),
        P(("tensor", "dp"), None),
        P("dp", "tensor"),
        P(("tensor", "dp")),
        P(("tensor", "dp"), None),
        P(),
    )
    return jax.shard_map(
        on_device, mesh=mesh, in_specs=in_specs, out_specs=out_specs, check_vma=False
    )
```

profile of v0, /device:TPU:0, one launch (start us, length us, event | category | flops | bytes accessed | tf_op | source)
XLA Modules:
  0.0 1026.0 jit_solution(11230917446306738538)
XLA Ops:
  7.2 5.2 copy.65
  18.4 3.7 copy.67
  28.7 47.5 %all-gather.5.cloned.1.call-done = bf16[2,1024,768]{2,1,0:T(8,128)(2,1)} async-done(((bf16[2,512,768]{2,1,0:T(8,128)(2,1)}), bf16[2,1024,768]{2,1,0:T(8,128)(2,1)}) %all-gather.5.cloned.1.call-update) | async-done | bytes 3145744 | tf_op jit(solution)/shard_map/all_gather | solution.py:130
  76.2 6.8 convolution_bitcast_fusion
  90.9 5.6 squeeze.35
  103.8 3.9 convert_element_type.203
  114.3 5.6 squeeze.34
  124.6 54.6 %while.26 = (s32[]{:T(128)}, bf16[2,1024,6,64]{1,3,2,0:T(8,128)(2,1)}, f32[2,6,1024]{2,1,0:T(8,128)}, bf16[2,1024,6,64]{1,3,2,0:T(8,128)(2,1)}, s32[2,1024]{1,0:...) while((s32[]{:T(128)}, ...), condition=%wide.region_7.8_spmd, body=%wide.region_2.7_spmd.sunk | while | flops 1692272128 | bytes 111457016 | solution.py:146
  127.7 3.6 fusion.157
  131.4 3.6 fusion.158
  135.1 3.9 fusion.159
  146.0 3.9 fusion.162
  154.7 3.6 fusion.157
  162.1 3.9 fusion.159
  173.0 3.9 fusion.162
  179.2 4.9 convolution_convert_fusion.5
  185.5 42.1 %reduce-scatter.14.cloned.1.call-done = bf16[2,512,767]{2,1,0:T(8,128)(2,1)} async-done(((bf16[2,1024,767]{2,1,0:T(8,128)(2,1)}), bf16[2,512,767]{2,1,0:T(8,128)(2,1)}) %reduce-scatter.14.cloned.1.call-update) | async-done | bytes 1570832 | tf_op jit(solution)/shard_map/reduce_scatter | solution.py:151
  227.6 4.0 fusion.94
  235.1 3.9 add_add_fusion.2
  244.7 29.4 %all-gather.9.cloned.1.call-done = bf16[2,1024,767]{1,0,2:T(2,128)(2,1)} async-done(((bf16[2,512,767]{1,0,2:T(2,128)(2,1)}), bf16[2,1024,767]{1,0,2:T(2,128)(2,1)}) %all-gather.9.cloned.1.call-update) | async-done | bytes 3141648 | tf_op jit(solution)/shard_map/all_gather | solution.py:174
  274.1 4.3 pad.21
  281.1 39.4 %all-gather.7.cloned.1.call-done = bf16[2,1024,768]{2,1,0:T(8,128)(2,1)} async-done(((bf16[2,512,768]{2,1,0:T(8,128)(2,1)}), bf16[2,1024,768]{2,1,0:T(8,128)(2,1)}) %all-gather.7.cloned.1.call-update) | async-done | bytes 3145744 | tf_op jit(solution)/shard_map/all_gather | solution.py:157
  320.5 13.5 %multiply_convert_fusion.2 = (bf16[2048,1536]{1,0:T(8,128)(2,1)}, f32[2048,1536]{1,0:T(8,128)}) fusion(f32[1536]{0:T(1024)S(1)} %convert_element_type.208, bf16[2048,768]{1,0:T(8,128)(2,1)} %bitcast.353, bf16[768,1536]{1,0:T(8,128)(2,1)S(1)} %copy-done), kind=kOutput, calls=%fused_computation.125 | convolution fusion | flops 4863295488 | bytes 24385536 | tf_op jit(solution)/shard_map/dot_general | solution.py:158
  334.1 15.3 %fusion.97 = (bf16[1536]{0:T(1024)(128)(2,1)}, bf16[2048,1536]{1,0:T(8,128)(2,1)S(1)}) fusion(f32[2048,1536]{1,0:T(8,128)} %get-tuple-element.273, f32[1536]{0:T(1024)S(1)} %convert_element_type.208, bf16[2048,767]{0,1:T(8,128)(2,1)S(1)} %bitcast.318, bf16[1536,767]{1,0:T(8,128)(2,1)S(1)} %copy-done.63), kind=kOutput, calls=%fused_computation.195 | convolution fusion | flops 4894751232 | bytes 24381440 | tf_op jit(solution)/shard_map/dot_general | solution.py:179
  349.4 6.4 convolution_convert_fusion.2
  361.9 37.5 %reduce-scatter.18.cloned.1.call-done = bf16[2,512,768]{2,1,0:T(8,128)(2,1)} async-done(((bf16[2,1024,768]{2,1,0:T(8,128)(2,1)}), bf16[2,512,768]{2,1,0:T(8,128)(2,1)}) %reduce-scatter.18.cloned.1.call-update) | async-done | bytes 1572880 | tf_op jit(solution)/shard_map/reduce_scatter | solution.py:188
  412.4 44.9 %all-gather.11.cloned.1.call-done = bf16[2,1024,767]{1,0,2:T(2,128)(2,1)} async-done(((bf16[2,512,767]{1,0,2:T(2,128)(2,1)}), bf16[2,1024,767]{1,0,2:T(2,128)(2,1)}) %all-gather.11.cloned.1.call-update) | async-done | bytes 3141648 | tf_op jit(solution)/shard_map/all_gather | solution.py:196
  457.3 4.3 pad.22
  472.4 133.8 %while.27 = (s32[]{:T(128)}, bf16[2,1024,6,64]{1,3,2,0:T(8,128)(2,1)}, bf16[2,1024,6,64]{1,3,2,0:T(8,128)(2,1)}, bf16[2,1024,6,64]{1,3,2,0:T(8,128)(2,1)}, bf16[...) while((s32[]{:T(128)}, ...), condition=%wide.region_17.18_spmd, body=%wide.region_14.17_spmd.sunk | while | flops 4128632320 | bytes 286275584 | solution.py:205
  482.6 4.4 fusion.183
  487.0 5.5 bitcast_dynamic-update-slice_fusion.5
  492.5 8.4 multiply_reduce_fusion.10
  500.9 9.6 multiply_convert_fusion.7
  510.5 5.2 fusion.178
  515.7 8.1 multiply_reduce_fusion.11
  523.8 7.0 multiply_convert_fusion.8
  549.2 4.4 fusion.183
  553.6 5.5 bitcast_dynamic-update-slice_fusion.5
  559.1 8.4 multiply_reduce_fusion.10
  567.6 9.6 multiply_convert_fusion.7
  577.2 5.2 fusion.178
  582.4 8.1 multiply_reduce_fusion.11
  590.5 7.0 multiply_convert_fusion.8
  614.7 3.8 stack.48
  627.9 4.9 convert_bitcast_fusion.1
  632.9 4.0 copy.94
  638.5 9.4 convolution_convert_fusion
  647.9 9.3 convolution_convert_fusion.1
  663.4 9.0 convolution_convert_fusion.3
  678.4 25.3 %reduce-scatter.26.cloned.1.call-done = bf16[384,767]{1,0:T(8,128)(2,1)} async-done(((bf16[1536,767]{1,0:T(8,128)(2,1)}), bf16[384,767]{1,0:T(8,128)(2,1)}) %reduce-scatter.26.cloned.1.call-update) | async-done | bytes 589072 | tf_op jit(solution)/shard_map/reduce_scatter | solution.py:263
  703.7 35.6 %reduce-scatter.24.cloned.1.call-done = bf16[192,1536]{1,0:T(8,128)(2,1)} async-done(((bf16[768,1536]{1,0:T(8,128)(2,1)}), bf16[192,1536]{1,0:T(8,128)(2,1)}) %reduce-scatter.24.cloned.1.call-update) | async-done | bytes 589840 | tf_op jit(solution)/shard_map/reduce_scatter | solution.py:257
  739.4 25.2 %reduce-scatter.22.cloned.1.call-done = bf16[96,767]{1,0:T(8,128)(2,1)} async-done(((bf16[384,767]{1,0:T(8,128)(2,1)}), bf16[96,767]{1,0:T(8,128)(2,1)}) %reduce-scatter.22.cloned.1.call-update) | async-done | bytes 147280 | tf_op jit(solution)/shard_map/reduce_scatter | solution.py:254
  764.7 7.0 copy.87
  771.6 9.1 bitcast_convert_fusion
  780.8 3.7 convert_reduce_fusion
  785.7 6.1 all-reduce
  791.9 18.4 %reduce-scatter.16.cloned.1.call-done = bf16[2,512,767]{2,1,0:T(8,128)(2,1)} async-done(((bf16[2,1024,767]{2,1,0:T(8,128)(2,1)}), bf16[2,512,767]{2,1,0:T(8,128)(2,1)}) %reduce-scatter.16.cloned.1.call-update) | async-done | bytes 1570832 | tf_op jit(solution)/shard_map/reduce_scatter | solution.py:166
  813.2 4.9 copy.90
  818.2 14.5 %reduce-scatter.30.cloned.1.call-done = bf16[96,2]{1,0:T(8,128)(2,1)} async-done(((bf16[384,2]{1,0:T(8,128)(2,1)}), bf16[96,2]{1,0:T(8,128)(2,1)}) %reduce-scatter.30.cloned.1.call-update) | async-done | bytes 400
  833.5 11.8 %all-reduce.2 = (bf16[2,96]{1,0:T(2,128)(2,1)S(1)}, bf16[384]{0:T(512)(128)(2,1)S(1)}) all-reduce(bf16[2,96]{1,0:T(2,128)(2,1)S(1)} %copy.97, bf16[384]{0:T(512)(128)(2,1)S(1)} %dynamic-slice.1), channel_id=1, replica_groups=mesh['dp'=4,'group'=4,'tensor'=2] {'group'}, use_global_device_ids=true, to_apply=%region_28.29 | all-reduce | flops 576 | bytes 2304 | tf_op jit(solution)/shard_map/psum | solution.py:269
  846.5 71.2 %all-reduce.6.cloned.1.call-done = (bf16[3,192,384]{1,2,0:T(8,128)(2,1)}, bf16[96,767]{1,0:T(8,128)(2,1)}, bf16[192,1536]{1,0:T(8,128)(2,1)}, bf16[384,767]{1,0:T(8,128)(2,1)}) async-done(((bf16[3,192,384]{1,2,0:T(8,128)(2,1)}, bf16[96,767]{1,0:T(8,128)(2,1)}, bf16[192,1536]{1,0:T(8,128)(2,1)}, bf16[384,767]{1,0:T(8,128)(2,1)}), (bf16[3,192,384]{1,2,0:T(8,128)(2,1)}, bf16[96,767]{1,0:T(8,128)(2,1)}, ...) | async-done | bytes 1768528 | tf_op jit(solution)/shard_map/psum | solution.py:268
  926.0 36.2 %reduce-scatter.20.cloned.1.call-done = bf16[2,512,768]{2,1,0:T(8,128)(2,1)} async-done(((bf16[2,1024,768]{2,1,0:T(8,128)(2,1)}), bf16[2,512,768]{2,1,0:T(8,128)(2,1)}) %reduce-scatter.20.cloned.1.call-update) | async-done | bytes 1572880 | tf_op jit(solution)/shard_map/reduce_scatter | solution.py:224
  974.5 5.2 reshape.591
  979.7 39.6 %all-reduce.1 = (f32[2,768]{1,0:T(2,128)}, f32[2,767]{1,0:T(2,128)}) all-reduce(f32[2,768]{1,0:T(2,128)S(1)} %pad_maximum_fusion.4, f32[2,767]{1,0:T(2,128)S(1)} %pad_maximum_fusion.5), channel_id=1, replica_groups=mesh['dp'=4,'group'=4,'tensor'=2] {'dp','group','tensor'}, use_global_device_ids=true, to_apply=%region_22.23 | all-reduce | flops 3070 | bytes 24560 | tf_op jit(solution)/shard_map/psum | solution.py:238
  (355 shorter events, 203.5 us)
Async XLA Ops:
  7.2 313.4 %copy-start = (bf16[768,1536]{1,0:T(8,128)(2,1)S(1)}, bf16[768,1536]{1,0:T(8,128)(2,1)}, u32[]{:S(2)}) copy-start(bf16[768,1536]{1,0:T(8,128)(2,1)} %param.21) | copy-start | bytes 7077892
  7.2 69.0 %all-gather.5.cloned.1.call-start = ((), (), s32[]{:S(2)}) async-start(), calls=%async_computation.9 | async-start | bytes 4718592 | tf_op jit(solution)/shard_map/all_gather | solution.py:130
  12.4 5.1 copy-start.58
  18.1 6.7 copy-start.40
  18.1 3.9 copy-start.43
  18.3 6.5 copy-start.31
  24.8 3.6 copy-start.51
  24.8 3.5 copy-start.45
  24.9 3.6 copy-start.60
  28.4 199.2 %reduce-scatter.14.cloned.1.call-start = ((), (), s32[]{:S(2)}) async-start(), calls=%async_computation.10 | async-start | bytes 4718592 | tf_op jit(solution)/shard_map/reduce_scatter | solution.py:151
  124.6 54.6 %copy-start.65 = (bf16[384,767]{1,0:T(8,128)(2,1)S(1)}, bf16[384,767]{1,0:T(8,128)(2,1)}, u32[]{:S(2)}) copy-start(bf16[384,767]{1,0:T(8,128)(2,1)} %param.20) | copy-start | bytes 1767172
  131.4 3.7 copy-start.8
  135.0 3.9 copy-start.2
  146.0 4.5 copy-start.36
  158.4 3.7 copy-start.8
  162.0 3.9 copy-start.2
  173.0 4.5 copy-start.36
  184.1 90.0 %all-gather.9.cloned.1.call-start = ((), (), s32[]{:S(2)}) async-start(), calls=%async_computation.13 | async-start | bytes 4712448 | tf_op jit(solution)/shard_map/all_gather | solution.py:174
  184.8 135.7 %all-gather.7.cloned.1.call-start = ((), (), s32[]{:S(2)}) async-start(), calls=%async_computation.11 | async-start | bytes 4718592 | tf_op jit(solution)/shard_map/all_gather | solution.py:157
  231.9 9.2 copy-start.32
  241.0 3.6 copy-start.56
  244.6 154.8 %reduce-scatter.18.cloned.1.call-start = ((), (), s32[]{:S(2)}) async-start(), calls=%async_computation.14 | async-start | bytes 4718592 | tf_op jit(solution)/shard_map/reduce_scatter | solution.py:188
  320.5 13.5 %copy-start.33 = (bf16[96,8,2,1024]{3,1,2,0:T(8,128)(2,1)S(1)}, bf16[96,8,2,1024]{3,1,2,0:T(8,128)(2,1)}, u32[]{:S(2)}) copy-start(bf16[96,8,2,1024]{3,1,2,0:T(8,128)(2,1)} %copy.101) | copy-start | bytes 9437188
  320.5 13.5 %copy-start.63 = (bf16[1536,767]{1,0:T(8,128)(2,1)S(1)}, bf16[1536,767]{1,0:T(8,128)(2,1)}, u32[]{:S(2)}) copy-start(bf16[1536,767]{1,0:T(8,128)(2,1)} %param.23) | copy-start | bytes 7068676
  349.4 6.4 copy-start.68
  355.8 101.5 %all-gather.11.cloned.1.call-start = ((), (), s32[]{:S(2)}) async-start(), calls=%async_computation.15 | async-start | bytes 4712448 | tf_op jit(solution)/shard_map/all_gather | solution.py:196
  359.4 40.0 %copy-start.11 = (f32[2,512,767]{2,1,0:T(8,128)S(1)}, f32[2,512,767]{2,1,0:T(8,128)}, u32[]{:S(2)}) copy-start(f32[2,512,767]{2,1,0:T(8,128)} %get-tuple-element.243) | copy-start | bytes 9424900
  412.3 263.4 %reduce-scatter.28.cloned.1.call-start = ((), (), s32[]{:S(2)}) async-start(), calls=%async_computation.20 | async-start | bytes 2211840
  467.0 5.5 copy-start.3
  476.3 10.7 %copy-start.5 = (pred[512,1024]{1,0:T(8,128)(4,1)}, pred[512,1024]{1,0:T(8,128)(4,1)S(1)}, u32[]{:S(2)}) copy-start(pred[512,1024]{1,0:T(8,128)(4,1)S(1)} %get-tuple-element.421) | copy-start | bytes 1572868 | tf_op jit(solution)/shard_map/while
  510.5 5.2 copy-start.6
  510.5 5.2 copy-start.9
  523.8 7.0 copy-start.4
  542.9 10.7 %copy-start.5 = (pred[512,1024]{1,0:T(8,128)(4,1)}, pred[512,1024]{1,0:T(8,128)(4,1)S(1)}, u32[]{:S(2)}) copy-start(pred[512,1024]{1,0:T(8,128)(4,1)S(1)} %get-tuple-element.421) | copy-start | bytes 1572868 | tf_op jit(solution)/shard_map/while
  577.2 5.2 copy-start.6
  577.2 5.2 copy-start.9
  590.5 7.0 copy-start.4
  606.3 5.6 copy-start.23
  611.9 6.6 copy-start.27
  624.4 3.5 copy-start.61
  638.4 65.3 %reduce-scatter.26.cloned.1.call-start = ((), (), s32[]{:S(2)}) async-start(), calls=%async_computation.19 | async-start | bytes 2949120 | tf_op jit(solution)/shard_map/reduce_scatter | solution.py:263
  638.5 9.4 copy-start.62
  647.9 91.5 %reduce-scatter.24.cloned.1.call-start = ((), (), s32[]{:S(2)}) async-start(), calls=%async_computation.18 | async-start | bytes 2949120 | tf_op jit(solution)/shard_map/reduce_scatter | solution.py:257
  657.3 3.7 copy-start.35
  657.3 107.3 %reduce-scatter.22.cloned.1.call-start = ((), (), s32[]{:S(2)}) async-start(), calls=%async_computation.17 | async-start | bytes 737280 | tf_op jit(solution)/shard_map/reduce_scatter | solution.py:254
  663.3 147.0 %reduce-scatter.16.cloned.1.call-start = ((), (), s32[]{:S(2)}) async-start(), calls=%async_computation.12 | async-start | bytes 4718592 | tf_op jit(solution)/shard_map/reduce_scatter | solution.py:166
  672.4 160.3 %reduce-scatter.30.cloned.1.call-start = ((), (), s32[]{:S(2)}) async-start(), calls=%async_computation.21 | async-start | bytes 122880
  675.6 242.1 %all-reduce.6.cloned.1.call-start = ((), (), s32[]{:S(2)}) async-start(), calls=%async_computation.22 | async-start | bytes 3833856 | tf_op jit(solution)/shard_map/psum | solution.py:268
  764.6 197.6 %reduce-scatter.20.cloned.1.call-start = ((), (), s32[]{:S(2)}) async-start(), calls=%async_computation.16 | async-start | bytes 4718592 | tf_op jit(solution)/shard_map/reduce_scatter | solution.py:224
  764.6 7.0 copy-start.64
  780.7 3.7 copy-start.67
  780.7 5.0 copy-start.57
  780.7 29.6 %copy-start.12 = (f32[2,512,767]{2,1,0:T(8,128)S(1)}, f32[2,512,767]{2,1,0:T(8,128)}, u32[]{:S(2)}) copy-start(f32[2,512,767]{2,1,0:T(8,128)} %get-tuple-element.243) | copy-start | bytes 9424900
  780.7 29.6 %copy-start.55 = (f32[767]{0:T(1024)S(1)}, f32[767]{0:T(1024)}, u32[]{:S(2)}) copy-start(f32[767]{0:T(1024)} %get-tuple-element.192) | copy-start | bytes 9208
  813.2 4.9 copy-start.53
  813.2 4.9 copy-start.54
  818.1 144.0 %copy-start.10 = (f32[2,512,767]{2,1,0:T(8,128)S(1)}, f32[2,512,767]{2,1,0:T(8,128)}, u32[]{:S(2)}) copy-start(f32[2,512,767]{2,1,0:T(8,128)} %convert_element_type.195) | copy-start | bytes 9424900
  818.1 144.0 %copy-start.41 = (f32[768]{0:T(1024)S(1)}, f32[768]{0:T(1024)}, u32[]{:S(2)}) copy-start(f32[768]{0:T(1024)} %copy-done.40) | copy-start | bytes 9220
  818.1 144.0 %copy-start.46 = (f32[2,512]{1,0:T(2,128)S(1)}, f32[2,512]{1,0:T(2,128)}, u32[]{:S(2)}) copy-start(f32[2,512]{1,0:T(2,128)} %copy-done.45) | copy-start | bytes 12292
  923.7 41.2 %copy-start.50 = (f32[1024]{0:T(1024)S(1)}, f32[1024]{0:T(1024)}, u32[]{:S(2)}) copy-start(f32[1024]{0:T(1024)} %copy-done.49) | copy-start | bytes 12292
  964.9 3.3 copy-start.13
  968.2 3.8 copy-start.17
  968.2 3.8 copy-start.48
  972.0 47.2 %copy-start.1 = (bf16[768,1536]{1,0:T(8,128)(2,1)S(1)}, bf16[768,1536]{1,0:T(8,128)(2,1)}, u32[]{:S(2)}) copy-start(bf16[768,1536]{1,0:T(8,128)(2,1)} %param.21) | copy-start | bytes 7077892
  (37 other events, 76.3 us)
Sparse Core Ops, SparseCore 0:
  28.5 47.6 all-gather.4
  184.2 43.3 reduce-scatter.13
  229.2 44.8 all-gather.8
  275.6 44.9 all-gather.6
  355.9 43.3 reduce-scatter.17
  412.4 44.8 all-gather.10
  638.5 29.3 reduce-scatter.27
  670.6 33.0 reduce-scatter.25
  706.3 33.0 reduce-scatter.23
  742.5 22.0 reduce-scatter.21
  766.9 43.3 reduce-scatter.15
  813.1 19.5 reduce-scatter.29
  835.9 81.7 all-reduce.5
  919.8 42.3 reduce-scatter.19
where the time goes:
time: 1040 us; the launch traced here: 1030 us
  waiting for transfers between devices  468 us (45%)
  matrix products  207 us (20%)
  local copies, waits for them, and re-layouts  161 us (15%)
  other arithmetic  114 us (11%)
  blocking collectives  57.5 us (6%)
  between operations  15.6 us (2%)
    psum x1, waiting for transfers between devices, on_device(): lax.psum(shards[0].astype(jnp.bfloat16), 'group').astype(jnp.float32)  71.2 us
    unnamed x134, local copies, waits for them, and re-layouts  50.5 us
    all_gather x1, waiting for transfers between devices, on_device(): full_one = lax.all_gather(one_low, 'tensor', axis=1, tiled=True)  47.5 us
    all_gather x1, waiting for transfers between devices, on_device(): lax.all_gather(branch_seq, 'tensor', axis=1, tiled=True)  44.9 us
    reduce_scatter x1, waiting for transfers between devices, on_device(): lax.psum_scatter(branch_part.astype(jnp.bfloat16), 'tensor', scatter_dime...  42.1 us
    psum x1, blocking collectives, on_device(): lax.psum((gain_terms, bias_terms), ('dp', 'group', 'tensor'))  39.6 us
    all_gather x1, waiting for transfers between devices, on_device(): lax.all_gather(two_low, 'tensor', axis=1, tiled=True)  39.4 us
    reduce_scatter x1, waiting for transfers between devices, on_device(): lax.psum_scatter(two_part.astype(jnp.bfloat16), 'tensor', scatter_dimensi...  37.5 us
  transfers between devices with their start and end apart: 14, of which 13 were waited for; matrix products, arithmetic and copies ran while one was open for 10% of the time, Pallas kernels for 0%

commit v1 on v0

v1 whole, which is shorter than its diff:
```python
import functools
import jax
import jax.numpy as jnp
from jax import lax
from jax.sharding import PartitionSpec as P
from jax.experimental import pallas as pl
from jax.experimental.pallas import tpu as pltpu

D = 768
HD = 64
EPSILON = 1e-05
MASKED = -1e30
VMEM_CAP = 60 * 1024 * 1024
F32 = jnp.float32
BF16 = jnp.bfloat16


def dot_nn(a, b):
    return lax.dot_general(a, b, (((1,), (0,)), ((), ())), preferred_element_type=F32)


def dot_nt(a, b):
    return lax.dot_general(a, b, (((1,), (1,)), ((), ())), preferred_element_type=F32)


def dot_tn(a, b):
    return lax.dot_general(a, b, (((0,), (0,)), ((), ())), preferred_element_type=F32)


def column_sum(values):
    return jnp.sum(values, axis=0, keepdims=True)


def lane_of(shape):
    return lax.broadcasted_iota(jnp.int32, shape, len(shape) - 1)


def attend_forward_kernel(flags_ref, q_ref, k_ref, v_ref, out_ref, log_ref, *, block):
    length = q_ref.shape[0]
    row = lax.broadcasted_iota(jnp.int32, (block, block), 0)
    col = lax.broadcasted_iota(jnp.int32, (block, block), 1)
    causal = col <= row
    head_lane = lane_of((block, 128)) // HD
    for at in range(length // block):
        rows = pl.ds(at * block, block)
        seen = causal | (flags_ref[at] > 0)
        q_rows = q_ref[rows, :]
        reach = at * block
        parts = []
        for head in range(2):
            q_head = jnp.where(head_lane == head, q_rows, jnp.zeros_like(q_rows))
            near = jnp.where(seen, dot_nt(q_head, k_ref[rows, :]), MASKED)
            top = jnp.max(near, axis=-1, keepdims=True)
            if reach:
                far = dot_nt(q_head, k_ref[pl.ds(0, reach), :])
                top = jnp.maximum(top, jnp.max(far, axis=-1, keepdims=True))
            near = jnp.exp(near - top)
            total = jnp.sum(near, axis=-1, keepdims=True)
            mixed = dot_nn(near.astype(BF16), v_ref[rows, :])
            if reach:
                far = jnp.exp(far - top)
                total = total + jnp.sum(far, axis=-1, keepdims=True)
                mixed = mixed + dot_nn(far.astype(BF16), v_ref[pl.ds(0, reach), :])
            parts.append(mixed / total)
            logs = top + jnp.log(total)
            log_ref[0, pl.ds(head, 1), rows] = jnp.transpose(
                jnp.broadcast_to(logs, (block, 128)))[0:1, :]
        out_ref[rows, :] = jnp.where(head_lane == 0, parts[0], parts[1]).astype(BF16)


def attend_forward(flags, queries, key_rows, value_rows):
    length, width = queries.shape
    pairs = width // 128
    block = length // 4
    tile = pl.BlockSpec((length, 128), lambda h, f: (0, h))
    return pl.pallas_call(
        functools.partial(attend_forward_kernel, block=block),
        grid_spec=pltpu.PrefetchScalarGridSpec(
            num_scalar_prefetch=1, grid=(pairs,),
            in_specs=[tile, tile, tile],
            out_specs=[tile, pl.BlockSpec((1, 8, length), lambda h, f: (h, 0, 0))]),
        out_shape=[jax.ShapeDtypeStruct((length, width), BF16),
                   jax.ShapeDtypeStruct((pairs, 8, length), F32)],
        compiler_params=pltpu.CompilerParams(vmem_limit_bytes=VMEM_CAP),
        name="attend_forward",
    )(flags, queries, key_rows, value_rows)


def attend_backward_kernel(flags_ref, q_ref, k_ref, v_ref, up_ref, log_ref,
                           dq_ref, dk_ref, dv_ref, sum_ref, dk_acc, dv_acc, *, block):
    length = q_ref.shape[0]
    count = length // block
    key_at = lax.broadcasted_iota(jnp.int32, (block, block), 0)
    query_at = lax.broadcasted_iota(jnp.int32, (block, block), 1)
    causal = key_at <= query_at
    head_lane = lane_of((block, 128)) // HD
    full_lane = lane_of((length, 128)) // HD
    dq_sum = jnp.zeros((1, 128), F32)
    for at in reversed(range(count)):
        rows = pl.ds(at * block, block)
        reach = (at + 1) * block
        keys = pl.ds(0, reach)
        seen = causal | (flags_ref[at] > 0)
        dq = None
        for head in range(2):
            q_head = jnp.where(head_lane == head, q_ref[rows, :], jnp.zeros((block, 128), BF16))
            up_head = jnp.where(head_lane == head, up_ref[rows, :], jnp.zeros((block, 128), BF16))
            logs = log_ref[0, pl.ds(head, 1), rows]
            scores = dot_nt(k_ref[keys, :], q_head)
            last = jnp.where(seen, scores[reach - block :], MASKED)
            scores = last if at == 0 else jnp.concatenate([scores[: reach - block], last], 0)
            probs = jnp.exp(scores - logs)
            along = dot_nt(v_ref[keys, :], up_head)
            inner = jnp.sum(probs * along, axis=0, keepdims=True)
            low_grad = (probs * (along - inner)).astype(BF16)
            dv = dot_nn(probs.astype(BF16), up_head)
            dk = dot_nn(low_grad, q_head)
            if at == count - 1 and head == 0:
                dv_acc[keys, :] = dv
                dk_acc[keys, :] = dk
            else:
                dv_acc[keys, :] += dv
                dk_acc[keys, :] += dk
            k_head = jnp.where(full_lane[:reach] == head, k_ref[keys, :], jnp.zeros((reach, 128), BF16))
            part = dot_tn(low_grad, k_head)
            dq = part if dq is None else dq + part
        low_dq = (dq * HD ** (-0.5)).astype(BF16)
        dq_ref[rows, :] = low_dq
        dq_sum = dq_sum + column_sum(low_dq.astype(F32))
    dk_ref[...] = dk_acc[...].astype(BF16)
    low_dv = dv_acc[...].astype(BF16)
    dv_ref[...] = low_dv
    sum_ref[0:1, :] = dq_sum
    sum_ref[1:2, :] = column_sum(low_dv.astype(F32))


def attend_backward(flags, queries, key_rows, value_rows, upstream, log_sums, first, pairs):
    length, width = queries.shape
    block = length // 4
    tile = pl.BlockSpec((length, 128), lambda h, f: (0, h + first))
    out_tile = pl.BlockSpec((length, 128), lambda h, f: (0, h))
    out = jax.ShapeDtypeStruct((length, pairs * 128), BF16)
    return pl.pallas_call(
        functools.partial(attend_backward_kernel, block=block),
        grid_spec=pltpu.PrefetchScalarGridSpec(
            num_scalar_prefetch=1, grid=(pairs,),
            in_specs=[tile, tile, tile, tile,
                      pl.BlockSpec((1, 8, length), lambda h, f: (h + first, 0, 0))],
            out_specs=[out_tile, out_tile, out_tile, pl.BlockSpec((8, 128), lambda h, f: (0, h))],
            scratch_shapes=[pltpu.VMEM((length, 128), F32), pltpu.VMEM((length, 128), F32)]),
        out_shape=[out, out, out, jax.ShapeDtypeStruct((8, pairs * 128), F32)],
        compiler_params=pltpu.CompilerParams(vmem_limit_bytes=VMEM_CAP),
        name="attend_backward",
    )(flags, queries, key_rows, value_rows, upstream, log_sums)


def decompress(compact):
    total = jnp.sum(compact, axis=-1, keepdims=True)
    return jnp.where(lane_of(compact.shape) == D - 1, -total, compact)


def crms_back(normal, factor, gain, grad):
    scaled = gain * grad
    du = factor * (scaled - normal * jnp.mean(scaled * normal, axis=-1, keepdims=True))
    lane = lane_of(du.shape)
    last = jnp.sum(jnp.where(lane == D - 1, du, 0.0), axis=-1, keepdims=True)
    return jnp.where(lane == D - 1, 0.0, du - last)


def crms_normal(compact):
    full = decompress(compact)
    factor = lax.rsqrt(jnp.mean(full * full, axis=-1, keepdims=True) + EPSILON)
    return full * factor, factor


def project_kernel(place_ref, own_ref, other_ref, gain_ref, bias_ref, w_own, w_quarter,
                   normed_ref, q_ref, k_ref, v_ref, weight, sems, *, steps):
    at = pl.program_id(0)
    quarter = D // 4
    half = w_own.shape[2]

    def copies():
        out = [pltpu.make_async_copy(w_own, weight.at[:, :, pl.ds(0, half)], sems.at[0])]
        for rel in range(4):
            place = pl.multiple_of((place_ref[1] ^ rel) * quarter, quarter)
            out.append(pltpu.make_async_copy(
                w_quarter[rel], weight.at[:, pl.ds(place, quarter), pl.ds(half, half)],
                sems.at[rel + 1]))
        return out

    @pl.when(at == 0)
    def _():
        for copy in copies():
            copy.start()

    compact = jnp.where(at < steps // 2, own_ref[...], other_ref[...]).astype(F32)
    normal, _ = crms_normal(compact)
    normed = (normal * gain_ref[...]).astype(BF16)
    normed_ref[...] = normed

    @pl.when(at == 0)
    def _():
        for copy in copies():
            copy.wait()

    q_ref[...] = ((dot_nn(normed, weight[0]) + bias_ref[0:1, :]).astype(BF16).astype(F32)
                  * HD ** (-0.5)).astype(BF16)
    k_ref[...] = dot_nn(normed, weight[1]).astype(BF16)
    v_ref[...] = (dot_nn(normed, weight[2]) + bias_ref[1:2, :]).astype(BF16)


def row_maps(steps):
    half = steps // 2
    own = lambda i, s: (jnp.minimum(i, half - 1), 0)
    other = lambda i, s: (jnp.maximum(i - half, 0), 0)
    whole = lambda i, s: (jnp.where(i < half, s[0] * half + i, (1 - s[0]) * half + i - half), 0)
    return own, other, whole


ANY = pl.BlockSpec(memory_space=pl.ANY)


def project(place, own, other, gain, bias, w_own, w_quarter, steps=4):
    length = own.shape[0] * 2
    block = length // steps
    own_map, other_map, whole_map = row_maps(steps)
    fixed = lambda i, s: (0, 0)
    wide = pl.BlockSpec((block, D), whole_map)
    out = jax.ShapeDtypeStruct((length, D), BF16)

    def body(place_ref, own_ref, other_ref, gain_ref, bias_ref, w_own, a, b, c, d, *rest):
        project_kernel(place_ref, own_ref, other_ref, gain_ref, bias_ref, w_own, (a, b, c, d),
                       *rest, steps=steps)

    return pl.pallas_call(
        body,
        grid_spec=pltpu.PrefetchScalarGridSpec(
            num_scalar_prefetch=1, grid=(steps,),
            in_specs=[pl.BlockSpec((block, D), own_map), pl.BlockSpec((block, D), other_map),
                      pl.BlockSpec((1, D), fixed), pl.BlockSpec((2, D), fixed)] + [ANY] * 5,
            out_specs=[wide] * 4,
            scratch_shapes=[pltpu.VMEM((3, D, D), BF16), pltpu.SemaphoreType.DMA((5,))]),
        out_shape=[out] * 4,
        compiler_params=pltpu.CompilerParams(vmem_limit_bytes=VMEM_CAP),
        name="norm_project",
    )(place, own, other, gain, bias, w_own, *w_quarter)


SQRT_2_PI = 0.7978845608028654


def gelu_pair(v):
    square = v * v
    inner = v * (SQRT_2_PI + (SQRT_2_PI * 0.044715) * square)
    tanh = jnp.tanh(inner)
    cdf = 0.5 + 0.5 * tanh
    slope = SQRT_2_PI + (3 * SQRT_2_PI * 0.044715) * square
    back = cdf + (0.5 * v) * (1.0 - tanh * tanh) * slope
    return v * cdf, back


def middle_kernel(place_ref, att_ref, res_own, res_other, cot_own, cot_other, gain_ref, end_ref,
                  fcb_ref, weights, two_ref, active_ref, hidden_ref, own_out, send_out,
                  mid_ref, branch_ref, upgrad_ref, sums_ref,
                  out_w, fc_w, proj_w, sems, *, steps, chunk):
    at = pl.program_id(0)
    hid = fc_w.shape[1]
    half = hid // 2
    o_own, o_q, f_own, f_q, p_own, p_q = weights

    def copies(which):
        out = []
        if which == 0:
            out.append(pltpu.make_async_copy(o_own, out_w.at[pl.ds(0, D // 2), :], sems.at[0]))
        elif which == 1:
            out.append(pltpu.make_async_copy(f_own, fc_w.at[:, pl.ds(0, half)], sems.at[1]))
        else:
            out.append(pltpu.make_async_copy(p_own, proj_w.at[pl.ds(0, half), :], sems.at[2]))
        for rel in range(4):
            to = place_ref[1] ^ rel
            sem = sems.at[3 + 4 * which + rel]
            if which == 0:
                rows = D // 8
                out.append(pltpu.make_async_copy(
                    o_q[rel], out_w.at[pl.ds(pl.multiple_of(D // 2 + to * rows, rows), rows), :], sem))
            elif which == 1:
                rows = D // 4
                out.append(pltpu.make_async_copy(
                    f_q[rel], fc_w.at[pl.ds(pl.multiple_of(to * rows, rows), rows), pl.ds(half, half)], sem))
            else:
                rows = half // 4
                out.append(pltpu.make_async_copy(
                    p_q[rel], proj_w.at[pl.ds(pl.multiple_of(half + to * rows, rows), rows), :], sem))
        return out

    @pl.when(at == 0)
    def _():
        for which in range(3):
            for copy in copies(which):
                copy.start()
        sums_ref[...] = jnp.zeros_like(sums_ref)
        for copy in copies(0):
            copy.wait()

    mine = at < steps // 2
    compact = jnp.where(mine, res_own[...], res_other[...]).astype(F32)
    cot_low = jnp.where(mine, cot_own[...], cot_other[...])
    middle = compact + dot_nn(att_ref[...], out_w[...]) + end_ref[0:1, :]
    normal, factor = crms_normal(middle)
    gain = gain_ref[...]
    two = (normal * gain).astype(BF16)
    two_ref[...] = two

    @pl.when(at == 0)
    def _():
        for which in (1, 2):
            for copy in copies(which):
                copy.wait()

    mlp = jnp.zeros((two.shape[0], D), F32)
    two_grad = jnp.zeros((two.shape[0], D), F32)
    for start in range(0, hid, chunk):
        cols = pl.ds(start, chunk)
        pre = dot_nn(two, fc_w[:, cols]) + fcb_ref[0:1, cols]
        act, slope = gelu_pair(pre)
        act = act.astype(BF16)
        active_ref[:, cols] = act
        mlp = mlp + dot_nn(act, proj_w[cols, :])
        hidden = (dot_nt(cot_low, proj_w[cols, :]) * slope).astype(BF16)
        hidden_ref[:, cols] = hidden
        sums_ref[3:4, cols] += column_sum(hidden.astype(F32))
        two_grad = two_grad + dot_nt(hidden, fc_w[:, cols])
    block_out = (middle + mlp + end_ref[1:2, :]).astype(BF16)

    @pl.when(mine)
    def _():
        own_out[...] = block_out

    @pl.when(jnp.logical_not(mine))
    def _():
        send_out[...] = block_out

    cot = cot_low.astype(F32)
    mid_grad = cot + crms_back(normal, factor, gain, two_grad)
    mid_ref[...] = mid_grad
    branch = mid_grad.astype(BF16)
    branch_ref[...] = branch
    upgrad_ref[...] = dot_nt(branch, out_w[...]).astype(BF16)
    sums_ref[0:1, 0:D] += column_sum(two_grad * normal)
    sums_ref[1:2, 0:D] += column_sum(branch.astype(F32))
    sums_ref[2:3, 0:D] += column_sum(cot)


def middle_stage(place, att, res_own, res_other, cot_own, cot_other, gain, end_bias, fc_bias, weights,
                 steps=4, chunk=768):
    length = att.shape[0]
    hid = fc_bias.shape[1]
    block = length // steps
    own_map, other_map, whole_map = row_maps(steps)
    fixed = lambda i, s: (0, 0)
    o_own, o_q, f_own, f_q, p_own, p_q = weights
    flat = [o_own, *o_q, f_own, *f_q, p_own, *p_q]
    spec = lambda w, m: pl.BlockSpec((block, w), m)

    def body(place_ref, *refs):
        ins, rest = refs[:8], refs[8:]
        w, rest = rest[:15], rest[15:]
        packed = (w[0], w[1:5], w[5], w[6:10], w[10], w[11:15])
        middle_kernel(place_ref, *ins, packed, *rest, steps=steps, chunk=chunk)

    sd = jax.ShapeDtypeStruct
    return pl.pallas_call(
        body,
        grid_spec=pltpu.PrefetchScalarGridSpec(
            num_scalar_prefetch=1, grid=(steps,),
            in_specs=[spec(D, whole_map), spec(D, own_map), spec(D, other_map), spec(D, own_map),
                      spec(D, other_map), pl.BlockSpec((1, D), fixed), pl.BlockSpec((2, D), fixed),
                      pl.BlockSpec((1, hid), fixed)] + [ANY] * 15,
            out_specs=[spec(D, whole_map), spec(hid, whole_map), spec(hid, whole_map),
                       spec(D, own_map), spec(D, other_map),
                       spec(D, whole_map), spec(D, whole_map), spec(D, whole_map),
                       pl.BlockSpec((8, hid), fixed)],
            scratch_shapes=[pltpu.VMEM((D, D), BF16), pltpu.VMEM((D, hid), BF16),
                            pltpu.VMEM((hid, D), BF16), pltpu.SemaphoreType.DMA((15,))]),
        out_shape=[sd((length, D), BF16), sd((length, hid), BF16), sd((length, hid), BF16),
                   sd((length // 2, D), BF16), sd((length // 2, D), BF16),
                   sd((length, D), F32), sd((length, D), BF16), sd((length, D), BF16),
                   sd((8, hid), F32)],
        compiler_params=pltpu.CompilerParams(vmem_limit_bytes=VMEM_CAP),
        name="middle_stage",
    )(place, att, res_own, res_other, cot_own, cot_other, gain, end_bias, fc_bias, *flat)


def weight_grad_kernel(place_ref, *refs, rows, rights):
    left_ref = refs[0]
    right_refs = refs[1:1 + rights]
    keep_ref, send_ref = refs[1 + rights:]
    flip = (place_ref[1] & 1) == 1
    left = left_ref[...]
    for n, right in enumerate(right_refs):
        both = dot_tn(left, right[...]).astype(BF16)
        low, high = both[:rows], both[rows:]
        if rights == 1:
            keep_ref[0] = jnp.where(flip, high, low)
            send_ref[0] = jnp.where(flip, low, high)
        else:
            keep_ref[0, n] = jnp.where(flip, high, low)
            send_ref[0, n] = jnp.where(flip, low, high)


def weight_grad(place, left, rights, columns, col_at=0, left_cols=None, left_at=0):
    length = left.shape[0]
    span = left_cols or left.shape[1]
    rows = span // 4
    first = left_at * 2
    many = len(rights)
    width = columns
    shape = (2, rows, width) if many == 1 else (2, many, rows, width)
    out_map = (lambda j, s: (j ^ (s[1] >> 1), 0, 0)) if many == 1 else (
        lambda j, s: (j ^ (s[1] >> 1), 0, 0, 0))
    out_spec = pl.BlockSpec((1,) + shape[1:], out_map)
    out = jax.ShapeDtypeStruct(shape, BF16)
    return pl.pallas_call(
        functools.partial(weight_grad_kernel, rows=rows, rights=many),
        grid_spec=pltpu.PrefetchScalarGridSpec(
            num_scalar_prefetch=1, grid=(2,),
            in_specs=[pl.BlockSpec((length, 2 * rows), lambda j, s: (0, first + j))]
            + [pl.BlockSpec((length, width), lambda j, s: (0, col_at)) for _ in rights],
            out_specs=[out_spec, out_spec]),
        out_shape=[out, out],
        compiler_params=pltpu.CompilerParams(vmem_limit_bytes=VMEM_CAP),
        name="weight_grad",
    )(place, left, *rights)


def out_grad_kernel(place_ref, left_ref, right_ref, keep_ref, send_ref, *, rows):
    flip = (place_ref[1] & 1) == 1
    both = dot_tn(left_ref[...], right_ref[...]).astype(BF16)
    for side in range(2):
        for pair in range(2):
            at = (side * 4 + pair * 2) * rows
            low, high = both[at : at + rows], both[at + rows : at + 2 * rows]
            to = pair ^ (place_ref[1] >> 1)
            keep_ref[to, side] = jnp.where(flip, high, low)
            send_ref[to, side] = jnp.where(flip, low, high)


def out_grad(place, left, right):
    length, width = left.shape
    rows = width // 8
    out = jax.ShapeDtypeStruct((2, 2, rows, right.shape[1]), BF16)
    return pl.pallas_call(
        functools.partial(out_grad_kernel, rows=rows),
        grid_spec=pltpu.PrefetchScalarGridSpec(
            num_scalar_prefetch=1, grid=(1,),
            in_specs=[pl.BlockSpec(value.shape, lambda i, s: (0, 0)) for value in (left, right)],
            out_specs=[pl.BlockSpec(out.shape, lambda i, s: (0, 0, 0, 0))] * 2),
        out_shape=[out, out],
        compiler_params=pltpu.CompilerParams(vmem_limit_bytes=VMEM_CAP),
        name="out_grad",
    )(place, left, right)


def input_grad_kernel(place_ref, dq_refs, res_own, res_other, mid_ref, gain_ref, w_own, w_quarter,
                      own_out, send_out, sums_ref, weight, sems, *, steps):
    at = pl.program_id(0)
    quarter = D // 4
    half = w_own.shape[2]

    def copies():
        out = [pltpu.make_async_copy(w_own, weight.at[:, :, pl.ds(0, half)], sems.at[0])]
        for rel in range(4):
            place = pl.multiple_of((place_ref[1] ^ rel) * quarter, quarter)
            out.append(pltpu.make_async_copy(
                w_quarter[rel], weight.at[:, pl.ds(place, quarter), pl.ds(half, half)],
                sems.at[rel + 1]))
        return out

    @pl.when(at == 0)
    def _():
        for copy in copies():
            copy.start()
        sums_ref[...] = jnp.zeros_like(sums_ref)

    mine = at < steps // 2
    compact = jnp.where(mine, res_own[...], res_other[...]).astype(F32)
    normal, factor = crms_normal(compact)
    gain = gain_ref[...]

    @pl.when(at == 0)
    def _():
        for copy in copies():
            copy.wait()

    grad = None
    for n in range(6):
        part = dot_nt(dq_refs[n][...], weight[n % 3, :, pl.ds((n // 3) * half, half)])
        grad = part if grad is None else grad + part
    sums_ref[0:1, :] += column_sum(grad * normal)
    result = (mid_ref[...] + crms_back(normal, factor, gain, grad)).astype(BF16)

    @pl.when(mine)
    def _():
        own_out[...] = result

    @pl.when(jnp.logical_not(mine))
    def _():
        send_out[...] = result


def input_grad(place, head_grads, res_own, res_other, mid, gain, w_own, w_quarter, steps=4):
    length = mid.shape[0]
    block = length // steps
    own_map, other_map, whole_map = row_maps(steps)
    fixed = lambda i, s: (0, 0)
    half = head_grads[0].shape[1]

    def body(place_ref, *refs):
        grads, rest = refs[:6], refs[6:]
        res_own, res_other, mid_ref, gain_ref, w_own, a, b, c, d = rest[:9]
        input_grad_kernel(place_ref, grads, res_own, res_other, mid_ref, gain_ref, w_own,
                          (a, b, c, d), *rest[9:], steps=steps)

    sd = jax.ShapeDtypeStruct
    return pl.pallas_call(
        body,
        grid_spec=pltpu.PrefetchScalarGridSpec(
            num_scalar_prefetch=1, grid=(steps,),
            in_specs=[pl.BlockSpec((block, half), whole_map)] * 6
            + [pl.BlockSpec((block, D), own_map), pl.BlockSpec((block, D), other_map),
               pl.BlockSpec((block, D), whole_map), pl.BlockSpec((1, D), fixed)] + [ANY] * 5,
            out_specs=[pl.BlockSpec((block, D), own_map), pl.BlockSpec((block, D), other_map),
                       pl.BlockSpec((8, D), fixed)],
            scratch_shapes=[pltpu.VMEM((3, D, D), BF16), pltpu.SemaphoreType.DMA((5,))]),
        out_shape=[sd((length // 2, D), BF16), sd((length // 2, D), BF16), sd((8, D), F32)],
        compiler_params=pltpu.CompilerParams(vmem_limit_bytes=VMEM_CAP),
        name="input_grad",
    )(place, *head_grads, res_own, res_other, mid, gain, w_own, *w_quarter)


def swap(value, axis, bit, size):
    return lax.ppermute(value, axis, [(n, n ^ bit) for n in range(size)])


def fetch_other(shard, dim, sizes, quarter_at):
    n_dp, n_tensor = sizes
    rows = shard.shape[dim] // 4
    piece = lax.dynamic_slice_in_dim(shard, quarter_at * rows, rows, dim)
    first = swap(piece, "tensor", 1, n_tensor)
    third = swap(first, "dp", 2, n_dp)
    second = swap(first, "dp", 1, n_dp)
    fourth = swap(third, "dp", 1, n_dp)
    return first, second, third, fourth


def add_low(*values):
    total = values[0].astype(F32)
    for value in values[1:]:
        total = total + value.astype(F32)
    return total.astype(BF16)


def chain_sum(value, size, index):
    if size != 4:
        return lax.psum(value, "group")
    low = value.dtype
    inward = lax.ppermute(value, "group", [(0, 1), (3, 2)])
    part = (value.astype(F32) + inward.astype(F32)).astype(low)
    across = lax.ppermute(part, "group", [(1, 2), (2, 1)])
    total = (part.astype(F32) + across.astype(F32)).astype(low)
    outward = lax.ppermute(total, "group", [(1, 0), (2, 3)])
    return jnp.where((index == 1) | (index == 2), total, outward)


def pick(pair, index):
    return jnp.where(index == 0, pair[0], pair[1])


def reduce_x_first(own, other, n_dp, n_tensor):
    results = []
    arrived = [swap(pair[1], "dp", 1, n_dp) for pair in (own, other)]
    away = [add_low(pair[0][1], got[1]) for pair, got in zip((own, other), arrived)]
    arrived_x = [swap(value, "dp", 2, n_dp) for value in away]
    for pair, got, far in zip((own, other), arrived, arrived_x):
        results.append(add_low(pair[0][0], got[0], far))
    return add_low(results[0], swap(results[1], "tensor", 1, n_tensor))


def reduce_y_first(own, other, n_dp, n_tensor):
    arrived = [swap(pair[1], "dp", 1, n_dp) for pair in (own, other)]
    away = add_low(other[0], arrived[1])
    got = swap(away, "tensor", 1, n_tensor)
    far = add_low(own[0][1], arrived[0][1], got[1])
    return add_low(own[0][0], arrived[0][0], got[0], swap(far, "dp", 2, n_dp))


def all_sum(value, sizes, group_at):
    n_dp, n_group, n_tensor = sizes
    bit = 1
    while bit < n_dp:
        value = value + swap(value, "dp", bit, n_dp)
        bit *= 2
    value = value + swap(value, "tensor", 1, n_tensor)
    return chain_sum(value, n_group, group_at)


def on_device(sizes, residual_in, piece_ids, norm_gains, qkv_weight, qv_bias, out_weight, fc_weight,
              fc_bias, proj_weight, out_biases, cotangent):
    n_dp, n_group, n_tensor = sizes
    dp_at = lax.axis_index("dp")
    group_at = lax.axis_index("group")
    tensor_at = lax.axis_index("tensor")
    quarter_at = dp_at & 3
    place = jnp.stack([tensor_at, quarter_at]).astype(jnp.int32)
    pad = ((0, 0), (0, 1))

    def half_rows(value, at):
        return jnp.pad(lax.dynamic_index_in_dim(value, at, 0, keepdims=False), pad)

    res_own = half_rows(residual_in, tensor_at)
    res_other = swap(half_rows(residual_in, 1 - tensor_at), "tensor", 1, n_tensor)
    small_bias = jnp.concatenate([qv_bias.reshape(1, -1), fc_bias.reshape(1, -1)], axis=1)
    other_bias = swap(small_bias, "tensor", 1, n_tensor)
    qkv_other = fetch_other(qkv_weight, 1, (n_dp, n_tensor), quarter_at)
    out_own = jnp.pad(out_weight, pad)
    proj_own = jnp.pad(proj_weight, pad)
    out_other = fetch_other(out_own, 0, (n_dp, n_tensor), quarter_at)
    fc_other = fetch_other(fc_weight, 0, (n_dp, n_tensor), quarter_at)
    proj_other = fetch_other(proj_own, 0, (n_dp, n_tensor), quarter_at)
    cot_own = half_rows(cotangent, tensor_at)
    cot_other = swap(half_rows(cotangent, 1 - tensor_at), "tensor", 1, n_tensor)

    gains = norm_gains.astype(F32)
    end_biases = jnp.pad(out_biases, pad).astype(F32)
    half = qv_bias.shape[1]
    qv_other = other_bias[:, : 2 * half].reshape(2, half)
    qv_full = jnp.concatenate([qv_bias, qv_other], axis=1).astype(F32)
    fc_full = jnp.concatenate([fc_bias.reshape(1, -1), other_bias[:, 2 * half :]], axis=1).astype(F32)

    length = piece_ids.shape[1]
    flags = (lax.dynamic_index_in_dim(piece_ids, tensor_at, 0, keepdims=False)[:: length // 4] >= 0)
    flags = flags.astype(jnp.int32)

    normed_one, queries, key_rows, value_rows = project(
        place, res_own, res_other, gains[0:1], qv_full, qkv_weight, qkv_other)
    attended, log_sums = attend_forward(flags, queries, key_rows, value_rows)
    (normed_two, active, hidden_grad, out_mine, out_send, middle_grad, branch_grad, attended_grad,
     middle_sums) = middle_stage(
        place, attended, res_own, res_other, cot_own, cot_other, gains[1:2], end_biases, fc_full,
        (out_own, out_other, fc_weight, fc_other, proj_own, proj_other))
    cot_rows = jnp.where(tensor_at == 0, jnp.concatenate([cot_own, cot_other]),
                         jnp.concatenate([cot_other, cot_own]))

    pairs = half // 128
    first = attend_backward(flags, queries, key_rows, value_rows, attended_grad, log_sums, pairs, pairs)
    second = attend_backward(flags, queries, key_rows, value_rows, attended_grad, log_sums, 0, pairs)
    head_grads = list(second[:3]) + list(first[:3])
    in_mine, in_send, in_sums = input_grad(
        place, head_grads, res_own, res_other, middle_grad, gains[0:1], qkv_weight, qkv_other)

    hid = fc_bias.shape[0]
    if n_dp == 4:
        proj_grads = [weight_grad(place, active, [cot_rows], D, left_cols=hid, left_at=n) for n in range(2)]
        fc_grads = [weight_grad(place, normed_two, [hidden_grad], hid, col_at=n) for n in range(2)]
        out_keep, out_push = out_grad(place, attended, branch_grad)
        qkv_grads = [weight_grad(place, normed_one, list(part[:3]), half) for part in (second, first)]
        proj_shard = reduce_x_first(*proj_grads, n_dp, n_tensor)
        fc_shard = reduce_y_first(*fc_grads, n_dp, n_tensor)
        got = swap(out_push, "dp", 1, n_dp)
        far = swap(add_low(out_keep[1], got[1]), "dp", 2, n_dp)
        near = add_low(out_keep[0], got[0], far)
        out_shard = add_low(near[0], swap(near[1], "tensor", 1, n_tensor))
        qkv_shard = reduce_x_first(*qkv_grads, n_dp, n_tensor)
    else:
        def scatter(own, other, dim):
            total = [lax.psum_scatter(value.astype(BF16), "dp", scatter_dimension=dim, tiled=True)
                     for value in (own, other)]
            return add_low(total[0], swap(total[1], "tensor", 1, n_tensor))

        proj_shard = scatter(dot_tn(active[:, :hid], cot_rows), dot_tn(active[:, hid:], cot_rows), 0)
        fc_shard = scatter(dot_tn(normed_two, hidden_grad[:, :hid]), dot_tn(normed_two, hidden_grad[:, hid:]), 0)
        out_shard = scatter(dot_tn(attended[:, :half], branch_grad), dot_tn(attended[:, half:], branch_grad), 0)
        qkv_shard = scatter(
            *[jnp.stack([dot_tn(normed_one, value) for value in part[:3]], 1) for part in (second, first)], 0)

    proj_shard = chain_sum(proj_shard, n_group, group_at)
    fc_shard = chain_sum(fc_shard, n_group, group_at)
    out_shard = chain_sum(out_shard, n_group, group_at)
    qkv_shard = chain_sum(qkv_shard, n_group, group_at)

    def natural(own, other):
        return jnp.where(tensor_at == 0, jnp.concatenate([own, other], -1), jnp.concatenate([other, own], -1))

    small = jnp.concatenate([
        in_sums[0], middle_sums[0, :D], middle_sums[1, :D], middle_sums[2, :D],
        natural(second[3][0], first[3][0]), natural(second[3][1], first[3][1]),
        natural(middle_sums[3, :hid], middle_sums[3, hid:])]).reshape(-1, 128)
    small = all_sum(small, sizes, group_at).reshape(-1)
    grad_gains = small[: 2 * D].reshape(2, D)
    grad_out_biases = small[2 * D : 4 * D].reshape(2, D)[:, : D - 1]
    part = half // n_dp
    grad_qv_bias = lax.dynamic_slice_in_dim(
        small[4 * D : 6 * D].reshape(2, D), tensor_at * half + dp_at * part, part, 1)
    part = hid // n_dp
    grad_fc_bias = lax.dynamic_slice_in_dim(small[6 * D :], tensor_at * hid + dp_at * part, part, 0)

    def restore(mine, send):
        got = swap(send, "tensor", 1, n_tensor)
        return jnp.where(tensor_at == 0, jnp.stack([mine, got]), jnp.stack([got, mine]))[:, :, : D - 1]

    return (
        restore(out_mine, out_send),
        restore(in_mine, in_send),
        grad_gains,
        jnp.swapaxes(qkv_shard, 0, 1).astype(F32) if n_dp != 4 else qkv_shard.astype(F32),
        grad_qv_bias,
        out_shard[:, : D - 1].astype(F32),
        fc_shard.astype(F32),
        grad_fc_bias,
        proj_shard[:, : D - 1].astype(F32),
        grad_out_biases,
    )


def solution(mesh):
    sizes = (mesh.shape["dp"], mesh.shape["group"], mesh.shape["tensor"])
    in_specs = (
        P(("dp", "group"), "tensor", None),
        P(("dp", "group"), None),
        P(),
        P(None, None, "tensor"),
        P(None, "tensor"),
        P("tensor", None),
        P(None, "tensor"),
        P("tensor"),
        P("tensor", None),
        P(),
        P(("dp", "group"), "tensor", None),
    )
    out_specs = (
        P(("dp", "group"), "tensor", None),
        P(("dp", "group"), "tensor", None),
        P(),
        P(None, "dp", "tensor"),
        P(None, ("tensor", "dp")),
        P(("tensor", "dp"), None),
        P("dp", "tensor"),
        P(("tensor", "dp")),
        P(("tensor", "dp"), None),
        P(),
    )
    return jax.shard_map(
        functools.partial(on_device, sizes), mesh=mesh, in_specs=in_specs, out_specs=out_specs,
        check_vma=False)
```

time: 1040 us -> 466 us (0.45)
  waiting for transfers between devices: 468 us -> 132 us
  matrix products: 207 us -> 0 us
  Pallas kernels: 0 us -> 165 us
  local copies, waits for them, and re-layouts: 161 us -> 53.4 us
  other arithmetic: 114 us -> 27.4 us
  starting transfers between devices: 0.98 us -> 76.5 us
  blocking collectives: 57.5 us -> 0 us
  between operations: 15.6 us -> 1.66 us
    reduce_scatter x7 -> x0, waiting for transfers between devices: 220 us -> none  [the longest x1 42.1 us: on_device(): lax.psum_scatter(branch_part.astype(jnp.bfloat16), 'tensor', scatter_dime...]
    dot_general x40 -> x0, matrix products: 207 us -> none  [the longest x4 33.1 us: attend_backward(): jnp.einsum('qhd,khd->hqk', row_up, value_rows, preferred_element_type=jnp...]
    pallas_call x0 -> x13, Pallas kernels: none -> 165 us  [the longest x6 39.4 us: weight_grad(): pl.pallas_call(functools.partial(weight_grad_kernel, rows=rows, rights=ma...]
    all_gather x4 -> x0, waiting for transfers between devices: 161 us -> none  [the longest x1 47.5 us: on_device(): full_one = lax.all_gather(one_low, 'tensor', axis=1, tiled=True)]
    ppermute x0 -> x56, waiting for transfers between devices: none -> 132 us  [the longest x41 78.5 us: swap(): return lax.ppermute(value, axis, [(n, n ^ bit) for n in range(size)])]
    ppermute x0 -> x56, starting transfers between devices: none -> 76.5 us  [the longest x5 33.7 us: chain_sum(): inward = lax.ppermute(value, 'group', [(0, 1), (3, 2)])]
    psum x1 -> x0, waiting for transfers between devices: 71.2 us -> none  [on_device(): lax.psum(shards[0].astype(jnp.bfloat16), 'group').astype(jnp.float32)]
    psum x2 -> x0, blocking collectives: 51.4 us -> none  [the longest x1 39.6 us: on_device(): lax.psum((gain_terms, bias_terms), ('dp', 'group', 'tensor'))]
  transfers between devices with their start and end apart: 14 -> 56, of which waited for: 13 -> 24; matrix products, arithmetic and copies ran while one was open for 10% -> 16% of each run, Pallas kernels for 0% -> 17%
where the time goes in v1:
time: 466 us; the launch traced here: 457 us
  Pallas kernels  165 us (35%)
  waiting for transfers between devices  132 us (28%)
  starting transfers between devices  76.5 us (16%)
  local copies, waits for them, and re-layouts  53.4 us (11%)
  other arithmetic  27.4 us (6%)
    ppermute x41, waiting for transfers between devices, swap(): return lax.ppermute(value, axis, [(n, n ^ bit) for n in range(size)])  78.5 us
    pallas_call x6, Pallas kernels, weight_grad(): pl.pallas_call(functools.partial(weight_grad_kernel, rows=rows, rights=ma...  39.4 us
    pallas_call x1, Pallas kernels, middle_stage(): pl.pallas_call(body, grid_spec=pltpu.PrefetchScalarGridSpec(num_scalar_pr...  37.8 us
    pallas_call x2, Pallas kernels, attend_backward(): pl.pallas_call(functools.partial(attend_backward_kernel, block=block), gr...  36.6 us
    ppermute x5, waiting for transfers between devices, chain_sum(): outward = lax.ppermute(total, 'group', [(1, 0), (2, 3)])  34.2 us
    ppermute x5, starting transfers between devices, chain_sum(): inward = lax.ppermute(value, 'group', [(0, 1), (3, 2)])  33.7 us
    ppermute x41, starting transfers between devices, swap(): return lax.ppermute(value, axis, [(n, n ^ bit) for n in range(size)])  33 us
    dynamic_slice x5, local copies, waits for them, and re-layouts, half_rows(): return jnp.pad(lax.dynamic_index_in_dim(value, at, 0, keepdims=False), pad)  23.9 us
  transfers between devices with their start and end apart: 56, of which 24 were waited for; matrix products, arithmetic and copies ran while one was open for 16% of the time, Pallas kernels for 17%

profile of v1, /device:TPU:0, one launch (start us, length us, event | category | flops | bytes accessed | tf_op | source)
XLA Modules:
  0.0 456.5 jit_solution(17933970894435189545)
XLA Ops:
  1.9 3.0 collective-permute-start.2
  7.3 2.1 collective-permute-start.7
  9.4 1.9 constant_dynamic-slice_fusion.2
  12.2 2.0 collective-permute-start.15
  14.2 5.1 %collective-permute-done.7.refs_9_ = bf16[96,768]{1,0:T(8,128)(2,1)S(1)} collective-permute-done((bf16[96,768]{1,0:T(8,128)(2,1)S(1)}, bf16[96,768]{1,0:T(8,128)(2,1)S(1)}, u32[]{:S(2)}, u32[]{:S(2)}) %collective-permute-start.7) | collective-permute-done | bytes 147488 | tf_op jit(solution)/shard_map/ppermute | solution.py:542
  19.3 2.0 collective-permute-start.9
  21.4 10.1 %constant_dynamic-slice_fusion.4 = (bf16[1,512,767]{1,0,2:T(2,128)(2,1)}, bf16[1,512,767]{1,0,2:T(2,128)(2,1)}, bf16[1,512,767]{1,0,2:T(2,128)(2,1)}, bf16[1,512,767]{1,0,2:T(2,128)(2,1)}) fusion(bf16[2,512,767]{1,0,2:T(2,128)(2,1)} %param.21, s32[]{:T(128)S(6)} %select_n.109, s32[]{:T(128)S(6)} %select_n.108, bf16[2,512,767]{1,0,2:T(2,128)(2,1)} %param.11), kind=kLoop, calls=%fused_computation.79 | loop fusion | bytes 6283272 | tf_op jit(solution)/shard_map/jit(dynamic_index_in_dim)/dynamic_slice | solution.py:618
  31.5 3.4 copy.22
  35.9 2.0 collective-permute-start
  40.1 1.5 collective-permute-start.13
  41.6 3.0 collective-permute-done.15.refs_19_
  44.7 2.0 collective-permute-start.17
  47.9 4.7 %copy.24 = bf16[1,512,767]{2,1,0:T(8,128)(2,1)} copy(bf16[1,512,767]{1,0,2:T(2,128)(2,1)} %get-tuple-element.109) | data formatting | bytes 1570816 | tf_op jit(solution)/shard_map/jit(dynamic_index_in_dim)/dynamic_slice | solution.py:618
  52.6 2.1 pad.28
  55.3 5.3 %collective-permute-done.other_ref.refs_2_.refs_7_ = bf16[512,768]{1,0:T(8,128)(2,1)S(1)} collective-permute-done((bf16[512,768]{1,0:T(8,128)(2,1)}, bf16[512,768]{1,0:T(8,128)(2,1)S(1)}, u32[]{:S(2)}, u32[]{:S(2)}) %collective-permute-start) | collective-permute-done | bytes 786464 | tf_op jit(solution)/shard_map/ppermute | solution.py:542
  60.6 1.7 collective-permute-start.6
  63.4 5.2 %collective-permute-done.17.refs_21_ = bf16[384,768]{1,0:T(8,128)(2,1)} collective-permute-done((bf16[384,768]{1,0:T(8,128)(2,1)}, bf16[384,768]{1,0:T(8,128)(2,1)}, u32[]{:S(2)}, u32[]{:S(2)}) %collective-permute-start.17) | collective-permute-done | bytes 589856 | tf_op jit(solution)/shard_map/ppermute | solution.py:542
  69.8 1.6 pad.31.refs_18_
  72.3 3.6 copy.21
  76.8 2.2 copy.23
  81.2 10.2 %norm_project.1 = (bf16[1024,768]{1,0:T(8,128)(2,1)}, bf16[1024,768]{1,0:T(8,128)(2,1)}, bf16[1024,768]{1,0:T(8,128)(2,1)}, bf16[1024,768]{1,0:T(8,128)(2,1)}) custom-call(s32[2]{0:T(128)} %pad_add_fusion.place_ref, bf16[512,768]{1,0:T(8,128)(2,1)} %pad.25.own_ref.refs_1_.refs_6_, bf16[512,768]{1,0:T(8,128)(2,1)} %copy-done.3, ...), custom_call_target="tpu_custom_call" | custom-call | tf_op jit(solution)/shard_map/norm_project/pallas_call | solution.py:235
  91.4 22.7 %attend_forward.1 = (bf16[1024,768]{1,0:T(8,128)(2,1)}, f32[6,8,1024]{2,1,0:T(8,128)}) custom-call(s32[4]{0:T(128)} %compare_convert_fusion.flags_ref, bf16[1024,768]{1,0:T(8,128)(2,1)} %get-tuple-element.50.q_ref, bf16[1024,768]{1,0:T(8,128)(2,1)} %get-tuple-element.51.k_ref, bf16[1024,768]{1,0:T(8,128)(2,1)} %get-tuple-element.52.v_ref), custom_call_target="tpu_custom_call" | custom-call | tf_op jit(solution)/shard_map/attend_forward/pallas_call | solution.py:76
  114.1 37.8 %middle_stage.1 = (bf16[1024,768]{1,0:T(8,128)(2,1)}, bf16[1024,3072]{1,0:T(8,128)(2,1)}, bf16[1024,3072]{1,0:T(8,128)(2,1)}, bf16[512,768]{1,0:T(8,128)(2,1)}, ...) custom-call(s32[2]{0:T(128)} %pad_add_fusion.place_ref, ...), custom_call_target="tpu_custom_call" | custom-call | tf_op jit(solution)/shard_map/middle_stage/pallas_call | solution.py:372
  151.9 18.0 %attend_backward.2 = (bf16[1024,384]{1,0:T(8,128)(2,1)}, bf16[1024,384]{1,0:T(8,128)(2,1)}, bf16[1024,384]{1,0:T(8,128)(2,1)}, f32[8,384]{1,0:T(8,128)}) custom-call(s32[4]{0:T(128)} %compare_convert_fusion.flags_ref, bf16[1024,768]{1,0:T(8,128)(2,1)} %get-tuple-element.50.q_ref, bf16[1024,768]{1,0:T(8,128)(2,1)} %get-tuple-element.51.k_ref, ...), custom_call_target="tpu_custom_call" | custom-call | tf_op jit(solution)/shard_map/attend_backward/pallas_call | solution.py:143
  169.9 18.6 %attend_backward.3 = (bf16[1024,384]{1,0:T(8,128)(2,1)}, bf16[1024,384]{1,0:T(8,128)(2,1)}, bf16[1024,384]{1,0:T(8,128)(2,1)}, f32[8,384]{1,0:T(8,128)}) custom-call(s32[4]{0:T(128)} %compare_convert_fusion.flags_ref, bf16[1024,768]{1,0:T(8,128)(2,1)} %get-tuple-element.50.q_ref, bf16[1024,768]{1,0:T(8,128)(2,1)} %get-tuple-element.51.k_ref, ...), custom_call_target="tpu_custom_call" | custom-call | tf_op jit(solution)/shard_map/attend_backward/pallas_call | solution.py:143
  190.3 13.6 %input_grad.1 = (bf16[512,768]{1,0:T(8,128)(2,1)}, bf16[512,768]{1,0:T(8,128)(2,1)}, f32[8,768]{1,0:T(8,128)}) custom-call(s32[2]{0:T(128)} %pad_add_fusion.place_ref, bf16[1024,384]{1,0:T(8,128)(2,1)} %get-tuple-element.58.refs_0_.refs_1_, bf16[1024,384]{1,0:T(8,128)(2,1)} %get-tuple-element.59.refs_1_.refs_2_, ...), custom_call_target="tpu_custom_call" | custom-call | tf_op jit(solution)/shard_map/input_grad/pallas_call | solution.py:525
  209.2 2.4 collective-permute-done.22
  211.9 3.7 collective-permute-done.23
  215.6 3.5 collective-permute-start.24
  219.0 1.6 collective-permute-done.24
  222.6 3.1 maximum_select_fusion.refs_1_
  225.8 6.7 %weight_grad.10 = (bf16[2,384,768]{2,1,0:T(8,128)(2,1)}, bf16[2,384,768]{2,1,0:T(8,128)(2,1)}) custom-call(s32[2]{0:T(128)} %pad_add_fusion.place_ref, bf16[1024,3072]{1,0:T(8,128)(2,1)} %get-tuple-element.85.refs_0_, bf16[1024,768]{1,0:T(8,128)(2,1)} %maximum_select_fusion.refs_1_), custom_call_target="tpu_custom_call" | custom-call | tf_op jit(solution)/shard_map/weight_grad/pallas_call | solution.py:423
  232.5 6.5 %weight_grad.11 = (bf16[2,384,768]{2,1,0:T(8,128)(2,1)}, bf16[2,384,768]{2,1,0:T(8,128)(2,1)}) custom-call(s32[2]{0:T(128)} %pad_add_fusion.place_ref, bf16[1024,3072]{1,0:T(8,128)(2,1)} %get-tuple-element.85.refs_0_, bf16[1024,768]{1,0:T(8,128)(2,1)} %maximum_select_fusion.refs_1_), custom_call_target="tpu_custom_call" | custom-call | tf_op jit(solution)/shard_map/weight_grad/pallas_call | solution.py:423
  239.0 6.8 %weight_grad.8 = (bf16[2,192,1536]{2,1,0:T(8,128)(2,1)}, bf16[2,192,1536]{2,1,0:T(8,128)(2,1)}) custom-call(s32[2]{0:T(128)} %pad_add_fusion.place_ref, bf16[1024,768]{1,0:T(8,128)(2,1)} %get-tuple-element.79.refs_0_, bf16[1024,3072]{1,0:T(8,128)(2,1)} %get-tuple-element.80.refs_1_), custom_call_target="tpu_custom_call" | custom-call | tf_op jit(solution)/shard_map/weight_grad/pallas_call | solution.py:423
  245.8 6.7 %weight_grad.9 = (bf16[2,192,1536]{2,1,0:T(8,128)(2,1)}, bf16[2,192,1536]{2,1,0:T(8,128)(2,1)}) custom-call(s32[2]{0:T(128)} %pad_add_fusion.place_ref, bf16[1024,768]{1,0:T(8,128)(2,1)} %get-tuple-element.79.refs_0_, bf16[1024,3072]{1,0:T(8,128)(2,1)} %get-tuple-element.80.refs_1_), custom_call_target="tpu_custom_call" | custom-call | tf_op jit(solution)/shard_map/weight_grad/pallas_call | solution.py:423
  252.5 6.3 %weight_grad.6 = (bf16[2,3,192,384]{3,2,1,0:T(8,128)(2,1)}, bf16[2,3,192,384]{3,2,1,0:T(8,128)(2,1)}) custom-call(s32[2]{0:T(128)} %pad_add_fusion.place_ref, bf16[1024,768]{1,0:T(8,128)(2,1)} %get-tuple-element.71.refs_0_, bf16[1024,384]{1,0:T(8,128)(2,1)} %get-tuple-element.58.refs_0_.refs_1_, bf16[1024,384]{1,0:T(8,128)(2,1)} %get-tuple-element.59.refs_1_.refs_2_, ...), custom_call_target="tpu_custom_call" | custom-call | tf_op jit(solution)/shard_map/weight_grad/pallas_call | solution.py:423
  258.8 6.3 %weight_grad.7 = (bf16[2,3,192,384]{3,2,1,0:T(8,128)(2,1)}, bf16[2,3,192,384]{3,2,1,0:T(8,128)(2,1)}) custom-call(s32[2]{0:T(128)} %pad_add_fusion.place_ref, bf16[1024,768]{1,0:T(8,128)(2,1)} %get-tuple-element.71.refs_0_, bf16[1024,384]{1,0:T(8,128)(2,1)} %get-tuple-element.61.refs_3_.refs_1_, bf16[1024,384]{1,0:T(8,128)(2,1)} %get-tuple-element.62.refs_4_.refs_2_, ...), custom_call_target="tpu_custom_call" | custom-call | tf_op jit(solution)/shard_map/weight_grad/pallas_call | solution.py:423
  265.1 5.1 %out_grad.1 = (bf16[2,2,96,768]{3,2,1,0:T(8,128)(2,1)}, bf16[2,2,96,768]{3,2,1,0:T(8,128)(2,1)}) custom-call(s32[2]{0:T(128)} %pad_add_fusion.place_ref, bf16[1024,768]{1,0:T(8,128)(2,1)} %get-tuple-element.53.refs_0_.left_ref, bf16[1024,768]{1,0:T(8,128)(2,1)} %get-tuple-element.76.right_ref), custom_call_target="tpu_custom_call" | custom-call | tf_op jit(solution)/shard_map/out_grad/pallas_call | solution.py:452
  271.2 1.6 collective-permute-start.19
  275.3 2.0 fusion.14
  277.3 14.0 %collective-permute-done.20 = bf16[512,768]{1,0:T(8,128)(2,1)S(1)} collective-permute-done((bf16[512,768]{1,0:T(8,128)(2,1)}, bf16[512,768]{1,0:T(8,128)(2,1)S(1)}, u32[]{:S(2)}, u32[]{:S(2)}) %collective-permute-start.20) | collective-permute-done | bytes 786464 | tf_op jit(solution)/shard_map/ppermute | solution.py:542
  292.2 1.8 fusion
  294.0 3.0 copy.26
  297.0 10.9 %collective-permute-done.19 = bf16[512,768]{1,0:T(8,128)(2,1)} collective-permute-done((bf16[512,768]{1,0:T(8,128)(2,1)}, bf16[512,768]{1,0:T(8,128)(2,1)}, u32[]{:S(2)}, u32[]{:S(2)}) %collective-permute-start.19) | collective-permute-done | bytes 786464 | tf_op jit(solution)/shard_map/ppermute | solution.py:542
  307.9 1.8 fusion.1
  309.7 3.2 copy.25
  312.9 1.6 collective-permute-start.36
  317.2 5.2 %collective-permute-done.36 = bf16[2,96,768]{2,1,0:T(8,128)(2,1)S(1)} collective-permute-done((bf16[2,96,768]{2,1,0:T(8,128)(2,1)S(1)}, bf16[2,96,768]{2,1,0:T(8,128)(2,1)S(1)}, u32[]{:S(2)}, u32[]{:S(2)}) %collective-permute-start.36) | collective-permute-done | bytes 294944 | tf_op jit(solution)/shard_map/ppermute | solution.py:542
  322.4 1.5 collective-permute-start.30
  329.6 5.9 %collective-permute-done.30 = bf16[3,192,384]{2,1,0:T(8,128)(2,1)S(1)} collective-permute-done((bf16[3,192,384]{2,1,0:T(8,128)(2,1)S(1)}, bf16[3,192,384]{2,1,0:T(8,128)(2,1)S(1)}, u32[]{:S(2)}, u32[]{:S(2)}) %collective-permute-start.30) | collective-permute-done | bytes 442400 | tf_op jit(solution)/shard_map/ppermute | solution.py:542
  335.5 1.5 collective-permute-start.28
  338.2 9.9 %collective-permute-done.51 = bf16[384,768]{1,0:T(8,128)(2,1)S(1)} collective-permute-done((bf16[384,768]{1,0:T(8,128)(2,1)S(1)}, bf16[384,768]{1,0:T(8,128)(2,1)S(1)}, u32[]{:S(2)}, u32[]{:S(2)}) %collective-permute-start.51) | collective-permute-done | bytes 589856 | tf_op jit(solution)/shard_map/ppermute | solution.py:542
  351.5 1.8 collective-permute-done.43
  354.0 2.5 collective-permute-done.37
  357.6 9.3 %collective-permute-start.38 = (bf16[96,768]{1,0:T(8,128)(2,1)S(1)}, bf16[96,768]{1,0:T(8,128)(2,1)S(1)}, u32[]{:S(2)}, u32[]{:S(2)}) collective-permute-start(bf16[96,768]{1,0:T(8,128)(2,1)S(1)} %fusion.15), channel_id=1, source_target_pairs={{0,2},{6,4},{1,3},{7,5},{8,10},{14,12},{9,11},{15,13},{16,18},{22,... | collective-permute-start | bytes 442376 | tf_op jit(solution)/shard_map/ppermute | solution.py:567
  368.2 8.4 %collective-permute-start.32 = (bf16[3,192,384]{2,1,0:T(8,128)(2,1)S(1)}, bf16[3,192,384]{2,1,0:T(8,128)(2,1)S(1)}, u32[]{:S(2)}, u32[]{:S(2)}) collective-permute-start(bf16[3,192,384]{2,1,0:T(8,128)(2,1)S(1)} %add_convert_fusion.11), channel_id=1, source_target_pairs={{0,2},{6,4},{1,3},{7,5},{8,10},{14,12},{9,11},{15,13},{16,18},{22,... | collective-permute-start | bytes 1327112 | tf_op jit(solution)/shard_map/ppermute | solution.py:567
  378.4 9.3 %collective-permute-start.53 = (bf16[384,768]{1,0:T(8,128)(2,1)S(1)}, bf16[384,768]{1,0:T(8,128)(2,1)S(1)}, u32[]{:S(2)}, u32[]{:S(2)}) collective-permute-start(bf16[384,768]{1,0:T(8,128)(2,1)S(1)} %add_convert_fusion.3), channel_id=1, source_target_pairs={{0,2},{6,4},{1,3},{7,5},{8,10},{14,12},{9,11},{15,13},{16,18},{22,... | collective-permute-start | bytes 1769480 | tf_op jit(solution)/shard_map/ppermute | solution.py:567
  388.1 3.2 collective-permute-start.45
  392.8 8.7 %collective-permute-done.53 = bf16[384,768]{1,0:T(8,128)(2,1)S(1)} collective-permute-done((bf16[384,768]{1,0:T(8,128)(2,1)S(1)}, bf16[384,768]{1,0:T(8,128)(2,1)S(1)}, u32[]{:S(2)}, u32[]{:S(2)}) %collective-permute-start.53) | collective-permute-done | bytes 589856 | tf_op jit(solution)/shard_map/ppermute | solution.py:567
  402.4 9.3 %collective-permute-done.45 = bf16[192,1536]{1,0:T(8,128)(2,1)S(1)} collective-permute-done((bf16[192,1536]{1,0:T(8,128)(2,1)S(1)}, bf16[192,1536]{1,0:T(8,128)(2,1)S(1)}, u32[]{:S(2)}, u32[]{:S(2)}) %collective-permute-start.45) | collective-permute-done | bytes 589856 | tf_op jit(solution)/shard_map/ppermute | solution.py:567
  418.2 5.7 %collective-permute-done.40 = bf16[96,768]{1,0:T(8,128)(2,1)S(1)} collective-permute-done((bf16[96,768]{1,0:T(8,128)(2,1)S(1)}, bf16[96,768]{1,0:T(8,128)(2,1)S(1)}, u32[]{:S(2)}, u32[]{:S(2)}) %collective-permute-start.40) | collective-permute-done | bytes 147488 | tf_op jit(solution)/shard_map/ppermute | solution.py:571
  424.6 8.7 %collective-permute-done.34 = bf16[3,192,384]{2,1,0:T(8,128)(2,1)S(1)} collective-permute-done((bf16[3,192,384]{2,1,0:T(8,128)(2,1)S(1)}, bf16[3,192,384]{2,1,0:T(8,128)(2,1)S(1)}, u32[]{:S(2)}, u32[]{:S(2)}) %collective-permute-start.34) | collective-permute-done | bytes 442400 | tf_op jit(solution)/shard_map/ppermute | solution.py:571
  434.3 11.7 %collective-permute-done.55 = bf16[384,768]{1,0:T(8,128)(2,1)S(1)} collective-permute-done((bf16[384,768]{1,0:T(8,128)(2,1)S(1)}, bf16[384,768]{1,0:T(8,128)(2,1)S(1)}, u32[]{:S(2)}, u32[]{:S(2)}) %collective-permute-start.55) | collective-permute-done | bytes 589856 | tf_op jit(solution)/shard_map/ppermute | solution.py:571
  447.1 8.1 %collective-permute-done.47 = bf16[192,1536]{1,0:T(8,128)(2,1)S(1)} collective-permute-done((bf16[192,1536]{1,0:T(8,128)(2,1)S(1)}, bf16[192,1536]{1,0:T(8,128)(2,1)S(1)}, u32[]{:S(2)}, u32[]{:S(2)}) %collective-permute-start.47) | collective-permute-done | bytes 589856 | tf_op jit(solution)/shard_map/ppermute | solution.py:571
  (202 shorter events, 60.3 us)
Async XLA Ops:
  0.6 46.1 %copy-start = (s32[2,1024]{1,0:T(2,128)S(1)}, s32[2,1024]{1,0:T(2,128)}, u32[]{:S(2)}) copy-start(s32[2,1024]{1,0:T(2,128)} %param.12) | copy-start | bytes 24580
  1.9 19.4 %collective-permute-start.2 = (bf16[3,192,384]{2,1,0:T(8,128)(2,1)S(1)}, bf16[3,192,384]{2,1,0:T(8,128)(2,1)}, u32[]{:S(2)}, u32[]{:S(2)}) collective-permute-start(bf16[3,192,384]{2,1,0:T(8,128)(2,1)S(1)} %constant_dynamic-slice_fusion.6), channel_id=1, source_target_pairs={{0,1},{1,0},{2,3},{3,2},{4,5},{5,4},{6,7},{7,6},{8,9},{9,8},{10,11... | collective-permute-start | bytes 1327112 | tf_op jit(solution)/shard_map/ppermute | solution.py:542
  6.3 29.6 %collective-permute-start.1 = (bf16[1,2304]{1,0:T(2,128)(2,1)S(1)}, bf16[1,2304]{1,0:T(2,128)(2,1)S(1)}, u32[]{:S(2)}, u32[]{:S(2)}) collective-permute-start(bf16[1,2304]{1,0:T(2,128)(2,1)S(1)} %pad_maximum_fusion.4), channel_id=1, source_target_pairs={{0,1},{1,0},{2,3},{3,2},{4,5},{5,4},{6,7},{7,6},{8,9},{9,8},{10,11... | collective-permute-start | bytes 13832 | tf_op jit(solution)/shard_map/ppermute | solution.py:542
  7.3 11.9 %collective-permute-start.7 = (bf16[96,768]{1,0:T(8,128)(2,1)S(1)}, bf16[96,768]{1,0:T(8,128)(2,1)S(1)}, u32[]{:S(2)}, u32[]{:S(2)}) collective-permute-start(bf16[96,768]{1,0:T(8,128)(2,1)S(1)} %constant_dynamic-slice_fusion.3), channel_id=1, source_target_pairs={{0,1},{1,0},{2,3},{3,2},{4,5},{5,4},{6,7},{7,6},{8,9},{9,8},{10,11... | collective-permute-start | bytes 442376 | tf_op jit(solution)/shard_map/ppermute | solution.py:542
  11.3 28.8 %collective-permute-start.11 = (bf16[192,1536]{1,0:T(8,128)(2,1)}, bf16[192,1536]{1,0:T(8,128)(2,1)}, u32[]{:S(2)}, u32[]{:S(2)}) collective-permute-start(bf16[192,1536]{1,0:T(8,128)(2,1)} %constant_dynamic-slice_fusion.2), channel_id=1, source_target_pairs={{0,1},{1,0},{2,3},{3,2},{4,5},{5,4},{6,7},{7,6},{8,9},{9,8},{10,11... | collective-permute-start | bytes 1769480 | tf_op jit(solution)/shard_map/ppermute | solution.py:542
  12.2 32.5 %collective-permute-start.15 = (bf16[384,768]{1,0:T(8,128)(2,1)}, bf16[384,768]{1,0:T(8,128)(2,1)}, u32[]{:S(2)}, u32[]{:S(2)}) collective-permute-start(bf16[384,768]{1,0:T(8,128)(2,1)} %constant_dynamic-slice_fusion.1), channel_id=1, source_target_pairs={{0,1},{1,0},{2,3},{3,2},{4,5},{5,4},{6,7},{7,6},{8,9},{9,8},{10,11... | collective-permute-start | bytes 1769480 | tf_op jit(solution)/shard_map/ppermute | solution.py:542
  19.3 18.6 %copy-start.20 = (bf16[96,768]{1,0:T(8,128)(2,1)}, bf16[96,768]{1,0:T(8,128)(2,1)S(1)}, u32[]{:S(2)}) copy-start(bf16[96,768]{1,0:T(8,128)(2,1)S(1)} %collective-permute-done.7.refs_9_) | copy-start | bytes 442372
  19.3 18.6 %collective-permute-start.9 = (bf16[96,768]{1,0:T(8,128)(2,1)S(1)}, bf16[96,768]{1,0:T(8,128)(2,1)S(1)}, u32[]{:S(2)}, u32[]{:S(2)}) collective-permute-start(bf16[96,768]{1,0:T(8,128)(2,1)S(1)} %collective-permute-done.7.refs_9_), channel_id=1, source_target_pairs={{0,16},{8,24},{16,0},{24,8},{1,17},{9,25},{17,1},{25,9},{2,18},{10... | collective-permute-start | bytes 442376 | tf_op jit(solution)/shard_map/ppermute | solution.py:542
  21.3 25.6 %collective-permute-start.4 = (bf16[3,192,384]{2,1,0:T(8,128)(2,1)}, bf16[3,192,384]{2,1,0:T(8,128)(2,1)}, u32[]{:S(2)}, u32[]{:S(2)}) collective-permute-start(bf16[3,192,384]{2,1,0:T(8,128)(2,1)} %collective-permute-done.2.a.refs_11_), channel_id=1, source_target_pairs={{0,16},{8,24},{16,0},{24,8},{1,17},{9,25},{17,1},{25,9},{2,18},{10... | collective-permute-start | bytes 1327112 | tf_op jit(solution)/shard_map/ppermute | solution.py:542
  35.9 24.7 %collective-permute-start = (bf16[512,768]{1,0:T(8,128)(2,1)}, bf16[512,768]{1,0:T(8,128)(2,1)S(1)}, u32[]{:S(2)}, u32[]{:S(2)}) collective-permute-start(bf16[512,768]{1,0:T(8,128)(2,1)} %pad.26), channel_id=1, source_target_pairs={{0,1},{1,0},{2,3},{3,2},{4,5},{5,4},{6,7},{7,6},{8,9},{9,8},{10,11... | collective-permute-start | bytes 2359304 | tf_op jit(solution)/shard_map/ppermute | solution.py:542
  37.9 16.8 %copy-start.21 = (bf16[96,768]{1,0:T(8,128)(2,1)}, bf16[96,768]{1,0:T(8,128)(2,1)S(1)}, u32[]{:S(2)}) copy-start(bf16[96,768]{1,0:T(8,128)(2,1)S(1)} %collective-permute-done.9.refs_11_) | copy-start | bytes 442372
  37.9 1.4 collective-permute-start.8
  40.0 6.8 %collective-permute-start.10 = (bf16[96,768]{1,0:T(8,128)(2,1)S(1)}, bf16[96,768]{1,0:T(8,128)(2,1)S(1)}, u32[]{:S(2)}, u32[]{:S(2)}) collective-permute-start(bf16[96,768]{1,0:T(8,128)(2,1)S(1)} %collective-permute-done.9.refs_11_), channel_id=1, source_target_pairs={{0,8},{8,0},{16,24},{24,16},{1,9},{9,1},{17,25},{25,17},{2,10},{10... | collective-permute-start | bytes 442376 | tf_op jit(solution)/shard_map/ppermute | solution.py:542
  40.1 22.8 %collective-permute-start.13 = (bf16[192,1536]{1,0:T(8,128)(2,1)}, bf16[192,1536]{1,0:T(8,128)(2,1)}, u32[]{:S(2)}, u32[]{:S(2)}) collective-permute-start(bf16[192,1536]{1,0:T(8,128)(2,1)} %collective-permute-done.11.refs_14_), channel_id=1, source_target_pairs={{0,16},{8,24},{16,0},{24,8},{1,17},{9,25},{17,1},{25,9},{2,18},{10... | collective-permute-start | bytes 1769480 | tf_op jit(solution)/shard_map/ppermute | solution.py:542
  44.7 24.0 %collective-permute-start.17 = (bf16[384,768]{1,0:T(8,128)(2,1)}, bf16[384,768]{1,0:T(8,128)(2,1)}, u32[]{:S(2)}, u32[]{:S(2)}) collective-permute-start(bf16[384,768]{1,0:T(8,128)(2,1)} %collective-permute-done.15.refs_19_), channel_id=1, source_target_pairs={{0,16},{8,24},{16,0},{24,8},{1,17},{9,25},{17,1},{25,9},{2,18},{10... | collective-permute-start | bytes 1769480 | tf_op jit(solution)/shard_map/ppermute | solution.py:542
  46.8 16.1 %collective-permute-start.3 = (bf16[3,192,384]{2,1,0:T(8,128)(2,1)}, bf16[3,192,384]{2,1,0:T(8,128)(2,1)}, u32[]{:S(2)}, u32[]{:S(2)}) collective-permute-start(bf16[3,192,384]{2,1,0:T(8,128)(2,1)} %collective-permute-done.2.a.refs_11_), channel_id=1, source_target_pairs={{0,8},{8,0},{16,24},{24,16},{1,9},{9,1},{17,25},{25,17},{2,10},{10... | collective-permute-start | bytes 1327112 | tf_op jit(solution)/shard_map/ppermute | solution.py:542
  46.9 21.8 %collective-permute-start.5 = (bf16[3,192,384]{2,1,0:T(8,128)(2,1)}, bf16[3,192,384]{2,1,0:T(8,128)(2,1)}, u32[]{:S(2)}, u32[]{:S(2)}) collective-permute-start(bf16[3,192,384]{2,1,0:T(8,128)(2,1)} %collective-permute-done.4.c.refs_13_), channel_id=1, source_target_pairs={{0,8},{8,0},{16,24},{24,16},{1,9},{9,1},{17,25},{25,17},{2,10},{10... | collective-permute-start | bytes 1327112 | tf_op jit(solution)/shard_map/ppermute | solution.py:542
  60.6 53.5 %collective-permute-start.6 = (bf16[512,768]{1,0:T(8,128)(2,1)}, bf16[512,768]{1,0:T(8,128)(2,1)}, u32[]{:S(2)}, u32[]{:S(2)}) collective-permute-start(bf16[512,768]{1,0:T(8,128)(2,1)} %pad.28), channel_id=1, source_target_pairs={{0,1},{1,0},{2,3},{3,2},{4,5},{5,4},{6,7},{7,6},{8,9},{9,8},{10,11... | collective-permute-start | bytes 2359304 | tf_op jit(solution)/shard_map/ppermute | solution.py:542
  62.9 51.2 %collective-permute-start.12 = (bf16[192,1536]{1,0:T(8,128)(2,1)}, bf16[192,1536]{1,0:T(8,128)(2,1)}, u32[]{:S(2)}, u32[]{:S(2)}) collective-permute-start(bf16[192,1536]{1,0:T(8,128)(2,1)} %collective-permute-done.11.refs_14_), channel_id=1, source_target_pairs={{0,8},{8,0},{16,24},{24,16},{1,9},{9,1},{17,25},{25,17},{2,10},{10... | collective-permute-start | bytes 1769480 | tf_op jit(solution)/shard_map/ppermute | solution.py:542
  62.9 51.2 %collective-permute-start.16 = (bf16[384,768]{1,0:T(8,128)(2,1)}, bf16[384,768]{1,0:T(8,128)(2,1)}, u32[]{:S(2)}, u32[]{:S(2)}) collective-permute-start(bf16[384,768]{1,0:T(8,128)(2,1)} %collective-permute-done.15.refs_19_), channel_id=1, source_target_pairs={{0,8},{8,0},{16,24},{24,16},{1,9},{9,1},{17,25},{25,17},{2,10},{10... | collective-permute-start | bytes 1769480 | tf_op jit(solution)/shard_map/ppermute | solution.py:542
  68.7 45.4 %collective-permute-start.14 = (bf16[192,1536]{1,0:T(8,128)(2,1)}, bf16[192,1536]{1,0:T(8,128)(2,1)}, u32[]{:S(2)}, u32[]{:S(2)}) collective-permute-start(bf16[192,1536]{1,0:T(8,128)(2,1)} %collective-permute-done.13.refs_16_), channel_id=1, source_target_pairs={{0,8},{8,0},{16,24},{24,16},{1,9},{9,1},{17,25},{25,17},{2,10},{10... | collective-permute-start | bytes 1769480 | tf_op jit(solution)/shard_map/ppermute | solution.py:542
  68.7 45.4 %collective-permute-start.18 = (bf16[384,768]{1,0:T(8,128)(2,1)}, bf16[384,768]{1,0:T(8,128)(2,1)}, u32[]{:S(2)}, u32[]{:S(2)}) collective-permute-start(bf16[384,768]{1,0:T(8,128)(2,1)} %collective-permute-done.17.refs_21_), channel_id=1, source_target_pairs={{0,8},{8,0},{16,24},{24,16},{1,9},{9,1},{17,25},{25,17},{2,10},{10... | collective-permute-start | bytes 1769480 | tf_op jit(solution)/shard_map/ppermute | solution.py:542
  190.3 32.4 %copy-start.4 = (bf16[512,768]{1,0:T(8,128)(2,1)S(1)}, bf16[512,768]{1,0:T(8,128)(2,1)}, u32[]{:S(2)}) copy-start(bf16[512,768]{1,0:T(8,128)(2,1)} %pad.27.refs_3_) | copy-start | bytes 2359300
  206.4 1.3 collective-permute-start.21
  207.7 3.9 collective-permute-start.22
  211.6 4.0 collective-permute-start.23
  215.6 5.1 %collective-permute-start.24 = (f32[60,128]{1,0:T(8,128)S(1)}, f32[60,128]{1,0:T(8,128)S(1)}, u32[]{:S(2)}, u32[]{:S(2)}) collective-permute-start(f32[60,128]{1,0:T(8,128)S(1)} %add.192), channel_id=1, source_target_pairs={{0,2},{6,4},{1,3},{7,5},{8,10},{14,12},{9,11},{15,13},{16,18},{22,... | collective-permute-start | bytes 92168 | tf_op jit(solution)/shard_map/ppermute | solution.py:567
  220.6 0.7 collective-permute-start.25
  221.3 49.9 %collective-permute-start.26 = (f32[60,128]{1,0:T(8,128)S(1)}, f32[60,128]{1,0:T(8,128)S(1)}, u32[]{:S(2)}, u32[]{:S(2)}) collective-permute-start(f32[60,128]{1,0:T(8,128)S(1)} %add.194), channel_id=1, source_target_pairs={{2,0},{4,6},{3,1},{5,7},{10,8},{12,14},{11,9},{13,15},{18,16},{20,... | collective-permute-start | bytes 92168 | tf_op jit(solution)/shard_map/ppermute | solution.py:571
  265.1 27.1 %copy-start.14 = (bf16[512,768]{1,0:T(8,128)(2,1)S(1)}, bf16[512,768]{1,0:T(8,128)(2,1)}, u32[]{:S(2)}) copy-start(bf16[512,768]{1,0:T(8,128)(2,1)} %get-tuple-element.65) | copy-start | bytes 2359300
  270.2 5.1 %collective-permute-start.35 = (bf16[2,2,96,768]{3,2,1,0:T(8,128)(2,1)}, bf16[2,2,96,768]{3,2,1,0:T(8,128)(2,1)S(1)}, u32[]{:S(2)}, u32[]{:S(2)}) collective-permute-start(bf16[2,2,96,768]{3,2,1,0:T(8,128)(2,1)} %get-tuple-element.78), channel_id=1, source_target_pairs={{0,8},{8,0},{16,24},{24,16},{1,9},{9,1},{17,25},{25,17},{2,10},{10... | collective-permute-start | bytes 1769480 | tf_op jit(solution)/shard_map/ppermute | solution.py:542
  270.2 42.7 %collective-permute-start.27 = (bf16[2,3,192,384]{3,2,1,0:T(8,128)(2,1)}, bf16[2,3,192,384]{3,2,1,0:T(8,128)(2,1)}, u32[]{:S(2)}, u32[]{:S(2)}) collective-permute-start(bf16[2,3,192,384]{3,2,1,0:T(8,128)(2,1)} %get-tuple-element.73), channel_id=1, source_target_pairs={{0,8},{8,0},{16,24},{24,16},{1,9},{9,1},{17,25},{25,17},{2,10},{10... | collective-permute-start | bytes 2654216 | tf_op jit(solution)/shard_map/ppermute | solution.py:542
  270.8 45.0 %collective-permute-start.29 = (bf16[2,3,192,384]{3,2,1,0:T(8,128)(2,1)}, bf16[2,3,192,384]{3,2,1,0:T(8,128)(2,1)}, u32[]{:S(2)}, u32[]{:S(2)}) collective-permute-start(bf16[2,3,192,384]{3,2,1,0:T(8,128)(2,1)} %get-tuple-element.75), channel_id=1, source_target_pairs={{0,8},{8,0},{16,24},{24,16},{1,9},{9,1},{17,25},{25,17},{2,10},{10... | collective-permute-start | bytes 2654216 | tf_op jit(solution)/shard_map/ppermute | solution.py:542
  270.8 20.5 %collective-permute-start.20 = (bf16[512,768]{1,0:T(8,128)(2,1)}, bf16[512,768]{1,0:T(8,128)(2,1)S(1)}, u32[]{:S(2)}, u32[]{:S(2)}) collective-permute-start(bf16[512,768]{1,0:T(8,128)(2,1)} %get-tuple-element.66), channel_id=1, source_target_pairs={{0,1},{1,0},{2,3},{3,2},{4,5},{5,4},{6,7},{7,6},{8,9},{9,8},{10,11... | collective-permute-start | bytes 2359304 | tf_op jit(solution)/shard_map/ppermute | solution.py:542
  271.2 36.6 %collective-permute-start.19 = (bf16[512,768]{1,0:T(8,128)(2,1)}, bf16[512,768]{1,0:T(8,128)(2,1)}, u32[]{:S(2)}, u32[]{:S(2)}) collective-permute-start(bf16[512,768]{1,0:T(8,128)(2,1)} %get-tuple-element.55), channel_id=1, source_target_pairs={{0,1},{1,0},{2,3},{3,2},{4,5},{5,4},{6,7},{7,6},{8,9},{9,8},{10,11... | collective-permute-start | bytes 2359304 | tf_op jit(solution)/shard_map/ppermute | solution.py:542
  275.3 16.0 %copy-start.17 = (bf16[2,2,96,768]{3,2,1,0:T(8,128)(2,1)}, bf16[2,2,96,768]{3,2,1,0:T(8,128)(2,1)S(1)}, u32[]{:S(2)}) copy-start(bf16[2,2,96,768]{3,2,1,0:T(8,128)(2,1)S(1)} %collective-permute-done.35) | copy-start | bytes 1769476
  275.3 48.7 %collective-permute-start.42 = (bf16[2,192,1536]{2,1,0:T(8,128)(2,1)}, bf16[2,192,1536]{2,1,0:T(8,128)(2,1)S(1)}, u32[]{:S(2)}, u32[]{:S(2)}) collective-permute-start(bf16[2,192,1536]{2,1,0:T(8,128)(2,1)} %get-tuple-element.84), channel_id=1, source_target_pairs={{0,8},{8,0},{16,24},{24,16},{1,9},{9,1},{17,25},{25,17},{2,10},{10... | collective-permute-start | bytes 3538952 | tf_op jit(solution)/shard_map/ppermute | solution.py:542
  291.3 35.9 %collective-permute-start.48 = (bf16[2,384,768]{2,1,0:T(8,128)(2,1)}, bf16[2,384,768]{2,1,0:T(8,128)(2,1)}, u32[]{:S(2)}, u32[]{:S(2)}) collective-permute-start(bf16[2,384,768]{2,1,0:T(8,128)(2,1)} %get-tuple-element.87), channel_id=1, source_target_pairs={{0,8},{8,0},{16,24},{24,16},{1,9},{9,1},{17,25},{25,17},{2,10},{10... | collective-permute-start | bytes 3538952 | tf_op jit(solution)/shard_map/ppermute | solution.py:542
  307.9 17.0 %collective-permute-start.50 = (bf16[2,384,768]{2,1,0:T(8,128)(2,1)}, bf16[2,384,768]{2,1,0:T(8,128)(2,1)}, u32[]{:S(2)}, u32[]{:S(2)}) collective-permute-start(bf16[2,384,768]{2,1,0:T(8,128)(2,1)} %get-tuple-element.89), channel_id=1, source_target_pairs={{0,8},{8,0},{16,24},{24,16},{1,9},{9,1},{17,25},{25,17},{2,10},{10... | collective-permute-start | bytes 3538952 | tf_op jit(solution)/shard_map/ppermute | solution.py:542
  312.9 9.5 %collective-permute-start.36 = (bf16[2,96,768]{2,1,0:T(8,128)(2,1)S(1)}, bf16[2,96,768]{2,1,0:T(8,128)(2,1)S(1)}, u32[]{:S(2)}, u32[]{:S(2)}) collective-permute-start(bf16[2,96,768]{2,1,0:T(8,128)(2,1)S(1)} %copy-done.19), channel_id=1, source_target_pairs={{0,16},{8,24},{16,0},{24,8},{1,17},{9,25},{17,1},{25,9},{2,18},{10... | collective-permute-start | bytes 884744 | tf_op jit(solution)/shard_map/ppermute | solution.py:542
  315.8 35.2 %collective-permute-start.41 = (bf16[2,192,1536]{2,1,0:T(8,128)(2,1)}, bf16[2,192,1536]{2,1,0:T(8,128)(2,1)S(1)}, u32[]{:S(2)}, u32[]{:S(2)}) collective-permute-start(bf16[2,192,1536]{2,1,0:T(8,128)(2,1)} %get-tuple-element.82), channel_id=1, source_target_pairs={{0,8},{8,0},{16,24},{24,16},{1,9},{9,1},{17,25},{25,17},{2,10},{10... | collective-permute-start | bytes 3538952 | tf_op jit(solution)/shard_map/ppermute | solution.py:542
  322.4 13.1 %collective-permute-start.30 = (bf16[3,192,384]{2,1,0:T(8,128)(2,1)S(1)}, bf16[3,192,384]{2,1,0:T(8,128)(2,1)S(1)}, u32[]{:S(2)}, u32[]{:S(2)}) collective-permute-start(bf16[3,192,384]{2,1,0:T(8,128)(2,1)S(1)} %fusion.13), channel_id=1, source_target_pairs={{0,16},{8,24},{16,0},{24,8},{1,17},{9,25},{17,1},{25,9},{2,18},{10... | collective-permute-start | bytes 1327112 | tf_op jit(solution)/shard_map/ppermute | solution.py:542
  324.4 29.0 %collective-permute-start.43 = (bf16[2,192,1536]{2,1,0:T(8,128)(2,1)S(1)}, bf16[2,192,1536]{2,1,0:T(8,128)(2,1)S(1)}, u32[]{:S(2)}, u32[]{:S(2)}) collective-permute-start(bf16[2,192,1536]{2,1,0:T(8,128)(2,1)S(1)} %add_convert_fusion), channel_id=1, source_target_pairs={{0,1},{1,0},{2,3},{3,2},{4,5},{5,4},{6,7},{7,6},{8,9},{9,8},{10,11... | collective-permute-start | bytes 3538952 | tf_op jit(solution)/shard_map/ppermute | solution.py:542
  326.6 21.6 %collective-permute-start.51 = (bf16[384,768]{1,0:T(8,128)(2,1)S(1)}, bf16[384,768]{1,0:T(8,128)(2,1)S(1)}, u32[]{:S(2)}, u32[]{:S(2)}) collective-permute-start(bf16[384,768]{1,0:T(8,128)(2,1)S(1)} %fusion.9), channel_id=1, source_target_pairs={{0,16},{8,24},{16,0},{24,8},{1,17},{9,25},{17,1},{25,9},{2,18},{10... | collective-permute-start | bytes 1769480 | tf_op jit(solution)/shard_map/ppermute | solution.py:542
  327.2 29.3 %collective-permute-start.37 = (bf16[96,768]{1,0:T(8,128)(2,1)S(1)}, bf16[96,768]{1,0:T(8,128)(2,1)S(1)}, u32[]{:S(2)}, u32[]{:S(2)}) collective-permute-start(bf16[96,768]{1,0:T(8,128)(2,1)S(1)} %slice_bitcast_fusion), channel_id=1, source_target_pairs={{0,1},{1,0},{2,3},{3,2},{4,5},{5,4},{6,7},{7,6},{8,9},{9,8},{10,11... | collective-permute-start | bytes 442376 | tf_op jit(solution)/shard_map/ppermute | solution.py:542
  335.5 22.1 %collective-permute-start.28 = (bf16[3,192,384]{2,1,0:T(8,128)(2,1)S(1)}, bf16[3,192,384]{2,1,0:T(8,128)(2,1)S(1)}, u32[]{:S(2)}, u32[]{:S(2)}) collective-permute-start(bf16[3,192,384]{2,1,0:T(8,128)(2,1)S(1)} %fusion.12), channel_id=1, source_target_pairs={{0,16},{8,24},{16,0},{24,8},{1,17},{9,25},{17,1},{25,9},{2,18},{10... | collective-permute-start | bytes 1327112 | tf_op jit(solution)/shard_map/ppermute | solution.py:542
  338.2 15.6 %copy-start.10 = (bf16[2,192,1536]{2,1,0:T(8,128)(2,1)S(1)}, bf16[2,192,1536]{2,1,0:T(8,128)(2,1)}, u32[]{:S(2)}) copy-start(bf16[2,192,1536]{2,1,0:T(8,128)(2,1)} %get-tuple-element.81) | copy-start | bytes 3538948
  348.1 28.4 %collective-permute-start.49 = (bf16[384,768]{1,0:T(8,128)(2,1)S(1)}, bf16[384,768]{1,0:T(8,128)(2,1)S(1)}, u32[]{:S(2)}, u32[]{:S(2)}) collective-permute-start(bf16[384,768]{1,0:T(8,128)(2,1)S(1)} %fusion.8), channel_id=1, source_target_pairs={{0,16},{8,24},{16,0},{24,8},{1,17},{9,25},{17,1},{25,9},{2,18},{10... | collective-permute-start | bytes 1769480 | tf_op jit(solution)/shard_map/ppermute | solution.py:542
  351.0 16.0 %copy-start.12 = (bf16[2,3,192,384]{3,2,1,0:T(8,128)(2,1)S(1)}, bf16[2,3,192,384]{3,2,1,0:T(8,128)(2,1)}, u32[]{:S(2)}) copy-start(bf16[2,3,192,384]{3,2,1,0:T(8,128)(2,1)} %get-tuple-element.72) | copy-start | bytes 2654212
  351.0 15.9 %collective-permute-start.31 = (bf16[3,192,384]{2,1,0:T(8,128)(2,1)S(1)}, bf16[3,192,384]{2,1,0:T(8,128)(2,1)S(1)}, u32[]{:S(2)}, u32[]{:S(2)}) collective-permute-start(bf16[3,192,384]{2,1,0:T(8,128)(2,1)S(1)} %fusion.5), channel_id=1, source_target_pairs={{0,1},{1,0},{2,3},{3,2},{4,5},{5,4},{6,7},{7,6},{8,9},{9,8},{10,11... | collective-permute-start | bytes 1327112 | tf_op jit(solution)/shard_map/ppermute | solution.py:542
  353.3 23.7 %collective-permute-start.52 = (bf16[384,768]{1,0:T(8,128)(2,1)S(1)}, bf16[384,768]{1,0:T(8,128)(2,1)S(1)}, u32[]{:S(2)}, u32[]{:S(2)}) collective-permute-start(bf16[384,768]{1,0:T(8,128)(2,1)S(1)} %fusion.2), channel_id=1, source_target_pairs={{0,1},{1,0},{2,3},{3,2},{4,5},{5,4},{6,7},{7,6},{8,9},{9,8},{10,11... | collective-permute-start | bytes 1769480 | tf_op jit(solution)/shard_map/ppermute | solution.py:542
  356.5 31.3 %collective-permute-start.44 = (bf16[192,1536]{1,0:T(8,128)(2,1)S(1)}, bf16[192,1536]{1,0:T(8,128)(2,1)S(1)}, u32[]{:S(2)}, u32[]{:S(2)}) collective-permute-start(bf16[192,1536]{1,0:T(8,128)(2,1)S(1)} %fusion.7), channel_id=1, source_target_pairs={{0,16},{8,24},{16,0},{24,8},{1,17},{9,25},{17,1},{25,9},{2,18},{10... | collective-permute-start | bytes 1769480 | tf_op jit(solution)/shard_map/ppermute | solution.py:542
  357.6 33.7 %collective-permute-start.38 = (bf16[96,768]{1,0:T(8,128)(2,1)S(1)}, bf16[96,768]{1,0:T(8,128)(2,1)S(1)}, u32[]{:S(2)}, u32[]{:S(2)}) collective-permute-start(bf16[96,768]{1,0:T(8,128)(2,1)S(1)} %fusion.15), channel_id=1, source_target_pairs={{0,2},{6,4},{1,3},{7,5},{8,10},{14,12},{9,11},{15,13},{16,18},{22,... | collective-permute-start | bytes 442376 | tf_op jit(solution)/shard_map/ppermute | solution.py:567
  368.2 23.8 %collective-permute-start.32 = (bf16[3,192,384]{2,1,0:T(8,128)(2,1)S(1)}, bf16[3,192,384]{2,1,0:T(8,128)(2,1)S(1)}, u32[]{:S(2)}, u32[]{:S(2)}) collective-permute-start(bf16[3,192,384]{2,1,0:T(8,128)(2,1)S(1)} %add_convert_fusion.11), channel_id=1, source_target_pairs={{0,2},{6,4},{1,3},{7,5},{8,10},{14,12},{9,11},{15,13},{16,18},{22,... | collective-permute-start | bytes 1327112 | tf_op jit(solution)/shard_map/ppermute | solution.py:567
  378.4 23.1 %collective-permute-start.53 = (bf16[384,768]{1,0:T(8,128)(2,1)S(1)}, bf16[384,768]{1,0:T(8,128)(2,1)S(1)}, u32[]{:S(2)}, u32[]{:S(2)}) collective-permute-start(bf16[384,768]{1,0:T(8,128)(2,1)S(1)} %add_convert_fusion.3), channel_id=1, source_target_pairs={{0,2},{6,4},{1,3},{7,5},{8,10},{14,12},{9,11},{15,13},{16,18},{22,... | collective-permute-start | bytes 1769480 | tf_op jit(solution)/shard_map/ppermute | solution.py:567
  388.1 23.5 %collective-permute-start.45 = (bf16[192,1536]{1,0:T(8,128)(2,1)S(1)}, bf16[192,1536]{1,0:T(8,128)(2,1)S(1)}, u32[]{:S(2)}, u32[]{:S(2)}) collective-permute-start(bf16[192,1536]{1,0:T(8,128)(2,1)S(1)} %fusion.4), channel_id=1, source_target_pairs={{0,2},{6,4},{1,3},{7,5},{8,10},{14,12},{9,11},{15,13},{16,18},{22,... | collective-permute-start | bytes 1769480 | tf_op jit(solution)/shard_map/ppermute | solution.py:567
  391.3 21.2 %collective-permute-start.39 = (bf16[96,768]{1,0:T(8,128)(2,1)S(1)}, bf16[96,768]{1,0:T(8,128)(2,1)S(1)}, u32[]{:S(2)}, u32[]{:S(2)}) collective-permute-start(bf16[96,768]{1,0:T(8,128)(2,1)S(1)} %add_convert_fusion.16), channel_id=1, source_target_pairs={{2,4},{4,2},{3,5},{5,3},{10,12},{12,10},{11,13},{13,11},{18,20},{2... | collective-permute-start | bytes 442376 | tf_op jit(solution)/shard_map/ppermute | solution.py:569
  392.1 21.7 %collective-permute-start.33 = (bf16[3,192,384]{2,1,0:T(8,128)(2,1)S(1)}, bf16[3,192,384]{2,1,0:T(8,128)(2,1)S(1)}, u32[]{:S(2)}, u32[]{:S(2)}) collective-permute-start(bf16[3,192,384]{2,1,0:T(8,128)(2,1)S(1)} %add_convert_fusion.10), channel_id=1, source_target_pairs={{2,4},{4,2},{3,5},{5,3},{10,12},{12,10},{11,13},{13,11},{18,20},{2... | collective-permute-start | bytes 1327112 | tf_op jit(solution)/shard_map/ppermute | solution.py:569
  401.7 13.6 %collective-permute-start.54 = (bf16[384,768]{1,0:T(8,128)(2,1)S(1)}, bf16[384,768]{1,0:T(8,128)(2,1)S(1)}, u32[]{:S(2)}, u32[]{:S(2)}) collective-permute-start(bf16[384,768]{1,0:T(8,128)(2,1)S(1)} %add_convert_fusion.2), channel_id=1, source_target_pairs={{2,4},{4,2},{3,5},{5,3},{10,12},{12,10},{11,13},{13,11},{18,20},{2... | collective-permute-start | bytes 1769480 | tf_op jit(solution)/shard_map/ppermute | solution.py:569
  411.8 5.0 %collective-permute-start.46 = (bf16[192,1536]{1,0:T(8,128)(2,1)S(1)}, bf16[192,1536]{1,0:T(8,128)(2,1)S(1)}, u32[]{:S(2)}, u32[]{:S(2)}) collective-permute-start(bf16[192,1536]{1,0:T(8,128)(2,1)S(1)} %add_convert_fusion.7), channel_id=1, source_target_pairs={{2,4},{4,2},{3,5},{5,3},{10,12},{12,10},{11,13},{13,11},{18,20},{2... | collective-permute-start | bytes 1769480 | tf_op jit(solution)/shard_map/ppermute | solution.py:569
  412.6 11.3 %collective-permute-start.40 = (bf16[96,768]{1,0:T(8,128)(2,1)S(1)}, bf16[96,768]{1,0:T(8,128)(2,1)S(1)}, u32[]{:S(2)}, u32[]{:S(2)}) collective-permute-start(bf16[96,768]{1,0:T(8,128)(2,1)S(1)} %add_convert_fusion.15), channel_id=1, source_target_pairs={{2,0},{4,6},{3,1},{5,7},{10,8},{12,14},{11,9},{13,15},{18,16},{20,... | collective-permute-start | bytes 442376 | tf_op jit(solution)/shard_map/ppermute | solution.py:571
  414.0 19.4 %collective-permute-start.34 = (bf16[3,192,384]{2,1,0:T(8,128)(2,1)S(1)}, bf16[3,192,384]{2,1,0:T(8,128)(2,1)S(1)}, u32[]{:S(2)}, u32[]{:S(2)}) collective-permute-start(bf16[3,192,384]{2,1,0:T(8,128)(2,1)S(1)} %add_convert_fusion.9), channel_id=1, source_target_pairs={{2,0},{4,6},{3,1},{5,7},{10,8},{12,14},{11,9},{13,15},{18,16},{20,... | collective-permute-start | bytes 1327112 | tf_op jit(solution)/shard_map/ppermute | solution.py:571
  415.4 30.5 %collective-permute-start.55 = (bf16[384,768]{1,0:T(8,128)(2,1)S(1)}, bf16[384,768]{1,0:T(8,128)(2,1)S(1)}, u32[]{:S(2)}, u32[]{:S(2)}) collective-permute-start(bf16[384,768]{1,0:T(8,128)(2,1)S(1)} %add_convert_fusion.1), channel_id=1, source_target_pairs={{2,0},{4,6},{3,1},{5,7},{10,8},{12,14},{11,9},{13,15},{18,16},{20,... | collective-permute-start | bytes 1769480 | tf_op jit(solution)/shard_map/ppermute | solution.py:571
  416.9 38.3 %collective-permute-start.47 = (bf16[192,1536]{1,0:T(8,128)(2,1)S(1)}, bf16[192,1536]{1,0:T(8,128)(2,1)S(1)}, u32[]{:S(2)}, u32[]{:S(2)}) collective-permute-start(bf16[192,1536]{1,0:T(8,128)(2,1)S(1)} %add_convert_fusion.6), channel_id=1, source_target_pairs={{2,0},{4,6},{3,1},{5,7},{10,8},{12,14},{11,9},{13,15},{18,16},{20,... | collective-permute-start | bytes 1769480 | tf_op jit(solution)/shard_map/ppermute | solution.py:571
  (19 other events, 127.8 us)

commit v2 on v1

v2 whole, which is shorter than its diff:
```python
import functools
import jax
import jax.numpy as jnp
from jax import lax
from jax.sharding import PartitionSpec as P
from jax.experimental import pallas as pl
from jax.experimental.pallas import tpu as pltpu

D = 768
HD = 64
EPSILON = 1e-05
MASKED = -1e30
VMEM_CAP = 60 * 1024 * 1024
F32 = jnp.float32
BF16 = jnp.bfloat16
COST_FLOPS = 0.4e9


def cost(micros):
    return pl.CostEstimate(flops=int(micros * COST_FLOPS), bytes_accessed=int(micros * 4e5), transcendentals=0)


def after(value, *others):
    return lax.optimization_barrier((value, *others))[0]


def dot_nn(a, b):
    return lax.dot_general(a, b, (((1,), (0,)), ((), ())), preferred_element_type=F32)


def dot_nt(a, b):
    return lax.dot_general(a, b, (((1,), (1,)), ((), ())), preferred_element_type=F32)


def dot_tn(a, b):
    return lax.dot_general(a, b, (((0,), (0,)), ((), ())), preferred_element_type=F32)


def dot_tn_halves(left, right):
    half = left.shape[0] // 2
    return (dot_tn(left[pl.ds(0, half), :], right[pl.ds(0, half), :])
            + dot_tn(left[pl.ds(half, half), :], right[pl.ds(half, half), :]))


def column_sum(values):
    return jnp.sum(values, axis=0, keepdims=True)


def lane_of(shape):
    return lax.broadcasted_iota(jnp.int32, shape, len(shape) - 1)


def attend_forward_kernel(flags_ref, q_ref, k_ref, v_ref, out_ref, log_ref, *, block):
    length = q_ref.shape[0]
    row = lax.broadcasted_iota(jnp.int32, (block, block), 0)
    col = lax.broadcasted_iota(jnp.int32, (block, block), 1)
    causal = col <= row
    head_lane = lane_of((block, 128)) // HD
    for at in range(length // block):
        rows = pl.ds(at * block, block)
        seen = causal | (flags_ref[at] > 0)
        q_rows = q_ref[rows, :]
        reach = at * block
        parts = []
        for head in range(2):
            q_head = jnp.where(head_lane == head, q_rows, jnp.zeros_like(q_rows))
            near = jnp.where(seen, dot_nt(q_head, k_ref[rows, :]), MASKED)
            top = jnp.max(near, axis=-1, keepdims=True)
            if reach:
                far = dot_nt(q_head, k_ref[pl.ds(0, reach), :])
                top = jnp.maximum(top, jnp.max(far, axis=-1, keepdims=True))
            near = jnp.exp(near - top)
            total = jnp.sum(near, axis=-1, keepdims=True)
            mixed = dot_nn(near.astype(BF16), v_ref[rows, :])
            if reach:
                far = jnp.exp(far - top)
                total = total + jnp.sum(far, axis=-1, keepdims=True)
                mixed = mixed + dot_nn(far.astype(BF16), v_ref[pl.ds(0, reach), :])
            parts.append(mixed / total)
            logs = top + jnp.log(total)
            log_ref[0, pl.ds(head, 1), rows] = jnp.transpose(
                jnp.broadcast_to(logs, (block, 128)))[0:1, :]
        out_ref[rows, :] = jnp.where(head_lane == 0, parts[0], parts[1]).astype(BF16)


def attend_forward(flags, queries, key_rows, value_rows, first, pairs, into=None):
    length, width = queries.shape
    block = length // 4
    tile = pl.BlockSpec((length, 128), lambda h, f: (0, h + first))
    more = [] if into is None else list(into)

    def body(flags_ref, q_ref, k_ref, v_ref, *rest):
        attend_forward_kernel(flags_ref, q_ref, k_ref, v_ref, *rest[len(more):], block=block)

    return pl.pallas_call(
        body,
        grid_spec=pltpu.PrefetchScalarGridSpec(
            num_scalar_prefetch=1, grid=(pairs,),
            in_specs=[tile, tile, tile] + [pl.BlockSpec(memory_space=pl.ANY)] * len(more),
            out_specs=[tile, pl.BlockSpec((1, 8, length), lambda h, f: (h + first, 0, 0))]),
        out_shape=[jax.ShapeDtypeStruct((length, width), BF16),
                   jax.ShapeDtypeStruct((width // 128, 8, length), F32)],
        input_output_aliases={4 + n: n for n in range(len(more))},
        compiler_params=pltpu.CompilerParams(vmem_limit_bytes=VMEM_CAP),
        cost_estimate=cost(3.8 * pairs),
        name="attend_forward",
    )(flags, queries, key_rows, value_rows, *more)


def attend_backward_kernel(flags_ref, q_ref, k_ref, v_ref, up_ref, log_ref,
                           grad_ref, sum_ref, dk_acc, dv_acc, *, block):
    length = q_ref.shape[0]
    count = length // block
    key_at = lax.broadcasted_iota(jnp.int32, (block, block), 0)
    query_at = lax.broadcasted_iota(jnp.int32, (block, block), 1)
    causal = key_at <= query_at
    head_lane = lane_of((block, 128)) // HD
    full_lane = lane_of((length, 128)) // HD
    dq_sum = jnp.zeros((1, 128), F32)
    for at in reversed(range(count)):
        rows = pl.ds(at * block, block)
        reach = (at + 1) * block
        keys = pl.ds(0, reach)
        seen = causal | (flags_ref[at] > 0)
        dq = None
        for head in range(2):
            q_head = jnp.where(head_lane == head, q_ref[rows, :], jnp.zeros((block, 128), BF16))
            up_head = jnp.where(head_lane == head, up_ref[rows, :], jnp.zeros((block, 128), BF16))
            logs = log_ref[0, pl.ds(head, 1), rows]
            scores = dot_nt(k_ref[keys, :], q_head)
            last = jnp.where(seen, scores[reach - block :], MASKED)
            scores = last if at == 0 else jnp.concatenate([scores[: reach - block], last], 0)
            probs = jnp.exp(scores - logs)
            along = dot_nt(v_ref[keys, :], up_head)
            inner = jnp.sum(probs * along, axis=0, keepdims=True)
            low_grad = (probs * (along - inner)).astype(BF16)
            dv = dot_nn(probs.astype(BF16), up_head)
            dk = dot_nn(low_grad, q_head)
            if at == count - 1 and head == 0:
                dv_acc[keys, :] = dv
                dk_acc[keys, :] = dk
            else:
                dv_acc[keys, :] += dv
                dk_acc[keys, :] += dk
            k_head = jnp.where(full_lane[:reach] == head, k_ref[keys, :], jnp.zeros((reach, 128), BF16))
            part = dot_tn(low_grad, k_head)
            dq = part if dq is None else dq + part
        low_dq = (dq * HD ** (-0.5)).astype(BF16)
        grad_ref[0, rows, :] = low_dq
        dq_sum = dq_sum + column_sum(low_dq.astype(F32))
    grad_ref[1] = dk_acc[...].astype(BF16)
    low_dv = dv_acc[...].astype(BF16)
    grad_ref[2] = low_dv
    sum_ref[...] = jnp.zeros_like(sum_ref)
    sum_ref[0:1, :] = dq_sum
    sum_ref[1:2, :] = column_sum(low_dv.astype(F32))


def attend_backward(flags, queries, key_rows, value_rows, upstream, log_sums, first, pairs):
    length = queries.shape[0]
    width = pairs * 128
    tile = pl.BlockSpec((length, 128), lambda h, f: (0, h + first))
    return pl.pallas_call(
        functools.partial(attend_backward_kernel, block=length // 4),
        grid_spec=pltpu.PrefetchScalarGridSpec(
            num_scalar_prefetch=1, grid=(pairs,),
            in_specs=[tile, tile, tile, tile,
                      pl.BlockSpec((1, 8, length), lambda h, f: (h + first, 0, 0))],
            out_specs=[pl.BlockSpec((3, length, 128), lambda h, f: (0, 0, h)),
                       pl.BlockSpec((8, 128), lambda h, f: (0, h))],
            scratch_shapes=[pltpu.VMEM((length, 128), F32), pltpu.VMEM((length, 128), F32)]),
        out_shape=[jax.ShapeDtypeStruct((3, length, width), BF16), jax.ShapeDtypeStruct((8, width), F32)],
        compiler_params=pltpu.CompilerParams(vmem_limit_bytes=VMEM_CAP),
        cost_estimate=cost(6.1 * pairs),
        name="attend_backward",
    )(flags, queries, key_rows, value_rows, upstream, log_sums)


def unpack_kernel(place_ref, rows_ref, own_ref, send_ref):
    packed = rows_ref[...]
    packed = packed.reshape(packed.shape[0] * 2, packed.shape[2])
    shape = (packed.shape[0], D)
    row = lax.broadcasted_iota(jnp.int32, shape, 0)
    column = lax.broadcasted_iota(jnp.int32, shape, 1)
    for seq, out_ref in ((1 - place_ref[0], send_ref), (place_ref[0], own_ref)):
        choose = jnp.where(row == 2 * column + seq, 1.0, 0.0).astype(BF16)
        out_ref[...] = dot_tn(packed, choose).astype(BF16)


def unpack_rows(place, rows):
    packed = rows.transpose(2, 0, 1)
    out = jax.ShapeDtypeStruct((rows.shape[1], D), BF16)
    return pl.pallas_call(
        unpack_kernel,
        grid_spec=pltpu.PrefetchScalarGridSpec(
            num_scalar_prefetch=1, grid=(1,),
            in_specs=[pl.BlockSpec(packed.shape, lambda i, s: (0, 0, 0))],
            out_specs=[pl.BlockSpec(out.shape, lambda i, s: (0, 0))] * 2),
        out_shape=[out, out],
        compiler_params=pltpu.CompilerParams(vmem_limit_bytes=VMEM_CAP),
        cost_estimate=cost(5),
        name="unpack_rows",
    )(place, packed)


def decompress(compact):
    total = jnp.sum(compact, axis=-1, keepdims=True)
    return jnp.where(lane_of(compact.shape) == D - 1, -total, compact)


def crms_back(normal, factor, gain, grad):
    scaled = gain * grad
    du = factor * (scaled - normal * jnp.mean(scaled * normal, axis=-1, keepdims=True))
    lane = lane_of(du.shape)
    last = jnp.sum(jnp.where(lane == D - 1, du, 0.0), axis=-1, keepdims=True)
    return jnp.where(lane == D - 1, 0.0, du - last)


def crms_normal(compact):
    full = decompress(compact)
    factor = lax.rsqrt(jnp.mean(full * full, axis=-1, keepdims=True) + EPSILON)
    return full * factor, factor


def project_kernel(place_ref, own_ref, other_ref, gain_ref, bias_ref, w_own, w_quarter,
                   normed_ref, q_ref, k_ref, v_ref, weight, sems, *, steps):
    at = pl.program_id(0)
    quarter = D // 4
    half = w_own.shape[2]

    def copies():
        out = [pltpu.make_async_copy(w_own, weight.at[:, :, pl.ds(0, half)], sems.at[0])]
        for rel in range(4):
            place = pl.multiple_of((place_ref[1] ^ rel) * quarter, quarter)
            out.append(pltpu.make_async_copy(
                w_quarter[rel], weight.at[:, pl.ds(place, quarter), pl.ds(half, half)],
                sems.at[rel + 1]))
        return out

    @pl.when(at == 0)
    def _():
        for copy in copies():
            copy.start()

    compact = jnp.where(at < steps // 2, own_ref[...], other_ref[...]).astype(F32)
    normal, _ = crms_normal(compact)
    normed = (normal * gain_ref[...]).astype(BF16)
    normed_ref[...] = normed

    @pl.when(at == 0)
    def _():
        for copy in copies():
            copy.wait()

    q_ref[...] = ((dot_nn(normed, weight[0]) + bias_ref[0:1, :]).astype(BF16).astype(F32)
                  * HD ** (-0.5)).astype(BF16)
    k_ref[...] = dot_nn(normed, weight[1]).astype(BF16)
    v_ref[...] = (dot_nn(normed, weight[2]) + bias_ref[1:2, :]).astype(BF16)


def row_maps(steps):
    half = steps // 2
    own = lambda i, s: (jnp.minimum(i, half - 1), 0)
    other = lambda i, s: (jnp.maximum(i - half, 0), 0)
    whole = lambda i, s: (jnp.where(i < half, s[0] * half + i, (1 - s[0]) * half + i - half), 0)
    return own, other, whole


ANY = pl.BlockSpec(memory_space=pl.ANY)


def project(place, own, other, gain, bias, w_own, w_quarter, steps=4):
    length = own.shape[0] * 2
    block = length // steps
    own_map, other_map, whole_map = row_maps(steps)
    fixed = lambda i, s: (0, 0)
    wide = pl.BlockSpec((block, D), whole_map)
    out = jax.ShapeDtypeStruct((length, D), BF16)

    def body(place_ref, own_ref, other_ref, gain_ref, bias_ref, w_own, a, b, c, d, *rest):
        project_kernel(place_ref, own_ref, other_ref, gain_ref, bias_ref, w_own, (a, b, c, d),
                       *rest, steps=steps)

    return pl.pallas_call(
        body,
        grid_spec=pltpu.PrefetchScalarGridSpec(
            num_scalar_prefetch=1, grid=(steps,),
            in_specs=[pl.BlockSpec((block, D), own_map), pl.BlockSpec((block, D), other_map),
                      pl.BlockSpec((1, D), fixed), pl.BlockSpec((2, D), fixed)] + [ANY] * 5,
            out_specs=[wide] * 4,
            scratch_shapes=[pltpu.VMEM((3, D, D), BF16), pltpu.SemaphoreType.DMA((5,))]),
        out_shape=[out] * 4,
        compiler_params=pltpu.CompilerParams(vmem_limit_bytes=VMEM_CAP),
        cost_estimate=cost(10),
        name="norm_project",
    )(place, own, other, gain, bias, w_own, *w_quarter)


SQRT_2_PI = 0.7978845608028654


def gelu_pair(v):
    square = v * v
    inner = v * (SQRT_2_PI + (SQRT_2_PI * 0.044715) * square)
    tanh = jnp.tanh(inner)
    cdf = 0.5 + 0.5 * tanh
    slope = SQRT_2_PI + (3 * SQRT_2_PI * 0.044715) * square
    back = cdf + (0.5 * v) * (1.0 - tanh * tanh) * slope
    return v * cdf, back


def middle_kernel(place_ref, att_ref, res_own, res_other, cot_own, cot_other, gain_ref, end_ref,
                  fcb_ref, weights, two_ref, active_ref, hidden_ref, own_out, send_out,
                  mid_ref, branch_ref, upgrad_ref, sums_ref, own_sums, other_sums,
                  out_w, fc_w, proj_w, sems, *, steps, chunk):
    at = pl.program_id(0)
    hid = fc_w.shape[1]
    half = hid // 2
    o_own, f_own, p_own, quarters, proj_quarters = weights

    def copies(which):
        if which == 0:
            own, target = o_own, out_w.at[pl.ds(0, D // 2), :]
        elif which == 1:
            own, target = f_own, fc_w.at[:, pl.ds(0, half)]
        else:
            own, target = p_own, proj_w.at[pl.ds(0, half), :]
        out = [pltpu.make_async_copy(own, target, sems.at[which, 0])]
        for rel in range(4):
            source = proj_quarters[rel] if which == 2 else quarters[rel]
            to = place_ref[2 if which == 2 else 1] ^ rel
            if which == 0:
                moves = [(0, D // 8, out_w, D // 2 + to * (D // 8), None)]
            elif which == 1:
                moves = [(D // 8 + n * (D // 4), D // 4, fc_w, to * (D // 4), half + n * D)
                         for n in range(half // D)]
            else:
                moves = [(0, half // 4, proj_w, half + to * (half // 4), None)]
            for n, (start, rows, into, row, col) in enumerate(moves):
                spot = pl.ds(pl.multiple_of(row, rows), rows)
                out.append(pltpu.make_async_copy(
                    source.at[pl.ds(start, rows), :],
                    into.at[spot, :] if col is None else into.at[spot, pl.ds(col, D)],
                    sems.at[which, 1 + 2 * rel + n]))
        return out

    @pl.when(at == 0)
    def _():
        for which in range(3):
            for copy in copies(which):
                copy.start()
        for ref in (sums_ref, own_sums, other_sums):
            ref[...] = jnp.zeros_like(ref)
        for copy in copies(0):
            copy.wait()

    mine = at < steps // 2
    compact = jnp.where(mine, res_own[...], res_other[...]).astype(F32)
    cot_low = jnp.where(mine, cot_own[...], cot_other[...])
    middle = compact + dot_nn(att_ref[...], out_w[...]) + end_ref[0:1, :]
    normal, factor = crms_normal(middle)
    gain = gain_ref[...]
    two = (normal * gain).astype(BF16)
    two_ref[...] = two

    @pl.when(at == 0)
    def _():
        for which in (1, 2):
            for copy in copies(which):
                copy.wait()

    mlp = jnp.zeros((two.shape[0], D), F32)
    two_grad = jnp.zeros((two.shape[0], D), F32)
    for start in range(0, hid, chunk):
        cols = pl.ds(start, chunk)
        pre = dot_nn(two, fc_w[:, cols]) + fcb_ref[0:1, cols]
        act, slope = gelu_pair(pre)
        act = act.astype(BF16)
        active_ref[:, cols] = act
        mlp = mlp + dot_nn(act, proj_w[cols, :])
        hidden = (dot_nt(cot_low, proj_w[cols, :]) * slope).astype(BF16)
        hidden_ref[:, cols] = hidden
        to = own_sums if start < half else other_sums
        to[0:1, pl.ds(start % half, chunk)] += column_sum(hidden.astype(F32))
        two_grad = two_grad + dot_nt(hidden, fc_w[:, cols])
    block_out = (middle + mlp + end_ref[1:2, :]).astype(BF16)

    @pl.when(mine)
    def _():
        own_out[...] = block_out

    @pl.when(jnp.logical_not(mine))
    def _():
        send_out[...] = block_out

    cot = cot_low.astype(F32)
    mid_grad = cot + crms_back(normal, factor, gain, two_grad)
    mid_ref[...] = mid_grad
    branch = mid_grad.astype(BF16)
    branch_ref[...] = branch
    upgrad_ref[...] = dot_nt(branch, out_w[...]).astype(BF16)
    sums_ref[0:1, :] += column_sum(two_grad * normal)
    sums_ref[1:2, :] += column_sum(branch.astype(F32))
    sums_ref[2:3, :] += column_sum(cot)


def middle_stage(place, att, res_own, res_other, cot_own, cot_other, gain, end_bias, fc_bias, weights,
                 steps=4, chunk=768):
    length = att.shape[0]
    hid = fc_bias.shape[1]
    block = length // steps
    own_map, other_map, whole_map = row_maps(steps)
    fixed = lambda i, s: (0, 0)
    flat = [*weights[:3], *weights[3], *weights[4]]
    spec = lambda w, m: pl.BlockSpec((block, w), m)

    def body(place_ref, *refs):
        ins, rest = refs[:8], refs[8:]
        w, rest = rest[:11], rest[11:]
        packed = (*w[:3], w[3:7], w[7:])
        middle_kernel(place_ref, *ins, packed, *rest, steps=steps, chunk=chunk)

    sd = jax.ShapeDtypeStruct
    return pl.pallas_call(
        body,
        grid_spec=pltpu.PrefetchScalarGridSpec(
            num_scalar_prefetch=1, grid=(steps,),
            in_specs=[spec(D, whole_map), spec(D, own_map), spec(D, other_map), spec(D, own_map),
                      spec(D, other_map), pl.BlockSpec((1, D), fixed), pl.BlockSpec((2, D), fixed),
                      pl.BlockSpec((1, hid), fixed)] + [ANY] * 11,
            out_specs=[spec(D, whole_map), spec(hid, whole_map), spec(hid, whole_map),
                       spec(D, own_map), spec(D, other_map),
                       spec(D, whole_map), spec(D, whole_map), spec(D, whole_map),
                       pl.BlockSpec((8, D), fixed), pl.BlockSpec((8, hid // 2), fixed),
                       pl.BlockSpec((8, hid // 2), fixed)],
            scratch_shapes=[pltpu.VMEM((D, D), BF16), pltpu.VMEM((D, hid), BF16),
                            pltpu.VMEM((hid, D), BF16), pltpu.SemaphoreType.DMA((3, 9))]),
        out_shape=[sd((length, D), BF16), sd((length, hid), BF16), sd((length, hid), BF16),
                   sd((length // 2, D), BF16), sd((length // 2, D), BF16),
                   sd((length, D), F32), sd((length, D), BF16), sd((length, D), BF16),
                   sd((8, D), F32), sd((8, hid // 2), F32), sd((8, hid // 2), F32)],
        compiler_params=pltpu.CompilerParams(vmem_limit_bytes=VMEM_CAP),
        cost_estimate=cost(38),
        name="middle_stage",
    )(place, att, res_own, res_other, cot_own, cot_other, gain, end_bias, fc_bias, *flat)


def fc_grad_kernel(place_ref, left_ref, right_ref, keep_ref, send_ref, *, rows):
    flip = (place_ref[1] & 1) == 1
    both = dot_tn_halves(left_ref, right_ref).astype(BF16)
    for pair in range(2):
        low, high = both[2 * pair * rows : (2 * pair + 1) * rows], both[(2 * pair + 1) * rows : (2 * pair + 2) * rows]
        to = pair ^ (place_ref[1] >> 1)
        keep_ref[to, 0] = jnp.where(flip, high, low)
        send_ref[to, 0] = jnp.where(flip, low, high)


def fc_grad(place, left, right, chunk=768):
    length, width = left.shape
    rows = width // 4
    half = right.shape[1] // 2
    parts = half // chunk
    out = jax.ShapeDtypeStruct((2, 2, rows, half), BF16)
    out_spec = pl.BlockSpec((2, 1, rows, chunk), lambda n, s: (0, n // parts, 0, n % parts))
    return pl.pallas_call(
        functools.partial(fc_grad_kernel, rows=rows),
        grid_spec=pltpu.PrefetchScalarGridSpec(
            num_scalar_prefetch=1, grid=(2 * parts,),
            in_specs=[pl.BlockSpec((length, width), lambda n, s: (0, 0)),
                      pl.BlockSpec((length, chunk), lambda n, s: (0, n))],
            out_specs=[out_spec, out_spec]),
        out_shape=[out, out],
        compiler_params=pltpu.CompilerParams(vmem_limit_bytes=VMEM_CAP),
        cost_estimate=cost(10),
        name="fc_grad",
    )(place, left, right)


def qkv_grad_kernel(place_ref, left_ref, right_ref, keep_ref, send_ref, *, rows):
    flip = (place_ref[1] & 1) == 1
    half = left_ref.shape[0] // 2
    width = right_ref.shape[2]
    both = None
    for n in range(2):
        part = pl.ds(n * half, half)
        right = jnp.concatenate([right_ref[c, part, :] for c in range(3)], axis=1)
        here = dot_tn(left_ref[part, :], right)
        both = here if both is None else both + here
    both = both.astype(BF16)
    for c in range(3):
        low = both[:rows, c * width : (c + 1) * width]
        high = both[rows:, c * width : (c + 1) * width]
        keep_ref[0, c] = jnp.where(flip, high, low)
        send_ref[0, c] = jnp.where(flip, low, high)


def qkv_grad(place, left, rights):
    length, width = left.shape
    rows = width // 4
    cols = rights.shape[2]
    out = jax.ShapeDtypeStruct((2, 3, rows, cols), BF16)
    out_spec = pl.BlockSpec((1, 3, rows, cols), lambda j, s: (j ^ (s[1] >> 1), 0, 0, 0))
    return pl.pallas_call(
        functools.partial(qkv_grad_kernel, rows=rows),
        grid_spec=pltpu.PrefetchScalarGridSpec(
            num_scalar_prefetch=1, grid=(2,),
            in_specs=[pl.BlockSpec((length, 2 * rows), lambda j, s: (0, j)),
                      pl.BlockSpec((3, length, cols), lambda j, s: (0, 0, 0))],
            out_specs=[out_spec, out_spec]),
        out_shape=[out, out],
        compiler_params=pltpu.CompilerParams(vmem_limit_bytes=VMEM_CAP),
        cost_estimate=cost(5),
        name="qkv_grad",
    )(place, left, rights)


def proj_grad_kernel(place_ref, own_act, other_act, own_cot, other_cot, keep_ref, send_ref, *, rows):
    flip = (place_ref[1] & 1) == 1
    both = (dot_tn(own_act[...], own_cot[...]) + dot_tn(other_act[...], other_cot[...])).astype(BF16)
    low, high = both[:rows], both[rows:]
    keep_ref[0, 0] = jnp.where(flip, high, low)
    send_ref[0, 0] = jnp.where(flip, low, high)


def proj_grad(place, active, cot_own, cot_other):
    length, width = active.shape
    rows = width // 8
    out = jax.ShapeDtypeStruct((2, 2, rows, D), BF16)
    out_spec = pl.BlockSpec((1, 1, rows, D), lambda n, j, s: (j ^ (s[1] >> 1), n, 0, 0))
    cot_spec = pl.BlockSpec((length // 2, D), lambda n, j, s: (0, 0))
    return pl.pallas_call(
        functools.partial(proj_grad_kernel, rows=rows),
        grid_spec=pltpu.PrefetchScalarGridSpec(
            num_scalar_prefetch=1, grid=(2, 2),
            in_specs=[pl.BlockSpec((length // 2, 2 * rows), lambda n, j, s: (s[0], n * 2 + j)),
                      pl.BlockSpec((length // 2, 2 * rows), lambda n, j, s: (1 - s[0], n * 2 + j)),
                      cot_spec, cot_spec],
            out_specs=[out_spec, out_spec]),
        out_shape=[out, out],
        compiler_params=pltpu.CompilerParams(vmem_limit_bytes=VMEM_CAP),
        cost_estimate=cost(13),
        name="proj_grad",
    )(place, active, active, cot_own, cot_other)


def out_grad_kernel(place_ref, left_ref, right_ref, keep_ref, send_ref, *, rows):
    flip = (place_ref[1] & 1) == 1
    both = dot_tn_halves(left_ref, right_ref).astype(BF16)
    for side in range(2):
        for pair in range(2):
            at = (side * 4 + pair * 2) * rows
            low, high = both[at : at + rows], both[at + rows : at + 2 * rows]
            to = pair ^ (place_ref[1] >> 1)
            keep_ref[to, side] = jnp.where(flip, high, low)
            send_ref[to, side] = jnp.where(flip, low, high)


def out_grad(place, left, right):
    length, width = left.shape
    rows = width // 8
    out = jax.ShapeDtypeStruct((2, 2, rows, right.shape[1]), BF16)
    return pl.pallas_call(
        functools.partial(out_grad_kernel, rows=rows),
        grid_spec=pltpu.PrefetchScalarGridSpec(
            num_scalar_prefetch=1, grid=(1,),
            in_specs=[pl.BlockSpec(value.shape, lambda i, s: (0, 0)) for value in (left, right)],
            out_specs=[pl.BlockSpec(out.shape, lambda i, s: (0, 0, 0, 0))] * 2),
        out_shape=[out, out],
        compiler_params=pltpu.CompilerParams(vmem_limit_bytes=VMEM_CAP),
        cost_estimate=cost(5),
        name="out_grad",
    )(place, left, right)


def input_grad_kernel(place_ref, own_grad, other_grad, res_own, res_other, mid_ref, gain_ref, w_own, w_quarter,
                      own_out, send_out, sums_ref, weight, sems, *, steps):
    at = pl.program_id(0)
    quarter = D // 4
    half = w_own.shape[2]

    def copies():
        out = []
        for c in range(3):
            out.append(pltpu.make_async_copy(
                w_own.at[c], weight.at[:, pl.ds(c * half, half)], sems.at[c, 0]))
            for rel in range(4):
                place = pl.multiple_of((place_ref[1] ^ rel) * quarter, quarter)
                out.append(pltpu.make_async_copy(
                    w_quarter[rel].at[c], weight.at[pl.ds(place, quarter), pl.ds((3 + c) * half, half)],
                    sems.at[c, rel + 1]))
        return out

    @pl.when(at == 0)
    def _():
        for copy in copies():
            copy.start()
        sums_ref[...] = jnp.zeros_like(sums_ref)

    mine = at < steps // 2
    compact = jnp.where(mine, res_own[...], res_other[...]).astype(F32)
    normal, factor = crms_normal(compact)

    @pl.when(at == 0)
    def _():
        for copy in copies():
            copy.wait()

    left = jnp.concatenate([own_grad[c] for c in range(3)] + [other_grad[c] for c in range(3)], axis=1)
    grad = dot_nt(left, weight[...])
    sums_ref[0:1, :] += column_sum(grad * normal)
    result = (mid_ref[...] + crms_back(normal, factor, gain_ref[...], grad)).astype(BF16)

    @pl.when(mine)
    def _():
        own_out[...] = result

    @pl.when(jnp.logical_not(mine))
    def _():
        send_out[...] = result


def input_grad(place, own_grad, other_grad, res_own, res_other, mid, gain, w_own, w_quarter, steps=4):
    length = mid.shape[0]
    block = length // steps
    own_map, other_map, whole_map = row_maps(steps)
    fixed = lambda i, s: (0, 0)
    half = own_grad.shape[2]
    grad_spec = pl.BlockSpec((3, block, half), lambda i, s: (0, whole_map(i, s)[0], 0))

    def body(place_ref, *refs):
        input_grad_kernel(place_ref, *refs[:7], refs[7:11], *refs[11:], steps=steps)

    sd = jax.ShapeDtypeStruct
    return pl.pallas_call(
        body,
        grid_spec=pltpu.PrefetchScalarGridSpec(
            num_scalar_prefetch=1, grid=(steps,),
            in_specs=[grad_spec, grad_spec, pl.BlockSpec((block, D), own_map), pl.BlockSpec((block, D), other_map),
                      pl.BlockSpec((block, D), whole_map), pl.BlockSpec((1, D), fixed)] + [ANY] * 5,
            out_specs=[pl.BlockSpec((block, D), own_map), pl.BlockSpec((block, D), other_map),
                       pl.BlockSpec((8, D), fixed)],
            scratch_shapes=[pltpu.VMEM((D, 3 * D), BF16), pltpu.SemaphoreType.DMA((3, 5))]),
        out_shape=[sd((length // 2, D), BF16), sd((length // 2, D), BF16), sd((8, D), F32)],
        compiler_params=pltpu.CompilerParams(vmem_limit_bytes=VMEM_CAP),
        cost_estimate=cost(9),
        name="input_grad",
    )(place, own_grad, other_grad, res_own, res_other, mid, gain, w_own, *w_quarter)


FORWARD_SPLIT = ((0, 2), (2, 3), (5, 1))


def swap(value, axis, bit, size):
    return lax.ppermute(value, axis, [(n, n ^ bit) for n in range(size)])


def meet(*values):
    return lax.optimization_barrier(values)


def add_low(*values):
    total = values[0].astype(F32)
    for value in values[1:]:
        total = total + value.astype(F32)
    return total.astype(BF16)


def fours(value, axis, size):
    return [swap(value, axis, rel, size) for rel in (1, 2, 3)]


def sum_fours(value, others):
    return (value + others[0]) + (others[1] + others[2])


def quarter_of(value, index):
    rows = value.shape[0] // 4
    return lax.dynamic_slice_in_dim(value, index * rows, rows, 0)


def in_order(parts, index):
    odd, high = (index & 1) == 1, (index & 2) == 2
    flip = lambda flag, a, b: (jnp.where(flag, b, a), jnp.where(flag, a, b))
    parts = [*flip(odd, parts[0], parts[1]), *flip(odd, parts[2], parts[3])]
    first, third = flip(high, parts[0], parts[2])
    second, fourth = flip(high, parts[1], parts[3])
    return jnp.concatenate([first, second, third, fourth], 0)


def on_device(sizes, residual_in, piece_ids, norm_gains, qkv_weight, qv_bias, out_weight, fc_weight,
              fc_bias, proj_weight, out_biases, cotangent):
    n_dp, n_group, n_tensor = sizes["dp"], sizes["group"], sizes["tensor"]
    dp_at = lax.axis_index("dp")
    group_at = lax.axis_index("group")
    tensor_at = lax.axis_index("tensor")
    quarter_at = dp_at & 3
    proj_at = (dp_at & 1) | ((group_at & 1) << 1)
    place = jnp.stack([tensor_at, quarter_at, proj_at]).astype(jnp.int32)
    pad = ((0, 0), (0, 1))
    half = qv_bias.shape[1]
    hid = fc_bias.shape[0]
    pairs = half // 128
    y_swap = lambda value: swap(value, "tensor", 1, n_tensor)
    x_swap = lambda value: swap(value, "dp", 2, n_dp)
    c_swap = lambda value: swap(value, "dp", 1, n_dp)
    z_swap = lambda value: swap(value, "group", 1, n_group)

    def piece_of(shard, dim, at):
        rows = shard.shape[dim] // 4
        return lax.dynamic_slice_in_dim(shard, at * rows, rows, dim)

    qkv_piece = piece_of(qkv_weight, 1, quarter_at)
    qkv_y = y_swap(qkv_piece)
    res_own, res_send = unpack_rows(after(place, qkv_piece), residual_in)
    small_bias = jnp.concatenate([qv_bias.reshape(1, -1), fc_bias.reshape(1, -1)], axis=1)
    qkv_y, res_own, res_send, small_bias, out_gated, fc_gated, proj_gated = meet(
        qkv_y, res_own, res_send, small_bias, out_weight, fc_weight, proj_weight)
    res_other = y_swap(res_send)
    other_bias = y_swap(small_bias)
    qkv_x = x_swap(qkv_y)
    qkv_c = c_swap(qkv_y)
    fc_piece = piece_of(fc_gated, 0, quarter_at)
    mix = jnp.concatenate([jnp.pad(piece_of(out_gated, 0, quarter_at), pad)]
                          + [fc_piece[:, n : n + D] for n in range(0, hid, D)], 0)
    proj_piece = jnp.pad(piece_of(proj_gated, 0, proj_at), pad)
    cot_own, cot_send = unpack_rows(after(place, mix, proj_piece), cotangent)
    out_own = jnp.pad(out_gated, pad)
    proj_own = jnp.pad(proj_gated, pad)
    qkv_x, qkv_c, res_other, other_bias, mix, proj_piece, cot_send, out_own, proj_own = meet(
        qkv_x, qkv_c, res_other, other_bias, mix, proj_piece, cot_send, out_own, proj_own)
    mix_y = y_swap(mix)
    qkv_cx = c_swap(qkv_x)
    qkv_others = (qkv_y, qkv_c, qkv_x, qkv_cx)

    gains = norm_gains.astype(F32)
    end_biases = jnp.pad(out_biases, pad).astype(F32)
    qv_other = other_bias[:, : 2 * half].reshape(2, half)
    qv_full = jnp.concatenate([qv_bias, qv_other], axis=1).astype(F32)
    fc_full = jnp.concatenate([fc_bias.reshape(1, -1), other_bias[:, 2 * half :]], axis=1).astype(F32)
    length = piece_ids.shape[1]
    flags = (lax.dynamic_index_in_dim(piece_ids, tensor_at, 0, keepdims=False)[:: length // 4] >= 0)
    flags = flags.astype(jnp.int32)

    normed_one, queries, key_rows, value_rows = project(
        place, res_own, res_other, gains[0:1], qv_full, qkv_weight, qkv_others)
    queries, proj_piece = meet(queries, proj_piece)
    attended = None
    proj_y = y_swap(proj_piece)
    for n, (start, count) in enumerate(FORWARD_SPLIT):
        if n == 1:
            attended[0], attended[1], queries, mix_y, cot_send = meet(*attended, queries, mix_y, cot_send)
            mix_x, mix_c = x_swap(mix_y), c_swap(mix_y)
            cot_other = y_swap(cot_send)
        elif n == 2:
            attended[0], attended[1], queries, proj_y = meet(*attended, queries, proj_y)
            proj_x, proj_c = z_swap(proj_y), c_swap(proj_y)
        attended = list(attend_forward(flags, queries, key_rows, value_rows, start, count, attended))
    attended, log_sums, mix_x, proj_x = meet(*attended, mix_x, proj_x)
    mix_others = (mix_y, mix_c, mix_x, c_swap(mix_x))
    proj_others = (proj_y, proj_c, proj_x, c_swap(proj_x))

    (normed_two, active, hidden_grad, out_mine, out_send, middle_grad, branch_grad, attended_grad,
     middle_sums, own_sums, other_sums) = middle_stage(
        place, attended, res_own, res_other, cot_own, cot_other, gains[1:2], end_biases, fc_full,
        (out_own, fc_weight, proj_own, mix_others, proj_others))
    backward = functools.partial(attend_backward, flags, queries, key_rows, value_rows)
    restore = lambda mine, got: jnp.where(
        tensor_at == 0, jnp.stack([mine, got]), jnp.stack([got, mine]))[:, :, : D - 1]

    if n_dp == 4 and n_group == 4:
        out_got = y_swap(out_send)
        proj_k, proj_s = proj_grad(after(place, middle_sums), active, cot_own, cot_other)
        proj_c = c_swap(proj_s)
        fc_k, fc_s = fc_grad(after(place, proj_k), normed_two, hidden_grad)
        fc_k, fc_s, proj_k, proj_c, out_got = meet(fc_k, fc_s, proj_k, proj_c, out_got)
        fc_c = c_swap(fc_s)
        proj_f = add_low(proj_k[1], proj_c[1])
        proj_x = x_swap(proj_f)
        out_k, out_s = out_grad(after(place, proj_f), attended, branch_grad)
        out_k, out_s, fc_k, fc_c = meet(out_k, out_s, fc_k, fc_c)
        out_c = c_swap(out_s)
        fc_away = add_low(fc_k[:, 1], fc_c[:, 1])
        fc_y = y_swap(fc_away)
        first, first_sums = backward(after(attended_grad, fc_away), log_sums, pairs, pairs)
        first, first_sums, proj_k, proj_c, proj_x, out_k, out_c = meet(
            first, first_sums, proj_k, proj_c, proj_x, out_k, out_c)
        proj_r = [add_low(proj_k[0, n], proj_c[0, n], proj_x[n]) for n in range(2)]
        proj_y = y_swap(proj_r[1])
        out_f = add_low(out_k[1], out_c[1])
        out_x = x_swap(out_f)
        qo_k, qo_s = qkv_grad(after(place, proj_r[1], out_f), normed_one, first)
        qo_k, qo_s, fc_k, fc_c, fc_y, out_k, out_c, out_x = meet(qo_k, qo_s, fc_k, fc_c, fc_y, out_k, out_c, out_x)
        qo_c = c_swap(qo_s)
        fc_far = add_low(fc_k[1, 0], fc_c[1, 0], fc_y[1])
        fc_x = x_swap(fc_far)
        out_r = [add_low(out_k[0, n], out_c[0, n], out_x[n]) for n in range(2)]
        out_y = y_swap(out_r[1])
        second, second_sums = backward(after(attended_grad, fc_far, out_r[1]), log_sums, 0, pairs)
        second, second_sums, proj_y, fc_x, out_y, qo_k, qo_c = meet(
            second, second_sums, proj_y, fc_x, out_y, qo_k, qo_c)
        proj_shard = add_low(proj_r[0], proj_y)
        fc_shard = add_low(fc_k[0, 0], fc_c[0, 0], fc_y[0], fc_x)
        proj_shard, fc_shard = lax.psum((proj_shard, fc_shard), "group")
        qo_f = add_low(qo_k[1], qo_c[1])
        qo_x = x_swap(qo_f)
        qm_k, qm_s = qkv_grad(after(place, qo_f), normed_one, second)
        qm_k, qm_s, qo_k, qo_c, qo_x = meet(qm_k, qm_s, qo_k, qo_c, qo_x)
        qm_c = c_swap(qm_s)
        qo_r = add_low(qo_k[0], qo_c[0], qo_x)
        qo_y = y_swap(qo_r)
        small_y = [y_swap(value) for value in meet(middle_sums, other_sums, first_sums, qo_r)[:3]]
        block_out = restore(after(out_mine, qo_r), out_got)
        qm_k, qm_c, block_out = meet(qm_k, qm_c, block_out)
        qm_f = add_low(qm_k[1], qm_c[1])
        qm_x = x_swap(qm_f)
        in_mine, in_send, in_sums = input_grad(
            after(place, qm_f), second, first, res_own, res_other, middle_grad, gains[0:1], qkv_weight, qkv_others)
        in_mine, in_send, in_sums, qm_x, qo_y, *small_y = meet(in_mine, in_send, in_sums, qm_x, qo_y, *small_y)
        in_y = y_swap(in_sums)
        in_got = y_swap(in_send)
        small = jnp.concatenate(
            [middle_sums + small_y[0], own_sums + small_y[1], second_sums + small_y[2]], 1)
        small_dp = fours(small, "dp", n_dp)
        last = jnp.concatenate([add_low(qm_k[0], qm_c[0], qm_x, qo_y).reshape(-1, D), add_low(out_r[0], out_y)], 0)
        last_z = [swap(quarter_of(last, group_at ^ rel), "group", rel, n_group) for rel in (1, 2, 3)]
        small, in_sums, in_y, *small_dp = meet(small, in_sums, in_y, *small_dp)
        in_sums = in_sums + in_y
        in_dp = fours(in_sums, "dp", n_dp)
        small = sum_fours(small, small_dp)
        last, in_sums, *others = meet(last, in_sums, *last_z, *in_dp)
        total = add_low(quarter_of(last, group_at), *others[:3])
        total_z = fours(total, "group", n_group)
        in_sums = sum_fours(in_sums, others[3:])
        in_z = fours(in_sums, "group", n_group)
        small_z = fours(small, "group", n_group)
        small = sum_fours(small, small_z)
        in_sums = sum_fours(in_sums, in_z)
        total, small, in_sums, proj_shard, fc_shard = meet(total, small, in_sums, proj_shard, fc_shard)
        last = in_order([total] + total_z, group_at).astype(F32)
        qkv_shard = last[: 3 * D // 8].reshape(3, D // 4, half)
        out_shard = last[3 * D // 8 :]
    else:
        first, first_sums = backward(attended_grad, log_sums, pairs, pairs)
        second, second_sums = backward(attended_grad, log_sums, 0, pairs)
        in_mine, in_send, in_sums = input_grad(
            place, second, first, res_own, res_other, middle_grad, gains[0:1], qkv_weight, qkv_others)
        in_got = y_swap(in_send)
        block_out = restore(out_mine, y_swap(out_send))

        def scatter(own, other):
            total = [lax.psum_scatter(value.astype(BF16), "dp", scatter_dimension=0, tiled=True)
                     for value in (own, other)]
            return lax.psum(add_low(total[0], y_swap(total[1])), "group")

        cot_rows = jnp.where(tensor_at == 0, jnp.concatenate([cot_own, cot_other]),
                             jnp.concatenate([cot_other, cot_own]))
        proj_shard = scatter(dot_tn(active[:, :hid], cot_rows), dot_tn(active[:, hid:], cot_rows))
        fc_shard = scatter(dot_tn(normed_two, hidden_grad[:, :hid]), dot_tn(normed_two, hidden_grad[:, hid:]))
        out_shard = scatter(dot_tn(attended[:, :half], branch_grad), dot_tn(attended[:, half:], branch_grad))
        qkv_shard = jnp.swapaxes(scatter(
            *[jnp.stack([dot_tn(normed_one, part[c]) for c in range(3)], 1) for part in (second, first)]), 0, 1)
        small = jnp.concatenate([
            middle_sums + y_swap(middle_sums), own_sums + y_swap(other_sums), second_sums + y_swap(first_sums)], 1)
        small = lax.psum(small, ("dp", "group"))
        in_sums = lax.psum(in_sums, ("dp", "group", "tensor"))

    grad_gains = jnp.concatenate([in_sums[0:1], small[0:1, :D]], 0)
    grad_out_biases = small[1:3, : D - 1]
    part = hid // n_dp
    grad_fc_bias = lax.dynamic_slice(small, (0, D + dp_at * part), (1, part)).reshape(part)
    part = half // n_dp
    grad_qv_bias = lax.dynamic_slice(small, (0, D + hid + dp_at * part), (2, part))

    return (
        block_out,
        restore(in_mine, in_got),
        grad_gains,
        qkv_shard.astype(F32),
        grad_qv_bias,
        out_shard[:, : D - 1].astype(F32),
        fc_shard.astype(F32),
        grad_fc_bias,
        proj_shard[:, : D - 1].astype(F32),
        grad_out_biases,
    )


def solution(mesh):
    sizes = dict(mesh.shape)
    in_specs = (
        P(("dp", "group"), "tensor", None),
        P(("dp", "group"), None),
        P(),
        P(None, None, "tensor"),
        P(None, "tensor"),
        P("tensor", None),
        P(None, "tensor"),
        P("tensor"),
        P("tensor", None),
        P(),
        P(("dp", "group"), "tensor", None),
    )
    out_specs = (
        P(("dp", "group"), "tensor", None),
        P(("dp", "group"), "tensor", None),
        P(),
        P(None, "dp", "tensor"),
        P(None, ("tensor", "dp")),
        P(("tensor", "dp"), None),
        P("dp", "tensor"),
        P(("tensor", "dp")),
        P(("tensor", "dp"), None),
        P(),
    )
    return jax.shard_map(
        functools.partial(on_device, sizes), mesh=mesh, in_specs=in_specs, out_specs=out_specs,
        check_vma=False)
```

time: 466 us -> 371 us (0.80)
  waiting for transfers between devices: 132 us -> 47.9 us
  local copies, waits for them, and re-layouts: 53.4 us -> 20.8 us
  other arithmetic: 27.4 us -> 41.2 us
  between operations: 1.66 us -> 15 us
  starting transfers between devices: 76.5 us -> 66.6 us
  Pallas kernels: 165 us -> 174 us
    ppermute x15 -> x0, waiting for transfers between devices: 53.7 us -> none  [the longest x5 34.2 us: chain_sum(): outward = lax.ppermute(total, 'group', [(1, 0), (2, 3)])]
    ppermute x15 -> x0, starting transfers between devices: 43.5 us -> none  [the longest x5 33.7 us: chain_sum(): inward = lax.ppermute(value, 'group', [(0, 1), (3, 2)])]
    ppermute x41 -> x53, starting transfers between devices: 33 us -> 66.6 us  [swap(): return lax.ppermute(value, axis, [(n, n ^ bit) for n in range(size)])]
    ppermute x41 -> x53, waiting for transfers between devices: 78.5 us -> 47.8 us  [swap(): return lax.ppermute(value, axis, [(n, n ^ bit) for n in range(size)])]
    dynamic_slice x11 -> x5, local copies, waits for them, and re-layouts: 30.1 us -> 2.36 us  [the longest x3 1.13 us: piece_of(): return lax.dynamic_slice_in_dim(shard, at * rows, rows, dim)]
    convert_element_type x14, other arithmetic: 13 us -> 24.2 us  [add_low(): return total.astype(BF16)]
    pallas_call x9 -> x11, Pallas kernels: 98.7 us -> 108 us  [the longest x2 36.6 us: attend_backward(): pl.pallas_call(functools.partial(attend_backward_kernel, block=length //...]
    pad x6 -> x3, local copies, waits for them, and re-layouts: 7.46 us -> 2.6 us  [the longest x1 1.66 us: on_device(): proj_own = jnp.pad(proj_gated, pad)]
  transfers between devices with their start and end apart: 56 -> 54, of which waited for: 24 -> 14; matrix products, arithmetic and copies ran while one was open for 16% -> 14% of each run, Pallas kernels for 17% -> 35%
where the time goes in v2:
time: 371 us; the launch traced here: 366 us
  Pallas kernels  174 us (47%)
  starting transfers between devices  66.6 us (18%)
  waiting for transfers between devices  47.9 us (13%)
  other arithmetic  41.2 us (11%)
  local copies, waits for them, and re-layouts  20.8 us (6%)
  between operations  15 us (4%)
    ppermute x53, starting transfers between devices, swap(): return lax.ppermute(value, axis, [(n, n ^ bit) for n in range(size)])  66.6 us
    ppermute x53, waiting for transfers between devices, swap(): return lax.ppermute(value, axis, [(n, n ^ bit) for n in range(size)])  47.8 us
    pallas_call x1, Pallas kernels, middle_stage(): pl.pallas_call(body, grid_spec=pltpu.PrefetchScalarGridSpec(num_scalar_pr...  37.9 us
    pallas_call x2, Pallas kernels, attend_backward(): pl.pallas_call(functools.partial(attend_backward_kernel, block=length //...  36.6 us
    pallas_call x3, Pallas kernels, attend_forward(): pl.pallas_call(body, grid_spec=pltpu.PrefetchScalarGridSpec(num_scalar_pr...  27.7 us
    convert_element_type x14, other arithmetic, add_low(): return total.astype(BF16)  24.2 us
    pallas_call x1, Pallas kernels, input_grad(): pl.pallas_call(body, grid_spec=pltpu.PrefetchScalarGridSpec(num_scalar_pr...  12.6 us
    pallas_call x2, Pallas kernels, qkv_grad(): pl.pallas_call(functools.partial(qkv_grad_kernel, rows=rows), grid_spec=p...  12.2 us
  transfers between devices with their start and end apart: 54, of which 14 were waited for; matrix products, arithmetic and copies ran while one was open for 14% of the time, Pallas kernels for 35%

profile of v2, /device:TPU:0, one launch (start us, length us, event | category | flops | bytes accessed | tf_op | source)
XLA Modules:
  0.0 365.5 jit_solution(12955120866569974620)
XLA Ops:
  8.3 3.0 collective-permute-start
  13.3 1.4 fusion.24
  14.7 5.9 %unpack_rows.2 = (bf16[512,768]{1,0:T(8,128)(2,1)}, bf16[512,768]{1,0:T(8,128)(2,1)}) custom-call(s32[3]{0:T(128)} %pad_add_fusion.place_ref, bf16[767,2,512]{2,1,0:T(2,128)(2,1)} %bitcast.74), custom_call_target="tpu_custom_call" | custom-call | flops 2000000000 | bytes 2000000 | tf_op jit(solution)/shard_map/unpack_rows/pallas_call | solution.py:193
  21.6 1.7 collective-permute-start.3
  23.5 1.5 collective-permute-start.1
  27.6 5.8 %unpack_rows.3 = (bf16[512,768]{1,0:T(8,128)(2,1)}, bf16[512,768]{1,0:T(8,128)(2,1)}) custom-call(s32[3]{0:T(128)} %pad_add_fusion.place_ref, bf16[767,2,512]{2,1,0:T(2,128)(2,1)} %bitcast.75), custom_call_target="tpu_custom_call" | custom-call | flops 2000000000 | bytes 2000000 | tf_op jit(solution)/shard_map/unpack_rows/pallas_call | solution.py:193
  33.4 1.7 pad.22.refs_10_
  35.9 4.8 %collective-permute-done.4 = bf16[1,2304]{1,0:T(2,128)(2,1)S(1)} collective-permute-done((bf16[1,2304]{1,0:T(2,128)(2,1)S(1)}, bf16[1,2304]{1,0:T(2,128)(2,1)S(1)}, u32[]{:S(2)}, u32[]{:S(2)}) %collective-permute-start.4) | collective-permute-done | bytes 4640 | tf_op jit(solution)/shard_map/ppermute | solution.py:654
  41.6 1.5 collective-permute-start.6
  45.1 10.6 %norm_project.1 = (bf16[1024,768]{1,0:T(8,128)(2,1)}, bf16[1024,768]{1,0:T(8,128)(2,1)}, bf16[1024,768]{1,0:T(8,128)(2,1)}, bf16[1024,768]{1,0:T(8,128)(2,1)}) custom-call(s32[3]{0:T(128)} %pad_add_fusion.place_ref, bf16[512,768]{1,0:T(8,128)(2,1)} %get-tuple-element.166.own_ref.refs_1_.refs_2_, ...), custom_call_target="tpu_custom_call" | custom-call | flops 4000000000 | bytes 4000000 | tf_op jit(solution)/shard_map/norm_project/pallas_call | solution.py:284
  56.4 9.2 %attend_forward.3 = (bf16[1024,768]{1,0:T(8,128)(2,1)}, f32[6,8,1024]{2,1,0:T(8,128)}) custom-call(s32[4]{0:T(128)} %compare_convert_fusion.flags_ref, bf16[1024,768]{1,0:T(8,128)(2,1)} %get-tuple-element.194.q_ref, bf16[1024,768]{1,0:T(8,128)(2,1)} %get-tuple-element.182.k_ref, bf16[1024,768]{1,0:T(8,128)(2,1)} %get-tuple-element.183.v_ref), custom_call_target="tpu_custom_call" | custom-call | flops 3040000000 | bytes 3040000 | tf_op jit(solution)/shard_map/attend_forward/pallas_call | solution.py:95
  65.6 1.5 collective-permute-start.8
  67.1 12.6 %attend_forward.4 = (bf16[1024,768]{1,0:T(8,128)(2,1)}, f32[6,8,1024]{2,1,0:T(8,128)}) custom-call(s32[4]{0:T(128)} %compare_convert_fusion.flags_ref, bf16[1024,768]{1,0:T(8,128)(2,1)} %get-tuple-element.194.q_ref, bf16[1024,768]{1,0:T(8,128)(2,1)} %get-tuple-element.182.k_ref, ...), custom_call_target="tpu_custom_call", output_to_operand_aliasing={{0}: (4, {}), {1}: (5, {})} | custom-call | flops 4560000000 | bytes 4559999 | tf_op jit(solution)/shard_map/attend_forward/pallas_call | solution.py:95
  79.7 1.6 collective-permute-start.9
  81.3 1.6 collective-permute-start.10
  82.9 5.8 %attend_forward.5 = (bf16[1024,768]{1,0:T(8,128)(2,1)}, f32[6,8,1024]{2,1,0:T(8,128)}) custom-call(s32[4]{0:T(128)} %compare_convert_fusion.flags_ref, bf16[1024,768]{1,0:T(8,128)(2,1)} %get-tuple-element.194.q_ref, bf16[1024,768]{1,0:T(8,128)(2,1)} %get-tuple-element.182.k_ref, ...), custom_call_target="tpu_custom_call", output_to_operand_aliasing={{0}: (4, {}), {1}: (5, {})} | custom-call | flops 1520000000 | bytes 1520000 | tf_op jit(solution)/shard_map/attend_forward/pallas_call | solution.py:95
  88.8 6.0 %collective-permute-done.9.refs_17_ = bf16[384,768]{1,0:T(8,128)(2,1)} collective-permute-done((bf16[384,768]{1,0:T(8,128)(2,1)}, bf16[384,768]{1,0:T(8,128)(2,1)}, u32[]{:S(2)}, u32[]{:S(2)}) %collective-permute-start.9) | collective-permute-done | bytes 589856 | tf_op jit(solution)/shard_map/ppermute | solution.py:654
  96.5 4.8 %collective-permute-done.10.refs_4_.other_cot = bf16[512,768]{1,0:T(8,128)(2,1)S(1)} collective-permute-done((bf16[512,768]{1,0:T(8,128)(2,1)S(1)}, bf16[512,768]{1,0:T(8,128)(2,1)S(1)}, u32[]{:S(2)}, u32[]{:S(2)}) %collective-permute-start.10) | collective-permute-done | bytes 786464 | tf_op jit(solution)/shard_map/ppermute | solution.py:654
  102.8 37.9 %middle_stage.1 = (bf16[1024,768]{1,0:T(8,128)(2,1)}, bf16[1024,3072]{1,0:T(8,128)(2,1)}, bf16[1024,3072]{1,0:T(8,128)(2,1)}, bf16[512,768]{1,0:T(8,128)(2,1)}, ...) custom-call(s32[3]{0:T(128)} %pad_add_fusion.place_ref, ...), custom_call_target="tpu_custom_call" | custom-call | flops 15200000000 | bytes 15200000 | tf_op jit(solution)/shard_map/middle_stage/pallas_call | solution.py:424
  140.7 9.8 %proj_grad.1 = (bf16[2,2,384,768]{3,2,1,0:T(8,128)(2,1)}, bf16[2,2,384,768]{3,2,1,0:T(8,128)(2,1)}) custom-call(s32[3]{0:T(128)} %pad_add_fusion.place_ref, bf16[1024,3072]{1,0:T(8,128)(2,1)} %get-tuple-element.211.own_act.other_act, bf16[1024,3072]{1,0:T(8,128)(2,1)} %get-tuple-element.211.own_act.other_act, ...), custom_call_target="tpu_custom_call" | custom-call | flops 5200000000 | bytes 5200000 | tf_op jit(solution)/shard_map/proj_grad/pallas_call | solution.py:531
  150.6 1.6 collective-permute-start.16
  152.1 10.1 %fc_grad.1 = (bf16[2,2,192,1536]{3,2,1,0:T(8,128)(2,1)}, bf16[2,2,192,1536]{3,2,1,0:T(8,128)(2,1)}) custom-call(s32[3]{0:T(128)} %pad_add_fusion.place_ref, bf16[1024,768]{1,0:T(8,128)(2,1)} %get-tuple-element.214.left_ref, bf16[1024,3072]{1,0:T(8,128)(2,1)} %get-tuple-element.215.right_ref), custom_call_target="tpu_custom_call" | custom-call | flops 4000000000 | bytes 4000000 | tf_op jit(solution)/shard_map/fc_grad/pallas_call | solution.py:465
  162.2 8.5 %collective-permute-done.16 = bf16[512,768]{1,0:T(8,128)(2,1)S(1)} collective-permute-done((bf16[512,768]{1,0:T(8,128)(2,1)}, bf16[512,768]{1,0:T(8,128)(2,1)S(1)}, u32[]{:S(2)}, u32[]{:S(2)}) %collective-permute-start.16) | collective-permute-done | bytes 786464 | tf_op jit(solution)/shard_map/ppermute | solution.py:654
  170.8 2.9 fusion.3
  174.2 5.0 %out_grad.1 = (bf16[2,2,96,768]{3,2,1,0:T(8,128)(2,1)}, bf16[2,2,96,768]{3,2,1,0:T(8,128)(2,1)}) custom-call(s32[3]{0:T(128)} %pad_add_fusion.place_ref, bf16[1024,768]{1,0:T(8,128)(2,1)} %get-tuple-element.201.refs_0_.left_ref, bf16[1024,768]{1,0:T(8,128)(2,1)} %get-tuple-element.223.right_ref), custom_call_target="tpu_custom_call" | custom-call | flops 2000000000 | bytes 2000000 | tf_op jit(solution)/shard_map/out_grad/pallas_call | solution.py:562
  179.2 1.9 fusion.4
  181.1 1.6 collective-permute-start.20
  182.6 18.4 %attend_backward.2 = (bf16[3,1024,384]{2,1,0:T(8,128)(2,1)}, f32[8,384]{1,0:T(8,128)}) custom-call(s32[4]{0:T(128)} %compare_convert_fusion.flags_ref, bf16[1024,768]{1,0:T(8,128)(2,1)} %get-tuple-element.194.q_ref, bf16[1024,768]{1,0:T(8,128)(2,1)} %get-tuple-element.182.k_ref, bf16[1024,768]{1,0:T(8,128)(2,1)} %get-tuple-element.183.v_ref, ...), custom_call_target="tpu_custom_call" | custom-call | flops 7320000000 | bytes 7319999 | tf_op jit(solution)/shard_map/attend_backward/pallas_call | solution.py:163
  203.8 2.3 fusion.9
  206.1 1.5 collective-permute-start.22
  207.6 6.0 %qkv_grad.2 = (bf16[2,3,192,384]{3,2,1,0:T(8,128)(2,1)}, bf16[2,3,192,384]{3,2,1,0:T(8,128)(2,1)}) custom-call(s32[3]{0:T(128)} %pad_add_fusion.place_ref, bf16[1024,768]{1,0:T(8,128)(2,1)} %get-tuple-element.242.left_ref, bf16[3,1024,384]{2,1,0:T(8,128)(2,1)} %get-tuple-element.243.right_ref.refs_1_), custom_call_target="tpu_custom_call" | custom-call | flops 2000000000 | bytes 2000000 | tf_op jit(solution)/shard_map/qkv_grad/pallas_call | solution.py:503
  213.6 2.5 fusion.8
  216.1 1.5 collective-permute-start.23
  219.3 18.2 %attend_backward.3 = (bf16[3,1024,384]{2,1,0:T(8,128)(2,1)}, f32[8,384]{1,0:T(8,128)}) custom-call(s32[4]{0:T(128)} %compare_convert_fusion.flags_ref, bf16[1024,768]{1,0:T(8,128)(2,1)} %get-tuple-element.194.q_ref, bf16[1024,768]{1,0:T(8,128)(2,1)} %get-tuple-element.182.k_ref, bf16[1024,768]{1,0:T(8,128)(2,1)} %get-tuple-element.183.v_ref, ...), custom_call_target="tpu_custom_call" | custom-call | flops 7320000000 | bytes 7319999 | tf_op jit(solution)/shard_map/attend_backward/pallas_call | solution.py:163
  239.9 6.2 %qkv_grad.3 = (bf16[2,3,192,384]{3,2,1,0:T(8,128)(2,1)}, bf16[2,3,192,384]{3,2,1,0:T(8,128)(2,1)}) custom-call(s32[3]{0:T(128)} %pad_add_fusion.place_ref, bf16[1024,768]{1,0:T(8,128)(2,1)} %get-tuple-element.242.left_ref, bf16[3,1024,384]{2,1,0:T(8,128)(2,1)} %get-tuple-element.260.right_ref.refs_0_), custom_call_target="tpu_custom_call" | custom-call | flops 2000000000 | bytes 2000000 | tf_op jit(solution)/shard_map/qkv_grad/pallas_call | solution.py:503
  246.1 2.6 add_convert_fusion.2
  248.7 3.1 collective-permute-done.26
  251.8 2.7 fusion.6
  254.5 2.1 fusion.12
  256.6 1.5 collective-permute-start.29
  258.1 2.3 fusion.1
  264.0 1.5 collective-permute-start.30
  266.0 12.6 %input_grad.1 = (bf16[512,768]{1,0:T(8,128)(2,1)}, bf16[512,768]{1,0:T(8,128)(2,1)}, f32[8,768]{1,0:T(8,128)}) custom-call(s32[3]{0:T(128)} %pad_add_fusion.place_ref, bf16[3,1024,384]{2,1,0:T(8,128)(2,1)} %get-tuple-element.260.right_ref.refs_0_, bf16[3,1024,384]{2,1,0:T(8,128)(2,1)} %get-tuple-element.243.right_ref.refs_1_, ...), custom_call_target="tpu_custom_call" | custom-call | flops 3600000000 | bytes 3600000 | tf_op jit(solution)/shard_map/input_grad/pallas_call | solution.py:634
  278.6 3.0 copy.27
  284.1 1.4 collective-permute-start.36
  285.9 1.5 fusion.11
  287.5 1.4 collective-permute-start.34
  289.0 2.4 collective-permute-done.34
  292.8 2.5 collective-permute-start.39
  296.5 1.4 collective-permute-start.42
  297.9 2.4 collective-permute-done.42
  300.4 1.4 collective-permute-start.33
  302.0 2.4 collective-permute-done.38
  304.4 8.7 %collective-permute-done.40 = bf16[96,768]{1,0:T(8,128)(2,1)S(1)} collective-permute-done((bf16[96,768]{1,0:T(8,128)(2,1)S(1)}, bf16[96,768]{1,0:T(8,128)(2,1)S(1)}, u32[]{:S(2)}, u32[]{:S(2)}) %collective-permute-start.40) | collective-permute-done | bytes 147488 | tf_op jit(solution)/shard_map/ppermute | solution.py:654
  313.1 10.6 %collective-permute-start.47 = (f32[8,768]{1,0:T(8,128)S(1)}, f32[8,768]{1,0:T(8,128)S(1)}, u32[]{:S(2)}, u32[]{:S(2)}) collective-permute-start(f32[8,768]{1,0:T(8,128)S(1)} %add_add_fusion.3), channel_id=1, source_target_pairs={{0,2},{2,0},{4,6},{6,4},{1,3},{3,1},{5,7},{7,5},{8,10},{10,8},{12,... | collective-permute-start | bytes 73736 | tf_op jit(solution)/shard_map/ppermute | solution.py:654
  323.7 2.6 collective-permute-start.48
  326.3 1.4 collective-permute-start.49
  327.8 2.5 collective-permute-start.45
  330.8 2.7 collective-permute-start.46
  334.6 6.6 %collective-permute-start.51 = (bf16[96,768]{1,0:T(8,128)(2,1)S(1)}, bf16[96,768]{1,0:T(8,128)(2,1)S(1)}, u32[]{:S(2)}, u32[]{:S(2)}) collective-permute-start(bf16[96,768]{1,0:T(8,128)(2,1)S(1)} %add_convert_fusion.6), channel_id=1, source_target_pairs={{0,4},{2,6},{4,0},{6,2},{1,5},{3,7},{5,1},{7,3},{8,12},{10,14},{12... | collective-permute-start | bytes 442376 | tf_op jit(solution)/shard_map/ppermute | solution.py:654
  342.1 2.2 slice_convert_fusion
  347.9 2.6 collective-permute-done.51
  353.4 1.8 fusion
  355.2 3.0 copy.28
  (182 shorter events, 40.8 us)
Async XLA Ops:
  7.2 16.2 %copy-start = (s32[2,1024]{1,0:T(2,128)S(1)}, s32[2,1024]{1,0:T(2,128)}, u32[]{:S(2)}) copy-start(s32[2,1024]{1,0:T(2,128)} %param.12) | copy-start | bytes 24580
  7.2 334.9 %all-reduce.8.cloned.1.call-start = ((), (), s32[]{:S(2)}) async-start(), calls=%async_computation | async-start | bytes 2359296 | tf_op jit(solution)/shard_map/psum | solution.py:803
  8.3 13.3 %collective-permute-start = (bf16[3,192,384]{2,1,0:T(8,128)(2,1)S(1)}, bf16[3,192,384]{2,1,0:T(8,128)(2,1)}, u32[]{:S(2)}, u32[]{:S(2)}) collective-permute-start(bf16[3,192,384]{2,1,0:T(8,128)(2,1)S(1)} %constant_dynamic-slice_fusion.5), channel_id=1, source_target_pairs={{0,1},{1,0},{2,3},{3,2},{4,5},{5,4},{6,7},{7,6},{8,9},{9,8},{10,11... | collective-permute-start | bytes 1327112 | tf_op jit(solution)/shard_map/ppermute | solution.py:654
  14.7 10.3 %copy-start.2 = (bf16[1536,767]{1,0:T(8,128)(2,1)S(1)}, bf16[1536,767]{1,0:T(8,128)(2,1)}, u32[]{:S(2)}) copy-start(bf16[1536,767]{1,0:T(8,128)(2,1)} %param.19) | copy-start | bytes 7068676
  21.6 19.2 %collective-permute-start.3 = (bf16[512,768]{1,0:T(8,128)(2,1)}, bf16[512,768]{1,0:T(8,128)(2,1)}, u32[]{:S(2)}, u32[]{:S(2)}) collective-permute-start(bf16[512,768]{1,0:T(8,128)(2,1)} %get-tuple-element.168), channel_id=1, source_target_pairs={{0,1},{1,0},{2,3},{3,2},{4,5},{5,4},{6,7},{7,6},{8,9},{9,8},{10,11... | collective-permute-start | bytes 2359304 | tf_op jit(solution)/shard_map/ppermute | solution.py:654
  23.5 17.3 %collective-permute-start.1 = (bf16[3,192,384]{2,1,0:T(8,128)(2,1)}, bf16[3,192,384]{2,1,0:T(8,128)(2,1)}, u32[]{:S(2)}, u32[]{:S(2)}) collective-permute-start(bf16[3,192,384]{2,1,0:T(8,128)(2,1)} %collective-permute-done.a.refs_7_), channel_id=1, source_target_pairs={{0,16},{8,24},{16,0},{24,8},{1,17},{9,25},{17,1},{25,9},{2,18},{10... | collective-permute-start | bytes 1327112 | tf_op jit(solution)/shard_map/ppermute | solution.py:654
  25.0 15.8 %collective-permute-start.2 = (bf16[3,192,384]{2,1,0:T(8,128)(2,1)}, bf16[3,192,384]{2,1,0:T(8,128)(2,1)S(1)}, u32[]{:S(2)}, u32[]{:S(2)}) collective-permute-start(bf16[3,192,384]{2,1,0:T(8,128)(2,1)} %collective-permute-done.a.refs_7_), channel_id=1, source_target_pairs={{0,8},{8,0},{16,24},{24,16},{1,9},{9,1},{17,25},{25,17},{2,10},{10... | collective-permute-start | bytes 1327112 | tf_op jit(solution)/shard_map/ppermute | solution.py:654
  27.1 13.6 %collective-permute-start.4 = (bf16[1,2304]{1,0:T(2,128)(2,1)S(1)}, bf16[1,2304]{1,0:T(2,128)(2,1)S(1)}, u32[]{:S(2)}, u32[]{:S(2)}) collective-permute-start(bf16[1,2304]{1,0:T(2,128)(2,1)S(1)} %copy-done.16), channel_id=1, source_target_pairs={{0,1},{1,0},{2,3},{3,2},{4,5},{5,4},{6,7},{7,6},{8,9},{9,8},{10,11... | collective-permute-start | bytes 13832 | tf_op jit(solution)/shard_map/ppermute | solution.py:654
  40.8 3.6 collective-permute-start.5
  41.6 24.0 %collective-permute-start.6 = (bf16[480,768]{1,0:T(8,128)(2,1)}, bf16[480,768]{1,0:T(8,128)(2,1)S(1)}, u32[]{:S(2)}, u32[]{:S(2)}) collective-permute-start(bf16[480,768]{1,0:T(8,128)(2,1)} %fusion.14), channel_id=1, source_target_pairs={{0,1},{1,0},{2,3},{3,2},{4,5},{5,4},{6,7},{7,6},{8,9},{9,8},{10,11... | collective-permute-start | bytes 2211848 | tf_op jit(solution)/shard_map/ppermute | solution.py:654
  55.7 24.0 %collective-permute-start.7 = (bf16[384,768]{1,0:T(8,128)(2,1)S(1)}, bf16[384,768]{1,0:T(8,128)(2,1)}, u32[]{:S(2)}, u32[]{:S(2)}) collective-permute-start(bf16[384,768]{1,0:T(8,128)(2,1)S(1)} %pad.20), channel_id=1, source_target_pairs={{0,1},{1,0},{2,3},{3,2},{4,5},{5,4},{6,7},{7,6},{8,9},{9,8},{10,11... | collective-permute-start | bytes 1769480 | tf_op jit(solution)/shard_map/ppermute | solution.py:654
  65.6 15.7 %copy-start.20 = (bf16[480,768]{1,0:T(8,128)(2,1)}, bf16[480,768]{1,0:T(8,128)(2,1)S(1)}, u32[]{:S(2)}) copy-start(bf16[480,768]{1,0:T(8,128)(2,1)S(1)} %collective-permute-done.6.refs_11_) | copy-start | bytes 2211844
  65.6 15.7 %copy-start.18 = (bf16[512,768]{1,0:T(8,128)(2,1)S(1)}, bf16[512,768]{1,0:T(8,128)(2,1)}, u32[]{:S(2)}) copy-start(bf16[512,768]{1,0:T(8,128)(2,1)} %get-tuple-element.203) | copy-start | bytes 2359300
  65.6 23.1 %collective-permute-start.8 = (bf16[480,768]{1,0:T(8,128)(2,1)S(1)}, bf16[480,768]{1,0:T(8,128)(2,1)S(1)}, u32[]{:S(2)}, u32[]{:S(2)}) collective-permute-start(bf16[480,768]{1,0:T(8,128)(2,1)S(1)} %collective-permute-done.6.refs_11_), channel_id=1, source_target_pairs={{0,16},{8,24},{16,0},{24,8},{1,17},{9,25},{17,1},{25,9},{2,18},{10... | collective-permute-start | bytes 2211848 | tf_op jit(solution)/shard_map/ppermute | solution.py:654
  79.7 15.6 %copy-start.17 = (bf16[2,767]{1,0:T(2,128)(2,1)S(1)}, bf16[2,767]{1,0:T(2,128)(2,1)}, u32[]{:S(2)}) copy-start(bf16[2,767]{1,0:T(2,128)(2,1)} %param.20) | copy-start | bytes 9208
  79.7 16.2 %slice-start = ((bf16[1,2304]{1,0:T(2,128)(2,1)}), bf16[1,1536]{1,0:T(2,128)(2,1)S(1)}, s32[]{:S(2)}) async-start(bf16[1,2304]{1,0:T(2,128)(2,1)} %copy-done.14), calls=%async_computation.1 | async-start | bytes 12288 | tf_op jit(solution)/shard_map/slice | solution.py:739
  79.7 15.1 %collective-permute-start.9 = (bf16[384,768]{1,0:T(8,128)(2,1)}, bf16[384,768]{1,0:T(8,128)(2,1)}, u32[]{:S(2)}, u32[]{:S(2)}) collective-permute-start(bf16[384,768]{1,0:T(8,128)(2,1)} %collective-permute-done.7.refs_15_), channel_id=1, source_target_pairs={{0,2},{2,0},{4,6},{6,4},{1,3},{3,1},{5,7},{7,5},{8,10},{10,8},{12,... | collective-permute-start | bytes 1769480 | tf_op jit(solution)/shard_map/ppermute | solution.py:654
  81.3 15.2 %collective-permute-start.11 = (bf16[480,768]{1,0:T(8,128)(2,1)S(1)}, bf16[480,768]{1,0:T(8,128)(2,1)S(1)}, u32[]{:S(2)}, u32[]{:S(2)}) collective-permute-start(bf16[480,768]{1,0:T(8,128)(2,1)S(1)} %collective-permute-done.6.refs_11_), channel_id=1, source_target_pairs={{0,8},{8,0},{16,24},{24,16},{1,9},{9,1},{17,25},{25,17},{2,10},{10... | collective-permute-start | bytes 2211848 | tf_op jit(solution)/shard_map/ppermute | solution.py:654
  81.3 20.0 %collective-permute-start.10 = (bf16[512,768]{1,0:T(8,128)(2,1)S(1)}, bf16[512,768]{1,0:T(8,128)(2,1)S(1)}, u32[]{:S(2)}, u32[]{:S(2)}) collective-permute-start(bf16[512,768]{1,0:T(8,128)(2,1)S(1)} %copy-done.18), channel_id=1, source_target_pairs={{0,1},{1,0},{2,3},{3,2},{4,5},{5,4},{6,7},{7,6},{8,9},{9,8},{10,11... | collective-permute-start | bytes 2359304 | tf_op jit(solution)/shard_map/ppermute | solution.py:654
  88.8 13.8 %copy-start.21 = (bf16[480,768]{1,0:T(8,128)(2,1)}, bf16[480,768]{1,0:T(8,128)(2,1)S(1)}, u32[]{:S(2)}) copy-start(bf16[480,768]{1,0:T(8,128)(2,1)S(1)} %collective-permute-done.8.refs_13_) | copy-start | bytes 2211844
  94.8 6.5 %collective-permute-start.12 = (bf16[480,768]{1,0:T(8,128)(2,1)S(1)}, bf16[480,768]{1,0:T(8,128)(2,1)S(1)}, u32[]{:S(2)}, u32[]{:S(2)}) collective-permute-start(bf16[480,768]{1,0:T(8,128)(2,1)S(1)} %collective-permute-done.8.refs_13_), channel_id=1, source_target_pairs={{0,8},{8,0},{16,24},{24,16},{1,9},{9,1},{17,25},{25,17},{2,10},{10... | collective-permute-start | bytes 2211848 | tf_op jit(solution)/shard_map/ppermute | solution.py:654
  94.8 6.5 %collective-permute-start.13 = (bf16[384,768]{1,0:T(8,128)(2,1)}, bf16[384,768]{1,0:T(8,128)(2,1)S(1)}, u32[]{:S(2)}, u32[]{:S(2)}) collective-permute-start(bf16[384,768]{1,0:T(8,128)(2,1)} %collective-permute-done.7.refs_15_), channel_id=1, source_target_pairs={{0,8},{8,0},{16,24},{24,16},{1,9},{9,1},{17,25},{25,17},{2,10},{10... | collective-permute-start | bytes 1769480 | tf_op jit(solution)/shard_map/ppermute | solution.py:654
  95.3 6.0 %collective-permute-start.14 = (bf16[384,768]{1,0:T(8,128)(2,1)}, bf16[384,768]{1,0:T(8,128)(2,1)S(1)}, u32[]{:S(2)}, u32[]{:S(2)}) collective-permute-start(bf16[384,768]{1,0:T(8,128)(2,1)} %collective-permute-done.9.refs_17_), channel_id=1, source_target_pairs={{0,8},{8,0},{16,24},{24,16},{1,9},{9,1},{17,25},{25,17},{2,10},{10... | collective-permute-start | bytes 1769480 | tf_op jit(solution)/shard_map/ppermute | solution.py:654
  96.5 6.1 %copy-start.22 = (bf16[480,768]{1,0:T(8,128)(2,1)}, bf16[480,768]{1,0:T(8,128)(2,1)S(1)}, u32[]{:S(2)}) copy-start(bf16[480,768]{1,0:T(8,128)(2,1)S(1)} %collective-permute-done.11.refs_12_) | copy-start | bytes 2211844
  150.6 20.2 %collective-permute-start.15 = (bf16[2,2,384,768]{3,2,1,0:T(8,128)(2,1)}, bf16[2,2,384,768]{3,2,1,0:T(8,128)(2,1)}, u32[]{:S(2)}, u32[]{:S(2)}) collective-permute-start(bf16[2,2,384,768]{3,2,1,0:T(8,128)(2,1)} %get-tuple-element.218), channel_id=1, source_target_pairs={{0,8},{8,0},{16,24},{24,16},{1,9},{9,1},{17,25},{25,17},{2,10},{10... | collective-permute-start | bytes 7077896 | tf_op jit(solution)/shard_map/ppermute | solution.py:654
  150.6 20.2 %collective-permute-start.16 = (bf16[512,768]{1,0:T(8,128)(2,1)}, bf16[512,768]{1,0:T(8,128)(2,1)S(1)}, u32[]{:S(2)}, u32[]{:S(2)}) collective-permute-start(bf16[512,768]{1,0:T(8,128)(2,1)} %get-tuple-element.219), channel_id=1, source_target_pairs={{0,1},{1,0},{2,3},{3,2},{4,5},{5,4},{6,7},{7,6},{8,9},{9,8},{10,11... | collective-permute-start | bytes 2359304 | tf_op jit(solution)/shard_map/ppermute | solution.py:654
  152.1 18.6 %copy-start.3 = (bf16[2,2,384,768]{3,2,1,0:T(8,128)(2,1)S(1)}, bf16[2,2,384,768]{3,2,1,0:T(8,128)(2,1)}, u32[]{:S(2)}) copy-start(bf16[2,2,384,768]{3,2,1,0:T(8,128)(2,1)} %get-tuple-element.236) | copy-start | bytes 7077892
  170.7 8.4 %collective-permute-start.17 = (bf16[2,2,192,1536]{3,2,1,0:T(8,128)(2,1)}, bf16[2,2,192,1536]{3,2,1,0:T(8,128)(2,1)}, u32[]{:S(2)}, u32[]{:S(2)}) collective-permute-start(bf16[2,2,192,1536]{3,2,1,0:T(8,128)(2,1)} %get-tuple-element.227), channel_id=1, source_target_pairs={{0,8},{8,0},{16,24},{24,16},{1,9},{9,1},{17,25},{25,17},{2,10},{10... | collective-permute-start | bytes 7077896 | tf_op jit(solution)/shard_map/ppermute | solution.py:654
  173.7 28.4 %collective-permute-start.18 = (bf16[2,384,768]{2,1,0:T(8,128)(2,1)}, bf16[2,384,768]{2,1,0:T(8,128)(2,1)}, u32[]{:S(2)}, u32[]{:S(2)}) collective-permute-start(bf16[2,384,768]{2,1,0:T(8,128)(2,1)} %fusion.3), channel_id=1, source_target_pairs={{0,16},{8,24},{16,0},{24,8},{1,17},{9,25},{17,1},{25,9},{2,18},{10... | collective-permute-start | bytes 3538952 | tf_op jit(solution)/shard_map/ppermute | solution.py:654
  181.1 32.6 %collective-permute-start.20 = (bf16[2,192,1536]{2,1,0:T(8,128)(2,1)S(1)}, bf16[2,192,1536]{2,1,0:T(8,128)(2,1)}, u32[]{:S(2)}, u32[]{:S(2)}) collective-permute-start(bf16[2,192,1536]{2,1,0:T(8,128)(2,1)S(1)} %fusion.4), channel_id=1, source_target_pairs={{0,1},{1,0},{2,3},{3,2},{4,5},{5,4},{6,7},{7,6},{8,9},{9,8},{10,11... | collective-permute-start | bytes 3538952 | tf_op jit(solution)/shard_map/ppermute | solution.py:654
  182.6 19.4 %collective-permute-start.19 = (bf16[2,2,96,768]{3,2,1,0:T(8,128)(2,1)}, bf16[2,2,96,768]{3,2,1,0:T(8,128)(2,1)}, u32[]{:S(2)}, u32[]{:S(2)}) collective-permute-start(bf16[2,2,96,768]{3,2,1,0:T(8,128)(2,1)} %get-tuple-element.235), channel_id=1, source_target_pairs={{0,8},{8,0},{16,24},{24,16},{1,9},{9,1},{17,25},{25,17},{2,10},{10... | collective-permute-start | bytes 1769480 | tf_op jit(solution)/shard_map/ppermute | solution.py:654
  203.2 10.4 %collective-permute-start.21 = (bf16[2,96,768]{2,1,0:T(8,128)(2,1)S(1)}, bf16[2,96,768]{2,1,0:T(8,128)(2,1)}, u32[]{:S(2)}, u32[]{:S(2)}) collective-permute-start(bf16[2,96,768]{2,1,0:T(8,128)(2,1)S(1)} %fusion.17), channel_id=1, source_target_pairs={{0,16},{8,24},{16,0},{24,8},{1,17},{9,25},{17,1},{25,9},{2,18},{10... | collective-permute-start | bytes 884744 | tf_op jit(solution)/shard_map/ppermute | solution.py:654
  206.1 31.3 %collective-permute-start.22 = (bf16[384,768]{1,0:T(8,128)(2,1)}, bf16[384,768]{1,0:T(8,128)(2,1)}, u32[]{:S(2)}, u32[]{:S(2)}) collective-permute-start(bf16[384,768]{1,0:T(8,128)(2,1)} %fusion.9), channel_id=1, source_target_pairs={{0,1},{1,0},{2,3},{3,2},{4,5},{5,4},{6,7},{7,6},{8,9},{9,8},{10,11... | collective-permute-start | bytes 1769480 | tf_op jit(solution)/shard_map/ppermute | solution.py:654
  216.1 21.4 %collective-permute-start.23 = (bf16[192,1536]{1,0:T(8,128)(2,1)}, bf16[192,1536]{1,0:T(8,128)(2,1)}, u32[]{:S(2)}, u32[]{:S(2)}) collective-permute-start(bf16[192,1536]{1,0:T(8,128)(2,1)} %fusion.8), channel_id=1, source_target_pairs={{0,16},{8,24},{16,0},{24,8},{1,17},{9,25},{17,1},{25,9},{2,18},{10... | collective-permute-start | bytes 1769480 | tf_op jit(solution)/shard_map/ppermute | solution.py:654
  217.6 19.9 %collective-permute-start.25 = (bf16[2,3,192,384]{3,2,1,0:T(8,128)(2,1)}, bf16[2,3,192,384]{3,2,1,0:T(8,128)(2,1)}, u32[]{:S(2)}, u32[]{:S(2)}) collective-permute-start(bf16[2,3,192,384]{3,2,1,0:T(8,128)(2,1)} %get-tuple-element.256), channel_id=1, source_target_pairs={{0,8},{8,0},{16,24},{24,16},{1,9},{9,1},{17,25},{25,17},{2,10},{10... | collective-permute-start | bytes 2654216 | tf_op jit(solution)/shard_map/ppermute | solution.py:654
  218.7 19.4 %copy-start.5 = (bf16[2,3,192,384]{3,2,1,0:T(8,128)(2,1)S(1)}, bf16[2,3,192,384]{3,2,1,0:T(8,128)(2,1)}, u32[]{:S(2)}) copy-start(bf16[2,3,192,384]{3,2,1,0:T(8,128)(2,1)} %get-tuple-element.266) | copy-start | bytes 2654212
  218.7 18.8 %collective-permute-start.24 = (bf16[96,768]{1,0:T(8,128)(2,1)S(1)}, bf16[96,768]{1,0:T(8,128)(2,1)S(1)}, u32[]{:S(2)}, u32[]{:S(2)}) collective-permute-start(bf16[96,768]{1,0:T(8,128)(2,1)S(1)} %fusion.19), channel_id=1, source_target_pairs={{0,1},{1,0},{2,3},{3,2},{4,5},{5,4},{6,7},{7,6},{8,9},{9,8},{10,11... | collective-permute-start | bytes 442376 | tf_op jit(solution)/shard_map/ppermute | solution.py:654
  239.3 12.5 %collective-permute-start.26 = (bf16[3,192,384]{2,1,0:T(8,128)(2,1)S(1)}, bf16[3,192,384]{2,1,0:T(8,128)(2,1)}, u32[]{:S(2)}, u32[]{:S(2)}) collective-permute-start(bf16[3,192,384]{2,1,0:T(8,128)(2,1)S(1)} %fusion.15), channel_id=1, source_target_pairs={{0,16},{8,24},{16,0},{24,8},{1,17},{9,25},{17,1},{25,9},{2,18},{10... | collective-permute-start | bytes 1327112 | tf_op jit(solution)/shard_map/ppermute | solution.py:654
  251.8 8.7 %collective-permute-start.27 = (bf16[2,3,192,384]{3,2,1,0:T(8,128)(2,1)}, bf16[2,3,192,384]{3,2,1,0:T(8,128)(2,1)}, u32[]{:S(2)}, u32[]{:S(2)}) collective-permute-start(bf16[2,3,192,384]{3,2,1,0:T(8,128)(2,1)} %get-tuple-element.264), channel_id=1, source_target_pairs={{0,8},{8,0},{16,24},{24,16},{1,9},{9,1},{17,25},{25,17},{2,10},{10... | collective-permute-start | bytes 2654216 | tf_op jit(solution)/shard_map/ppermute | solution.py:654
  256.6 25.0 %collective-permute-start.29 = (bf16[3,192,384]{2,1,0:T(8,128)(2,1)}, bf16[3,192,384]{2,1,0:T(8,128)(2,1)S(1)}, u32[]{:S(2)}, u32[]{:S(2)}) collective-permute-start(bf16[3,192,384]{2,1,0:T(8,128)(2,1)} %fusion.12), channel_id=1, source_target_pairs={{0,1},{1,0},{2,3},{3,2},{4,5},{5,4},{6,7},{7,6},{8,9},{9,8},{10,11... | collective-permute-start | bytes 1327112 | tf_op jit(solution)/shard_map/ppermute | solution.py:654
  261.6 20.0 %collective-permute-start.28 = (bf16[3,192,384]{2,1,0:T(8,128)(2,1)S(1)}, bf16[3,192,384]{2,1,0:T(8,128)(2,1)}, u32[]{:S(2)}, u32[]{:S(2)}) collective-permute-start(bf16[3,192,384]{2,1,0:T(8,128)(2,1)S(1)} %fusion.16), channel_id=1, source_target_pairs={{0,16},{8,24},{16,0},{24,8},{1,17},{9,25},{17,1},{25,9},{2,18},{10... | collective-permute-start | bytes 1327112 | tf_op jit(solution)/shard_map/ppermute | solution.py:654
  263.4 18.3 %collective-permute-start.31 = (f32[8,1536]{1,0:T(8,128)}, f32[8,1536]{1,0:T(8,128)}, u32[]{:S(2)}, u32[]{:S(2)}) collective-permute-start(f32[8,1536]{1,0:T(8,128)} %get-tuple-element.282), channel_id=1, source_target_pairs={{0,1},{1,0},{2,3},{3,2},{4,5},{5,4},{6,7},{7,6},{8,9},{9,8},{10,11... | collective-permute-start | bytes 147464 | tf_op jit(solution)/shard_map/ppermute | solution.py:654
  264.0 17.7 %collective-permute-start.30 = (f32[8,768]{1,0:T(8,128)}, f32[8,768]{1,0:T(8,128)}, u32[]{:S(2)}, u32[]{:S(2)}) collective-permute-start(f32[8,768]{1,0:T(8,128)} %get-tuple-element.281), channel_id=1, source_target_pairs={{0,1},{1,0},{2,3},{3,2},{4,5},{5,4},{6,7},{7,6},{8,9},{9,8},{10,11... | collective-permute-start | bytes 73736 | tf_op jit(solution)/shard_map/ppermute | solution.py:654
  265.5 16.2 %collective-permute-start.32 = (f32[8,384]{1,0:T(8,128)}, f32[8,384]{1,0:T(8,128)}, u32[]{:S(2)}, u32[]{:S(2)}) collective-permute-start(f32[8,384]{1,0:T(8,128)} %get-tuple-element.283), channel_id=1, source_target_pairs={{0,1},{1,0},{2,3},{3,2},{4,5},{5,4},{6,7},{7,6},{8,9},{9,8},{10,11... | collective-permute-start | bytes 36872 | tf_op jit(solution)/shard_map/ppermute | solution.py:654
  284.0 7.5 %collective-permute-start.35 = (f32[8,2688]{1,0:T(8,128)S(1)}, f32[8,2688]{1,0:T(8,128)S(1)}, u32[]{:S(2)}, u32[]{:S(2)}) collective-permute-start(f32[8,2688]{1,0:T(8,128)S(1)} %pad_maximum_fusion.5), channel_id=1, source_target_pairs={{0,8},{8,0},{16,24},{24,16},{1,9},{9,1},{17,25},{25,17},{2,10},{10... | collective-permute-start | bytes 258056 | tf_op jit(solution)/shard_map/ppermute | solution.py:654
  284.1 7.4 %collective-permute-start.36 = (f32[8,2688]{1,0:T(8,128)S(1)}, f32[8,2688]{1,0:T(8,128)S(1)}, u32[]{:S(2)}, u32[]{:S(2)}) collective-permute-start(f32[8,2688]{1,0:T(8,128)S(1)} %pad_maximum_fusion.5), channel_id=1, source_target_pairs={{0,16},{8,24},{16,0},{24,8},{1,17},{9,25},{17,1},{25,9},{2,18},{10... | collective-permute-start | bytes 258056 | tf_op jit(solution)/shard_map/ppermute | solution.py:654
  285.5 6.0 %collective-permute-start.37 = (f32[8,2688]{1,0:T(8,128)S(1)}, f32[8,2688]{1,0:T(8,128)S(1)}, u32[]{:S(2)}, u32[]{:S(2)}) collective-permute-start(f32[8,2688]{1,0:T(8,128)S(1)} %pad_maximum_fusion.5), channel_id=1, source_target_pairs={{0,24},{8,16},{16,8},{24,0},{1,25},{9,17},{17,9},{25,1},{2,26},{10... | collective-permute-start | bytes 258056 | tf_op jit(solution)/shard_map/ppermute | solution.py:654
  287.5 3.9 %collective-permute-start.34 = (f32[8,768]{1,0:T(8,128)S(1)}, f32[8,768]{1,0:T(8,128)S(1)}, u32[]{:S(2)}, u32[]{:S(2)}) collective-permute-start(f32[8,768]{1,0:T(8,128)S(1)} %copy-done.15), channel_id=1, source_target_pairs={{0,1},{1,0},{2,3},{3,2},{4,5},{5,4},{6,7},{7,6},{8,9},{9,8},{10,11... | collective-permute-start | bytes 73736 | tf_op jit(solution)/shard_map/ppermute | solution.py:654
  291.5 6.4 %collective-permute-start.41 = (f32[8,768]{1,0:T(8,128)S(1)}, f32[8,768]{1,0:T(8,128)S(1)}, u32[]{:S(2)}, u32[]{:S(2)}) collective-permute-start(f32[8,768]{1,0:T(8,128)S(1)} %add.246), channel_id=1, source_target_pairs={{0,8},{8,0},{16,24},{24,16},{1,9},{9,1},{17,25},{25,17},{2,10},{10... | collective-permute-start | bytes 73736 | tf_op jit(solution)/shard_map/ppermute | solution.py:654
  292.1 12.3 %collective-permute-start.38 = (bf16[96,768]{1,0:T(8,128)(2,1)S(1)}, bf16[96,768]{1,0:T(8,128)(2,1)S(1)}, u32[]{:S(2)}, u32[]{:S(2)}) collective-permute-start(bf16[96,768]{1,0:T(8,128)(2,1)S(1)} %get-tuple-element.335), channel_id=1, source_target_pairs={{0,2},{2,0},{4,6},{6,4},{1,3},{3,1},{5,7},{7,5},{8,10},{10,8},{12,... | collective-permute-start | bytes 442376 | tf_op jit(solution)/shard_map/ppermute | solution.py:654
  292.8 11.6 %collective-permute-start.39 = (bf16[96,768]{1,0:T(8,128)(2,1)S(1)}, bf16[96,768]{1,0:T(8,128)(2,1)S(1)}, u32[]{:S(2)}, u32[]{:S(2)}) collective-permute-start(bf16[96,768]{1,0:T(8,128)(2,1)S(1)} %get-tuple-element.336), channel_id=1, source_target_pairs={{0,4},{2,6},{4,0},{6,2},{1,5},{3,7},{5,1},{7,3},{8,12},{10,14},{12... | collective-permute-start | bytes 442376 | tf_op jit(solution)/shard_map/ppermute | solution.py:654
  295.2 17.8 %collective-permute-start.40 = (bf16[96,768]{1,0:T(8,128)(2,1)S(1)}, bf16[96,768]{1,0:T(8,128)(2,1)S(1)}, u32[]{:S(2)}, u32[]{:S(2)}) collective-permute-start(bf16[96,768]{1,0:T(8,128)(2,1)S(1)} %get-tuple-element.334), channel_id=1, source_target_pairs={{0,6},{2,4},{4,2},{6,0},{1,7},{3,5},{5,3},{7,1},{8,14},{10,12},{12... | collective-permute-start | bytes 442376 | tf_op jit(solution)/shard_map/ppermute | solution.py:654
  296.5 3.8 %collective-permute-start.42 = (f32[8,768]{1,0:T(8,128)S(1)}, f32[8,768]{1,0:T(8,128)S(1)}, u32[]{:S(2)}, u32[]{:S(2)}) collective-permute-start(f32[8,768]{1,0:T(8,128)S(1)} %add.246), channel_id=1, source_target_pairs={{0,16},{8,24},{16,0},{24,8},{1,17},{9,25},{17,1},{25,9},{2,18},{10... | collective-permute-start | bytes 73736 | tf_op jit(solution)/shard_map/ppermute | solution.py:654
  297.9 3.8 %collective-permute-start.43 = (f32[8,768]{1,0:T(8,128)S(1)}, f32[8,768]{1,0:T(8,128)S(1)}, u32[]{:S(2)}, u32[]{:S(2)}) collective-permute-start(f32[8,768]{1,0:T(8,128)S(1)} %add.246), channel_id=1, source_target_pairs={{0,24},{8,16},{16,8},{24,0},{1,25},{9,17},{17,9},{25,1},{2,26},{10... | collective-permute-start | bytes 73736 | tf_op jit(solution)/shard_map/ppermute | solution.py:654
  300.4 52.2 %collective-permute-start.33 = (bf16[512,768]{1,0:T(8,128)(2,1)}, bf16[512,768]{1,0:T(8,128)(2,1)S(1)}, u32[]{:S(2)}, u32[]{:S(2)}) collective-permute-start(bf16[512,768]{1,0:T(8,128)(2,1)} %get-tuple-element.285), channel_id=1, source_target_pairs={{0,1},{1,0},{2,3},{3,2},{4,5},{5,4},{6,7},{7,6},{8,9},{9,8},{10,11... | collective-permute-start | bytes 2359304 | tf_op jit(solution)/shard_map/ppermute | solution.py:654
  301.7 32.9 %collective-permute-start.44 = (f32[8,2688]{1,0:T(8,128)S(1)}, f32[8,2688]{1,0:T(8,128)S(1)}, u32[]{:S(2)}, u32[]{:S(2)}) collective-permute-start(f32[8,2688]{1,0:T(8,128)S(1)} %add_add_fusion.1), channel_id=1, source_target_pairs={{0,2},{2,0},{4,6},{6,4},{1,3},{3,1},{5,7},{7,5},{8,10},{10,8},{12,... | collective-permute-start | bytes 258056 | tf_op jit(solution)/shard_map/ppermute | solution.py:654
  313.1 14.7 %collective-permute-start.47 = (f32[8,768]{1,0:T(8,128)S(1)}, f32[8,768]{1,0:T(8,128)S(1)}, u32[]{:S(2)}, u32[]{:S(2)}) collective-permute-start(f32[8,768]{1,0:T(8,128)S(1)} %add_add_fusion.3), channel_id=1, source_target_pairs={{0,2},{2,0},{4,6},{6,4},{1,3},{3,1},{5,7},{7,5},{8,10},{10,8},{12,... | collective-permute-start | bytes 73736 | tf_op jit(solution)/shard_map/ppermute | solution.py:654
  323.7 7.1 %collective-permute-start.48 = (f32[8,768]{1,0:T(8,128)S(1)}, f32[8,768]{1,0:T(8,128)S(1)}, u32[]{:S(2)}, u32[]{:S(2)}) collective-permute-start(f32[8,768]{1,0:T(8,128)S(1)} %add_add_fusion.3), channel_id=1, source_target_pairs={{0,4},{2,6},{4,0},{6,2},{1,5},{3,7},{5,1},{7,3},{8,12},{10,14},{12... | collective-permute-start | bytes 73736 | tf_op jit(solution)/shard_map/ppermute | solution.py:654
  326.3 7.1 %collective-permute-start.49 = (f32[8,768]{1,0:T(8,128)S(1)}, f32[8,768]{1,0:T(8,128)S(1)}, u32[]{:S(2)}, u32[]{:S(2)}) collective-permute-start(f32[8,768]{1,0:T(8,128)S(1)} %add_add_fusion.3), channel_id=1, source_target_pairs={{0,6},{2,4},{4,2},{6,0},{1,7},{3,5},{5,3},{7,1},{8,14},{10,12},{12... | collective-permute-start | bytes 73736 | tf_op jit(solution)/shard_map/ppermute | solution.py:654
  327.8 13.5 %collective-permute-start.45 = (f32[8,2688]{1,0:T(8,128)S(1)}, f32[8,2688]{1,0:T(8,128)S(1)}, u32[]{:S(2)}, u32[]{:S(2)}) collective-permute-start(f32[8,2688]{1,0:T(8,128)S(1)} %add_add_fusion.1), channel_id=1, source_target_pairs={{0,4},{2,6},{4,0},{6,2},{1,5},{3,7},{5,1},{7,3},{8,12},{10,14},{12... | collective-permute-start | bytes 258056 | tf_op jit(solution)/shard_map/ppermute | solution.py:654
  330.8 11.2 %collective-permute-start.46 = (f32[8,2688]{1,0:T(8,128)S(1)}, f32[8,2688]{1,0:T(8,128)S(1)}, u32[]{:S(2)}, u32[]{:S(2)}) collective-permute-start(f32[8,2688]{1,0:T(8,128)S(1)} %add_add_fusion.1), channel_id=1, source_target_pairs={{0,6},{2,4},{4,2},{6,0},{1,7},{3,5},{5,3},{7,1},{8,14},{10,12},{12... | collective-permute-start | bytes 258056 | tf_op jit(solution)/shard_map/ppermute | solution.py:654
  333.5 14.4 %collective-permute-start.50 = (bf16[96,768]{1,0:T(8,128)(2,1)S(1)}, bf16[96,768]{1,0:T(8,128)(2,1)S(1)}, u32[]{:S(2)}, u32[]{:S(2)}) collective-permute-start(bf16[96,768]{1,0:T(8,128)(2,1)S(1)} %add_convert_fusion.6), channel_id=1, source_target_pairs={{0,6},{2,4},{4,2},{6,0},{1,7},{3,5},{5,3},{7,1},{8,14},{10,12},{12... | collective-permute-start | bytes 442376 | tf_op jit(solution)/shard_map/ppermute | solution.py:654
  334.6 15.9 %collective-permute-start.51 = (bf16[96,768]{1,0:T(8,128)(2,1)S(1)}, bf16[96,768]{1,0:T(8,128)(2,1)S(1)}, u32[]{:S(2)}, u32[]{:S(2)}) collective-permute-start(bf16[96,768]{1,0:T(8,128)(2,1)S(1)} %add_convert_fusion.6), channel_id=1, source_target_pairs={{0,4},{2,6},{4,0},{6,2},{1,5},{3,7},{5,1},{7,3},{8,12},{10,14},{12... | collective-permute-start | bytes 442376 | tf_op jit(solution)/shard_map/ppermute | solution.py:654
  341.3 9.2 %collective-permute-start.52 = (bf16[96,768]{1,0:T(8,128)(2,1)S(1)}, bf16[96,768]{1,0:T(8,128)(2,1)S(1)}, u32[]{:S(2)}, u32[]{:S(2)}) collective-permute-start(bf16[96,768]{1,0:T(8,128)(2,1)S(1)} %add_convert_fusion.6), channel_id=1, source_target_pairs={{0,2},{2,0},{4,6},{6,4},{1,3},{3,1},{5,7},{7,5},{8,10},{10,8},{12,... | collective-permute-start | bytes 442376 | tf_op jit(solution)/shard_map/ppermute | solution.py:654
  (19 other events, 42.8 us)
Sparse Core Ops, SparseCore 0:
  263.5 68.9 all-reduce.7

commit v3 on v2

--- a/solution.py
+++ b/solution.py
@@ -158,7 +158,6 @@
 
 def attend_backward(flags, queries, key_rows, value_rows, upstream, log_sums, first, pairs):
     length = queries.shape[0]
-    width = pairs * 128
     tile = pl.BlockSpec((length, 128), lambda h, f: (0, h + first))
     return pl.pallas_call(
         functools.partial(attend_backward_kernel, block=length // 4),
@@ -169,38 +168,45 @@
             out_specs=[pl.BlockSpec((3, length, 128), lambda h, f: (0, 0, h)),
                        pl.BlockSpec((8, 128), lambda h, f: (0, h))],
             scratch_shapes=[pltpu.VMEM((length, 128), F32), pltpu.VMEM((length, 128), F32)]),
-        out_shape=[jax.ShapeDtypeStruct((3, length, width), BF16), jax.ShapeDtypeStruct((8, width), F32)],
+        out_shape=[jax.ShapeDtypeStruct((3, length, pairs * 128), BF16),
+                   jax.ShapeDtypeStruct((8, pairs * 128), F32)],
         compiler_params=pltpu.CompilerParams(vmem_limit_bytes=VMEM_CAP),
-        cost_estimate=cost(6.1 * pairs),
+        cost_estimate=cost(1 + 6 * pairs),
         name="attend_backward",
     )(flags, queries, key_rows, value_rows, upstream, log_sums)
 
 
-def unpack_kernel(place_ref, rows_ref, own_ref, send_ref):
+def unpack_kernel(place_ref, rows_ref, *refs):
+    own_ref, send_ref = refs[-2:]
     packed = rows_ref[...]
     packed = packed.reshape(packed.shape[0] * 2, packed.shape[2])
     shape = (packed.shape[0], D)
     row = lax.broadcasted_iota(jnp.int32, shape, 0)
     column = lax.broadcasted_iota(jnp.int32, shape, 1)
-    for seq, out_ref in ((1 - place_ref[0], send_ref), (place_ref[0], own_ref)):
-        choose = jnp.where(row == 2 * column + seq, 1.0, 0.0).astype(BF16)
-        out_ref[...] = dot_tn(packed, choose).astype(BF16)
-
-
-def unpack_rows(place, rows):
+    pick = lambda seq: dot_tn(packed, jnp.where(row == 2 * column + seq, 1.0, 0.0).astype(BF16)).astype(BF16)
+    count = own_ref.shape[0]
+    send_ref[pl.ds(0, count), :] = pick(1 - place_ref[0])
+    if len(refs) > 2:
+        send_ref[pl.ds(count, refs[0].shape[0]), :] = refs[0][...]
+    own_ref[...] = pick(place_ref[0])
+
+
+def unpack_rows(place, rows, *extra):
     packed = rows.transpose(2, 0, 1)
-    out = jax.ShapeDtypeStruct((rows.shape[1], D), BF16)
+    count = rows.shape[1]
+    counts = [count, count + sum(value.shape[0] for value in extra)]
+    fixed = lambda value: pl.BlockSpec(value.shape, lambda i, s: (0,) * len(value.shape))
     return pl.pallas_call(
         unpack_kernel,
         grid_spec=pltpu.PrefetchScalarGridSpec(
             num_scalar_prefetch=1, grid=(1,),
-            in_specs=[pl.BlockSpec(packed.shape, lambda i, s: (0, 0, 0))],
-            out_specs=[pl.BlockSpec(out.shape, lambda i, s: (0, 0))] * 2),
-        out_shape=[out, out],
+            in_specs=[fixed(packed)] + [fixed(value) for value in extra],
+            out_specs=[pl.BlockSpec((n, D), lambda i, s: (0, 0)) for n in counts]),
+        out_shape=[jax.ShapeDtypeStruct((n, D), BF16) for n in counts],
         compiler_params=pltpu.CompilerParams(vmem_limit_bytes=VMEM_CAP),
         cost_estimate=cost(5),
         name="unpack_rows",
-    )(place, packed)
+    )(place, packed, *extra)
 
 
 def decompress(compact):
@@ -310,7 +316,7 @@
 
 
 def middle_kernel(place_ref, att_ref, res_own, res_other, cot_own, cot_other, gain_ref, end_ref,
-                  fcb_ref, weights, two_ref, active_ref, hidden_ref, own_out, send_out,
+                  fcb_ref, weights, two_ref, active_ref, hidden_ref, own_out, send_first, send_second,
                   mid_ref, branch_ref, upgrad_ref, sums_ref, own_sums, other_sums,
                   out_w, fc_w, proj_w, sems, *, steps, chunk):
     at = pl.program_id(0)
@@ -389,9 +395,13 @@
     def _():
         own_out[...] = block_out
 
-    @pl.when(jnp.logical_not(mine))
-    def _():
-        send_out[...] = block_out
+    @pl.when(at == steps // 2)
+    def _():
+        send_first[...] = block_out
+
+    @pl.when(at == steps // 2 + 1)
+    def _():
+        send_second[...] = block_out
 
     cot = cot_low.astype(F32)
     mid_grad = cot + crms_back(normal, factor, gain, two_grad)
@@ -429,14 +439,14 @@
                       spec(D, other_map), pl.BlockSpec((1, D), fixed), pl.BlockSpec((2, D), fixed),
                       pl.BlockSpec((1, hid), fixed)] + [ANY] * 11,
             out_specs=[spec(D, whole_map), spec(hid, whole_map), spec(hid, whole_map),
-                       spec(D, own_map), spec(D, other_map),
+                       spec(D, own_map), spec(D, fixed), spec(D, fixed),
                        spec(D, whole_map), spec(D, whole_map), spec(D, whole_map),
                        pl.BlockSpec((8, D), fixed), pl.BlockSpec((8, hid // 2), fixed),
                        pl.BlockSpec((8, hid // 2), fixed)],
             scratch_shapes=[pltpu.VMEM((D, D), BF16), pltpu.VMEM((D, hid), BF16),
                             pltpu.VMEM((hid, D), BF16), pltpu.SemaphoreType.DMA((3, 9))]),
         out_shape=[sd((length, D), BF16), sd((length, hid), BF16), sd((length, hid), BF16),
-                   sd((length // 2, D), BF16), sd((length // 2, D), BF16),
+                   sd((length // 2, D), BF16), sd((block, D), BF16), sd((block, D), BF16),
                    sd((length, D), F32), sd((length, D), BF16), sd((length, D), BF16),
                    sd((8, D), F32), sd((8, hid // 2), F32), sd((8, hid // 2), F32)],
         compiler_params=pltpu.CompilerParams(vmem_limit_bytes=VMEM_CAP),
@@ -445,73 +455,111 @@
     )(place, att, res_own, res_other, cot_own, cot_other, gain, end_bias, fc_bias, *flat)
 
 
-def fc_grad_kernel(place_ref, left_ref, right_ref, keep_ref, send_ref, *, rows):
+def fc_out_grad_kernel(place_ref, left_ref, right_ref, att_ref, branch_ref, keep_ref, send_ref, rest, *, rows, parts):
+    at = pl.program_id(0)
     flip = (place_ref[1] & 1) == 1
+    out_rows = att_ref.shape[1] // 4
+
+    @pl.when(at == 0)
+    def _():
+        rest[...] = dot_tn_halves(att_ref, branch_ref).astype(BF16)
+
     both = dot_tn_halves(left_ref, right_ref).astype(BF16)
+    strip = out_rows // parts
     for pair in range(2):
+        to = pair ^ (place_ref[1] >> 1)
         low, high = both[2 * pair * rows : (2 * pair + 1) * rows], both[(2 * pair + 1) * rows : (2 * pair + 2) * rows]
-        to = pair ^ (place_ref[1] >> 1)
-        keep_ref[to, 0] = jnp.where(flip, high, low)
-        send_ref[to, 0] = jnp.where(flip, low, high)
-
-
-def fc_grad(place, left, right, chunk=768):
+        keep_ref[to, pl.ds(0, rows), :] = jnp.where(flip, high, low)
+        send_ref[to, pl.ds(0, rows), :] = jnp.where(flip, low, high)
+        base = 2 * pair * out_rows + at * strip
+        low = rest[pl.ds(pl.multiple_of(base, strip), strip), :]
+        high = rest[pl.ds(pl.multiple_of(base + out_rows, strip), strip), :]
+        keep_ref[to, pl.ds(rows, strip), :] = jnp.where(flip, high, low)
+        send_ref[to, pl.ds(rows, strip), :] = jnp.where(flip, low, high)
+
+
+def fc_out_grad(place, left, right, attended, branch, side, chunk=768):
     length, width = left.shape
     rows = width // 4
     half = right.shape[1] // 2
     parts = half // chunk
-    out = jax.ShapeDtypeStruct((2, 2, rows, half), BF16)
-    out_spec = pl.BlockSpec((2, 1, rows, chunk), lambda n, s: (0, n // parts, 0, n % parts))
+    att = attended.shape[1] // 2
+    strip = att // 4 // parts
+    out = jax.ShapeDtypeStruct((2, rows + strip, half), BF16)
+    out_spec = pl.BlockSpec((2, rows + strip, chunk), lambda n, s: (0, 0, n))
+    fixed = lambda value: pl.BlockSpec(value.shape, lambda n, s: (0, 0))
     return pl.pallas_call(
-        functools.partial(fc_grad_kernel, rows=rows),
+        functools.partial(fc_out_grad_kernel, rows=rows, parts=parts),
         grid_spec=pltpu.PrefetchScalarGridSpec(
-            num_scalar_prefetch=1, grid=(2 * parts,),
-            in_specs=[pl.BlockSpec((length, width), lambda n, s: (0, 0)),
-                      pl.BlockSpec((length, chunk), lambda n, s: (0, n))],
-            out_specs=[out_spec, out_spec]),
+            num_scalar_prefetch=1, grid=(parts,),
+            in_specs=[fixed(left), pl.BlockSpec((length, chunk), lambda n, s: (0, n + side * parts)),
+                      pl.BlockSpec((length, att), lambda n, s: (0, side)), fixed(branch)],
+            out_specs=[out_spec, out_spec],
+            scratch_shapes=[pltpu.VMEM((att, branch.shape[1]), BF16)]),
         out_shape=[out, out],
         compiler_params=pltpu.CompilerParams(vmem_limit_bytes=VMEM_CAP),
-        cost_estimate=cost(10),
-        name="fc_grad",
-    )(place, left, right)
-
-
-def qkv_grad_kernel(place_ref, left_ref, right_ref, keep_ref, send_ref, *, rows):
+        cost_estimate=cost(7),
+        name="fc_out_grad",
+    )(place, left, right, attended, branch)
+
+
+def qkv_grad_kernel(place_ref, left_ref, *refs, rows, parts, pieces):
+    right_refs, weight_refs = refs[:parts], refs[parts : parts + pieces]
+    keep_ref, send_ref, sum_ref, total = refs[parts + pieces :]
     flip = (place_ref[1] & 1) == 1
     half = left_ref.shape[0] // 2
-    width = right_ref.shape[2]
+    width = sum(ref.shape[2] for ref in right_refs)
     both = None
     for n in range(2):
         part = pl.ds(n * half, half)
-        right = jnp.concatenate([right_ref[c, part, :] for c in range(3)], axis=1)
+        right = jnp.concatenate([ref[c, part, :] for c in range(3) for ref in right_refs], axis=1)
         here = dot_tn(left_ref[part, :], right)
         both = here if both is None else both + here
-    both = both.astype(BF16)
-    for c in range(3):
-        low = both[:rows, c * width : (c + 1) * width]
-        high = both[rows:, c * width : (c + 1) * width]
-        keep_ref[0, c] = jnp.where(flip, high, low)
-        send_ref[0, c] = jnp.where(flip, low, high)
-
-
-def qkv_grad(place, left, rights):
+    low_both = both.astype(BF16)
+    for pair in range(2):
+        to = pair ^ (place_ref[1] >> 1)
+        for c in range(3):
+            cols = slice(c * width, (c + 1) * width)
+            low = low_both[2 * pair * rows : (2 * pair + 1) * rows, cols]
+            high = low_both[(2 * pair + 1) * rows : (2 * pair + 2) * rows, cols]
+            keep_ref[to, c] = jnp.where(flip, high, low)
+            send_ref[to, c] = jnp.where(flip, low, high)
+    sum_ref[...] = jnp.zeros_like(sum_ref)
+    if pieces > 1:
+        total[...] = both
+    span = both.shape[0] // pieces
+    for n in range(pieces):
+        at = pl.multiple_of((place_ref[1] ^ n) * span, span) if pieces > 1 else 0
+        folded = jnp.zeros((span, 128), F32)
+        for c in range(3):
+            here = total[pl.ds(at, span), pl.ds(c * width, width)] if pieces > 1 else both[:, c * width : (c + 1) * width]
+            product = here * weight_refs[n][c].astype(F32)
+            for k in range(0, width, 128):
+                folded = folded + product[:, k : k + 128]
+        total[pl.ds(at, span), pl.ds(0, 128)] = folded
+    sum_ref[0:1, :] = column_sum(jnp.transpose(total[:, 0:128]))
+
+
+def qkv_grad(place, left, rights, weights, col_at=0):
     length, width = left.shape
     rows = width // 4
-    cols = rights.shape[2]
+    cols = sum(value.shape[2] for value in rights)
     out = jax.ShapeDtypeStruct((2, 3, rows, cols), BF16)
-    out_spec = pl.BlockSpec((1, 3, rows, cols), lambda j, s: (j ^ (s[1] >> 1), 0, 0, 0))
+    whole = lambda value: pl.BlockSpec(value.shape, lambda i, s: (0,) * len(value.shape))
+    sums = jax.ShapeDtypeStruct((8, width), F32)
     return pl.pallas_call(
-        functools.partial(qkv_grad_kernel, rows=rows),
+        functools.partial(qkv_grad_kernel, rows=rows, parts=len(rights), pieces=len(weights)),
         grid_spec=pltpu.PrefetchScalarGridSpec(
-            num_scalar_prefetch=1, grid=(2,),
-            in_specs=[pl.BlockSpec((length, 2 * rows), lambda j, s: (0, j)),
-                      pl.BlockSpec((3, length, cols), lambda j, s: (0, 0, 0))],
-            out_specs=[out_spec, out_spec]),
-        out_shape=[out, out],
+            num_scalar_prefetch=1, grid=(1,),
+            in_specs=[whole(value) for value in (left, *rights)]
+            + [pl.BlockSpec((3, value.shape[1], cols), lambda i, s: (0, 0, col_at)) for value in weights],
+            out_specs=[whole(out), whole(out), whole(sums)],
+            scratch_shapes=[pltpu.VMEM((width, 3 * cols), F32)]),
+        out_shape=[out, out, sums],
         compiler_params=pltpu.CompilerParams(vmem_limit_bytes=VMEM_CAP),
-        cost_estimate=cost(5),
+        cost_estimate=cost(6.5),
         name="qkv_grad",
-    )(place, left, rights)
+    )(place, left, *rights, *weights)
 
 
 def proj_grad_kernel(place_ref, own_act, other_act, own_cot, other_cot, keep_ref, send_ref, *, rows):
@@ -543,37 +591,8 @@
     )(place, active, active, cot_own, cot_other)
 
 
-def out_grad_kernel(place_ref, left_ref, right_ref, keep_ref, send_ref, *, rows):
-    flip = (place_ref[1] & 1) == 1
-    both = dot_tn_halves(left_ref, right_ref).astype(BF16)
-    for side in range(2):
-        for pair in range(2):
-            at = (side * 4 + pair * 2) * rows
-            low, high = both[at : at + rows], both[at + rows : at + 2 * rows]
-            to = pair ^ (place_ref[1] >> 1)
-            keep_ref[to, side] = jnp.where(flip, high, low)
-            send_ref[to, side] = jnp.where(flip, low, high)
-
-
-def out_grad(place, left, right):
-    length, width = left.shape
-    rows = width // 8
-    out = jax.ShapeDtypeStruct((2, 2, rows, right.shape[1]), BF16)
-    return pl.pallas_call(
-        functools.partial(out_grad_kernel, rows=rows),
-        grid_spec=pltpu.PrefetchScalarGridSpec(
-            num_scalar_prefetch=1, grid=(1,),
-            in_specs=[pl.BlockSpec(value.shape, lambda i, s: (0, 0)) for value in (left, right)],
-            out_specs=[pl.BlockSpec(out.shape, lambda i, s: (0, 0, 0, 0))] * 2),
-        out_shape=[out, out],
-        compiler_params=pltpu.CompilerParams(vmem_limit_bytes=VMEM_CAP),
-        cost_estimate=cost(5),
-        name="out_grad",
-    )(place, left, right)
-
-
-def input_grad_kernel(place_ref, own_grad, other_grad, res_own, res_other, mid_ref, gain_ref, w_own, w_quarter,
-                      own_out, send_out, sums_ref, weight, sems, *, steps):
+def input_grad_kernel(place_ref, own_grads, other_grads, res_own, res_other, mid_ref, gain_ref, w_own, w_quarter,
+                      own_out, send_out, weight, sems, *, steps):
     at = pl.program_id(0)
     quarter = D // 4
     half = w_own.shape[2]
@@ -594,7 +613,6 @@
     def _():
         for copy in copies():
             copy.start()
-        sums_ref[...] = jnp.zeros_like(sums_ref)
 
     mine = at < steps // 2
     compact = jnp.where(mine, res_own[...], res_other[...]).astype(F32)
@@ -605,9 +623,8 @@
         for copy in copies():
             copy.wait()
 
-    left = jnp.concatenate([own_grad[c] for c in range(3)] + [other_grad[c] for c in range(3)], axis=1)
+    left = jnp.concatenate([ref[c] for part in (own_grads, other_grads) for c in range(3) for ref in part], axis=1)
     grad = dot_nt(left, weight[...])
-    sums_ref[0:1, :] += column_sum(grad * normal)
     result = (mid_ref[...] + crms_back(normal, factor, gain_ref[...], grad)).astype(BF16)
 
     @pl.when(mine)
@@ -619,35 +636,32 @@
         send_out[...] = result
 
 
-def input_grad(place, own_grad, other_grad, res_own, res_other, mid, gain, w_own, w_quarter, steps=4):
+def input_grad(place, own_grads, other_grads, res_own, res_other, mid, gain, w_own, w_quarter, steps=4):
     length = mid.shape[0]
     block = length // steps
     own_map, other_map, whole_map = row_maps(steps)
     fixed = lambda i, s: (0, 0)
-    half = own_grad.shape[2]
-    grad_spec = pl.BlockSpec((3, block, half), lambda i, s: (0, whole_map(i, s)[0], 0))
+    mine, many = len(own_grads), len(own_grads) + len(other_grads)
+    grad_spec = lambda value: pl.BlockSpec((3, block, value.shape[2]), lambda i, s: (0, whole_map(i, s)[0], 0))
 
     def body(place_ref, *refs):
-        input_grad_kernel(place_ref, *refs[:7], refs[7:11], *refs[11:], steps=steps)
+        rest = refs[many:]
+        input_grad_kernel(place_ref, refs[:mine], refs[mine:many], *rest[:5], rest[5:9], *rest[9:], steps=steps)
 
     sd = jax.ShapeDtypeStruct
     return pl.pallas_call(
         body,
         grid_spec=pltpu.PrefetchScalarGridSpec(
             num_scalar_prefetch=1, grid=(steps,),
-            in_specs=[grad_spec, grad_spec, pl.BlockSpec((block, D), own_map), pl.BlockSpec((block, D), other_map),
+            in_specs=[grad_spec(value) for value in (*own_grads, *other_grads)] + [pl.BlockSpec((block, D), own_map), pl.BlockSpec((block, D), other_map),
                       pl.BlockSpec((block, D), whole_map), pl.BlockSpec((1, D), fixed)] + [ANY] * 5,
-            out_specs=[pl.BlockSpec((block, D), own_map), pl.BlockSpec((block, D), other_map),
-                       pl.BlockSpec((8, D), fixed)],
+            out_specs=[pl.BlockSpec((block, D), own_map), pl.BlockSpec((block, D), other_map)],
             scratch_shapes=[pltpu.VMEM((D, 3 * D), BF16), pltpu.SemaphoreType.DMA((3, 5))]),
-        out_shape=[sd((length // 2, D), BF16), sd((length // 2, D), BF16), sd((8, D), F32)],
+        out_shape=[sd((length // 2, D), BF16), sd((length // 2, D), BF16)],
         compiler_params=pltpu.CompilerParams(vmem_limit_bytes=VMEM_CAP),
         cost_estimate=cost(9),
         name="input_grad",
-    )(place, own_grad, other_grad, res_own, res_other, mid, gain, w_own, *w_quarter)
-
-
-FORWARD_SPLIT = ((0, 2), (2, 3), (5, 1))
+    )(place, *own_grads, *other_grads, res_own, res_other, mid, gain, w_own, *w_quarter)
 
 
 def swap(value, axis, bit, size):
@@ -665,26 +679,16 @@
     return total.astype(BF16)
 
 
-def fours(value, axis, size):
-    return [swap(value, axis, rel, size) for rel in (1, 2, 3)]
-
-
-def sum_fours(value, others):
-    return (value + others[0]) + (others[1] + others[2])
-
-
-def quarter_of(value, index):
-    rows = value.shape[0] // 4
-    return lax.dynamic_slice_in_dim(value, index * rows, rows, 0)
-
-
-def in_order(parts, index):
-    odd, high = (index & 1) == 1, (index & 2) == 2
-    flip = lambda flag, a, b: (jnp.where(flag, b, a), jnp.where(flag, a, b))
-    parts = [*flip(odd, parts[0], parts[1]), *flip(odd, parts[2], parts[3])]
-    first, third = flip(high, parts[0], parts[2])
-    second, fourth = flip(high, parts[1], parts[3])
-    return jnp.concatenate([first, second, third, fourth], 0)
+def chain_in(value):
+    return lax.ppermute(value, "group", [(0, 1), (3, 2)])
+
+
+def chain_across(value):
+    return lax.ppermute(value, "group", [(1, 2), (2, 1)])
+
+
+def chain_out(value):
+    return lax.ppermute(value, "group", [(1, 0), (2, 3)])
 
 
 def on_device(sizes, residual_in, piece_ids, norm_gains, qkv_weight, qv_bias, out_weight, fc_weight,
@@ -711,55 +715,51 @@
 
     qkv_piece = piece_of(qkv_weight, 1, quarter_at)
     qkv_y = y_swap(qkv_piece)
-    res_own, res_send = unpack_rows(after(place, qkv_piece), residual_in)
-    small_bias = jnp.concatenate([qv_bias.reshape(1, -1), fc_bias.reshape(1, -1)], axis=1)
-    qkv_y, res_own, res_send, small_bias, out_gated, fc_gated, proj_gated = meet(
-        qkv_y, res_own, res_send, small_bias, out_weight, fc_weight, proj_weight)
+    bias_rows = jnp.concatenate([fc_bias.reshape(-1, D), qv_bias.reshape(1, D), jnp.zeros((13, D), BF16)], 0)
+    res_own, res_send = unpack_rows(after(place, qkv_piece), residual_in, bias_rows)
+    qkv_y, res_own, res_send, out_gated, fc_gated, proj_gated = meet(
+        qkv_y, res_own, res_send, out_weight, fc_weight, proj_weight)
     res_other = y_swap(res_send)
-    other_bias = y_swap(small_bias)
     qkv_x = x_swap(qkv_y)
     qkv_c = c_swap(qkv_y)
     fc_piece = piece_of(fc_gated, 0, quarter_at)
     mix = jnp.concatenate([jnp.pad(piece_of(out_gated, 0, quarter_at), pad)]
                           + [fc_piece[:, n : n + D] for n in range(0, hid, D)], 0)
     proj_piece = jnp.pad(piece_of(proj_gated, 0, proj_at), pad)
+    qkv_c, mix, proj_piece = meet(qkv_c, mix, proj_piece)
+    mix_y, proj_y = y_swap(mix), y_swap(proj_piece)
     cot_own, cot_send = unpack_rows(after(place, mix, proj_piece), cotangent)
     out_own = jnp.pad(out_gated, pad)
     proj_own = jnp.pad(proj_gated, pad)
-    qkv_x, qkv_c, res_other, other_bias, mix, proj_piece, cot_send, out_own, proj_own = meet(
-        qkv_x, qkv_c, res_other, other_bias, mix, proj_piece, cot_send, out_own, proj_own)
-    mix_y = y_swap(mix)
+    qkv_x, res_other, out_own, proj_own, cot_send = meet(qkv_x, res_other, out_own, proj_own, cot_send)
     qkv_cx = c_swap(qkv_x)
     qkv_others = (qkv_y, qkv_c, qkv_x, qkv_cx)
 
     gains = norm_gains.astype(F32)
     end_biases = jnp.pad(out_biases, pad).astype(F32)
-    qv_other = other_bias[:, : 2 * half].reshape(2, half)
-    qv_full = jnp.concatenate([qv_bias, qv_other], axis=1).astype(F32)
-    fc_full = jnp.concatenate([fc_bias.reshape(1, -1), other_bias[:, 2 * half :]], axis=1).astype(F32)
+    count = residual_in.shape[1]
+    bias_other = res_other[count : count + 8].astype(F32)
+    fc_rows = hid // D
+    qv_full = jnp.concatenate([qv_bias.astype(F32), bias_other[fc_rows].reshape(2, half)], axis=1)
+    fc_full = jnp.concatenate([fc_bias.astype(F32).reshape(1, -1), bias_other[:fc_rows].reshape(1, -1)], axis=1)
     length = piece_ids.shape[1]
     flags = (lax.dynamic_index_in_dim(piece_ids, tensor_at, 0, keepdims=False)[:: length // 4] >= 0)
     flags = flags.astype(jnp.int32)
 
     normed_one, queries, key_rows, value_rows = project(
         place, res_own, res_other, gains[0:1], qv_full, qkv_weight, qkv_others)
-    queries, proj_piece = meet(queries, proj_piece)
-    attended = None
-    proj_y = y_swap(proj_piece)
-    for n, (start, count) in enumerate(FORWARD_SPLIT):
-        if n == 1:
-            attended[0], attended[1], queries, mix_y, cot_send = meet(*attended, queries, mix_y, cot_send)
-            mix_x, mix_c = x_swap(mix_y), c_swap(mix_y)
-            cot_other = y_swap(cot_send)
-        elif n == 2:
-            attended[0], attended[1], queries, proj_y = meet(*attended, queries, proj_y)
-            proj_x, proj_c = z_swap(proj_y), c_swap(proj_y)
-        attended = list(attend_forward(flags, queries, key_rows, value_rows, start, count, attended))
-    attended, log_sums, mix_x, proj_x = meet(*attended, mix_x, proj_x)
+    queries, cot_send = meet(queries, cot_send)
+    cot_other = y_swap(cot_send)
+    attended = attend_forward(flags, queries, key_rows, value_rows, 0, pairs)
+    *attended, queries, mix_y, proj_y = meet(*attended, queries, mix_y, proj_y)
+    mix_x, mix_c = x_swap(mix_y), c_swap(mix_y)
+    proj_x, proj_c = z_swap(proj_y), c_swap(proj_y)
+    attended = attend_forward(flags, queries, key_rows, value_rows, pairs, pairs, attended)
+    attended, log_sums, mix_x, proj_x, cot_other = meet(*attended, mix_x, proj_x, cot_other)
     mix_others = (mix_y, mix_c, mix_x, c_swap(mix_x))
     proj_others = (proj_y, proj_c, proj_x, c_swap(proj_x))
 
-    (normed_two, active, hidden_grad, out_mine, out_send, middle_grad, branch_grad, attended_grad,
+    (normed_two, active, hidden_grad, out_mine, *out_send, middle_grad, branch_grad, attended_grad,
      middle_sums, own_sums, other_sums) = middle_stage(
         place, attended, res_own, res_other, cot_own, cot_other, gains[1:2], end_biases, fc_full,
         (out_own, fc_weight, proj_own, mix_others, proj_others))
@@ -767,85 +767,114 @@
     restore = lambda mine, got: jnp.where(
         tensor_at == 0, jnp.stack([mine, got]), jnp.stack([got, mine]))[:, :, : D - 1]
 
+    def small_outputs(small):
+        part, first = hid // n_dp, half // n_dp
+        return (jnp.concatenate([small[0:1, :D], small[0:1, D : 2 * D]], 0),
+                lax.dynamic_slice(small, (0, 2 * D + hid + dp_at * first), (2, first)),
+                lax.dynamic_slice(small, (0, 2 * D + dp_at * part), (1, part)).reshape(part),
+                small[1:3, D : 2 * D - 1])
+
     if n_dp == 4 and n_group == 4:
-        out_got = y_swap(out_send)
+        out_got = [y_swap(value) for value in out_send]
         proj_k, proj_s = proj_grad(after(place, middle_sums), active, cot_own, cot_other)
+        proj_k, proj_s, out_got[0] = meet(proj_k, proj_s, out_got[0])
         proj_c = c_swap(proj_s)
-        fc_k, fc_s = fc_grad(after(place, proj_k), normed_two, hidden_grad)
-        fc_k, fc_s, proj_k, proj_c, out_got = meet(fc_k, fc_s, proj_k, proj_c, out_got)
-        fc_c = c_swap(fc_s)
+        weights_of = lambda gate, side: fc_out_grad(
+            after(place, gate), normed_two, hidden_grad, attended, branch_grad, side)
+        fo_k, fo_s = weights_of(proj_k, 1)
+        fo_k, fo_s, proj_k, proj_c = meet(fo_k, fo_s, proj_k, proj_c)
+        fo_c = c_swap(fo_s)
         proj_f = add_low(proj_k[1], proj_c[1])
         proj_x = x_swap(proj_f)
-        out_k, out_s = out_grad(after(place, proj_f), attended, branch_grad)
-        out_k, out_s, fc_k, fc_c = meet(out_k, out_s, fc_k, fc_c)
-        out_c = c_swap(out_s)
-        fc_away = add_low(fc_k[:, 1], fc_c[:, 1])
+        fm_k, fm_s = weights_of(proj_f, 0)
+        fm_k, fm_s, fo_k, fo_c, *out_got = meet(fm_k, fm_s, fo_k, fo_c, *out_got)
+        fm_c = c_swap(fm_s)
+        fc_away = add_low(fo_k, fo_c)
         fc_y = y_swap(fc_away)
         first, first_sums = backward(after(attended_grad, fc_away), log_sums, pairs, pairs)
-        first, first_sums, proj_k, proj_c, proj_x, out_k, out_c = meet(
-            first, first_sums, proj_k, proj_c, proj_x, out_k, out_c)
+        first, first_sums, proj_k, proj_c, proj_x, fm_k, fm_c = meet(
+            first, first_sums, proj_k, proj_c, proj_x, fm_k, fm_c)
         proj_r = [add_low(proj_k[0, n], proj_c[0, n], proj_x[n]) for n in range(2)]
         proj_y = y_swap(proj_r[1])
-        out_f = add_low(out_k[1], out_c[1])
-        out_x = x_swap(out_f)
-        qo_k, qo_s = qkv_grad(after(place, proj_r[1], out_f), normed_one, first)
-        qo_k, qo_s, fc_k, fc_c, fc_y, out_k, out_c, out_x = meet(qo_k, qo_s, fc_k, fc_c, fc_y, out_k, out_c, out_x)
+        qo_k, qo_s, qo_sum = qkv_grad(after(place, proj_r[1]), normed_one, [first], qkv_others)
+        qo_k, qo_s, fm_k, fm_c, fc_y = meet(qo_k, qo_s, fm_k, fm_c, fc_y)
         qo_c = c_swap(qo_s)
-        fc_far = add_low(fc_k[1, 0], fc_c[1, 0], fc_y[1])
+        fc_far = add_low(fm_k[1], fm_c[1], fc_y[1])
         fc_x = x_swap(fc_far)
-        out_r = [add_low(out_k[0, n], out_c[0, n], out_x[n]) for n in range(2)]
-        out_y = y_swap(out_r[1])
-        second, second_sums = backward(after(attended_grad, fc_far, out_r[1]), log_sums, 0, pairs)
-        second, second_sums, proj_y, fc_x, out_y, qo_k, qo_c = meet(
-            second, second_sums, proj_y, fc_x, out_y, qo_k, qo_c)
+        own_a, sums_a = backward(after(attended_grad, fc_far), log_sums, 0, pairs - 1)
+        own_a, sums_a, proj_y, fc_x, qo_k, qo_c = meet(own_a, sums_a, proj_y, fc_x, qo_k, qo_c)
         proj_shard = add_low(proj_r[0], proj_y)
-        fc_shard = add_low(fc_k[0, 0], fc_c[0, 0], fc_y[0], fc_x)
-        proj_shard, fc_shard = lax.psum((proj_shard, fc_shard), "group")
+        proj_z = chain_in(proj_shard)
+        fc_shard = add_low(fm_k[0], fm_c[0], fc_y[0], fc_x)
+        fc_z = chain_in(fc_shard)
         qo_f = add_low(qo_k[1], qo_c[1])
         qo_x = x_swap(qo_f)
-        qm_k, qm_s = qkv_grad(after(place, qo_f), normed_one, second)
-        qm_k, qm_s, qo_k, qo_c, qo_x = meet(qm_k, qm_s, qo_k, qo_c, qo_x)
+        own_b, sums_b = backward(after(attended_grad, qo_f, proj_shard, fc_shard), log_sums, pairs - 1, 1)
+        qm_k, qm_s, qm_sum = qkv_grad(after(place, own_b), normed_one, [own_a, own_b], [qkv_weight])
+        qm_k, qm_s, qm_sum, qo_k, qo_c, qo_x, proj_shard, proj_z = meet(
+            qm_k, qm_s, qm_sum, qo_k, qo_c, qo_x, proj_shard, proj_z)
         qm_c = c_swap(qm_s)
         qo_r = add_low(qo_k[0], qo_c[0], qo_x)
         qo_y = y_swap(qo_r)
-        small_y = [y_swap(value) for value in meet(middle_sums, other_sums, first_sums, qo_r)[:3]]
-        block_out = restore(after(out_mine, qo_r), out_got)
-        qm_k, qm_c, block_out = meet(qm_k, qm_c, block_out)
+        proj_shard = add_low(proj_shard, proj_z)
+        proj_z = chain_across(proj_shard)
+        in_sums = (qm_sum + qo_sum) / gains[0:1]
+        small = jnp.concatenate([in_sums, middle_sums, own_sums, sums_a, sums_b], 1)
+        small_y = y_swap(jnp.concatenate([in_sums, middle_sums, other_sums, first_sums], 1))
+        qm_k, qm_c, qo_r, proj_shard, small, small_y = meet(qm_k, qm_c, qo_r, proj_shard, small, small_y)
         qm_f = add_low(qm_k[1], qm_c[1])
         qm_x = x_swap(qm_f)
-        in_mine, in_send, in_sums = input_grad(
-            after(place, qm_f), second, first, res_own, res_other, middle_grad, gains[0:1], qkv_weight, qkv_others)
-        in_mine, in_send, in_sums, qm_x, qo_y, *small_y = meet(in_mine, in_send, in_sums, qm_x, qo_y, *small_y)
-        in_y = y_swap(in_sums)
+        small = small + small_y
+        small_c = c_swap(small)
+        in_mine, in_send = input_grad(
+            after(place, qm_f, small), [own_a, own_b], [first], res_own, res_other, middle_grad, gains[0:1],
+            qkv_weight, qkv_others)
+        in_mine, in_send, qm_x, qo_y, fc_shard, fc_z, proj_shard, proj_z, small, small_c = meet(
+            in_mine, in_send, qm_x, qo_y, fc_shard, fc_z, proj_shard, proj_z, small, small_c)
+        last = add_low(qm_k[0], qm_c[0], qm_x, qo_y)
+        last_z = z_swap(last)
+        fc_shard = add_low(fc_shard, fc_z)
+        fc_z = chain_across(fc_shard)
+        proj_shard = add_low(proj_shard, proj_z)
+        proj_z = chain_out(proj_shard)
         in_got = y_swap(in_send)
-        small = jnp.concatenate(
-            [middle_sums + small_y[0], own_sums + small_y[1], second_sums + small_y[2]], 1)
-        small_dp = fours(small, "dp", n_dp)
-        last = jnp.concatenate([add_low(qm_k[0], qm_c[0], qm_x, qo_y).reshape(-1, D), add_low(out_r[0], out_y)], 0)
-        last_z = [swap(quarter_of(last, group_at ^ rel), "group", rel, n_group) for rel in (1, 2, 3)]
-        small, in_sums, in_y, *small_dp = meet(small, in_sums, in_y, *small_dp)
-        in_sums = in_sums + in_y
-        in_dp = fours(in_sums, "dp", n_dp)
-        small = sum_fours(small, small_dp)
-        last, in_sums, *others = meet(last, in_sums, *last_z, *in_dp)
-        total = add_low(quarter_of(last, group_at), *others[:3])
-        total_z = fours(total, "group", n_group)
-        in_sums = sum_fours(in_sums, others[3:])
-        in_z = fours(in_sums, "group", n_group)
-        small_z = fours(small, "group", n_group)
-        small = sum_fours(small, small_z)
-        in_sums = sum_fours(in_sums, in_z)
-        total, small, in_sums, proj_shard, fc_shard = meet(total, small, in_sums, proj_shard, fc_shard)
-        last = in_order([total] + total_z, group_at).astype(F32)
-        qkv_shard = last[: 3 * D // 8].reshape(3, D // 4, half)
-        out_shard = last[3 * D // 8 :]
+        small = small + small_c
+        small_x = x_swap(small)
+        block_out = restore(after(out_mine, last, fc_shard, proj_shard, small), jnp.concatenate(out_got, 0))
+        last, last_z, block_out, small, small_x = meet(last, last_z, block_out, small, small_x)
+        low_part, high_part = add_low(last[:2], last_z[:2]), add_low(last[2:], last_z[2:])
+        low_z = swap(low_part, "group", 2, n_group)
+        high_z = swap(high_part, "group", 2, n_group)
+        small = small + small_x
+        small_z = z_swap(small)
+        middle_one = (group_at == 1) | (group_at == 2)
+        fc_shard, fc_z, proj_shard, proj_z, in_mine, in_got, low_part, low_z, small, small_z = meet(
+            fc_shard, fc_z, proj_shard, proj_z, in_mine, in_got, low_part, low_z, small, small_z)
+        fc_shard = add_low(fc_shard, fc_z)
+        fc_z = chain_out(fc_shard)
+        small = small + small_z
+        small_z = swap(small, "group", 2, n_group)
+        in_out = restore(after(in_mine, fc_shard, small), in_got)
+        proj_shard = jnp.where(middle_one, proj_shard, proj_z)[:, : D - 1].astype(F32)
+        low_part = add_low(low_part, low_z).astype(F32)
+        in_out, proj_shard, low_part, small, small_z = meet(in_out, proj_shard, low_part, small, small_z)
+        small = small_outputs(small + small_z)
+        high_part, high_z, in_out, proj_shard, low_part, fc_shard, fc_z, *small = meet(
+            high_part, high_z, in_out, proj_shard, low_part, fc_shard, fc_z, *small)
+        qkv_shard = jnp.concatenate([low_part, add_low(high_part, high_z).astype(F32)], 0)
+        fc_shard = jnp.where(middle_one, fc_shard, fc_z).astype(F32)
+        rest = fc_shard[D // 4 :]
+        out_shard = jnp.concatenate([rest[:, n : n + D - 1] for n in range(0, hid, D)], 0)
+        fc_shard = fc_shard[: D // 4]
     else:
         first, first_sums = backward(attended_grad, log_sums, pairs, pairs)
-        second, second_sums = backward(attended_grad, log_sums, 0, pairs)
-        in_mine, in_send, in_sums = input_grad(
-            place, second, first, res_own, res_other, middle_grad, gains[0:1], qkv_weight, qkv_others)
-        in_got = y_swap(in_send)
-        block_out = restore(out_mine, y_swap(out_send))
+        own, second_sums = backward(attended_grad, log_sums, 0, pairs)
+        in_mine, in_send = input_grad(
+            place, [own], [first], res_own, res_other, middle_grad, gains[0:1], qkv_weight, qkv_others)
+        in_out = restore(in_mine, y_swap(in_send))
+        block_out = restore(out_mine, y_swap(jnp.concatenate(out_send, 0)))
+        qo_sum = qkv_grad(place, normed_one, [first], qkv_others)[2]
+        qm_sum = qkv_grad(place, normed_one, [own], [qkv_weight])[2]
 
         def scatter(own, other):
             total = [lax.psum_scatter(value.astype(BF16), "dp", scatter_dimension=0, tiled=True)
@@ -857,30 +886,26 @@
         proj_shard = scatter(dot_tn(active[:, :hid], cot_rows), dot_tn(active[:, hid:], cot_rows))
         fc_shard = scatter(dot_tn(normed_two, hidden_grad[:, :hid]), dot_tn(normed_two, hidden_grad[:, hid:]))
         out_shard = scatter(dot_tn(attended[:, :half], branch_grad), dot_tn(attended[:, half:], branch_grad))
+        proj_shard, out_shard = proj_shard[:, : D - 1].astype(F32), out_shard[:, : D - 1].astype(F32)
+        fc_shard = fc_shard.astype(F32)
         qkv_shard = jnp.swapaxes(scatter(
-            *[jnp.stack([dot_tn(normed_one, part[c]) for c in range(3)], 1) for part in (second, first)]), 0, 1)
-        small = jnp.concatenate([
-            middle_sums + y_swap(middle_sums), own_sums + y_swap(other_sums), second_sums + y_swap(first_sums)], 1)
-        small = lax.psum(small, ("dp", "group"))
-        in_sums = lax.psum(in_sums, ("dp", "group", "tensor"))
-
-    grad_gains = jnp.concatenate([in_sums[0:1], small[0:1, :D]], 0)
-    grad_out_biases = small[1:3, : D - 1]
-    part = hid // n_dp
-    grad_fc_bias = lax.dynamic_slice(small, (0, D + dp_at * part), (1, part)).reshape(part)
-    part = half // n_dp
-    grad_qv_bias = lax.dynamic_slice(small, (0, D + hid + dp_at * part), (2, part))
-
+            *[jnp.stack([dot_tn(normed_one, part[c]) for c in range(3)], 1) for part in (own, first)]), 0, 1)
+        in_sums = (qm_sum + qo_sum) / gains[0:1]
+        small = jnp.concatenate([in_sums, middle_sums, own_sums, second_sums], 1)
+        small = small + y_swap(jnp.concatenate([in_sums, middle_sums, other_sums, first_sums], 1))
+        small = small_outputs(lax.psum(small, ("dp", "group")))
+
+    grad_gains, grad_qv_bias, grad_fc_bias, grad_out_biases = small
     return (
         block_out,
-        restore(in_mine, in_got),
+        in_out,
         grad_gains,
         qkv_shard.astype(F32),
         grad_qv_bias,
-        out_shard[:, : D - 1].astype(F32),
-        fc_shard.astype(F32),
+        out_shard,
+        fc_shard,
         grad_fc_bias,
-        proj_shard[:, : D - 1].astype(F32),
+        proj_shard,
         grad_out_biases,
     )
 

time: 371 us -> 348 us (0.938)
  starting transfers between devices: 66.6 us -> 43.4 us
  between operations: 15 us -> 1.62 us
  waiting for transfers between devices: 47.9 us -> 55.2 us
    ppermute x53 -> x37, starting transfers between devices: 66.6 us -> 32.5 us  [swap(): return lax.ppermute(value, axis, [(n, n ^ bit) for n in range(size)])]
    ppermute x0 -> x6, waiting for transfers between devices: none -> 12.2 us  [the longest x2 12.1 us: chain_out(): return lax.ppermute(value, 'group', [(1, 0), (2, 3)])]
    ppermute x0 -> x6, starting transfers between devices: none -> 10.9 us  [the longest x2 5.81 us: chain_in(): return lax.ppermute(value, 'group', [(0, 1), (3, 2)])]
    ppermute x53 -> x37, waiting for transfers between devices: 47.8 us -> 43 us  [swap(): return lax.ppermute(value, axis, [(n, n ^ bit) for n in range(size)])]
    unnamed x59 -> x108, local copies, waits for them, and re-layouts: 10.7 us -> 13.7 us
    pallas_call x2 -> x3, Pallas kernels: 36.6 us -> 39.1 us  [attend_backward(): pl.pallas_call(functools.partial(attend_backward_kernel, block=length //...]
    pallas_call x3 -> x2, Pallas kernels: 27.7 us -> 25.3 us  [attend_forward(): pl.pallas_call(body, grid_spec=pltpu.PrefetchScalarGridSpec(num_scalar_pr...]
    convert_element_type x14 -> x16, other arithmetic: 24.2 us -> 25 us  [add_low(): return total.astype(BF16)]
  transfers between devices with their start and end apart: 54 -> 43, of which waited for: 14 -> 14; matrix products, arithmetic and copies ran while one was open for 14% -> 13% of each run, Pallas kernels for 35% -> 41%
where the time goes in v3:
time: 348 us; the launch traced here: 342 us
  Pallas kernels  177 us (51%)
  waiting for transfers between devices  55.2 us (16%)
  starting transfers between devices  43.4 us (12%)
  other arithmetic  41.1 us (12%)
  local copies, waits for them, and re-layouts  23.5 us (7%)
    ppermute x37, waiting for transfers between devices, swap(): return lax.ppermute(value, axis, [(n, n ^ bit) for n in range(size)])  43 us
    pallas_call x3, Pallas kernels, attend_backward(): pl.pallas_call(functools.partial(attend_backward_kernel, block=length //...  39.1 us
    pallas_call x1, Pallas kernels, middle_stage(): pl.pallas_call(body, grid_spec=pltpu.PrefetchScalarGridSpec(num_scalar_pr...  38 us
    ppermute x37, starting transfers between devices, swap(): return lax.ppermute(value, axis, [(n, n ^ bit) for n in range(size)])  32.5 us
    pallas_call x2, Pallas kernels, attend_forward(): pl.pallas_call(body, grid_spec=pltpu.PrefetchScalarGridSpec(num_scalar_pr...  25.3 us
    convert_element_type x16, other arithmetic, add_low(): return total.astype(BF16)  25 us
    pallas_call x2, Pallas kernels, fc_out_grad(): pl.pallas_call(functools.partial(fc_out_grad_kernel, rows=rows, parts=par...  16.9 us
    unnamed x108, local copies, waits for them, and re-layouts  13.7 us
  transfers between devices with their start and end apart: 43, of which 14 were waited for; matrix products, arithmetic and copies ran while one was open for 13% of the time, Pallas kernels for 41%

profile of v3, /device:TPU:0, one launch (start us, length us, event | category | flops | bytes accessed | tf_op | source)
XLA Modules:
  0.0 342.3 jit_solution(17533202367020015825)
XLA Ops:
  1.7 3.0 collective-permute-start
  8.3 6.1 %unpack_rows.2 = (bf16[512,768]{1,0:T(8,128)(2,1)}, bf16[528,768]{1,0:T(8,128)(2,1)}) custom-call(s32[3]{0:T(128)} %pad_add_fusion.place_ref, bf16[767,2,512]{2,1,0:T(2,128)(2,1)} %bitcast.58, bf16[16,768]{1,0:T(8,128)(2,1)} %maximum_maximum_fusion.refs_0_), custom_call_target="tpu_custom_call" | custom-call | flops 2000000000 | bytes 2000000 | tf_op jit(solution)/shard_map/unpack_rows/pallas_call | solution.py:199
  15.7 1.7 collective-permute-start.2
  18.0 1.5 collective-permute-start.1
  19.4 1.7 pad.20.refs_10_
  23.1 1.1 constant_dynamic-slice_fusion
  24.8 1.5 collective-permute-start.6
  26.3 5.7 %unpack_rows.3 = (bf16[512,768]{1,0:T(8,128)(2,1)}, bf16[512,768]{1,0:T(8,128)(2,1)}) custom-call(s32[3]{0:T(128)} %pad_add_fusion.place_ref, bf16[767,2,512]{2,1,0:T(2,128)(2,1)} %bitcast.59), custom_call_target="tpu_custom_call" | custom-call | flops 2000000000 | bytes 2000000 | tf_op jit(solution)/shard_map/unpack_rows/pallas_call | solution.py:199
  32.1 4.9 %collective-permute-done.2.other_ref.refs_2_.refs_4_ = bf16[528,768]{1,0:T(8,128)(2,1)S(1)} collective-permute-done((bf16[528,768]{1,0:T(8,128)(2,1)}, bf16[528,768]{1,0:T(8,128)(2,1)S(1)}, u32[]{:S(2)}, u32[]{:S(2)}) %collective-permute-start.2) | collective-permute-done | bytes 811040 | tf_op jit(solution)/shard_map/ppermute | solution.py:668
  37.7 1.3 collective-permute-done.4.d.refs_4_.refs_11_
  39.7 10.6 %norm_project.1 = (bf16[1024,768]{1,0:T(8,128)(2,1)}, bf16[1024,768]{1,0:T(8,128)(2,1)}, bf16[1024,768]{1,0:T(8,128)(2,1)}, bf16[1024,768]{1,0:T(8,128)(2,1)}) custom-call(s32[3]{0:T(128)} %pad_add_fusion.place_ref, bf16[512,768]{1,0:T(8,128)(2,1)} %get-tuple-element.181.own_ref.refs_1_.refs_3_, bf16[528,768]{1,0:T(8,128)(2,1)} %copy-done.38, ...), custom_call_target="tpu_custom_call" | custom-call | flops 4000000000 | bytes 4000000 | tf_op jit(solution)/shard_map/norm_project/pallas_call | solution.py:290
  50.3 1.8 collective-permute-start.9
  52.1 12.7 %attend_forward.2 = (bf16[1024,768]{1,0:T(8,128)(2,1)}, f32[6,8,1024]{2,1,0:T(8,128)}) custom-call(s32[4]{0:T(128)} %compare_convert_fusion.flags_ref, bf16[1024,768]{1,0:T(8,128)(2,1)} %get-tuple-element.201.q_ref, bf16[1024,768]{1,0:T(8,128)(2,1)} %get-tuple-element.197.k_ref, bf16[1024,768]{1,0:T(8,128)(2,1)} %get-tuple-element.198.v_ref), custom_call_target="tpu_custom_call" | custom-call | flops 4560000000 | bytes 4559999 | tf_op jit(solution)/shard_map/attend_forward/pallas_call | solution.py:95
  65.5 1.7 collective-permute-start.7
  67.2 1.6 collective-permute-start.8
  68.8 12.6 %attend_forward.3 = (bf16[1024,768]{1,0:T(8,128)(2,1)}, f32[6,8,1024]{2,1,0:T(8,128)}) custom-call(s32[4]{0:T(128)} %compare_convert_fusion.flags_ref, bf16[1024,768]{1,0:T(8,128)(2,1)} %get-tuple-element.201.q_ref, bf16[1024,768]{1,0:T(8,128)(2,1)} %get-tuple-element.197.k_ref, ...), custom_call_target="tpu_custom_call", output_to_operand_aliasing={{0}: (4, {}), {1}: (5, {})} | custom-call | flops 4560000000 | bytes 4559999 | tf_op jit(solution)/shard_map/attend_forward/pallas_call | solution.py:95
  81.4 1.9 collective-permute-done.7.refs_13_
  85.3 1.4 collective-permute-done.12.refs_16_
  88.6 38.0 %middle_stage.1 = (bf16[1024,768]{1,0:T(8,128)(2,1)}, bf16[1024,3072]{1,0:T(8,128)(2,1)}, bf16[1024,3072]{1,0:T(8,128)(2,1)}, bf16[512,768]{1,0:T(8,128)(2,1)}, ...) custom-call(s32[3]{0:T(128)} %pad_add_fusion.place_ref, ...), custom_call_target="tpu_custom_call" | custom-call | flops 15200000000 | bytes 15200000 | tf_op jit(solution)/shard_map/middle_stage/pallas_call | solution.py:434
  127.2 9.8 %proj_grad.1 = (bf16[2,2,384,768]{3,2,1,0:T(8,128)(2,1)}, bf16[2,2,384,768]{3,2,1,0:T(8,128)(2,1)}) custom-call(s32[3]{0:T(128)} %pad_add_fusion.place_ref, bf16[1024,3072]{1,0:T(8,128)(2,1)} %get-tuple-element.219.own_act.other_act, bf16[1024,3072]{1,0:T(8,128)(2,1)} %get-tuple-element.219.own_act.other_act, ...), custom_call_target="tpu_custom_call" | custom-call | flops 5200000000 | bytes 5200000 | tf_op jit(solution)/shard_map/proj_grad/pallas_call | solution.py:579
  138.0 8.4 %fc_out_grad.2 = (bf16[2,240,1536]{2,1,0:T(8,128)(2,1)}, bf16[2,240,1536]{2,1,0:T(8,128)(2,1)}) custom-call(s32[3]{0:T(128)} %pad_add_fusion.place_ref, bf16[1024,768]{1,0:T(8,128)(2,1)} %get-tuple-element.225.left_ref, bf16[1024,3072]{1,0:T(8,128)(2,1)} %get-tuple-element.226.right_ref, bf16[1024,768]{1,0:T(8,128)(2,1)} %get-tuple-element.209.refs_0_.att_ref, ...), custom_call_target="tpu_custom_call" | custom-call | flops 2800000000 | bytes 2800000 | tf_op jit(solution)/shard_map/fc_out_grad/pallas_call | solution.py:491
  147.7 2.6 fusion.4
  150.2 1.3 collective-permute-start.18
  151.5 8.6 %fc_out_grad.3 = (bf16[2,240,1536]{2,1,0:T(8,128)(2,1)}, bf16[2,240,1536]{2,1,0:T(8,128)(2,1)}) custom-call(s32[3]{0:T(128)} %pad_add_fusion.place_ref, bf16[1024,768]{1,0:T(8,128)(2,1)} %get-tuple-element.225.left_ref, bf16[1024,3072]{1,0:T(8,128)(2,1)} %get-tuple-element.226.right_ref, bf16[1024,768]{1,0:T(8,128)(2,1)} %get-tuple-element.209.refs_0_.att_ref, ...), custom_call_target="tpu_custom_call" | custom-call | flops 2800000000 | bytes 2800000 | tf_op jit(solution)/shard_map/fc_out_grad/pallas_call | solution.py:491
  160.2 3.3 add_convert_fusion
  163.5 1.5 collective-permute-start.20
  165.0 18.2 %attend_backward.3 = (bf16[3,1024,384]{2,1,0:T(8,128)(2,1)}, f32[8,384]{1,0:T(8,128)}) custom-call(s32[4]{0:T(128)} %compare_convert_fusion.flags_ref, bf16[1024,768]{1,0:T(8,128)(2,1)} %get-tuple-element.201.q_ref, bf16[1024,768]{1,0:T(8,128)(2,1)} %get-tuple-element.197.k_ref, bf16[1024,768]{1,0:T(8,128)(2,1)} %get-tuple-element.198.v_ref, ...), custom_call_target="tpu_custom_call" | custom-call | flops 7600000000 | bytes 7600000 | tf_op jit(solution)/shard_map/attend_backward/pallas_call | solution.py:162
  183.2 2.3 fusion.6
  185.4 6.8 %qkv_grad.2 = (bf16[2,3,192,384]{3,2,1,0:T(8,128)(2,1)}, bf16[2,3,192,384]{3,2,1,0:T(8,128)(2,1)}, f32[8,768]{1,0:T(8,128)}) custom-call(s32[3]{0:T(128)} %pad_add_fusion.place_ref, bf16[1024,768]{1,0:T(8,128)(2,1)} %get-tuple-element.252.left_ref, bf16[3,1024,384]{2,1,0:T(8,128)(2,1)} %get-tuple-element.253.refs_0_.refs_2_, ...), custom_call_target="tpu_custom_call" | custom-call | flops 2600000000 | bytes 2600000 | tf_op jit(solution)/shard_map/qkv_grad/pallas_call | solution.py:550
  192.2 6.3 %collective-permute-done.20 = bf16[2,240,1536]{2,1,0:T(8,128)(2,1)} collective-permute-done((bf16[2,240,1536]{2,1,0:T(8,128)(2,1)}, bf16[2,240,1536]{2,1,0:T(8,128)(2,1)}, u32[]{:S(2)}, u32[]{:S(2)}) %collective-permute-start.20) | collective-permute-done | bytes 1474592 | tf_op jit(solution)/shard_map/ppermute | solution.py:668
  198.5 2.7 fusion.12
  201.9 1.2 collective-permute-start.21
  203.8 13.1 %attend_backward.4 = (bf16[3,1024,256]{2,1,0:T(8,128)(2,1)}, f32[8,256]{1,0:T(8,128)}) custom-call(s32[4]{0:T(128)} %compare_convert_fusion.flags_ref, bf16[1024,768]{1,0:T(8,128)(2,1)} %get-tuple-element.201.q_ref, bf16[1024,768]{1,0:T(8,128)(2,1)} %get-tuple-element.197.k_ref, bf16[1024,768]{1,0:T(8,128)(2,1)} %get-tuple-element.198.v_ref, ...), custom_call_target="tpu_custom_call" | custom-call | flops 5200000000 | bytes 5200000 | tf_op jit(solution)/shard_map/attend_backward/pallas_call | solution.py:162
  217.6 2.8 collective-permute-done.22
  221.3 2.2 fusion.2
  223.5 1.7 add_convert_fusion.7
  225.2 3.5 %collective-permute-start.25 = (bf16[384,768]{1,0:T(8,128)(2,1)S(1)}, bf16[384,768]{1,0:T(8,128)(2,1)S(1)}, u32[]{:S(2)}, u32[]{:S(2)}) collective-permute-start(bf16[384,768]{1,0:T(8,128)(2,1)S(1)} %add_convert_fusion.7), channel_id=1, source_target_pairs={{0,2},{6,4},{1,3},{7,5},{8,10},{14,12},{9,11},{15,13},{16,18},{22,... | collective-permute-start | bytes 1769480 | tf_op jit(solution)/shard_map/ppermute | solution.py:683
  230.2 2.3 collective-permute-start.30
  232.5 7.9 %attend_backward.5 = (bf16[3,1024,128]{2,1,0:T(8,128)(2,1)}, f32[8,128]{1,0:T(8,128)}) custom-call(s32[4]{0:T(128)} %compare_convert_fusion.flags_ref, bf16[1024,768]{1,0:T(8,128)(2,1)} %get-tuple-element.201.q_ref, bf16[1024,768]{1,0:T(8,128)(2,1)} %get-tuple-element.197.k_ref, bf16[1024,768]{1,0:T(8,128)(2,1)} %get-tuple-element.198.v_ref, ...), custom_call_target="tpu_custom_call" | custom-call | flops 2800000000 | bytes 2800000 | tf_op jit(solution)/shard_map/attend_backward/pallas_call | solution.py:162
  240.4 6.9 %qkv_grad.3 = (bf16[2,3,192,384]{3,2,1,0:T(8,128)(2,1)}, bf16[2,3,192,384]{3,2,1,0:T(8,128)(2,1)}, f32[8,768]{1,0:T(8,128)}) custom-call(s32[3]{0:T(128)} %pad_add_fusion.place_ref, bf16[1024,768]{1,0:T(8,128)(2,1)} %get-tuple-element.252.left_ref, bf16[3,1024,256]{2,1,0:T(8,128)(2,1)} %get-tuple-element.273.refs_0_, ...), custom_call_target="tpu_custom_call" | custom-call | flops 2600000000 | bytes 2600000 | tf_op jit(solution)/shard_map/qkv_grad/pallas_call | solution.py:550
  249.2 1.5 collective-permute-start.27
  250.7 1.2 add_convert_fusion.6
  252.8 1.2 fusion.9
  255.6 1.5 collective-permute-start.28
  257.3 12.3 %input_grad.1 = (bf16[512,768]{1,0:T(8,128)(2,1)}, bf16[512,768]{1,0:T(8,128)(2,1)}) custom-call(s32[3]{0:T(128)} %pad_add_fusion.place_ref, bf16[3,1024,256]{2,1,0:T(8,128)(2,1)} %get-tuple-element.273.refs_0_, bf16[3,1024,128]{2,1,0:T(8,128)(2,1)} %get-tuple-element.271.refs_1_, bf16[3,1024,384]{2,1,0:T(8,128)(2,1)} %get-tuple-element.253.refs_0_.refs_2_, ...), custom_call_target="tpu_custom_call" | custom-call | flops 3600000000 | bytes 3600000 | tf_op jit(solution)/shard_map/input_grad/pallas_call | solution.py:652
  271.0 1.6 fusion.8
  272.7 1.6 collective-permute-start.33
  274.3 1.3 add_convert_fusion.3
  275.6 1.5 collective-permute-start.36
  277.1 1.2 collective-permute-start.38
  279.3 1.3 collective-permute-start.37
  280.9 4.8 %collective-permute-done.33 = bf16[3,192,384]{2,1,0:T(8,128)(2,1)S(1)} collective-permute-done((bf16[3,192,384]{2,1,0:T(8,128)(2,1)S(1)}, bf16[3,192,384]{2,1,0:T(8,128)(2,1)S(1)}, u32[]{:S(2)}, u32[]{:S(2)}) %collective-permute-start.33) | collective-permute-done | bytes 442400 | tf_op jit(solution)/shard_map/ppermute | solution.py:668
  288.5 2.5 collective-permute-start.40
  291.0 1.6 add_convert_fusion.13
  292.6 3.0 copy.23
  295.6 4.5 %collective-permute-done.40 = f32[8,3456]{1,0:T(8,128)} collective-permute-done((f32[8,3456]{1,0:T(8,128)S(1)}, f32[8,3456]{1,0:T(8,128)}, u32[]{:S(2)}, u32[]{:S(2)}) %collective-permute-start.40) | collective-permute-done | bytes 110624 | tf_op jit(solution)/shard_map/ppermute | solution.py:668
  300.8 11.7 %collective-permute-done.39 = bf16[2,192,384]{2,1,0:T(8,128)(2,1)S(1)} collective-permute-done((bf16[2,192,384]{2,1,0:T(8,128)(2,1)S(1)}, bf16[2,192,384]{2,1,0:T(8,128)(2,1)S(1)}, u32[]{:S(2)}, u32[]{:S(2)}) %collective-permute-start.39) | collective-permute-done | bytes 294944 | tf_op jit(solution)/shard_map/ppermute | solution.py:668
  313.7 1.3 add_convert_fusion.2
  315.0 1.4 collective-permute-start.42
  316.4 2.3 fusion.13
  318.9 1.8 fusion
  323.1 12.1 %collective-permute-done.42 = bf16[240,1536]{1,0:T(8,128)(2,1)S(1)} collective-permute-done((bf16[240,1536]{1,0:T(8,128)(2,1)S(1)}, bf16[240,1536]{1,0:T(8,128)(2,1)S(1)}, u32[]{:S(2)}, u32[]{:S(2)}) %collective-permute-start.42) | collective-permute-done | bytes 737312 | tf_op jit(solution)/shard_map/ppermute | solution.py:691
  335.4 1.1 slice.188
  336.5 3.0 copy.24
  (212 shorter events, 39.3 us)
Async XLA Ops:
  0.6 5.6 %copy-start = (s32[2,1024]{1,0:T(2,128)S(1)}, s32[2,1024]{1,0:T(2,128)}, u32[]{:S(2)}) copy-start(s32[2,1024]{1,0:T(2,128)} %param.12) | copy-start | bytes 24580
  1.7 13.2 %collective-permute-start = (bf16[3,192,384]{2,1,0:T(8,128)(2,1)S(1)}, bf16[3,192,384]{2,1,0:T(8,128)(2,1)S(1)}, u32[]{:S(2)}, u32[]{:S(2)}) collective-permute-start(bf16[3,192,384]{2,1,0:T(8,128)(2,1)S(1)} %constant_dynamic-slice_fusion.5), channel_id=1, source_target_pairs={{0,1},{1,0},{2,3},{3,2},{4,5},{5,4},{6,7},{7,6},{8,9},{9,8},{10,11... | collective-permute-start | bytes 1327112 | tf_op jit(solution)/shard_map/ppermute | solution.py:668
  8.3 6.1 %copy-start.33 = (bf16[2,768]{1,0:T(2,128)(2,1)S(1)}, bf16[2,768]{1,0:T(2,128)(2,1)}, u32[]{:S(2)}) copy-start(bf16[2,768]{1,0:T(2,128)(2,1)} %param.13) | copy-start | bytes 9220
  8.3 11.2 %copy-start.2 = (bf16[1536,767]{1,0:T(8,128)(2,1)S(1)}, bf16[1536,767]{1,0:T(8,128)(2,1)}, u32[]{:S(2)}) copy-start(bf16[1536,767]{1,0:T(8,128)(2,1)} %param.19) | copy-start | bytes 7068676
  15.7 21.2 %collective-permute-start.2 = (bf16[528,768]{1,0:T(8,128)(2,1)}, bf16[528,768]{1,0:T(8,128)(2,1)S(1)}, u32[]{:S(2)}, u32[]{:S(2)}) collective-permute-start(bf16[528,768]{1,0:T(8,128)(2,1)} %get-tuple-element.183), channel_id=1, source_target_pairs={{0,1},{1,0},{2,3},{3,2},{4,5},{5,4},{6,7},{7,6},{8,9},{9,8},{10,11... | collective-permute-start | bytes 2433032 | tf_op jit(solution)/shard_map/ppermute | solution.py:668
  17.9 6.3 %collective-permute-start.3 = (bf16[3,192,384]{2,1,0:T(8,128)(2,1)}, bf16[3,192,384]{2,1,0:T(8,128)(2,1)S(1)}, u32[]{:S(2)}, u32[]{:S(2)}) collective-permute-start(bf16[3,192,384]{2,1,0:T(8,128)(2,1)} %copy-done.46), channel_id=1, source_target_pairs={{0,8},{8,0},{16,24},{24,16},{1,9},{9,1},{17,25},{25,17},{2,10},{10... | collective-permute-start | bytes 1327112 | tf_op jit(solution)/shard_map/ppermute | solution.py:668
  18.0 14.1 %collective-permute-start.1 = (bf16[3,192,384]{2,1,0:T(8,128)(2,1)}, bf16[3,192,384]{2,1,0:T(8,128)(2,1)}, u32[]{:S(2)}, u32[]{:S(2)}) collective-permute-start(bf16[3,192,384]{2,1,0:T(8,128)(2,1)} %copy-done.46), channel_id=1, source_target_pairs={{0,16},{8,24},{16,0},{24,8},{1,17},{9,25},{17,1},{25,9},{2,18},{10... | collective-permute-start | bytes 1327112 | tf_op jit(solution)/shard_map/ppermute | solution.py:668
  24.2 7.8 %copy-start.47 = (bf16[3,192,384]{2,1,0:T(8,128)(2,1)}, bf16[3,192,384]{2,1,0:T(8,128)(2,1)S(1)}, u32[]{:S(2)}) copy-start(bf16[3,192,384]{2,1,0:T(8,128)(2,1)S(1)} %collective-permute-done.3.b.refs_2_.refs_9_) | copy-start | bytes 1327108
  24.2 41.2 %collective-permute-start.5 = (bf16[480,768]{1,0:T(8,128)(2,1)S(1)}, bf16[480,768]{1,0:T(8,128)(2,1)}, u32[]{:S(2)}, u32[]{:S(2)}) collective-permute-start(bf16[480,768]{1,0:T(8,128)(2,1)S(1)} %fusion.11), channel_id=1, source_target_pairs={{0,1},{1,0},{2,3},{3,2},{4,5},{5,4},{6,7},{7,6},{8,9},{9,8},{10,11... | collective-permute-start | bytes 2211848 | tf_op jit(solution)/shard_map/ppermute | solution.py:668
  24.8 40.7 %collective-permute-start.6 = (bf16[384,768]{1,0:T(8,128)(2,1)S(1)}, bf16[384,768]{1,0:T(8,128)(2,1)}, u32[]{:S(2)}, u32[]{:S(2)}) collective-permute-start(bf16[384,768]{1,0:T(8,128)(2,1)S(1)} %pad.22), channel_id=1, source_target_pairs={{0,1},{1,0},{2,3},{3,2},{4,5},{5,4},{6,7},{7,6},{8,9},{9,8},{10,11... | collective-permute-start | bytes 1769480 | tf_op jit(solution)/shard_map/ppermute | solution.py:668
  36.9 2.0 collective-permute-start.4
  50.3 33.0 %collective-permute-start.9 = (bf16[512,768]{1,0:T(8,128)(2,1)}, bf16[512,768]{1,0:T(8,128)(2,1)S(1)}, u32[]{:S(2)}, u32[]{:S(2)}) collective-permute-start(bf16[512,768]{1,0:T(8,128)(2,1)} %get-tuple-element.208), channel_id=1, source_target_pairs={{0,1},{1,0},{2,3},{3,2},{4,5},{5,4},{6,7},{7,6},{8,9},{9,8},{10,11... | collective-permute-start | bytes 2359304 | tf_op jit(solution)/shard_map/ppermute | solution.py:668
  65.5 18.5 %copy-start.37 = (bf16[2,767]{1,0:T(2,128)(2,1)S(1)}, bf16[2,767]{1,0:T(2,128)(2,1)}, u32[]{:S(2)}) copy-start(bf16[2,767]{1,0:T(2,128)(2,1)} %param.20) | copy-start | bytes 9208
  65.5 19.1 %copy-start.34 = (bf16[1536]{0:T(1024)(128)(2,1)S(1)}, bf16[1536]{0:T(1024)(128)(2,1)}, u32[]{:S(2)}) copy-start(bf16[1536]{0:T(1024)(128)(2,1)} %param.18) | copy-start | bytes 9220
  65.5 17.9 %collective-permute-start.7 = (bf16[480,768]{1,0:T(8,128)(2,1)}, bf16[480,768]{1,0:T(8,128)(2,1)S(1)}, u32[]{:S(2)}, u32[]{:S(2)}) collective-permute-start(bf16[480,768]{1,0:T(8,128)(2,1)} %collective-permute-done.5.refs_11_), channel_id=1, source_target_pairs={{0,16},{8,24},{16,0},{24,8},{1,17},{9,25},{17,1},{25,9},{2,18},{10... | collective-permute-start | bytes 2211848 | tf_op jit(solution)/shard_map/ppermute | solution.py:668
  67.2 14.2 %collective-permute-start.8 = (bf16[384,768]{1,0:T(8,128)(2,1)}, bf16[384,768]{1,0:T(8,128)(2,1)S(1)}, u32[]{:S(2)}, u32[]{:S(2)}) collective-permute-start(bf16[384,768]{1,0:T(8,128)(2,1)} %collective-permute-done.6.refs_15_), channel_id=1, source_target_pairs={{0,2},{2,0},{4,6},{6,4},{1,3},{3,1},{5,7},{7,5},{8,10},{10,8},{12,... | collective-permute-start | bytes 1769480 | tf_op jit(solution)/shard_map/ppermute | solution.py:668
  68.8 17.9 %collective-permute-start.10 = (bf16[480,768]{1,0:T(8,128)(2,1)}, bf16[480,768]{1,0:T(8,128)(2,1)S(1)}, u32[]{:S(2)}, u32[]{:S(2)}) collective-permute-start(bf16[480,768]{1,0:T(8,128)(2,1)} %collective-permute-done.5.refs_11_), channel_id=1, source_target_pairs={{0,8},{8,0},{16,24},{24,16},{1,9},{9,1},{17,25},{25,17},{2,10},{10... | collective-permute-start | bytes 2211848 | tf_op jit(solution)/shard_map/ppermute | solution.py:668
  83.4 4.2 %collective-permute-start.11 = (bf16[480,768]{1,0:T(8,128)(2,1)S(1)}, bf16[480,768]{1,0:T(8,128)(2,1)S(1)}, u32[]{:S(2)}, u32[]{:S(2)}) collective-permute-start(bf16[480,768]{1,0:T(8,128)(2,1)S(1)} %collective-permute-done.7.refs_13_), channel_id=1, source_target_pairs={{0,8},{8,0},{16,24},{24,16},{1,9},{9,1},{17,25},{25,17},{2,10},{10... | collective-permute-start | bytes 2211848 | tf_op jit(solution)/shard_map/ppermute | solution.py:668
  83.5 3.3 collective-permute-start.12
  83.9 3.6 %collective-permute-start.13 = (bf16[384,768]{1,0:T(8,128)(2,1)}, bf16[384,768]{1,0:T(8,128)(2,1)S(1)}, u32[]{:S(2)}, u32[]{:S(2)}) collective-permute-start(bf16[384,768]{1,0:T(8,128)(2,1)} %copy-done.43), channel_id=1, source_target_pairs={{0,8},{8,0},{16,24},{24,16},{1,9},{9,1},{17,25},{25,17},{2,10},{10... | collective-permute-start | bytes 1769480 | tf_op jit(solution)/shard_map/ppermute | solution.py:668
  126.6 11.4 %collective-permute-start.14 = (bf16[256,768]{1,0:T(8,128)(2,1)}, bf16[256,768]{1,0:T(8,128)(2,1)S(1)}, u32[]{:S(2)}, u32[]{:S(2)}) collective-permute-start(bf16[256,768]{1,0:T(8,128)(2,1)} %get-tuple-element.222), channel_id=1, source_target_pairs={{0,1},{1,0},{2,3},{3,2},{4,5},{5,4},{6,7},{7,6},{8,9},{9,8},{10,11... | collective-permute-start | bytes 1179656 | tf_op jit(solution)/shard_map/ppermute | solution.py:668
  138.0 8.4 %copy-start.24 = (bf16[256,768]{1,0:T(8,128)(2,1)}, bf16[256,768]{1,0:T(8,128)(2,1)S(1)}, u32[]{:S(2)}) copy-start(bf16[256,768]{1,0:T(8,128)(2,1)S(1)} %collective-permute-done.14) | copy-start | bytes 1179652
  138.0 8.4 %collective-permute-start.15 = (bf16[2,2,384,768]{3,2,1,0:T(8,128)(2,1)}, bf16[2,2,384,768]{3,2,1,0:T(8,128)(2,1)}, u32[]{:S(2)}, u32[]{:S(2)}) collective-permute-start(bf16[2,2,384,768]{3,2,1,0:T(8,128)(2,1)} %get-tuple-element.230), channel_id=1, source_target_pairs={{0,8},{8,0},{16,24},{24,16},{1,9},{9,1},{17,25},{25,17},{2,10},{10... | collective-permute-start | bytes 7077896 | tf_op jit(solution)/shard_map/ppermute | solution.py:668
  138.0 8.9 %copy-start.49 = (bf16[256,768]{1,0:T(8,128)(2,1)S(1)}, bf16[256,768]{1,0:T(8,128)(2,1)}, u32[]{:S(2)}) copy-start(bf16[256,768]{1,0:T(8,128)(2,1)} %get-tuple-element.239) | copy-start | bytes 1179652
  138.0 9.6 %copy-start.3 = (bf16[2,2,384,768]{3,2,1,0:T(8,128)(2,1)S(1)}, bf16[2,2,384,768]{3,2,1,0:T(8,128)(2,1)}, u32[]{:S(2)}) copy-start(bf16[2,2,384,768]{3,2,1,0:T(8,128)(2,1)} %get-tuple-element.248) | copy-start | bytes 7077892
  146.4 13.7 %collective-permute-start.16 = (bf16[2,240,1536]{2,1,0:T(8,128)(2,1)}, bf16[2,240,1536]{2,1,0:T(8,128)(2,1)}, u32[]{:S(2)}, u32[]{:S(2)}) collective-permute-start(bf16[2,240,1536]{2,1,0:T(8,128)(2,1)} %get-tuple-element.237), channel_id=1, source_target_pairs={{0,8},{8,0},{16,24},{24,16},{1,9},{9,1},{17,25},{25,17},{2,10},{10... | collective-permute-start | bytes 4423688 | tf_op jit(solution)/shard_map/ppermute | solution.py:668
  146.9 13.2 %collective-permute-start.17 = (bf16[256,768]{1,0:T(8,128)(2,1)S(1)}, bf16[256,768]{1,0:T(8,128)(2,1)S(1)}, u32[]{:S(2)}, u32[]{:S(2)}) collective-permute-start(bf16[256,768]{1,0:T(8,128)(2,1)S(1)} %copy-done.49), channel_id=1, source_target_pairs={{0,1},{1,0},{2,3},{3,2},{4,5},{5,4},{6,7},{7,6},{8,9},{9,8},{10,11... | collective-permute-start | bytes 1179656 | tf_op jit(solution)/shard_map/ppermute | solution.py:668
  150.2 32.9 %collective-permute-start.18 = (bf16[2,384,768]{2,1,0:T(8,128)(2,1)}, bf16[2,384,768]{2,1,0:T(8,128)(2,1)}, u32[]{:S(2)}, u32[]{:S(2)}) collective-permute-start(bf16[2,384,768]{2,1,0:T(8,128)(2,1)} %fusion.4), channel_id=1, source_target_pairs={{0,16},{8,24},{16,0},{24,8},{1,17},{9,25},{17,1},{25,9},{2,18},{10... | collective-permute-start | bytes 3538952 | tf_op jit(solution)/shard_map/ppermute | solution.py:668
  160.1 23.1 %collective-permute-start.19 = (bf16[2,240,1536]{2,1,0:T(8,128)(2,1)}, bf16[2,240,1536]{2,1,0:T(8,128)(2,1)}, u32[]{:S(2)}, u32[]{:S(2)}) collective-permute-start(bf16[2,240,1536]{2,1,0:T(8,128)(2,1)} %get-tuple-element.247), channel_id=1, source_target_pairs={{0,8},{8,0},{16,24},{24,16},{1,9},{9,1},{17,25},{25,17},{2,10},{10... | collective-permute-start | bytes 4423688 | tf_op jit(solution)/shard_map/ppermute | solution.py:668
  163.5 34.9 %collective-permute-start.20 = (bf16[2,240,1536]{2,1,0:T(8,128)(2,1)}, bf16[2,240,1536]{2,1,0:T(8,128)(2,1)}, u32[]{:S(2)}, u32[]{:S(2)}) collective-permute-start(bf16[2,240,1536]{2,1,0:T(8,128)(2,1)} %add_convert_fusion), channel_id=1, source_target_pairs={{0,1},{1,0},{2,3},{3,2},{4,5},{5,4},{6,7},{7,6},{8,9},{9,8},{10,11... | collective-permute-start | bytes 4423688 | tf_op jit(solution)/shard_map/ppermute | solution.py:668
  198.5 21.9 %collective-permute-start.23 = (bf16[2,3,192,384]{3,2,1,0:T(8,128)(2,1)}, bf16[2,3,192,384]{3,2,1,0:T(8,128)(2,1)S(1)}, u32[]{:S(2)}, u32[]{:S(2)}) collective-permute-start(bf16[2,3,192,384]{3,2,1,0:T(8,128)(2,1)} %get-tuple-element.265), channel_id=1, source_target_pairs={{0,8},{8,0},{16,24},{24,16},{1,9},{9,1},{17,25},{25,17},{2,10},{10... | collective-permute-start | bytes 2654216 | tf_op jit(solution)/shard_map/ppermute | solution.py:668
  201.2 19.2 %collective-permute-start.22 = (bf16[240,1536]{1,0:T(8,128)(2,1)}, bf16[240,1536]{1,0:T(8,128)(2,1)}, u32[]{:S(2)}, u32[]{:S(2)}) collective-permute-start(bf16[240,1536]{1,0:T(8,128)(2,1)} %fusion.12), channel_id=1, source_target_pairs={{0,16},{8,24},{16,0},{24,8},{1,17},{9,25},{17,1},{25,9},{2,18},{10... | collective-permute-start | bytes 2211848 | tf_op jit(solution)/shard_map/ppermute | solution.py:668
  201.9 15.7 %collective-permute-start.21 = (bf16[384,768]{1,0:T(8,128)(2,1)}, bf16[384,768]{1,0:T(8,128)(2,1)S(1)}, u32[]{:S(2)}, u32[]{:S(2)}) collective-permute-start(bf16[384,768]{1,0:T(8,128)(2,1)} %fusion.6), channel_id=1, source_target_pairs={{0,1},{1,0},{2,3},{3,2},{4,5},{5,4},{6,7},{7,6},{8,9},{9,8},{10,11... | collective-permute-start | bytes 1769480 | tf_op jit(solution)/shard_map/ppermute | solution.py:668
  223.5 5.2 %copy-start.7 = (bf16[2,3,192,384]{3,2,1,0:T(8,128)(2,1)S(1)}, bf16[2,3,192,384]{3,2,1,0:T(8,128)(2,1)}, u32[]{:S(2)}) copy-start(bf16[2,3,192,384]{3,2,1,0:T(8,128)(2,1)} %get-tuple-element.279) | copy-start | bytes 2654212
  225.2 22.0 %collective-permute-start.25 = (bf16[384,768]{1,0:T(8,128)(2,1)S(1)}, bf16[384,768]{1,0:T(8,128)(2,1)S(1)}, u32[]{:S(2)}, u32[]{:S(2)}) collective-permute-start(bf16[384,768]{1,0:T(8,128)(2,1)S(1)} %add_convert_fusion.7), channel_id=1, source_target_pairs={{0,2},{6,4},{1,3},{7,5},{8,10},{14,12},{9,11},{15,13},{16,18},{22,... | collective-permute-start | bytes 1769480 | tf_op jit(solution)/shard_map/ppermute | solution.py:683
  229.7 17.6 %collective-permute-start.24 = (bf16[3,192,384]{2,1,0:T(8,128)(2,1)}, bf16[3,192,384]{2,1,0:T(8,128)(2,1)S(1)}, u32[]{:S(2)}, u32[]{:S(2)}) collective-permute-start(bf16[3,192,384]{2,1,0:T(8,128)(2,1)} %fusion.14), channel_id=1, source_target_pairs={{0,16},{8,24},{16,0},{24,8},{1,17},{9,25},{17,1},{25,9},{2,18},{10... | collective-permute-start | bytes 1327112 | tf_op jit(solution)/shard_map/ppermute | solution.py:668
  230.2 39.4 %collective-permute-start.30 = (bf16[240,1536]{1,0:T(8,128)(2,1)S(1)}, bf16[240,1536]{1,0:T(8,128)(2,1)}, u32[]{:S(2)}, u32[]{:S(2)}) collective-permute-start(bf16[240,1536]{1,0:T(8,128)(2,1)S(1)} %fusion.2), channel_id=1, source_target_pairs={{0,2},{6,4},{1,3},{7,5},{8,10},{14,12},{9,11},{15,13},{16,18},{22,... | collective-permute-start | bytes 2211848 | tf_op jit(solution)/shard_map/ppermute | solution.py:683
  247.3 5.5 %copy-start.8 = (bf16[2,3,192,384]{3,2,1,0:T(8,128)(2,1)S(1)}, bf16[2,3,192,384]{3,2,1,0:T(8,128)(2,1)}, u32[]{:S(2)}) copy-start(bf16[2,3,192,384]{3,2,1,0:T(8,128)(2,1)} %get-tuple-element.279) | copy-start | bytes 2654212
  247.3 5.5 %copy-start.11 = (bf16[2,3,192,384]{3,2,1,0:T(8,128)(2,1)S(1)}, bf16[2,3,192,384]{3,2,1,0:T(8,128)(2,1)}, u32[]{:S(2)}) copy-start(bf16[2,3,192,384]{3,2,1,0:T(8,128)(2,1)} %copy-done.9) | copy-start | bytes 2654212
  249.1 5.5 %copy-start.31 = (f32[8,768]{1,0:T(8,128)S(1)}, f32[8,768]{1,0:T(8,128)}, u32[]{:S(2)}) copy-start(f32[8,768]{1,0:T(8,128)} %get-tuple-element.217) | copy-start | bytes 73732
  249.2 5.5 %copy-start.32 = (f32[8,1536]{1,0:T(8,128)S(1)}, f32[8,1536]{1,0:T(8,128)}, u32[]{:S(2)}) copy-start(f32[8,1536]{1,0:T(8,128)} %get-tuple-element.286) | copy-start | bytes 147460
  249.2 5.5 %copy-start.35 = (f32[8,256]{1,0:T(8,128)S(1)}, f32[8,256]{1,0:T(8,128)}, u32[]{:S(2)}) copy-start(f32[8,256]{1,0:T(8,128)} %get-tuple-element.287) | copy-start | bytes 24580
  249.2 5.5 %copy-start.36 = (f32[8,128]{1,0:T(8,128)S(1)}, f32[8,128]{1,0:T(8,128)}, u32[]{:S(2)}) copy-start(f32[8,128]{1,0:T(8,128)} %get-tuple-element.288) | copy-start | bytes 12292
  249.2 5.5 %copy-start.12 = (bf16[2,3,192,384]{3,2,1,0:T(8,128)(2,1)S(1)}, bf16[2,3,192,384]{3,2,1,0:T(8,128)(2,1)}, u32[]{:S(2)}) copy-start(bf16[2,3,192,384]{3,2,1,0:T(8,128)(2,1)} %get-tuple-element.291) | copy-start | bytes 2654212
  249.2 5.5 %collective-permute-start.27 = (f32[8,3456]{1,0:T(8,128)S(1)}, f32[8,3456]{1,0:T(8,128)S(1)}, u32[]{:S(2)}, u32[]{:S(2)}) collective-permute-start(f32[8,3456]{1,0:T(8,128)S(1)} %pad_maximum_fusion.6), channel_id=1, source_target_pairs={{0,1},{1,0},{2,3},{3,2},{4,5},{5,4},{6,7},{7,6},{8,9},{9,8},{10,11... | collective-permute-start | bytes 331784 | tf_op jit(solution)/shard_map/ppermute | solution.py:668
  250.7 4.0 %collective-permute-start.26 = (bf16[2,3,192,384]{3,2,1,0:T(8,128)(2,1)}, bf16[2,3,192,384]{3,2,1,0:T(8,128)(2,1)S(1)}, u32[]{:S(2)}, u32[]{:S(2)}) collective-permute-start(bf16[2,3,192,384]{3,2,1,0:T(8,128)(2,1)} %get-tuple-element.278), channel_id=1, source_target_pairs={{0,8},{8,0},{16,24},{24,16},{1,9},{9,1},{17,25},{25,17},{2,10},{10... | collective-permute-start | bytes 2654216 | tf_op jit(solution)/shard_map/ppermute | solution.py:668
  252.0 17.7 %collective-permute-start.31 = (bf16[384,768]{1,0:T(8,128)(2,1)S(1)}, bf16[384,768]{1,0:T(8,128)(2,1)S(1)}, u32[]{:S(2)}, u32[]{:S(2)}) collective-permute-start(bf16[384,768]{1,0:T(8,128)(2,1)S(1)} %add_convert_fusion.6), channel_id=1, source_target_pairs={{2,4},{4,2},{3,5},{5,3},{10,12},{12,10},{11,13},{13,11},{18,20},{2... | collective-permute-start | bytes 1769480 | tf_op jit(solution)/shard_map/ppermute | solution.py:687
  254.0 15.7 %collective-permute-start.29 = (bf16[3,192,384]{2,1,0:T(8,128)(2,1)S(1)}, bf16[3,192,384]{2,1,0:T(8,128)(2,1)}, u32[]{:S(2)}, u32[]{:S(2)}) collective-permute-start(bf16[3,192,384]{2,1,0:T(8,128)(2,1)S(1)} %fusion.9), channel_id=1, source_target_pairs={{0,1},{1,0},{2,3},{3,2},{4,5},{5,4},{6,7},{7,6},{8,9},{9,8},{10,11... | collective-permute-start | bytes 1327112 | tf_op jit(solution)/shard_map/ppermute | solution.py:668
  255.6 14.1 %collective-permute-start.28 = (bf16[3,192,384]{2,1,0:T(8,128)(2,1)S(1)}, bf16[3,192,384]{2,1,0:T(8,128)(2,1)}, u32[]{:S(2)}, u32[]{:S(2)}) collective-permute-start(bf16[3,192,384]{2,1,0:T(8,128)(2,1)S(1)} %fusion.15), channel_id=1, source_target_pairs={{0,16},{8,24},{16,0},{24,8},{1,17},{9,25},{17,1},{25,9},{2,18},{10... | collective-permute-start | bytes 1327112 | tf_op jit(solution)/shard_map/ppermute | solution.py:668
  257.2 12.5 %collective-permute-start.32 = (f32[8,3456]{1,0:T(8,128)S(1)}, f32[8,3456]{1,0:T(8,128)S(1)}, u32[]{:S(2)}, u32[]{:S(2)}) collective-permute-start(f32[8,3456]{1,0:T(8,128)S(1)} %add.185), channel_id=1, source_target_pairs={{0,8},{8,0},{16,24},{24,16},{1,9},{9,1},{17,25},{25,17},{2,10},{10... | collective-permute-start | bytes 331784 | tf_op jit(solution)/shard_map/ppermute | solution.py:668
  270.5 10.4 %collective-permute-start.34 = (f32[8,3456]{1,0:T(8,128)S(1)}, f32[8,3456]{1,0:T(8,128)S(1)}, u32[]{:S(2)}, u32[]{:S(2)}) collective-permute-start(f32[8,3456]{1,0:T(8,128)S(1)} %add.190), channel_id=1, source_target_pairs={{0,16},{8,24},{16,0},{24,8},{1,17},{9,25},{17,1},{25,9},{2,18},{10... | collective-permute-start | bytes 331784 | tf_op jit(solution)/shard_map/ppermute | solution.py:668
  272.7 5.7 %copy-start.17 = (bf16[384,768]{1,0:T(8,128)(2,1)S(1)}, bf16[384,768]{1,0:T(8,128)(2,1)}, u32[]{:S(2)}) copy-start(bf16[384,768]{1,0:T(8,128)(2,1)} %copy-done.16) | copy-start | bytes 1769476
  272.7 7.9 %copy-start.14 = (bf16[512,768]{1,0:T(8,128)(2,1)S(1)}, bf16[512,768]{1,0:T(8,128)(2,1)}, u32[]{:S(2)}) copy-start(bf16[512,768]{1,0:T(8,128)(2,1)} %get-tuple-element.309) | copy-start | bytes 2359300
  272.7 13.1 %collective-permute-start.33 = (bf16[3,192,384]{2,1,0:T(8,128)(2,1)S(1)}, bf16[3,192,384]{2,1,0:T(8,128)(2,1)S(1)}, u32[]{:S(2)}, u32[]{:S(2)}) collective-permute-start(bf16[3,192,384]{2,1,0:T(8,128)(2,1)S(1)} %fusion.8), channel_id=1, source_target_pairs={{0,2},{2,0},{4,6},{6,4},{1,3},{3,1},{5,7},{7,5},{8,10},{10,8},{12,... | collective-permute-start | bytes 1327112 | tf_op jit(solution)/shard_map/ppermute | solution.py:668
  275.6 37.0 %collective-permute-start.36 = (bf16[240,1536]{1,0:T(8,128)(2,1)S(1)}, bf16[240,1536]{1,0:T(8,128)(2,1)}, u32[]{:S(2)}, u32[]{:S(2)}) collective-permute-start(bf16[240,1536]{1,0:T(8,128)(2,1)S(1)} %add_convert_fusion.3), channel_id=1, source_target_pairs={{2,4},{4,2},{3,5},{5,3},{10,12},{12,10},{11,13},{13,11},{18,20},{2... | collective-permute-start | bytes 2211848 | tf_op jit(solution)/shard_map/ppermute | solution.py:687
  277.1 35.5 %collective-permute-start.38 = (bf16[512,768]{1,0:T(8,128)(2,1)}, bf16[512,768]{1,0:T(8,128)(2,1)}, u32[]{:S(2)}, u32[]{:S(2)}) collective-permute-start(bf16[512,768]{1,0:T(8,128)(2,1)} %get-tuple-element.316), channel_id=1, source_target_pairs={{0,1},{1,0},{2,3},{3,2},{4,5},{5,4},{6,7},{7,6},{8,9},{9,8},{10,11... | collective-permute-start | bytes 2359304 | tf_op jit(solution)/shard_map/ppermute | solution.py:668
  279.3 21.5 %collective-permute-start.37 = (bf16[384,768]{1,0:T(8,128)(2,1)}, bf16[384,768]{1,0:T(8,128)(2,1)}, u32[]{:S(2)}, u32[]{:S(2)}) collective-permute-start(bf16[384,768]{1,0:T(8,128)(2,1)} %add_convert_fusion.5), channel_id=1, source_target_pairs={{2,0},{4,6},{3,1},{5,7},{10,8},{12,14},{11,9},{13,15},{18,16},{20,... | collective-permute-start | bytes 1769480 | tf_op jit(solution)/shard_map/ppermute | solution.py:691
  280.9 5.7 %copy-start.30 = (f32[8,3456]{1,0:T(8,128)}, f32[8,3456]{1,0:T(8,128)S(1)}, u32[]{:S(2)}) copy-start(f32[8,3456]{1,0:T(8,128)S(1)} %collective-permute-done.34) | copy-start | bytes 331780
  286.6 9.0 %copy-start.4 = (bf16[2,192,384]{2,1,0:T(8,128)(2,1)}, bf16[2,192,384]{2,1,0:T(8,128)(2,1)S(1)}, u32[]{:S(2)}) copy-start(bf16[2,192,384]{2,1,0:T(8,128)(2,1)S(1)} %add_convert_fusion.11) | copy-start | bytes 884740
  286.6 25.9 %collective-permute-start.39 = (bf16[2,192,384]{2,1,0:T(8,128)(2,1)S(1)}, bf16[2,192,384]{2,1,0:T(8,128)(2,1)S(1)}, u32[]{:S(2)}, u32[]{:S(2)}) collective-permute-start(bf16[2,192,384]{2,1,0:T(8,128)(2,1)S(1)} %add_convert_fusion.11), channel_id=1, source_target_pairs={{0,4},{2,6},{4,0},{6,2},{1,5},{3,7},{5,1},{7,3},{8,12},{10,14},{12... | collective-permute-start | bytes 884744 | tf_op jit(solution)/shard_map/ppermute | solution.py:668
  288.5 11.7 %collective-permute-start.40 = (f32[8,3456]{1,0:T(8,128)S(1)}, f32[8,3456]{1,0:T(8,128)}, u32[]{:S(2)}, u32[]{:S(2)}) collective-permute-start(f32[8,3456]{1,0:T(8,128)S(1)} %add.193), channel_id=1, source_target_pairs={{0,2},{2,0},{4,6},{6,4},{1,3},{3,1},{5,7},{7,5},{8,10},{10,8},{12,... | collective-permute-start | bytes 331784 | tf_op jit(solution)/shard_map/ppermute | solution.py:668
  300.2 23.0 %collective-permute-start.35 = (bf16[1,192,384]{2,1,0:T(8,128)(2,1)}, bf16[1,192,384]{2,1,0:T(8,128)(2,1)S(1)}, u32[]{:S(2)}, u32[]{:S(2)}) collective-permute-start(bf16[1,192,384]{2,1,0:T(8,128)(2,1)} %add_convert_fusion.13), channel_id=1, source_target_pairs={{0,4},{2,6},{4,0},{6,2},{1,5},{3,7},{5,1},{7,3},{8,12},{10,14},{12... | collective-permute-start | bytes 442376 | tf_op jit(solution)/shard_map/ppermute | solution.py:668
  313.6 7.0 %collective-permute-start.41 = (f32[8,3456]{1,0:T(8,128)S(1)}, f32[8,3456]{1,0:T(8,128)S(1)}, u32[]{:S(2)}, u32[]{:S(2)}) collective-permute-start(f32[8,3456]{1,0:T(8,128)S(1)} %add.195), channel_id=1, source_target_pairs={{0,4},{2,6},{4,0},{6,2},{1,5},{3,7},{5,1},{7,3},{8,12},{10,14},{12... | collective-permute-start | bytes 331784 | tf_op jit(solution)/shard_map/ppermute | solution.py:668
  315.0 20.2 %collective-permute-start.42 = (bf16[240,1536]{1,0:T(8,128)(2,1)S(1)}, bf16[240,1536]{1,0:T(8,128)(2,1)S(1)}, u32[]{:S(2)}, u32[]{:S(2)}) collective-permute-start(bf16[240,1536]{1,0:T(8,128)(2,1)S(1)} %add_convert_fusion.2), channel_id=1, source_target_pairs={{2,0},{4,6},{3,1},{5,7},{10,8},{12,14},{11,9},{13,15},{18,16},{20,... | collective-permute-start | bytes 2211848 | tf_op jit(solution)/shard_map/ppermute | solution.py:691
  (29 other events, 76.9 us)

commit v4 on v3

--- a/solution.py
+++ b/solution.py
@@ -52,35 +52,28 @@
 
 def attend_forward_kernel(flags_ref, q_ref, k_ref, v_ref, out_ref, log_ref, *, block):
     length = q_ref.shape[0]
-    row = lax.broadcasted_iota(jnp.int32, (block, block), 0)
-    col = lax.broadcasted_iota(jnp.int32, (block, block), 1)
-    causal = col <= row
+    key_at = lax.broadcasted_iota(jnp.int32, (block, block), 0)
+    query_at = lax.broadcasted_iota(jnp.int32, (block, block), 1)
+    causal = key_at <= query_at
     head_lane = lane_of((block, 128)) // HD
     for at in range(length // block):
         rows = pl.ds(at * block, block)
+        reach = (at + 1) * block
+        keys = pl.ds(0, reach)
         seen = causal | (flags_ref[at] > 0)
-        q_rows = q_ref[rows, :]
-        reach = at * block
         parts = []
         for head in range(2):
-            q_head = jnp.where(head_lane == head, q_rows, jnp.zeros_like(q_rows))
-            near = jnp.where(seen, dot_nt(q_head, k_ref[rows, :]), MASKED)
-            top = jnp.max(near, axis=-1, keepdims=True)
-            if reach:
-                far = dot_nt(q_head, k_ref[pl.ds(0, reach), :])
-                top = jnp.maximum(top, jnp.max(far, axis=-1, keepdims=True))
-            near = jnp.exp(near - top)
-            total = jnp.sum(near, axis=-1, keepdims=True)
-            mixed = dot_nn(near.astype(BF16), v_ref[rows, :])
-            if reach:
-                far = jnp.exp(far - top)
-                total = total + jnp.sum(far, axis=-1, keepdims=True)
-                mixed = mixed + dot_nn(far.astype(BF16), v_ref[pl.ds(0, reach), :])
-            parts.append(mixed / total)
-            logs = top + jnp.log(total)
-            log_ref[0, pl.ds(head, 1), rows] = jnp.transpose(
-                jnp.broadcast_to(logs, (block, 128)))[0:1, :]
-        out_ref[rows, :] = jnp.where(head_lane == 0, parts[0], parts[1]).astype(BF16)
+            q_head = jnp.where(head_lane == head, q_ref[rows, :], jnp.zeros((block, 128), BF16))
+            scores = dot_nt(k_ref[keys, :], q_head)
+            last = jnp.where(seen, scores[reach - block :], MASKED)
+            scores = last if at == 0 else jnp.concatenate([scores[: reach - block], last], 0)
+            top = jnp.max(scores, axis=0, keepdims=True)
+            probs = jnp.exp(scores - top)
+            total = jnp.sum(probs, axis=0, keepdims=True)
+            log_ref[0, pl.ds(head, 1), rows] = top + jnp.log(total)
+            probs = (probs * (1.0 / total)).astype(BF16)
+            parts.append(dot_tn(probs, v_ref[keys, :]).astype(BF16))
+        out_ref[rows, :] = jnp.where(head_lane == 0, parts[0], parts[1])
 
 
 def attend_forward(flags, queries, key_rows, value_rows, first, pairs, into=None):
@@ -455,52 +448,35 @@
     )(place, att, res_own, res_other, cot_own, cot_other, gain, end_bias, fc_bias, *flat)
 
 
-def fc_out_grad_kernel(place_ref, left_ref, right_ref, att_ref, branch_ref, keep_ref, send_ref, rest, *, rows, parts):
-    at = pl.program_id(0)
+def fc_grad_kernel(place_ref, left_ref, right_ref, keep_ref, send_ref, *, rows):
     flip = (place_ref[1] & 1) == 1
-    out_rows = att_ref.shape[1] // 4
-
-    @pl.when(at == 0)
-    def _():
-        rest[...] = dot_tn_halves(att_ref, branch_ref).astype(BF16)
-
     both = dot_tn_halves(left_ref, right_ref).astype(BF16)
-    strip = out_rows // parts
     for pair in range(2):
         to = pair ^ (place_ref[1] >> 1)
         low, high = both[2 * pair * rows : (2 * pair + 1) * rows], both[(2 * pair + 1) * rows : (2 * pair + 2) * rows]
-        keep_ref[to, pl.ds(0, rows), :] = jnp.where(flip, high, low)
-        send_ref[to, pl.ds(0, rows), :] = jnp.where(flip, low, high)
-        base = 2 * pair * out_rows + at * strip
-        low = rest[pl.ds(pl.multiple_of(base, strip), strip), :]
-        high = rest[pl.ds(pl.multiple_of(base + out_rows, strip), strip), :]
-        keep_ref[to, pl.ds(rows, strip), :] = jnp.where(flip, high, low)
-        send_ref[to, pl.ds(rows, strip), :] = jnp.where(flip, low, high)
-
-
-def fc_out_grad(place, left, right, attended, branch, side, chunk=768):
+        keep_ref[to] = jnp.where(flip, high, low)
+        send_ref[to] = jnp.where(flip, low, high)
+
+
+def fc_grad(place, left, right, side, chunk=768):
     length, width = left.shape
     rows = width // 4
     half = right.shape[1] // 2
     parts = half // chunk
-    att = attended.shape[1] // 2
-    strip = att // 4 // parts
-    out = jax.ShapeDtypeStruct((2, rows + strip, half), BF16)
-    out_spec = pl.BlockSpec((2, rows + strip, chunk), lambda n, s: (0, 0, n))
-    fixed = lambda value: pl.BlockSpec(value.shape, lambda n, s: (0, 0))
+    out = jax.ShapeDtypeStruct((2, rows, half), BF16)
+    out_spec = pl.BlockSpec((2, rows, chunk), lambda n, s: (0, 0, n))
     return pl.pallas_call(
-        functools.partial(fc_out_grad_kernel, rows=rows, parts=parts),
+        functools.partial(fc_grad_kernel, rows=rows),
         grid_spec=pltpu.PrefetchScalarGridSpec(
             num_scalar_prefetch=1, grid=(parts,),
-            in_specs=[fixed(left), pl.BlockSpec((length, chunk), lambda n, s: (0, n + side * parts)),
-                      pl.BlockSpec((length, att), lambda n, s: (0, side)), fixed(branch)],
-            out_specs=[out_spec, out_spec],
-            scratch_shapes=[pltpu.VMEM((att, branch.shape[1]), BF16)]),
+            in_specs=[pl.BlockSpec((length, width), lambda n, s: (0, 0)),
+                      pl.BlockSpec((length, chunk), lambda n, s: (0, n + side * parts))],
+            out_specs=[out_spec, out_spec]),
         out_shape=[out, out],
         compiler_params=pltpu.CompilerParams(vmem_limit_bytes=VMEM_CAP),
-        cost_estimate=cost(7),
-        name="fc_out_grad",
-    )(place, left, right, attended, branch)
+        cost_estimate=cost(6),
+        name="fc_grad",
+    )(place, left, right)
 
 
 def qkv_grad_kernel(place_ref, left_ref, *refs, rows, parts, pieces):
@@ -562,33 +538,47 @@
     )(place, left, *rights, *weights)
 
 
-def proj_grad_kernel(place_ref, own_act, other_act, own_cot, other_cot, keep_ref, send_ref, *, rows):
+def proj_grad_kernel(place_ref, own_act, other_act, own_cot, other_cot, att_ref, branch_ref, keep_ref, send_ref, rest,
+                     *, rows):
+    side, pair = pl.program_id(0), pl.program_id(1)
     flip = (place_ref[1] & 1) == 1
+    out_rows = att_ref.shape[1] // 8
+
+    @pl.when((side == 0) & (pair == 0))
+    def _():
+        rest[...] = dot_tn_halves(att_ref, branch_ref).astype(BF16)
+
     both = (dot_tn(own_act[...], own_cot[...]) + dot_tn(other_act[...], other_cot[...])).astype(BF16)
+    base = pl.multiple_of((side * 4 + pair * 2) * out_rows, out_rows)
+    more_low, more_high = rest[pl.ds(base, out_rows), :], rest[pl.ds(base + out_rows, out_rows), :]
     low, high = both[:rows], both[rows:]
-    keep_ref[0, 0] = jnp.where(flip, high, low)
-    send_ref[0, 0] = jnp.where(flip, low, high)
-
-
-def proj_grad(place, active, cot_own, cot_other):
+    keep_ref[0, 0, pl.ds(0, rows), :] = jnp.where(flip, high, low)
+    send_ref[0, 0, pl.ds(0, rows), :] = jnp.where(flip, low, high)
+    keep_ref[0, 0, pl.ds(rows, out_rows), :] = jnp.where(flip, more_high, more_low)
+    send_ref[0, 0, pl.ds(rows, out_rows), :] = jnp.where(flip, more_low, more_high)
+
+
+def proj_grad(place, active, cot_own, cot_other, attended, branch):
     length, width = active.shape
     rows = width // 8
-    out = jax.ShapeDtypeStruct((2, 2, rows, D), BF16)
-    out_spec = pl.BlockSpec((1, 1, rows, D), lambda n, j, s: (j ^ (s[1] >> 1), n, 0, 0))
-    cot_spec = pl.BlockSpec((length // 2, D), lambda n, j, s: (0, 0))
+    out_rows = attended.shape[1] // 8
+    out = jax.ShapeDtypeStruct((2, 2, rows + out_rows, D), BF16)
+    out_spec = pl.BlockSpec((1, 1, rows + out_rows, D), lambda n, j, s: (j ^ (s[1] >> 1), n, 0, 0))
+    fixed = lambda count: pl.BlockSpec((count, D), lambda n, j, s: (0, 0))
     return pl.pallas_call(
         functools.partial(proj_grad_kernel, rows=rows),
         grid_spec=pltpu.PrefetchScalarGridSpec(
             num_scalar_prefetch=1, grid=(2, 2),
             in_specs=[pl.BlockSpec((length // 2, 2 * rows), lambda n, j, s: (s[0], n * 2 + j)),
                       pl.BlockSpec((length // 2, 2 * rows), lambda n, j, s: (1 - s[0], n * 2 + j)),
-                      cot_spec, cot_spec],
-            out_specs=[out_spec, out_spec]),
+                      fixed(length // 2), fixed(length // 2), fixed(length), fixed(length)],
+            out_specs=[out_spec, out_spec],
+            scratch_shapes=[pltpu.VMEM((attended.shape[1], D), BF16)]),
         out_shape=[out, out],
         compiler_params=pltpu.CompilerParams(vmem_limit_bytes=VMEM_CAP),
         cost_estimate=cost(13),
         name="proj_grad",
-    )(place, active, active, cot_own, cot_other)
+    )(place, active, active, cot_own, cot_other, attended, branch)
 
 
 def input_grad_kernel(place_ref, own_grads, other_grads, res_own, res_other, mid_ref, gain_ref, w_own, w_quarter,
@@ -662,6 +652,37 @@
         cost_estimate=cost(9),
         name="input_grad",
     )(place, *own_grads, *other_grads, res_own, res_other, mid, gain, w_own, *w_quarter)
+
+
+def pack_kernel(place_ref, own_ref, first_ref, second_ref, out_ref, *, steps):
+    straight = place_ref[0] == 0
+    own = jnp.transpose(own_ref[...].astype(F32))
+    other = jnp.where(pl.program_id(0) < steps // 2, first_ref[...], second_ref[...])
+    other = jnp.transpose(other.astype(F32))
+    count = out_ref.shape[0]
+    both = [jnp.where(straight, own, other)[:count], jnp.where(straight, other, own)[:count]]
+    out_ref[...] = jnp.stack(both, 1).astype(BF16)
+
+
+def pack_rows(place, own, first, second):
+    positions = own.shape[0]
+    steps = positions // 128
+    own_map, other_map, _ = row_maps(steps)
+    if second.shape[0] == positions:
+        other_map = lambda i, s: (jnp.maximum(i, steps // 2), 0)
+    packed = pl.pallas_call(
+        functools.partial(pack_kernel, steps=steps),
+        grid_spec=pltpu.PrefetchScalarGridSpec(
+            num_scalar_prefetch=1, grid=(steps,),
+            in_specs=[pl.BlockSpec((128, D), lambda i, s: (i, 0)), pl.BlockSpec((128, D), own_map),
+                      pl.BlockSpec((128, D), other_map)],
+            out_specs=pl.BlockSpec((D - 1, 2, 128), lambda i, s: (0, 0, i))),
+        out_shape=jax.ShapeDtypeStruct((D - 1, 2, positions), BF16),
+        compiler_params=pltpu.CompilerParams(vmem_limit_bytes=VMEM_CAP),
+        cost_estimate=cost(0.1),
+        name="pack_rows",
+    )(place, own, first, second)
+    return packed.transpose(1, 2, 0)
 
 
 def swap(value, axis, bit, size):
@@ -764,8 +785,7 @@
         place, attended, res_own, res_other, cot_own, cot_other, gains[1:2], end_biases, fc_full,
         (out_own, fc_weight, proj_own, mix_others, proj_others))
     backward = functools.partial(attend_backward, flags, queries, key_rows, value_rows)
-    restore = lambda mine, got: jnp.where(
-        tensor_at == 0, jnp.stack([mine, got]), jnp.stack([got, mine]))[:, :, : D - 1]
+    restore = functools.partial(pack_rows, place)
 
     def small_outputs(small):
         part, first = hid // n_dp, half // n_dp
@@ -776,34 +796,35 @@
 
     if n_dp == 4 and n_group == 4:
         out_got = [y_swap(value) for value in out_send]
-        proj_k, proj_s = proj_grad(after(place, middle_sums), active, cot_own, cot_other)
+        proj_k, proj_s = proj_grad(after(place, middle_sums), active, cot_own, cot_other, attended, branch_grad)
         proj_k, proj_s, out_got[0] = meet(proj_k, proj_s, out_got[0])
         proj_c = c_swap(proj_s)
-        weights_of = lambda gate, side: fc_out_grad(
-            after(place, gate), normed_two, hidden_grad, attended, branch_grad, side)
-        fo_k, fo_s = weights_of(proj_k, 1)
+        fo_k, fo_s = fc_grad(after(place, proj_k), normed_two, hidden_grad, 1)
         fo_k, fo_s, proj_k, proj_c = meet(fo_k, fo_s, proj_k, proj_c)
         fo_c = c_swap(fo_s)
-        proj_f = add_low(proj_k[1], proj_c[1])
-        proj_x = x_swap(proj_f)
-        fm_k, fm_s = weights_of(proj_f, 0)
+        proj_fo = add_low(proj_k[1, 1], proj_c[1, 1])
+        proj_xo = x_swap(proj_fo)
+        proj_fm = add_low(proj_k[1, 0], after(proj_c, proj_fo)[1, 0])
+        proj_xm = x_swap(proj_fm)
+        fm_k, fm_s = fc_grad(after(place, proj_fo, proj_fm), normed_two, hidden_grad, 0)
         fm_k, fm_s, fo_k, fo_c, *out_got = meet(fm_k, fm_s, fo_k, fo_c, *out_got)
         fm_c = c_swap(fm_s)
         fc_away = add_low(fo_k, fo_c)
         fc_y = y_swap(fc_away)
         first, first_sums = backward(after(attended_grad, fc_away), log_sums, pairs, pairs)
-        first, first_sums, proj_k, proj_c, proj_x, fm_k, fm_c = meet(
-            first, first_sums, proj_k, proj_c, proj_x, fm_k, fm_c)
-        proj_r = [add_low(proj_k[0, n], proj_c[0, n], proj_x[n]) for n in range(2)]
-        proj_y = y_swap(proj_r[1])
-        qo_k, qo_s, qo_sum = qkv_grad(after(place, proj_r[1]), normed_one, [first], qkv_others)
+        first, first_sums, proj_k, proj_c, proj_xo, fm_k, fm_c = meet(
+            first, first_sums, proj_k, proj_c, proj_xo, fm_k, fm_c)
+        proj_r = add_low(proj_k[0, 1], proj_c[0, 1], proj_xo)
+        proj_y = y_swap(proj_r)
+        qo_k, qo_s, qo_sum = qkv_grad(after(place, proj_r), normed_one, [first], qkv_others)
         qo_k, qo_s, fm_k, fm_c, fc_y = meet(qo_k, qo_s, fm_k, fm_c, fc_y)
         qo_c = c_swap(qo_s)
         fc_far = add_low(fm_k[1], fm_c[1], fc_y[1])
         fc_x = x_swap(fc_far)
         own_a, sums_a = backward(after(attended_grad, fc_far), log_sums, 0, pairs - 1)
-        own_a, sums_a, proj_y, fc_x, qo_k, qo_c = meet(own_a, sums_a, proj_y, fc_x, qo_k, qo_c)
-        proj_shard = add_low(proj_r[0], proj_y)
+        own_a, sums_a, proj_y, proj_xm, proj_k, proj_c, fc_x, qo_k, qo_c = meet(
+            own_a, sums_a, proj_y, proj_xm, proj_k, proj_c, fc_x, qo_k, qo_c)
+        proj_shard = add_low(proj_k[0, 0], proj_c[0, 0], proj_xm, proj_y)
         proj_z = chain_in(proj_shard)
         fc_shard = add_low(fm_k[0], fm_c[0], fc_y[0], fc_x)
         fc_z = chain_in(fc_shard)
@@ -814,65 +835,70 @@
         qm_k, qm_s, qm_sum, qo_k, qo_c, qo_x, proj_shard, proj_z = meet(
             qm_k, qm_s, qm_sum, qo_k, qo_c, qo_x, proj_shard, proj_z)
         qm_c = c_swap(qm_s)
+        in_sums = (qm_sum + qo_sum) / gains[0:1]
+        small = jnp.concatenate([in_sums, middle_sums, own_sums, other_sums, sums_a, sums_b, first_sums], 1)
+        small_z = z_swap(small)
         qo_r = add_low(qo_k[0], qo_c[0], qo_x)
         qo_y = y_swap(qo_r)
         proj_shard = add_low(proj_shard, proj_z)
         proj_z = chain_across(proj_shard)
-        in_sums = (qm_sum + qo_sum) / gains[0:1]
-        small = jnp.concatenate([in_sums, middle_sums, own_sums, sums_a, sums_b], 1)
-        small_y = y_swap(jnp.concatenate([in_sums, middle_sums, other_sums, first_sums], 1))
-        qm_k, qm_c, qo_r, proj_shard, small, small_y = meet(qm_k, qm_c, qo_r, proj_shard, small, small_y)
+        qm_k, qm_c, qo_r, proj_shard = meet(qm_k, qm_c, qo_r, proj_shard)
         qm_f = add_low(qm_k[1], qm_c[1])
         qm_x = x_swap(qm_f)
-        small = small + small_y
-        small_c = c_swap(small)
         in_mine, in_send = input_grad(
-            after(place, qm_f, small), [own_a, own_b], [first], res_own, res_other, middle_grad, gains[0:1],
+            after(place, qm_f), [own_a, own_b], [first], res_own, res_other, middle_grad, gains[0:1],
             qkv_weight, qkv_others)
-        in_mine, in_send, qm_x, qo_y, fc_shard, fc_z, proj_shard, proj_z, small, small_c = meet(
-            in_mine, in_send, qm_x, qo_y, fc_shard, fc_z, proj_shard, proj_z, small, small_c)
+        in_mine, in_send, qm_x, qo_y, proj_shard, proj_z, fc_shard, fc_z, small, small_z = meet(
+            in_mine, in_send, qm_x, qo_y, proj_shard, proj_z, fc_shard, fc_z, small, small_z)
+        small = small + small_z
+        small_z = swap(small, "group", 2, n_group)
         last = add_low(qm_k[0], qm_c[0], qm_x, qo_y)
-        last_z = z_swap(last)
+        last_z = chain_in(last)
         fc_shard = add_low(fc_shard, fc_z)
         fc_z = chain_across(fc_shard)
         proj_shard = add_low(proj_shard, proj_z)
         proj_z = chain_out(proj_shard)
         in_got = y_swap(in_send)
+        block_out = restore(after(out_mine, last, proj_shard, fc_shard, small), *out_got)
+        last, last_z, block_out, small, small_z, fc_shard, fc_z = meet(
+            last, last_z, block_out, small, small_z, fc_shard, fc_z)
+        small = small + small_z
+        small_c = c_swap(small)
+        last = add_low(last, last_z)
+        last_z = chain_across(last)
+        fc_shard = add_low(fc_shard, fc_z)
+        fc_z = chain_out(fc_shard)
+        middle_one = (group_at == 1) | (group_at == 2)
+        small, small_c, last, fc_shard, proj_shard, proj_z = meet(small, small_c, last, fc_shard, proj_shard, proj_z)
         small = small + small_c
         small_x = x_swap(small)
-        block_out = restore(after(out_mine, last, fc_shard, proj_shard, small), jnp.concatenate(out_got, 0))
-        last, last_z, block_out, small, small_x = meet(last, last_z, block_out, small, small_x)
-        low_part, high_part = add_low(last[:2], last_z[:2]), add_low(last[2:], last_z[2:])
-        low_z = swap(low_part, "group", 2, n_group)
-        high_z = swap(high_part, "group", 2, n_group)
+        proj_shard = jnp.where(middle_one, proj_shard, proj_z)
+        out_shard = proj_shard[hid // 4 :, : D - 1].astype(F32)
+        proj_shard = proj_shard[: hid // 4, : D - 1].astype(F32)
+        small, small_x, in_mine, in_got, last, last_z, fc_shard, proj_shard, out_shard = meet(
+            small, small_x, in_mine, in_got, last, last_z, fc_shard, proj_shard, out_shard)
+        last = add_low(last, last_z)
+        last_z = chain_out(last)
         small = small + small_x
-        small_z = z_swap(small)
-        middle_one = (group_at == 1) | (group_at == 2)
-        fc_shard, fc_z, proj_shard, proj_z, in_mine, in_got, low_part, low_z, small, small_z = meet(
-            fc_shard, fc_z, proj_shard, proj_z, in_mine, in_got, low_part, low_z, small, small_z)
-        fc_shard = add_low(fc_shard, fc_z)
-        fc_z = chain_out(fc_shard)
-        small = small + small_z
-        small_z = swap(small, "group", 2, n_group)
-        in_out = restore(after(in_mine, fc_shard, small), in_got)
-        proj_shard = jnp.where(middle_one, proj_shard, proj_z)[:, : D - 1].astype(F32)
-        low_part = add_low(low_part, low_z).astype(F32)
-        in_out, proj_shard, low_part, small, small_z = meet(in_out, proj_shard, low_part, small, small_z)
-        small = small_outputs(small + small_z)
-        high_part, high_z, in_out, proj_shard, low_part, fc_shard, fc_z, *small = meet(
-            high_part, high_z, in_out, proj_shard, low_part, fc_shard, fc_z, *small)
-        qkv_shard = jnp.concatenate([low_part, add_low(high_part, high_z).astype(F32)], 0)
+        split = 2 * D + hid
+        mine = jnp.concatenate([small[:, :split], small[:, split + hid : split + hid + half]], 1)
+        other = jnp.concatenate([small[:, : 2 * D], small[:, split : split + hid], small[:, split + hid + half :]], 1)
+        small_y = y_swap(other)
+        in_out = restore(after(in_mine, last), in_got, in_got)
+        in_out, mine, small_y, fc_shard, fc_z = meet(in_out, mine, small_y, fc_shard, fc_z)
+        small = small_outputs(mine + small_y)
         fc_shard = jnp.where(middle_one, fc_shard, fc_z).astype(F32)
-        rest = fc_shard[D // 4 :]
-        out_shard = jnp.concatenate([rest[:, n : n + D - 1] for n in range(0, hid, D)], 0)
-        fc_shard = fc_shard[: D // 4]
+        last, last_z, in_out, proj_shard, out_shard, fc_shard, *small = meet(
+            last, last_z, in_out, proj_shard, out_shard, fc_shard, *small)
+        qkv_shard = jnp.where(middle_one, last, last_z)
     else:
         first, first_sums = backward(attended_grad, log_sums, pairs, pairs)
         own, second_sums = backward(attended_grad, log_sums, 0, pairs)
         in_mine, in_send = input_grad(
             place, [own], [first], res_own, res_other, middle_grad, gains[0:1], qkv_weight, qkv_others)
-        in_out = restore(in_mine, y_swap(in_send))
-        block_out = restore(out_mine, y_swap(jnp.concatenate(out_send, 0)))
+        in_got = y_swap(in_send)
+        in_out = restore(in_mine, in_got, in_got)
+        block_out = restore(out_mine, *[y_swap(value) for value in out_send])
         qo_sum = qkv_grad(place, normed_one, [first], qkv_others)[2]
         qm_sum = qkv_grad(place, normed_one, [own], [qkv_weight])[2]
 

time: 348 us -> 324 us (0.931)
  waiting for transfers between devices: 55.2 us -> 29.2 us
  Pallas kernels: 177 us -> 186 us
  local copies, waits for them, and re-layouts: 23.5 us -> 16.1 us
  starting transfers between devices: 43.4 us -> 49.6 us
  other arithmetic: 41.1 us -> 35.2 us
    ppermute x37 -> x35, waiting for transfers between devices: 43 us -> 22.9 us  [swap(): return lax.ppermute(value, axis, [(n, n ^ bit) for n in range(size)])]
    pallas_call x2 -> x4, Pallas kernels: 16.9 us -> 26.1 us  [the longest x2 13.5 us: fc_grad(): pl.pallas_call(functools.partial(fc_grad_kernel, rows=rows), grid_spec=pl...]
    ppermute x2 -> x3, waiting for transfers between devices: 12.1 us -> 6.36 us  [chain_out(): return lax.ppermute(value, 'group', [(1, 0), (2, 3)])]
    unnamed x108 -> x92, local copies, waits for them, and re-layouts: 13.7 us -> 7.92 us
    ppermute x2 -> x3, starting transfers between devices: 5.81 us -> 9.89 us  [chain_in(): return lax.ppermute(value, 'group', [(0, 1), (3, 2)])]
    pallas_call x2, Pallas kernels: 25.3 us -> 21.7 us  [attend_forward(): pl.pallas_call(body, grid_spec=pltpu.PrefetchScalarGridSpec(num_scalar_pr...]
    convert_element_type x16 -> x17, other arithmetic: 25 us -> 24 us  [add_low(): return total.astype(BF16)]
    ppermute x37 -> x35, starting transfers between devices: 32.5 us -> 32.8 us  [swap(): return lax.ppermute(value, axis, [(n, n ^ bit) for n in range(size)])]
  transfers between devices with their start and end apart: 43 -> 44, of which waited for: 14 -> 10; matrix products, arithmetic and copies ran while one was open for 13% -> 11% of each run, Pallas kernels for 41% -> 47%
where the time goes in v4:
time: 324 us; the launch traced here: 318 us
  Pallas kernels  186 us (57%)
  starting transfers between devices  49.6 us (15%)
  other arithmetic  35.2 us (11%)
  waiting for transfers between devices  29.2 us (9%)
  local copies, waits for them, and re-layouts  16.1 us (5%)
    pallas_call x3, Pallas kernels, attend_backward(): pl.pallas_call(functools.partial(attend_backward_kernel, block=length //...  39.1 us
    pallas_call x1, Pallas kernels, middle_stage(): pl.pallas_call(body, grid_spec=pltpu.PrefetchScalarGridSpec(num_scalar_pr...  38 us
    ppermute x35, starting transfers between devices, swap(): return lax.ppermute(value, axis, [(n, n ^ bit) for n in range(size)])  32.8 us
    convert_element_type x17, other arithmetic, add_low(): return total.astype(BF16)  24 us
    ppermute x35, waiting for transfers between devices, swap(): return lax.ppermute(value, axis, [(n, n ^ bit) for n in range(size)])  22.9 us
    pallas_call x2, Pallas kernels, attend_forward(): pl.pallas_call(body, grid_spec=pltpu.PrefetchScalarGridSpec(num_scalar_pr...  21.7 us
    pallas_call x2, Pallas kernels, qkv_grad(): pl.pallas_call(functools.partial(qkv_grad_kernel, rows=rows, parts=len(ri...  13.7 us
    pallas_call x2, Pallas kernels, fc_grad(): pl.pallas_call(functools.partial(fc_grad_kernel, rows=rows), grid_spec=pl...  13.5 us
  transfers between devices with their start and end apart: 44, of which 10 were waited for; matrix products, arithmetic and copies ran while one was open for 11% of the time, Pallas kernels for 47%

profile of v4, /device:TPU:0, one launch (start us, length us, event | category | flops | bytes accessed | tf_op | source)
XLA Modules:
  0.0 317.8 jit_solution(1103992368601797923)
XLA Ops:
  1.7 3.0 collective-permute-start
  8.3 6.1 %unpack_rows.2 = (bf16[512,768]{1,0:T(8,128)(2,1)}, bf16[528,768]{1,0:T(8,128)(2,1)}) custom-call(s32[3]{0:T(128)} %pad_add_fusion.place_ref, bf16[767,2,512]{2,1,0:T(2,128)(2,1)} %bitcast.55, bf16[16,768]{1,0:T(8,128)(2,1)} %maximum_maximum_fusion.refs_0_), custom_call_target="tpu_custom_call" | custom-call | flops 2000000000 | bytes 2000000 | tf_op jit(solution)/shard_map/unpack_rows/pallas_call | solution.py:192
  15.0 1.7 collective-permute-start.2
  17.2 1.5 collective-permute-start.1
  18.7 1.7 pad.20.refs_10_
  24.1 1.5 collective-permute-start.6
  25.6 5.7 %unpack_rows.3 = (bf16[512,768]{1,0:T(8,128)(2,1)}, bf16[512,768]{1,0:T(8,128)(2,1)}) custom-call(s32[3]{0:T(128)} %pad_add_fusion.place_ref, bf16[767,2,512]{2,1,0:T(2,128)(2,1)} %bitcast.56), custom_call_target="tpu_custom_call" | custom-call | flops 2000000000 | bytes 2000000 | tf_op jit(solution)/shard_map/unpack_rows/pallas_call | solution.py:192
  31.3 4.9 %collective-permute-done.2.other_ref.refs_2_.refs_4_ = bf16[528,768]{1,0:T(8,128)(2,1)S(1)} collective-permute-done((bf16[528,768]{1,0:T(8,128)(2,1)}, bf16[528,768]{1,0:T(8,128)(2,1)S(1)}, u32[]{:S(2)}, u32[]{:S(2)}) %collective-permute-start.2) | collective-permute-done | bytes 811040 | tf_op jit(solution)/shard_map/ppermute | solution.py:689
  37.0 1.3 collective-permute-done.4.d.refs_4_.refs_11_
  39.0 10.6 %norm_project.1 = (bf16[1024,768]{1,0:T(8,128)(2,1)}, bf16[1024,768]{1,0:T(8,128)(2,1)}, bf16[1024,768]{1,0:T(8,128)(2,1)}, bf16[1024,768]{1,0:T(8,128)(2,1)}) custom-call(s32[3]{0:T(128)} %pad_add_fusion.place_ref, bf16[512,768]{1,0:T(8,128)(2,1)} %get-tuple-element.189.own_ref.refs_1_.refs_3_, bf16[528,768]{1,0:T(8,128)(2,1)} %copy-done.31, ...), custom_call_target="tpu_custom_call" | custom-call | flops 4000000000 | bytes 4000000 | tf_op jit(solution)/shard_map/norm_project/pallas_call | solution.py:283
  49.7 1.7 collective-permute-start.9
  51.4 10.9 %attend_forward.2 = (bf16[1024,768]{1,0:T(8,128)(2,1)}, f32[6,8,1024]{2,1,0:T(8,128)}) custom-call(s32[4]{0:T(128)} %compare_convert_fusion.flags_ref, bf16[1024,768]{1,0:T(8,128)(2,1)} %get-tuple-element.209.q_ref, bf16[1024,768]{1,0:T(8,128)(2,1)} %get-tuple-element.205.k_ref, bf16[1024,768]{1,0:T(8,128)(2,1)} %get-tuple-element.206.v_ref), custom_call_target="tpu_custom_call" | custom-call | flops 4560000000 | bytes 4559999 | tf_op jit(solution)/shard_map/attend_forward/pallas_call | solution.py:88
  62.2 2.5 collective-permute-done.6.refs_15_
  64.8 1.7 collective-permute-start.7
  66.5 1.6 collective-permute-start.8
  68.1 10.9 %attend_forward.3 = (bf16[1024,768]{1,0:T(8,128)(2,1)}, f32[6,8,1024]{2,1,0:T(8,128)}) custom-call(s32[4]{0:T(128)} %compare_convert_fusion.flags_ref, bf16[1024,768]{1,0:T(8,128)(2,1)} %get-tuple-element.209.q_ref, bf16[1024,768]{1,0:T(8,128)(2,1)} %get-tuple-element.205.k_ref, ...), custom_call_target="tpu_custom_call", output_to_operand_aliasing={{0}: (4, {}), {1}: (5, {})} | custom-call | flops 4560000000 | bytes 4559999 | tf_op jit(solution)/shard_map/attend_forward/pallas_call | solution.py:88
  79.0 1.8 collective-permute-done.7.refs_13_
  82.7 2.0 collective-permute-done.12.refs_16_
  86.4 38.0 %middle_stage.1 = (bf16[1024,768]{1,0:T(8,128)(2,1)}, bf16[1024,3072]{1,0:T(8,128)(2,1)}, bf16[1024,3072]{1,0:T(8,128)(2,1)}, bf16[512,768]{1,0:T(8,128)(2,1)}, ...) custom-call(s32[3]{0:T(128)} %pad_add_fusion.place_ref, ...), custom_call_target="tpu_custom_call" | custom-call | flops 15200000000 | bytes 15200000 | tf_op jit(solution)/shard_map/middle_stage/pallas_call | solution.py:427
  124.8 12.5 %proj_grad.1 = (bf16[2,2,480,768]{3,2,1,0:T(8,128)(2,1)}, bf16[2,2,480,768]{3,2,1,0:T(8,128)(2,1)}) custom-call(s32[3]{0:T(128)} %pad_add_fusion.place_ref, bf16[1024,3072]{1,0:T(8,128)(2,1)} %get-tuple-element.227.own_act.other_act, bf16[1024,3072]{1,0:T(8,128)(2,1)} %get-tuple-element.227.own_act.other_act, ...), custom_call_target="tpu_custom_call" | custom-call | flops 5200000000 | bytes 5200000 | tf_op jit(solution)/shard_map/proj_grad/pallas_call | solution.py:568
  138.1 6.6 %fc_grad.2 = (bf16[2,192,1536]{2,1,0:T(8,128)(2,1)}, bf16[2,192,1536]{2,1,0:T(8,128)(2,1)}) custom-call(s32[3]{0:T(128)} %pad_add_fusion.place_ref, bf16[1024,768]{1,0:T(8,128)(2,1)} %get-tuple-element.234.left_ref, bf16[1024,3072]{1,0:T(8,128)(2,1)} %get-tuple-element.235.right_ref), custom_call_target="tpu_custom_call" | custom-call | flops 2400000000 | bytes 2400000 | tf_op jit(solution)/shard_map/fc_grad/pallas_call | solution.py:468
  144.7 1.8 collective-permute-start.17
  146.5 2.2 fusion.10
  148.7 1.5 collective-permute-start.18
  150.2 2.2 fusion.11
  152.9 6.8 %fc_grad.3 = (bf16[2,192,1536]{2,1,0:T(8,128)(2,1)}, bf16[2,192,1536]{2,1,0:T(8,128)(2,1)}) custom-call(s32[3]{0:T(128)} %pad_add_fusion.place_ref, bf16[1024,768]{1,0:T(8,128)(2,1)} %get-tuple-element.234.left_ref, bf16[1024,3072]{1,0:T(8,128)(2,1)} %get-tuple-element.235.right_ref), custom_call_target="tpu_custom_call" | custom-call | flops 2400000000 | bytes 2400000 | tf_op jit(solution)/shard_map/fc_grad/pallas_call | solution.py:468
  159.9 3.0 add_convert_fusion
  163.2 18.2 %attend_backward.3 = (bf16[3,1024,384]{2,1,0:T(8,128)(2,1)}, f32[8,384]{1,0:T(8,128)}) custom-call(s32[4]{0:T(128)} %compare_convert_fusion.flags_ref, bf16[1024,768]{1,0:T(8,128)(2,1)} %get-tuple-element.209.q_ref, bf16[1024,768]{1,0:T(8,128)(2,1)} %get-tuple-element.205.k_ref, bf16[1024,768]{1,0:T(8,128)(2,1)} %get-tuple-element.206.v_ref, ...), custom_call_target="tpu_custom_call" | custom-call | flops 7600000000 | bytes 7600000 | tf_op jit(solution)/shard_map/attend_backward/pallas_call | solution.py:155
  181.4 2.3 fusion.2
  183.7 1.7 collective-permute-start.21
  185.4 6.8 %qkv_grad.2 = (bf16[2,3,192,384]{3,2,1,0:T(8,128)(2,1)}, bf16[2,3,192,384]{3,2,1,0:T(8,128)(2,1)}, f32[8,768]{1,0:T(8,128)}) custom-call(s32[3]{0:T(128)} %pad_add_fusion.place_ref, bf16[1024,768]{1,0:T(8,128)(2,1)} %get-tuple-element.261.left_ref, bf16[3,1024,384]{2,1,0:T(8,128)(2,1)} %get-tuple-element.262.refs_0_.refs_2_, ...), custom_call_target="tpu_custom_call" | custom-call | flops 2600000000 | bytes 2600000 | tf_op jit(solution)/shard_map/qkv_grad/pallas_call | solution.py:526
  192.2 2.4 fusion.12
  194.7 1.6 collective-permute-start.23
  196.2 13.0 %attend_backward.4 = (bf16[3,1024,256]{2,1,0:T(8,128)(2,1)}, f32[8,256]{1,0:T(8,128)}) custom-call(s32[4]{0:T(128)} %compare_convert_fusion.flags_ref, bf16[1024,768]{1,0:T(8,128)(2,1)} %get-tuple-element.209.q_ref, bf16[1024,768]{1,0:T(8,128)(2,1)} %get-tuple-element.205.k_ref, bf16[1024,768]{1,0:T(8,128)(2,1)} %get-tuple-element.206.v_ref, ...), custom_call_target="tpu_custom_call" | custom-call | flops 5200000000 | bytes 5200000 | tf_op jit(solution)/shard_map/attend_backward/pallas_call | solution.py:155
  209.3 1.4 collective-permute-done.23
  211.6 2.7 fusion.4
  214.4 2.1 fusion.1
  216.5 3.5 %collective-permute-start.26 = (bf16[480,768]{1,0:T(8,128)(2,1)S(1)}, bf16[480,768]{1,0:T(8,128)(2,1)S(1)}, u32[]{:S(2)}, u32[]{:S(2)}) collective-permute-start(bf16[480,768]{1,0:T(8,128)(2,1)S(1)} %fusion.1), channel_id=1, source_target_pairs={{0,2},{6,4},{1,3},{7,5},{8,10},{14,12},{9,11},{15,13},{16,18},{22,... | collective-permute-start | bytes 2211848 | tf_op jit(solution)/shard_map/ppermute | solution.py:704
  220.1 1.6 collective-permute-start.25
  221.8 2.3 collective-permute-start.31
  224.0 7.9 %attend_backward.5 = (bf16[3,1024,128]{2,1,0:T(8,128)(2,1)}, f32[8,128]{1,0:T(8,128)}) custom-call(s32[4]{0:T(128)} %compare_convert_fusion.flags_ref, bf16[1024,768]{1,0:T(8,128)(2,1)} %get-tuple-element.209.q_ref, bf16[1024,768]{1,0:T(8,128)(2,1)} %get-tuple-element.205.k_ref, bf16[1024,768]{1,0:T(8,128)(2,1)} %get-tuple-element.206.v_ref, ...), custom_call_target="tpu_custom_call" | custom-call | flops 2800000000 | bytes 2800000 | tf_op jit(solution)/shard_map/attend_backward/pallas_call | solution.py:155
  231.9 6.9 %qkv_grad.3 = (bf16[2,3,192,384]{3,2,1,0:T(8,128)(2,1)}, bf16[2,3,192,384]{3,2,1,0:T(8,128)(2,1)}, f32[8,768]{1,0:T(8,128)}) custom-call(s32[3]{0:T(128)} %pad_add_fusion.place_ref, bf16[1024,768]{1,0:T(8,128)(2,1)} %get-tuple-element.261.left_ref, bf16[3,1024,256]{2,1,0:T(8,128)(2,1)} %get-tuple-element.285.refs_0_, ...), custom_call_target="tpu_custom_call" | custom-call | flops 2600000000 | bytes 2600000 | tf_op jit(solution)/shard_map/qkv_grad/pallas_call | solution.py:526
  240.5 1.2 fusion.7
  244.0 3.8 %collective-permute-start.32 = (f32[8,5376]{1,0:T(8,128)S(1)}, f32[8,5376]{1,0:T(8,128)}, u32[]{:S(2)}, u32[]{:S(2)}) collective-permute-start(f32[8,5376]{1,0:T(8,128)S(1)} %constant_dynamic-update-slice_fusion), channel_id=1, source_target_pairs={{0,2},{2,0},{4,6},{6,4},{1,3},{3,1},{5,7},{7,5},{8,10},{10,8},{12,... | collective-permute-start | bytes 516104 | tf_op jit(solution)/shard_map/ppermute | solution.py:689
  247.8 12.5 %input_grad.1 = (bf16[512,768]{1,0:T(8,128)(2,1)}, bf16[512,768]{1,0:T(8,128)(2,1)}) custom-call(s32[3]{0:T(128)} %pad_add_fusion.place_ref, bf16[3,1024,256]{2,1,0:T(8,128)(2,1)} %get-tuple-element.285.refs_0_, bf16[3,1024,128]{2,1,0:T(8,128)(2,1)} %get-tuple-element.283.refs_1_, bf16[3,1024,384]{2,1,0:T(8,128)(2,1)} %get-tuple-element.262.refs_0_.refs_2_, ...), custom_call_target="tpu_custom_call" | custom-call | flops 3600000000 | bytes 3600000 | tf_op jit(solution)/shard_map/input_grad/pallas_call | solution.py:642
  261.2 1.4 add_convert_fusion.6
  262.6 1.5 collective-permute-start.35
  264.1 1.3 fusion.6
  265.4 4.1 %collective-permute-start.33 = (bf16[3,192,384]{2,1,0:T(8,128)(2,1)S(1)}, bf16[3,192,384]{2,1,0:T(8,128)(2,1)}, u32[]{:S(2)}, u32[]{:S(2)}) collective-permute-start(bf16[3,192,384]{2,1,0:T(8,128)(2,1)S(1)} %fusion.6), channel_id=1, source_target_pairs={{0,2},{6,4},{1,3},{7,5},{8,10},{14,12},{9,11},{15,13},{16,18},{22,... | collective-permute-start | bytes 1327112 | tf_op jit(solution)/shard_map/ppermute | solution.py:704
  270.7 1.3 collective-permute-start.37
  272.0 1.1 collective-permute-start.39
  273.2 6.3 %pack_rows.2 = bf16[767,2,512]{2,1,0:T(2,128)(2,1)} custom-call(s32[3]{0:T(128)} %pad_add_fusion.place_ref, bf16[512,768]{1,0:T(8,128)(2,1)} %get-tuple-element.319.own_ref, bf16[256,768]{1,0:T(8,128)(2,1)} %copy-done.17, bf16[256,768]{1,0:T(8,128)(2,1)} %copy-done.18), custom_call_target="tpu_custom_call" | custom-call | flops 40000000 | bytes 40000 | tf_op jit(solution)/shard_map/pack_rows/pallas_call | solution.py:673
  279.5 6.9 %collective-permute-done.34 = f32[8,5376]{1,0:T(8,128)S(1)} collective-permute-done((f32[8,5376]{1,0:T(8,128)S(1)}, f32[8,5376]{1,0:T(8,128)S(1)}, u32[]{:S(2)}, u32[]{:S(2)}) %collective-permute-start.34) | collective-permute-done | bytes 172064 | tf_op jit(solution)/shard_map/ppermute | solution.py:689
  286.4 1.2 add_convert_fusion.9
  288.3 1.3 add_convert_fusion.5
  289.6 1.3 collective-permute-start.43
  290.9 3.0 collective-permute-done.37
  293.9 1.6 collective-permute-start.38
  297.4 1.9 collective-permute-done.38
  299.5 1.4 collective-permute-start.42
  301.0 1.3 collective-permute-start.41
  302.4 6.3 %pack_rows.3 = bf16[767,2,512]{2,1,0:T(2,128)(2,1)} custom-call(s32[3]{0:T(128)} %pad_add_fusion.place_ref, bf16[512,768]{1,0:T(8,128)(2,1)} %get-tuple-element.340.own_ref, bf16[512,768]{1,0:T(8,128)(2,1)} %copy-done.3, bf16[512,768]{1,0:T(8,128)(2,1)} %copy-done.3), custom_call_target="tpu_custom_call" | custom-call | flops 40000000 | bytes 40000 | tf_op jit(solution)/shard_map/pack_rows/pallas_call | solution.py:673
  311.2 2.2 select_convert_fusion
  313.3 3.3 %collective-permute-done.41 = bf16[3,192,384]{2,1,0:T(8,128)(2,1)S(1)} collective-permute-done((bf16[3,192,384]{2,1,0:T(8,128)(2,1)S(1)}, bf16[3,192,384]{2,1,0:T(8,128)(2,1)S(1)}, u32[]{:S(2)}, u32[]{:S(2)}) %collective-permute-start.41) | collective-permute-done | bytes 442400 | tf_op jit(solution)/shard_map/ppermute | solution.py:712
  (199 shorter events, 29.7 us)
Async XLA Ops:
  0.6 5.6 %copy-start = (s32[2,1024]{1,0:T(2,128)S(1)}, s32[2,1024]{1,0:T(2,128)}, u32[]{:S(2)}) copy-start(s32[2,1024]{1,0:T(2,128)} %param.12) | copy-start | bytes 24580
  1.7 13.3 %collective-permute-start = (bf16[3,192,384]{2,1,0:T(8,128)(2,1)S(1)}, bf16[3,192,384]{2,1,0:T(8,128)(2,1)S(1)}, u32[]{:S(2)}, u32[]{:S(2)}) collective-permute-start(bf16[3,192,384]{2,1,0:T(8,128)(2,1)S(1)} %constant_dynamic-slice_fusion.5), channel_id=1, source_target_pairs={{0,1},{1,0},{2,3},{3,2},{4,5},{5,4},{6,7},{7,6},{8,9},{9,8},{10,11... | collective-permute-start | bytes 1327112 | tf_op jit(solution)/shard_map/ppermute | solution.py:689
  8.3 6.1 %copy-start.22 = (bf16[2,768]{1,0:T(2,128)(2,1)S(1)}, bf16[2,768]{1,0:T(2,128)(2,1)}, u32[]{:S(2)}) copy-start(bf16[2,768]{1,0:T(2,128)(2,1)} %param.13) | copy-start | bytes 9220
  8.3 10.4 %copy-start.2 = (bf16[1536,767]{1,0:T(8,128)(2,1)S(1)}, bf16[1536,767]{1,0:T(8,128)(2,1)}, u32[]{:S(2)}) copy-start(bf16[1536,767]{1,0:T(8,128)(2,1)} %param.19) | copy-start | bytes 7068676
  15.0 5.3 %copy-start.39 = (bf16[3,192,384]{2,1,0:T(8,128)(2,1)}, bf16[3,192,384]{2,1,0:T(8,128)(2,1)S(1)}, u32[]{:S(2)}) copy-start(bf16[3,192,384]{2,1,0:T(8,128)(2,1)S(1)} %collective-permute-done.a.refs_1_.refs_8_) | copy-start | bytes 1327108
  15.0 21.2 %collective-permute-start.2 = (bf16[528,768]{1,0:T(8,128)(2,1)}, bf16[528,768]{1,0:T(8,128)(2,1)S(1)}, u32[]{:S(2)}, u32[]{:S(2)}) collective-permute-start(bf16[528,768]{1,0:T(8,128)(2,1)} %get-tuple-element.191), channel_id=1, source_target_pairs={{0,1},{1,0},{2,3},{3,2},{4,5},{5,4},{6,7},{7,6},{8,9},{9,8},{10,11... | collective-permute-start | bytes 2433032 | tf_op jit(solution)/shard_map/ppermute | solution.py:689
  17.2 6.3 %collective-permute-start.3 = (bf16[3,192,384]{2,1,0:T(8,128)(2,1)S(1)}, bf16[3,192,384]{2,1,0:T(8,128)(2,1)S(1)}, u32[]{:S(2)}, u32[]{:S(2)}) collective-permute-start(bf16[3,192,384]{2,1,0:T(8,128)(2,1)S(1)} %collective-permute-done.a.refs_1_.refs_8_), channel_id=1, source_target_pairs={{0,8},{8,0},{16,24},{24,16},{1,9},{9,1},{17,25},{25,17},{2,10},{10... | collective-permute-start | bytes 1327112 | tf_op jit(solution)/shard_map/ppermute | solution.py:689
  17.2 14.1 %collective-permute-start.1 = (bf16[3,192,384]{2,1,0:T(8,128)(2,1)S(1)}, bf16[3,192,384]{2,1,0:T(8,128)(2,1)}, u32[]{:S(2)}, u32[]{:S(2)}) collective-permute-start(bf16[3,192,384]{2,1,0:T(8,128)(2,1)S(1)} %collective-permute-done.a.refs_1_.refs_8_), channel_id=1, source_target_pairs={{0,16},{8,24},{16,0},{24,8},{1,17},{9,25},{17,1},{25,9},{2,18},{10... | collective-permute-start | bytes 1327112 | tf_op jit(solution)/shard_map/ppermute | solution.py:689
  23.5 7.9 %copy-start.40 = (bf16[3,192,384]{2,1,0:T(8,128)(2,1)}, bf16[3,192,384]{2,1,0:T(8,128)(2,1)S(1)}, u32[]{:S(2)}) copy-start(bf16[3,192,384]{2,1,0:T(8,128)(2,1)S(1)} %collective-permute-done.3.b.refs_2_.refs_9_) | copy-start | bytes 1327108
  23.5 41.3 %collective-permute-start.5 = (bf16[480,768]{1,0:T(8,128)(2,1)S(1)}, bf16[480,768]{1,0:T(8,128)(2,1)}, u32[]{:S(2)}, u32[]{:S(2)}) collective-permute-start(bf16[480,768]{1,0:T(8,128)(2,1)S(1)} %fusion.9), channel_id=1, source_target_pairs={{0,1},{1,0},{2,3},{3,2},{4,5},{5,4},{6,7},{7,6},{8,9},{9,8},{10,11... | collective-permute-start | bytes 2211848 | tf_op jit(solution)/shard_map/ppermute | solution.py:689
  24.1 40.7 %collective-permute-start.6 = (bf16[384,768]{1,0:T(8,128)(2,1)S(1)}, bf16[384,768]{1,0:T(8,128)(2,1)}, u32[]{:S(2)}, u32[]{:S(2)}) collective-permute-start(bf16[384,768]{1,0:T(8,128)(2,1)S(1)} %pad.22), channel_id=1, source_target_pairs={{0,1},{1,0},{2,3},{3,2},{4,5},{5,4},{6,7},{7,6},{8,9},{9,8},{10,11... | collective-permute-start | bytes 1769480 | tf_op jit(solution)/shard_map/ppermute | solution.py:689
  36.2 2.0 collective-permute-start.4
  49.7 31.2 %collective-permute-start.9 = (bf16[512,768]{1,0:T(8,128)(2,1)}, bf16[512,768]{1,0:T(8,128)(2,1)S(1)}, u32[]{:S(2)}, u32[]{:S(2)}) collective-permute-start(bf16[512,768]{1,0:T(8,128)(2,1)} %get-tuple-element.216), channel_id=1, source_target_pairs={{0,1},{1,0},{2,3},{3,2},{4,5},{5,4},{6,7},{7,6},{8,9},{9,8},{10,11... | collective-permute-start | bytes 2359304 | tf_op jit(solution)/shard_map/ppermute | solution.py:689
  64.8 16.7 %copy-start.30 = (bf16[2,767]{1,0:T(2,128)(2,1)S(1)}, bf16[2,767]{1,0:T(2,128)(2,1)}, u32[]{:S(2)}) copy-start(bf16[2,767]{1,0:T(2,128)(2,1)} %param.20) | copy-start | bytes 9208
  64.8 17.3 %copy-start.26 = (bf16[1536]{0:T(1024)(128)(2,1)S(1)}, bf16[1536]{0:T(1024)(128)(2,1)}, u32[]{:S(2)}) copy-start(bf16[1536]{0:T(1024)(128)(2,1)} %param.18) | copy-start | bytes 9220
  64.8 16.0 %collective-permute-start.7 = (bf16[480,768]{1,0:T(8,128)(2,1)}, bf16[480,768]{1,0:T(8,128)(2,1)S(1)}, u32[]{:S(2)}, u32[]{:S(2)}) collective-permute-start(bf16[480,768]{1,0:T(8,128)(2,1)} %collective-permute-done.5.refs_11_), channel_id=1, source_target_pairs={{0,16},{8,24},{16,0},{24,8},{1,17},{9,25},{17,1},{25,9},{2,18},{10... | collective-permute-start | bytes 2211848 | tf_op jit(solution)/shard_map/ppermute | solution.py:689
  66.5 12.5 %collective-permute-start.8 = (bf16[384,768]{1,0:T(8,128)(2,1)}, bf16[384,768]{1,0:T(8,128)(2,1)S(1)}, u32[]{:S(2)}, u32[]{:S(2)}) collective-permute-start(bf16[384,768]{1,0:T(8,128)(2,1)} %collective-permute-done.6.refs_15_), channel_id=1, source_target_pairs={{0,2},{2,0},{4,6},{6,4},{1,3},{3,1},{5,7},{7,5},{8,10},{10,8},{12,... | collective-permute-start | bytes 1769480 | tf_op jit(solution)/shard_map/ppermute | solution.py:689
  68.1 16.7 %collective-permute-start.10 = (bf16[480,768]{1,0:T(8,128)(2,1)}, bf16[480,768]{1,0:T(8,128)(2,1)S(1)}, u32[]{:S(2)}, u32[]{:S(2)}) collective-permute-start(bf16[480,768]{1,0:T(8,128)(2,1)} %collective-permute-done.5.refs_11_), channel_id=1, source_target_pairs={{0,8},{8,0},{16,24},{24,16},{1,9},{9,1},{17,25},{25,17},{2,10},{10... | collective-permute-start | bytes 2211848 | tf_op jit(solution)/shard_map/ppermute | solution.py:689
  79.0 6.8 %copy-start.36 = (bf16[384,768]{1,0:T(8,128)(2,1)}, bf16[384,768]{1,0:T(8,128)(2,1)S(1)}, u32[]{:S(2)}) copy-start(bf16[384,768]{1,0:T(8,128)(2,1)S(1)} %collective-permute-done.8.refs_17_) | copy-start | bytes 1769476
  80.8 4.9 %copy-start.33 = (bf16[480,768]{1,0:T(8,128)(2,1)}, bf16[480,768]{1,0:T(8,128)(2,1)S(1)}, u32[]{:S(2)}) copy-start(bf16[480,768]{1,0:T(8,128)(2,1)S(1)} %collective-permute-done.7.refs_13_) | copy-start | bytes 2211844
  80.8 4.9 %copy-start.32 = (bf16[512,768]{1,0:T(8,128)(2,1)}, bf16[512,768]{1,0:T(8,128)(2,1)S(1)}, u32[]{:S(2)}) copy-start(bf16[512,768]{1,0:T(8,128)(2,1)S(1)} %collective-permute-done.9.refs_4_.other_cot) | copy-start | bytes 2359300
  80.8 4.0 %collective-permute-start.11 = (bf16[480,768]{1,0:T(8,128)(2,1)S(1)}, bf16[480,768]{1,0:T(8,128)(2,1)S(1)}, u32[]{:S(2)}, u32[]{:S(2)}) collective-permute-start(bf16[480,768]{1,0:T(8,128)(2,1)S(1)} %collective-permute-done.7.refs_13_), channel_id=1, source_target_pairs={{0,8},{8,0},{16,24},{24,16},{1,9},{9,1},{17,25},{25,17},{2,10},{10... | collective-permute-start | bytes 2211848 | tf_op jit(solution)/shard_map/ppermute | solution.py:689
  80.9 3.8 %collective-permute-start.12 = (bf16[384,768]{1,0:T(8,128)(2,1)}, bf16[384,768]{1,0:T(8,128)(2,1)S(1)}, u32[]{:S(2)}, u32[]{:S(2)}) collective-permute-start(bf16[384,768]{1,0:T(8,128)(2,1)} %collective-permute-done.6.refs_15_), channel_id=1, source_target_pairs={{0,8},{8,0},{16,24},{24,16},{1,9},{9,1},{17,25},{25,17},{2,10},{10... | collective-permute-start | bytes 1769480 | tf_op jit(solution)/shard_map/ppermute | solution.py:689
  81.4 3.4 %collective-permute-start.13 = (bf16[384,768]{1,0:T(8,128)(2,1)S(1)}, bf16[384,768]{1,0:T(8,128)(2,1)S(1)}, u32[]{:S(2)}, u32[]{:S(2)}) collective-permute-start(bf16[384,768]{1,0:T(8,128)(2,1)S(1)} %collective-permute-done.8.refs_17_), channel_id=1, source_target_pairs={{0,8},{8,0},{16,24},{24,16},{1,9},{9,1},{17,25},{25,17},{2,10},{10... | collective-permute-start | bytes 1769480 | tf_op jit(solution)/shard_map/ppermute | solution.py:689
  124.4 12.9 %collective-permute-start.14 = (bf16[256,768]{1,0:T(8,128)(2,1)}, bf16[256,768]{1,0:T(8,128)(2,1)S(1)}, u32[]{:S(2)}, u32[]{:S(2)}) collective-permute-start(bf16[256,768]{1,0:T(8,128)(2,1)} %get-tuple-element.231), channel_id=1, source_target_pairs={{0,1},{1,0},{2,3},{3,2},{4,5},{5,4},{6,7},{7,6},{8,9},{9,8},{10,11... | collective-permute-start | bytes 1179656 | tf_op jit(solution)/shard_map/ppermute | solution.py:689
  137.3 7.4 %collective-permute-start.15 = (bf16[2,2,480,768]{3,2,1,0:T(8,128)(2,1)}, bf16[2,2,480,768]{3,2,1,0:T(8,128)(2,1)}, u32[]{:S(2)}, u32[]{:S(2)}) collective-permute-start(bf16[2,2,480,768]{3,2,1,0:T(8,128)(2,1)} %get-tuple-element.238), channel_id=1, source_target_pairs={{0,8},{8,0},{16,24},{24,16},{1,9},{9,1},{17,25},{25,17},{2,10},{10... | collective-permute-start | bytes 8847368 | tf_op jit(solution)/shard_map/ppermute | solution.py:689
  138.1 8.4 %copy-start.4 = (bf16[2,2,480,768]{3,2,1,0:T(8,128)(2,1)S(1)}, bf16[2,2,480,768]{3,2,1,0:T(8,128)(2,1)}, u32[]{:S(2)}) copy-start(bf16[2,2,480,768]{3,2,1,0:T(8,128)(2,1)} %get-tuple-element.277) | copy-start | bytes 8847364
  144.7 15.1 %collective-permute-start.16 = (bf16[2,192,1536]{2,1,0:T(8,128)(2,1)}, bf16[2,192,1536]{2,1,0:T(8,128)(2,1)}, u32[]{:S(2)}, u32[]{:S(2)}) collective-permute-start(bf16[2,192,1536]{2,1,0:T(8,128)(2,1)} %get-tuple-element.246), channel_id=1, source_target_pairs={{0,8},{8,0},{16,24},{24,16},{1,9},{9,1},{17,25},{25,17},{2,10},{10... | collective-permute-start | bytes 3538952 | tf_op jit(solution)/shard_map/ppermute | solution.py:689
  144.7 15.0 %collective-permute-start.17 = (bf16[256,768]{1,0:T(8,128)(2,1)}, bf16[256,768]{1,0:T(8,128)(2,1)S(1)}, u32[]{:S(2)}, u32[]{:S(2)}) collective-permute-start(bf16[256,768]{1,0:T(8,128)(2,1)} %get-tuple-element.248), channel_id=1, source_target_pairs={{0,1},{1,0},{2,3},{3,2},{4,5},{5,4},{6,7},{7,6},{8,9},{9,8},{10,11... | collective-permute-start | bytes 1179656 | tf_op jit(solution)/shard_map/ppermute | solution.py:689
  148.7 32.7 %collective-permute-start.18 = (bf16[480,768]{1,0:T(8,128)(2,1)}, bf16[480,768]{1,0:T(8,128)(2,1)S(1)}, u32[]{:S(2)}, u32[]{:S(2)}) collective-permute-start(bf16[480,768]{1,0:T(8,128)(2,1)} %fusion.10), channel_id=1, source_target_pairs={{0,16},{8,24},{16,0},{24,8},{1,17},{9,25},{17,1},{25,9},{2,18},{10... | collective-permute-start | bytes 2211848 | tf_op jit(solution)/shard_map/ppermute | solution.py:689
  152.4 56.9 %collective-permute-start.22 = (bf16[480,768]{1,0:T(8,128)(2,1)}, bf16[480,768]{1,0:T(8,128)(2,1)}, u32[]{:S(2)}, u32[]{:S(2)}) collective-permute-start(bf16[480,768]{1,0:T(8,128)(2,1)} %fusion.11), channel_id=1, source_target_pairs={{0,16},{8,24},{16,0},{24,8},{1,17},{9,25},{17,1},{25,9},{2,18},{10... | collective-permute-start | bytes 2211848 | tf_op jit(solution)/shard_map/ppermute | solution.py:689
  159.8 21.6 %collective-permute-start.19 = (bf16[2,192,1536]{2,1,0:T(8,128)(2,1)}, bf16[2,192,1536]{2,1,0:T(8,128)(2,1)}, u32[]{:S(2)}, u32[]{:S(2)}) collective-permute-start(bf16[2,192,1536]{2,1,0:T(8,128)(2,1)} %get-tuple-element.256), channel_id=1, source_target_pairs={{0,8},{8,0},{16,24},{24,16},{1,9},{9,1},{17,25},{25,17},{2,10},{10... | collective-permute-start | bytes 3538952 | tf_op jit(solution)/shard_map/ppermute | solution.py:689
  162.8 29.4 %collective-permute-start.20 = (bf16[2,192,1536]{2,1,0:T(8,128)(2,1)}, bf16[2,192,1536]{2,1,0:T(8,128)(2,1)}, u32[]{:S(2)}, u32[]{:S(2)}) collective-permute-start(bf16[2,192,1536]{2,1,0:T(8,128)(2,1)} %add_convert_fusion), channel_id=1, source_target_pairs={{0,1},{1,0},{2,3},{3,2},{4,5},{5,4},{6,7},{7,6},{8,9},{9,8},{10,11... | collective-permute-start | bytes 3538952 | tf_op jit(solution)/shard_map/ppermute | solution.py:689
  183.7 27.0 %collective-permute-start.21 = (bf16[480,768]{1,0:T(8,128)(2,1)}, bf16[480,768]{1,0:T(8,128)(2,1)}, u32[]{:S(2)}, u32[]{:S(2)}) collective-permute-start(bf16[480,768]{1,0:T(8,128)(2,1)} %fusion.2), channel_id=1, source_target_pairs={{0,1},{1,0},{2,3},{3,2},{4,5},{5,4},{6,7},{7,6},{8,9},{9,8},{10,11... | collective-permute-start | bytes 2211848 | tf_op jit(solution)/shard_map/ppermute | solution.py:689
  192.2 18.5 %collective-permute-start.24 = (bf16[2,3,192,384]{3,2,1,0:T(8,128)(2,1)}, bf16[2,3,192,384]{3,2,1,0:T(8,128)(2,1)S(1)}, u32[]{:S(2)}, u32[]{:S(2)}) collective-permute-start(bf16[2,3,192,384]{3,2,1,0:T(8,128)(2,1)} %get-tuple-element.274), channel_id=1, source_target_pairs={{0,8},{8,0},{16,24},{24,16},{1,9},{9,1},{17,25},{25,17},{2,10},{10... | collective-permute-start | bytes 2654216 | tf_op jit(solution)/shard_map/ppermute | solution.py:689
  194.7 16.1 %collective-permute-start.23 = (bf16[192,1536]{1,0:T(8,128)(2,1)}, bf16[192,1536]{1,0:T(8,128)(2,1)}, u32[]{:S(2)}, u32[]{:S(2)}) collective-permute-start(bf16[192,1536]{1,0:T(8,128)(2,1)} %fusion.12), channel_id=1, source_target_pairs={{0,16},{8,24},{16,0},{24,8},{1,17},{9,25},{17,1},{25,9},{2,18},{10... | collective-permute-start | bytes 1769480 | tf_op jit(solution)/shard_map/ppermute | solution.py:689
  214.4 5.6 %copy-start.6 = (bf16[2,3,192,384]{3,2,1,0:T(8,128)(2,1)S(1)}, bf16[2,3,192,384]{3,2,1,0:T(8,128)(2,1)}, u32[]{:S(2)}) copy-start(bf16[2,3,192,384]{3,2,1,0:T(8,128)(2,1)} %get-tuple-element.291) | copy-start | bytes 2654212
  214.4 5.7 %copy-start.9 = (bf16[2,3,192,384]{3,2,1,0:T(8,128)(2,1)S(1)}, bf16[2,3,192,384]{3,2,1,0:T(8,128)(2,1)}, u32[]{:S(2)}) copy-start(bf16[2,3,192,384]{3,2,1,0:T(8,128)(2,1)} %copy-done.8) | copy-start | bytes 2654212
  216.5 22.4 %collective-permute-start.26 = (bf16[480,768]{1,0:T(8,128)(2,1)S(1)}, bf16[480,768]{1,0:T(8,128)(2,1)S(1)}, u32[]{:S(2)}, u32[]{:S(2)}) collective-permute-start(bf16[480,768]{1,0:T(8,128)(2,1)S(1)} %fusion.1), channel_id=1, source_target_pairs={{0,2},{6,4},{1,3},{7,5},{8,10},{14,12},{9,11},{15,13},{16,18},{22,... | collective-permute-start | bytes 2211848 | tf_op jit(solution)/shard_map/ppermute | solution.py:704
  220.1 18.7 %collective-permute-start.25 = (bf16[3,192,384]{2,1,0:T(8,128)(2,1)S(1)}, bf16[3,192,384]{2,1,0:T(8,128)(2,1)S(1)}, u32[]{:S(2)}, u32[]{:S(2)}) collective-permute-start(bf16[3,192,384]{2,1,0:T(8,128)(2,1)S(1)} %fusion.13), channel_id=1, source_target_pairs={{0,16},{8,24},{16,0},{24,8},{1,17},{9,25},{17,1},{25,9},{2,18},{10... | collective-permute-start | bytes 1327112 | tf_op jit(solution)/shard_map/ppermute | solution.py:689
  221.8 38.6 %collective-permute-start.31 = (bf16[192,1536]{1,0:T(8,128)(2,1)}, bf16[192,1536]{1,0:T(8,128)(2,1)}, u32[]{:S(2)}, u32[]{:S(2)}) collective-permute-start(bf16[192,1536]{1,0:T(8,128)(2,1)} %fusion.4), channel_id=1, source_target_pairs={{0,2},{6,4},{1,3},{7,5},{8,10},{14,12},{9,11},{15,13},{16,18},{22,... | collective-permute-start | bytes 1769480 | tf_op jit(solution)/shard_map/ppermute | solution.py:704
  238.8 3.5 %copy-start.23 = (f32[8,768]{1,0:T(8,128)S(1)}, f32[8,768]{1,0:T(8,128)}, u32[]{:S(2)}) copy-start(f32[8,768]{1,0:T(8,128)} %get-tuple-element.304) | copy-start | bytes 73732
  238.9 3.6 %collective-permute-start.27 = (bf16[2,3,192,384]{3,2,1,0:T(8,128)(2,1)}, bf16[2,3,192,384]{3,2,1,0:T(8,128)(2,1)S(1)}, u32[]{:S(2)}, u32[]{:S(2)}) collective-permute-start(bf16[2,3,192,384]{3,2,1,0:T(8,128)(2,1)} %get-tuple-element.290), channel_id=1, source_target_pairs={{0,8},{8,0},{16,24},{24,16},{1,9},{9,1},{17,25},{25,17},{2,10},{10... | collective-permute-start | bytes 2654216 | tf_op jit(solution)/shard_map/ppermute | solution.py:689
  239.6 3.7 %copy-start.11 = (bf16[2,3,192,384]{3,2,1,0:T(8,128)(2,1)S(1)}, bf16[2,3,192,384]{3,2,1,0:T(8,128)(2,1)}, u32[]{:S(2)}) copy-start(bf16[2,3,192,384]{3,2,1,0:T(8,128)(2,1)} %get-tuple-element.296) | copy-start | bytes 2654212
  239.6 4.4 %copy-start.27 = (f32[8,384]{1,0:T(8,128)S(1)}, f32[8,384]{1,0:T(8,128)}, u32[]{:S(2)}) copy-start(f32[8,384]{1,0:T(8,128)} %get-tuple-element.309) | copy-start | bytes 36868
  239.6 20.8 %collective-permute-start.30 = (bf16[480,768]{1,0:T(8,128)(2,1)S(1)}, bf16[480,768]{1,0:T(8,128)(2,1)S(1)}, u32[]{:S(2)}, u32[]{:S(2)}) collective-permute-start(bf16[480,768]{1,0:T(8,128)(2,1)S(1)} %add_convert_fusion.2), channel_id=1, source_target_pairs={{2,4},{4,2},{3,5},{5,3},{10,12},{12,10},{11,13},{13,11},{18,20},{2... | collective-permute-start | bytes 2211848 | tf_op jit(solution)/shard_map/ppermute | solution.py:708
  241.7 18.7 %collective-permute-start.29 = (bf16[3,192,384]{2,1,0:T(8,128)(2,1)S(1)}, bf16[3,192,384]{2,1,0:T(8,128)(2,1)S(1)}, u32[]{:S(2)}, u32[]{:S(2)}) collective-permute-start(bf16[3,192,384]{2,1,0:T(8,128)(2,1)S(1)} %fusion.7), channel_id=1, source_target_pairs={{0,1},{1,0},{2,3},{3,2},{4,5},{5,4},{6,7},{7,6},{8,9},{9,8},{10,11... | collective-permute-start | bytes 1327112 | tf_op jit(solution)/shard_map/ppermute | solution.py:689
  243.5 17.0 %collective-permute-start.28 = (bf16[3,192,384]{2,1,0:T(8,128)(2,1)S(1)}, bf16[3,192,384]{2,1,0:T(8,128)(2,1)}, u32[]{:S(2)}, u32[]{:S(2)}) collective-permute-start(bf16[3,192,384]{2,1,0:T(8,128)(2,1)S(1)} %fusion.14), channel_id=1, source_target_pairs={{0,16},{8,24},{16,0},{24,8},{1,17},{9,25},{17,1},{25,9},{2,18},{10... | collective-permute-start | bytes 1327112 | tf_op jit(solution)/shard_map/ppermute | solution.py:689
  244.0 16.3 %copy-start.19 = (f32[8,5376]{1,0:T(8,128)}, f32[8,5376]{1,0:T(8,128)S(1)}, u32[]{:S(2)}) copy-start(f32[8,5376]{1,0:T(8,128)S(1)} %constant_dynamic-update-slice_fusion) | copy-start | bytes 516100
  244.0 16.4 %collective-permute-start.32 = (f32[8,5376]{1,0:T(8,128)S(1)}, f32[8,5376]{1,0:T(8,128)}, u32[]{:S(2)}, u32[]{:S(2)}) collective-permute-start(f32[8,5376]{1,0:T(8,128)S(1)} %constant_dynamic-update-slice_fusion), channel_id=1, source_target_pairs={{0,2},{2,0},{4,6},{6,4},{1,3},{3,1},{5,7},{7,5},{8,10},{10,8},{12,... | collective-permute-start | bytes 516104 | tf_op jit(solution)/shard_map/ppermute | solution.py:689
  260.3 3.7 %copy-start.13 = (bf16[2,3,192,384]{3,2,1,0:T(8,128)(2,1)S(1)}, bf16[2,3,192,384]{3,2,1,0:T(8,128)(2,1)}, u32[]{:S(2)}) copy-start(bf16[2,3,192,384]{3,2,1,0:T(8,128)(2,1)} %copy-done.12) | copy-start | bytes 2654212
  262.6 23.7 %collective-permute-start.35 = (bf16[192,1536]{1,0:T(8,128)(2,1)S(1)}, bf16[192,1536]{1,0:T(8,128)(2,1)}, u32[]{:S(2)}, u32[]{:S(2)}) collective-permute-start(bf16[192,1536]{1,0:T(8,128)(2,1)S(1)} %add_convert_fusion.6), channel_id=1, source_target_pairs={{2,4},{4,2},{3,5},{5,3},{10,12},{12,10},{11,13},{13,11},{18,20},{2... | collective-permute-start | bytes 1769480 | tf_op jit(solution)/shard_map/ppermute | solution.py:708
  265.4 21.0 %collective-permute-start.33 = (bf16[3,192,384]{2,1,0:T(8,128)(2,1)S(1)}, bf16[3,192,384]{2,1,0:T(8,128)(2,1)}, u32[]{:S(2)}, u32[]{:S(2)}) collective-permute-start(bf16[3,192,384]{2,1,0:T(8,128)(2,1)S(1)} %fusion.6), channel_id=1, source_target_pairs={{0,2},{6,4},{1,3},{7,5},{8,10},{14,12},{9,11},{15,13},{16,18},{22,... | collective-permute-start | bytes 1327112 | tf_op jit(solution)/shard_map/ppermute | solution.py:704
  270.5 15.8 %collective-permute-start.34 = (f32[8,5376]{1,0:T(8,128)S(1)}, f32[8,5376]{1,0:T(8,128)S(1)}, u32[]{:S(2)}, u32[]{:S(2)}) collective-permute-start(f32[8,5376]{1,0:T(8,128)S(1)} %add.188), channel_id=1, source_target_pairs={{0,4},{2,6},{4,0},{6,2},{1,5},{3,7},{5,1},{7,3},{8,12},{10,14},{12... | collective-permute-start | bytes 516104 | tf_op jit(solution)/shard_map/ppermute | solution.py:689
  270.7 23.1 %collective-permute-start.37 = (bf16[480,768]{1,0:T(8,128)(2,1)S(1)}, bf16[480,768]{1,0:T(8,128)(2,1)S(1)}, u32[]{:S(2)}, u32[]{:S(2)}) collective-permute-start(bf16[480,768]{1,0:T(8,128)(2,1)S(1)} %add_convert_fusion.1), channel_id=1, source_target_pairs={{2,0},{4,6},{3,1},{5,7},{10,8},{12,14},{11,9},{13,15},{18,16},{20,... | collective-permute-start | bytes 2211848 | tf_op jit(solution)/shard_map/ppermute | solution.py:712
  272.0 25.4 %collective-permute-start.39 = (bf16[512,768]{1,0:T(8,128)(2,1)}, bf16[512,768]{1,0:T(8,128)(2,1)S(1)}, u32[]{:S(2)}, u32[]{:S(2)}) collective-permute-start(bf16[512,768]{1,0:T(8,128)(2,1)} %get-tuple-element.332), channel_id=1, source_target_pairs={{0,1},{1,0},{2,3},{3,2},{4,5},{5,4},{6,7},{7,6},{8,9},{9,8},{10,11... | collective-permute-start | bytes 2359304 | tf_op jit(solution)/shard_map/ppermute | solution.py:689
  286.4 7.5 %collective-permute-start.36 = (f32[8,5376]{1,0:T(8,128)S(1)}, f32[8,5376]{1,0:T(8,128)S(1)}, u32[]{:S(2)}, u32[]{:S(2)}) collective-permute-start(f32[8,5376]{1,0:T(8,128)S(1)} %add.189), channel_id=1, source_target_pairs={{0,8},{8,0},{16,24},{24,16},{1,9},{9,1},{17,25},{25,17},{2,10},{10... | collective-permute-start | bytes 516104 | tf_op jit(solution)/shard_map/ppermute | solution.py:689
  287.6 11.8 %collective-permute-start.40 = (bf16[3,192,384]{2,1,0:T(8,128)(2,1)S(1)}, bf16[3,192,384]{2,1,0:T(8,128)(2,1)S(1)}, u32[]{:S(2)}, u32[]{:S(2)}) collective-permute-start(bf16[3,192,384]{2,1,0:T(8,128)(2,1)S(1)} %add_convert_fusion.9), channel_id=1, source_target_pairs={{2,4},{4,2},{3,5},{5,3},{10,12},{12,10},{11,13},{13,11},{18,20},{2... | collective-permute-start | bytes 1327112 | tf_op jit(solution)/shard_map/ppermute | solution.py:708
  289.6 19.1 %collective-permute-start.43 = (bf16[192,1536]{1,0:T(8,128)(2,1)S(1)}, bf16[192,1536]{1,0:T(8,128)(2,1)}, u32[]{:S(2)}, u32[]{:S(2)}) collective-permute-start(bf16[192,1536]{1,0:T(8,128)(2,1)S(1)} %add_convert_fusion.5), channel_id=1, source_target_pairs={{2,0},{4,6},{3,1},{5,7},{10,8},{12,14},{11,9},{13,15},{18,16},{20,... | collective-permute-start | bytes 1769480 | tf_op jit(solution)/shard_map/ppermute | solution.py:712
  293.9 5.5 %collective-permute-start.38 = (f32[8,5376]{1,0:T(8,128)S(1)}, f32[8,5376]{1,0:T(8,128)S(1)}, u32[]{:S(2)}, u32[]{:S(2)}) collective-permute-start(f32[8,5376]{1,0:T(8,128)S(1)} %add.192), channel_id=1, source_target_pairs={{0,16},{8,24},{16,0},{24,8},{1,17},{9,25},{17,1},{25,9},{2,18},{10... | collective-permute-start | bytes 516104 | tf_op jit(solution)/shard_map/ppermute | solution.py:689
  297.4 4.9 %copy-start.3 = (bf16[512,768]{1,0:T(8,128)(2,1)}, bf16[512,768]{1,0:T(8,128)(2,1)S(1)}, u32[]{:S(2)}) copy-start(bf16[512,768]{1,0:T(8,128)(2,1)S(1)} %collective-permute-done.39.first_ref.second_ref) | copy-start | bytes 2359300
  299.5 9.2 %collective-permute-start.42 = (f32[8,3456]{1,0:T(8,128)S(1)}, f32[8,3456]{1,0:T(8,128)S(1)}, u32[]{:S(2)}, u32[]{:S(2)}) collective-permute-start(f32[8,3456]{1,0:T(8,128)S(1)} %pad_maximum_fusion.1), channel_id=1, source_target_pairs={{0,1},{1,0},{2,3},{3,2},{4,5},{5,4},{6,7},{7,6},{8,9},{9,8},{10,11... | collective-permute-start | bytes 331784 | tf_op jit(solution)/shard_map/ppermute | solution.py:689
  301.0 15.6 %collective-permute-start.41 = (bf16[3,192,384]{2,1,0:T(8,128)(2,1)S(1)}, bf16[3,192,384]{2,1,0:T(8,128)(2,1)S(1)}, u32[]{:S(2)}, u32[]{:S(2)}) collective-permute-start(bf16[3,192,384]{2,1,0:T(8,128)(2,1)S(1)} %add_convert_fusion.8), channel_id=1, source_target_pairs={{2,0},{4,6},{3,1},{5,7},{10,8},{12,14},{11,9},{13,15},{18,16},{20,... | collective-permute-start | bytes 1327112 | tf_op jit(solution)/shard_map/ppermute | solution.py:712
  311.2 6.5 %copy-start.1 = (s32[2,1024]{1,0:T(2,128)S(1)}, s32[2,1024]{1,0:T(2,128)}, u32[]{:S(2)}) copy-start(s32[2,1024]{1,0:T(2,128)} %param.12) | copy-start | bytes 24580
  (22 other events, 38.5 us)

commit v5 on v4

--- a/solution.py
+++ b/solution.py
@@ -10,7 +10,7 @@
 HD = 64
 EPSILON = 1e-05
 MASKED = -1e30
-VMEM_CAP = 60 * 1024 * 1024
+MIB = 1024 * 1024
 F32 = jnp.float32
 BF16 = jnp.bfloat16
 COST_FLOPS = 0.4e9
@@ -94,7 +94,7 @@
         out_shape=[jax.ShapeDtypeStruct((length, width), BF16),
                    jax.ShapeDtypeStruct((width // 128, 8, length), F32)],
         input_output_aliases={4 + n: n for n in range(len(more))},
-        compiler_params=pltpu.CompilerParams(vmem_limit_bytes=VMEM_CAP),
+        compiler_params=pltpu.CompilerParams(vmem_limit_bytes=6 * MIB),
         cost_estimate=cost(3.8 * pairs),
         name="attend_forward",
     )(flags, queries, key_rows, value_rows, *more)
@@ -163,7 +163,7 @@
             scratch_shapes=[pltpu.VMEM((length, 128), F32), pltpu.VMEM((length, 128), F32)]),
         out_shape=[jax.ShapeDtypeStruct((3, length, pairs * 128), BF16),
                    jax.ShapeDtypeStruct((8, pairs * 128), F32)],
-        compiler_params=pltpu.CompilerParams(vmem_limit_bytes=VMEM_CAP),
+        compiler_params=pltpu.CompilerParams(vmem_limit_bytes=9 * MIB),
         cost_estimate=cost(1 + 6 * pairs),
         name="attend_backward",
     )(flags, queries, key_rows, value_rows, upstream, log_sums)
@@ -196,7 +196,7 @@
             in_specs=[fixed(packed)] + [fixed(value) for value in extra],
             out_specs=[pl.BlockSpec((n, D), lambda i, s: (0, 0)) for n in counts]),
         out_shape=[jax.ShapeDtypeStruct((n, D), BF16) for n in counts],
-        compiler_params=pltpu.CompilerParams(vmem_limit_bytes=VMEM_CAP),
+        compiler_params=pltpu.CompilerParams(vmem_limit_bytes=6 * MIB),
         cost_estimate=cost(5),
         name="unpack_rows",
     )(place, packed, *extra)
@@ -289,7 +289,7 @@
             out_specs=[wide] * 4,
             scratch_shapes=[pltpu.VMEM((3, D, D), BF16), pltpu.SemaphoreType.DMA((5,))]),
         out_shape=[out] * 4,
-        compiler_params=pltpu.CompilerParams(vmem_limit_bytes=VMEM_CAP),
+        compiler_params=pltpu.CompilerParams(vmem_limit_bytes=11 * MIB),
         cost_estimate=cost(10),
         name="norm_project",
     )(place, own, other, gain, bias, w_own, *w_quarter)
@@ -442,7 +442,7 @@
                    sd((length // 2, D), BF16), sd((block, D), BF16), sd((block, D), BF16),
                    sd((length, D), F32), sd((length, D), BF16), sd((length, D), BF16),
                    sd((8, D), F32), sd((8, hid // 2), F32), sd((8, hid // 2), F32)],
-        compiler_params=pltpu.CompilerParams(vmem_limit_bytes=VMEM_CAP),
+        compiler_params=pltpu.CompilerParams(vmem_limit_bytes=36 * MIB),
         cost_estimate=cost(38),
         name="middle_stage",
     )(place, att, res_own, res_other, cot_own, cot_other, gain, end_bias, fc_bias, *flat)
@@ -454,27 +454,27 @@
     for pair in range(2):
         to = pair ^ (place_ref[1] >> 1)
         low, high = both[2 * pair * rows : (2 * pair + 1) * rows], both[(2 * pair + 1) * rows : (2 * pair + 2) * rows]
-        keep_ref[to] = jnp.where(flip, high, low)
-        send_ref[to] = jnp.where(flip, low, high)
-
-
-def fc_grad(place, left, right, side, chunk=768):
+        keep_ref[0, to] = jnp.where(flip, high, low)
+        send_ref[0, to] = jnp.where(flip, low, high)
+
+
+def fc_grad(place, left, right, chunk=768):
     length, width = left.shape
     rows = width // 4
     half = right.shape[1] // 2
     parts = half // chunk
-    out = jax.ShapeDtypeStruct((2, rows, half), BF16)
-    out_spec = pl.BlockSpec((2, rows, chunk), lambda n, s: (0, 0, n))
+    out = jax.ShapeDtypeStruct((2, 2, rows, half), BF16)
+    out_spec = pl.BlockSpec((1, 2, rows, chunk), lambda n, s: (n // parts, 0, 0, n % parts))
     return pl.pallas_call(
         functools.partial(fc_grad_kernel, rows=rows),
         grid_spec=pltpu.PrefetchScalarGridSpec(
-            num_scalar_prefetch=1, grid=(parts,),
+            num_scalar_prefetch=1, grid=(2 * parts,),
             in_specs=[pl.BlockSpec((length, width), lambda n, s: (0, 0)),
-                      pl.BlockSpec((length, chunk), lambda n, s: (0, n + side * parts))],
+                      pl.BlockSpec((length, chunk), lambda n, s: (0, n))],
             out_specs=[out_spec, out_spec]),
         out_shape=[out, out],
-        compiler_params=pltpu.CompilerParams(vmem_limit_bytes=VMEM_CAP),
-        cost_estimate=cost(6),
+        compiler_params=pltpu.CompilerParams(vmem_limit_bytes=12 * MIB),
+        cost_estimate=cost(12),
         name="fc_grad",
     )(place, left, right)
 
@@ -532,7 +532,7 @@
             out_specs=[whole(out), whole(out), whole(sums)],
             scratch_shapes=[pltpu.VMEM((width, 3 * cols), F32)]),
         out_shape=[out, out, sums],
-        compiler_params=pltpu.CompilerParams(vmem_limit_bytes=VMEM_CAP),
+        compiler_params=pltpu.CompilerParams(vmem_limit_bytes=17 * MIB),
         cost_estimate=cost(6.5),
         name="qkv_grad",
     )(place, left, *rights, *weights)
@@ -575,7 +575,7 @@
             out_specs=[out_spec, out_spec],
             scratch_shapes=[pltpu.VMEM((attended.shape[1], D), BF16)]),
         out_shape=[out, out],
-        compiler_params=pltpu.CompilerParams(vmem_limit_bytes=VMEM_CAP),
+        compiler_params=pltpu.CompilerParams(vmem_limit_bytes=19 * MIB),
         cost_estimate=cost(13),
         name="proj_grad",
     )(place, active, active, cot_own, cot_other, attended, branch)
@@ -648,7 +648,7 @@
             out_specs=[pl.BlockSpec((block, D), own_map), pl.BlockSpec((block, D), other_map)],
             scratch_shapes=[pltpu.VMEM((D, 3 * D), BF16), pltpu.SemaphoreType.DMA((3, 5))]),
         out_shape=[sd((length // 2, D), BF16), sd((length // 2, D), BF16)],
-        compiler_params=pltpu.CompilerParams(vmem_limit_bytes=VMEM_CAP),
+        compiler_params=pltpu.CompilerParams(vmem_limit_bytes=14 * MIB),
         cost_estimate=cost(9),
         name="input_grad",
     )(place, *own_grads, *other_grads, res_own, res_other, mid, gain, w_own, *w_quarter)
@@ -678,7 +678,7 @@
                       pl.BlockSpec((128, D), other_map)],
             out_specs=pl.BlockSpec((D - 1, 2, 128), lambda i, s: (0, 0, i))),
         out_shape=jax.ShapeDtypeStruct((D - 1, 2, positions), BF16),
-        compiler_params=pltpu.CompilerParams(vmem_limit_bytes=VMEM_CAP),
+        compiler_params=pltpu.CompilerParams(vmem_limit_bytes=4 * MIB),
         cost_estimate=cost(0.1),
         name="pack_rows",
     )(place, own, first, second)
@@ -799,34 +799,31 @@
         proj_k, proj_s = proj_grad(after(place, middle_sums), active, cot_own, cot_other, attended, branch_grad)
         proj_k, proj_s, out_got[0] = meet(proj_k, proj_s, out_got[0])
         proj_c = c_swap(proj_s)
-        fo_k, fo_s = fc_grad(after(place, proj_k), normed_two, hidden_grad, 1)
-        fo_k, fo_s, proj_k, proj_c = meet(fo_k, fo_s, proj_k, proj_c)
-        fo_c = c_swap(fo_s)
+        fc_k, fc_s = fc_grad(after(place, proj_k), normed_two, hidden_grad)
+        fc_k, fc_s, proj_k, proj_c, *out_got = meet(fc_k, fc_s, proj_k, proj_c, *out_got)
+        fc_c = c_swap(fc_s)
         proj_fo = add_low(proj_k[1, 1], proj_c[1, 1])
         proj_xo = x_swap(proj_fo)
         proj_fm = add_low(proj_k[1, 0], after(proj_c, proj_fo)[1, 0])
         proj_xm = x_swap(proj_fm)
-        fm_k, fm_s = fc_grad(after(place, proj_fo, proj_fm), normed_two, hidden_grad, 0)
-        fm_k, fm_s, fo_k, fo_c, *out_got = meet(fm_k, fm_s, fo_k, fo_c, *out_got)
-        fm_c = c_swap(fm_s)
-        fc_away = add_low(fo_k, fo_c)
+        fc_k, fc_c, proj_fo, proj_fm = meet(fc_k, fc_c, proj_fo, proj_fm)
+        fc_away = add_low(fc_k[1], fc_c[1])
         fc_y = y_swap(fc_away)
         first, first_sums = backward(after(attended_grad, fc_away), log_sums, pairs, pairs)
-        first, first_sums, proj_k, proj_c, proj_xo, fm_k, fm_c = meet(
-            first, first_sums, proj_k, proj_c, proj_xo, fm_k, fm_c)
+        first, first_sums, proj_k, proj_c, proj_xo = meet(first, first_sums, proj_k, proj_c, proj_xo)
         proj_r = add_low(proj_k[0, 1], proj_c[0, 1], proj_xo)
         proj_y = y_swap(proj_r)
         qo_k, qo_s, qo_sum = qkv_grad(after(place, proj_r), normed_one, [first], qkv_others)
-        qo_k, qo_s, fm_k, fm_c, fc_y = meet(qo_k, qo_s, fm_k, fm_c, fc_y)
+        qo_k, qo_s, fc_k, fc_c, fc_y = meet(qo_k, qo_s, fc_k, fc_c, fc_y)
         qo_c = c_swap(qo_s)
-        fc_far = add_low(fm_k[1], fm_c[1], fc_y[1])
+        fc_far = add_low(fc_k[0, 1], fc_c[0, 1], fc_y[1])
         fc_x = x_swap(fc_far)
         own_a, sums_a = backward(after(attended_grad, fc_far), log_sums, 0, pairs - 1)
         own_a, sums_a, proj_y, proj_xm, proj_k, proj_c, fc_x, qo_k, qo_c = meet(
             own_a, sums_a, proj_y, proj_xm, proj_k, proj_c, fc_x, qo_k, qo_c)
         proj_shard = add_low(proj_k[0, 0], proj_c[0, 0], proj_xm, proj_y)
         proj_z = chain_in(proj_shard)
-        fc_shard = add_low(fm_k[0], fm_c[0], fc_y[0], fc_x)
+        fc_shard = add_low(fc_k[0, 0], fc_c[0, 0], fc_y[0], fc_x)
         fc_z = chain_in(fc_shard)
         qo_f = add_low(qo_k[1], qo_c[1])
         qo_x = x_swap(qo_f)

time: 324 us -> 300 us (0.926)
  Pallas kernels: 186 us -> 145 us
  waiting for transfers between devices: 29.2 us -> 58.2 us
  other arithmetic: 35.2 us -> 15.2 us
  starting transfers between devices: 49.6 us -> 55.7 us
    ppermute x35 -> x34, waiting for transfers between devices: 22.9 us -> 43.4 us  [swap(): return lax.ppermute(value, axis, [(n, n ^ bit) for n in range(size)])]
    convert_element_type x17, other arithmetic: 24 us -> 8.65 us  [add_low(): return total.astype(BF16)]
    pallas_call x2 -> x1, Pallas kernels: 13.5 us -> 7.21 us  [fc_grad(): pl.pallas_call(functools.partial(fc_grad_kernel, rows=rows), grid_spec=pl...]
    pallas_call x2, Pallas kernels: 13.7 us -> 7.82 us  [qkv_grad(): pl.pallas_call(functools.partial(qkv_grad_kernel, rows=rows, parts=len(ri...]
    ppermute x3, starting transfers between devices: 9.89 us -> 15.1 us  [chain_in(): return lax.ppermute(value, 'group', [(0, 1), (3, 2)])]
    pallas_call x2, Pallas kernels: 11.8 us -> 6.66 us  [unpack_rows(): pl.pallas_call(unpack_kernel, grid_spec=pltpu.PrefetchScalarGridSpec(num_...]
    ppermute x3, waiting for transfers between devices: 0.01 us -> 4.91 us  [chain_in(): return lax.ppermute(value, 'group', [(0, 1), (3, 2)])]
    pallas_call x3, Pallas kernels: 39.1 us -> 34.3 us  [attend_backward(): pl.pallas_call(functools.partial(attend_backward_kernel, block=length //...]
  transfers between devices with their start and end apart: 44 -> 43, of which waited for: 10 -> 20; matrix products, arithmetic and copies ran while one was open for 11% -> 7% of each run, Pallas kernels for 47% -> 37%
where the time goes in v5:
time: 300 us; the launch traced here: 294 us
  Pallas kernels  145 us (48%)
  waiting for transfers between devices  58.2 us (19%)
  starting transfers between devices  55.7 us (19%)
  local copies, waits for them, and re-layouts  18.8 us (6%)
  other arithmetic  15.2 us (5%)
    ppermute x34, waiting for transfers between devices, swap(): return lax.ppermute(value, axis, [(n, n ^ bit) for n in range(size)])  43.4 us
    pallas_call x1, Pallas kernels, middle_stage(): pl.pallas_call(body, grid_spec=pltpu.PrefetchScalarGridSpec(num_scalar_pr...  35.2 us
    pallas_call x3, Pallas kernels, attend_backward(): pl.pallas_call(functools.partial(attend_backward_kernel, block=length //...  34.3 us
    ppermute x34, starting transfers between devices, swap(): return lax.ppermute(value, axis, [(n, n ^ bit) for n in range(size)])  33.6 us
    pallas_call x2, Pallas kernels, attend_forward(): pl.pallas_call(body, grid_spec=pltpu.PrefetchScalarGridSpec(num_scalar_pr...  18.8 us
    ppermute x3, starting transfers between devices, chain_in(): return lax.ppermute(value, 'group', [(0, 1), (3, 2)])  15.1 us
    unnamed x62, local copies, waits for them, and re-layouts  11.1 us
    ppermute x3, waiting for transfers between devices, chain_out(): return lax.ppermute(value, 'group', [(1, 0), (2, 3)])  9.89 us
  transfers between devices with their start and end apart: 43, of which 20 were waited for; matrix products, arithmetic and copies ran while one was open for 7% of the time, Pallas kernels for 37%

profile of v5, /device:TPU:0, one launch (start us, length us, event | category | flops | bytes accessed | tf_op | source)
XLA Modules:
  0.0 294.3 jit_solution(18019008778776646363)
XLA Ops:
  1.7 3.0 %collective-permute-start = (bf16[3,192,384]{2,1,0:T(8,128)(2,1)S(1)}, bf16[3,192,384]{2,1,0:T(8,128)(2,1)}, u32[]{:S(2)}, u32[]{:S(2)}) collective-permute-start(bf16[3,192,384]{2,1,0:T(8,128)(2,1)S(1)} %constant_dynamic-slice_fusion.5), channel_id=1, source_target_pairs={{0,1},{1,0},{2,3},{3,2},{4,5},{5,4},{6,7},{7,6},{8,9},{9,8},{10,11... | collective-permute-start | bytes 1327112 | tf_op jit(solution)/shard_map/ppermute | solution.py:689
  7.2 1.4 copy-done.7
  8.6 3.3 %unpack_rows.2 = (bf16[512,768]{1,0:T(8,128)(2,1)S(1)}, bf16[528,768]{1,0:T(8,128)(2,1)S(1)}) custom-call(s32[3]{0:T(128)S(1)} %pad_add_fusion.place_ref, bf16[767,2,512]{2,1,0:T(2,128)(2,1)S(1)} %bitcast.55, bf16[16,768]{1,0:T(8,128)(2,1)S(1)} %maximum_maximum_fusion.refs_0_), custom_call_target="tpu_custom_call" | custom-call | flops 2000000000 | bytes 2000000 | tf_op jit(solution)/shard_map/unpack_rows/pallas_call | solution.py:192
  12.0 3.1 %collective-permute-done.a.refs_1_.refs_8_ = bf16[3,192,384]{2,1,0:T(8,128)(2,1)} collective-permute-done((bf16[3,192,384]{2,1,0:T(8,128)(2,1)S(1)}, bf16[3,192,384]{2,1,0:T(8,128)(2,1)}, u32[]{:S(2)}, u32[]{:S(2)}) %collective-permute-start) | collective-permute-done | bytes 442400 | tf_op jit(solution)/shard_map/ppermute | solution.py:689
  15.0 1.7 collective-permute-start.2
  16.8 1.5 collective-permute-start.1
  18.3 1.7 pad.20.refs_10_
  21.3 1.2 constant_dynamic-slice_fusion
  24.7 1.5 collective-permute-start.6
  26.2 3.3 %unpack_rows.3 = (bf16[512,768]{1,0:T(8,128)(2,1)S(1)}, bf16[512,768]{1,0:T(8,128)(2,1)S(1)}) custom-call(s32[3]{0:T(128)S(1)} %pad_add_fusion.place_ref, bf16[767,2,512]{2,1,0:T(2,128)(2,1)S(1)} %bitcast.56), custom_call_target="tpu_custom_call" | custom-call | flops 2000000000 | bytes 2000000 | tf_op jit(solution)/shard_map/unpack_rows/pallas_call | solution.py:192
  30.4 5.6 %collective-permute-done.2.other_ref.refs_2_.refs_4_ = bf16[528,768]{1,0:T(8,128)(2,1)S(1)} collective-permute-done((bf16[528,768]{1,0:T(8,128)(2,1)S(1)}, bf16[528,768]{1,0:T(8,128)(2,1)S(1)}, u32[]{:S(2)}, u32[]{:S(2)}) %collective-permute-start.2) | collective-permute-done | bytes 811040 | tf_op jit(solution)/shard_map/ppermute | solution.py:689
  37.0 1.2 collective-permute-done.4.d.refs_4_.refs_11_
  38.2 1.1 copy-done.5
  40.3 1.1 copy-done.14
  41.5 7.8 %norm_project.1 = (bf16[1024,768]{1,0:T(8,128)(2,1)S(1)}, bf16[1024,768]{1,0:T(8,128)(2,1)S(1)}, bf16[1024,768]{1,0:T(8,128)(2,1)S(1)}, bf16[1024,768]{1,0:T(8,128)(2,1)S(1)}) custom-call(s32[3]{0:T(128)S(1)} %pad_add_fusion.place_ref, bf16[512,768]{1,0:T(8,128)(2,1)S(1)} %copy-done.14, bf16[528,768]{1,0:T(8,128)(2,1)S(1)} %copy-done.5, ...), custom_call_target="tpu_custom_call" | custom-call | flops 4000000000 | bytes 4000000 | tf_op jit(solution)/shard_map/norm_project/pallas_call | solution.py:283
  49.3 1.8 collective-permute-start.9
  51.1 9.4 %attend_forward.2 = (bf16[1024,768]{1,0:T(8,128)(2,1)S(1)}, f32[6,8,1024]{2,1,0:T(8,128)S(1)}) custom-call(s32[4]{0:T(128)S(1)} %compare_convert_fusion.flags_ref, bf16[1024,768]{1,0:T(8,128)(2,1)S(1)} %get-tuple-element.202.q_ref, bf16[1024,768]{1,0:T(8,128)(2,1)S(1)} %get-tuple-element.198.k_ref, bf16[1024,768]{1,0:T(8,128)(2,1)S(1)} %get-tuple-element.199.v_ref), custom_call_target="tpu_custom_call" | custom-call | flops 4560000000 | bytes 4559999 | tf_op jit(solution)/shard_map/attend_forward/pallas_call | solution.py:88
  60.5 4.1 %collective-permute-done.6.refs_15_ = bf16[384,768]{1,0:T(8,128)(2,1)} collective-permute-done((bf16[384,768]{1,0:T(8,128)(2,1)}, bf16[384,768]{1,0:T(8,128)(2,1)}, u32[]{:S(2)}, u32[]{:S(2)}) %collective-permute-start.6) | collective-permute-done | bytes 589856 | tf_op jit(solution)/shard_map/ppermute | solution.py:689
  64.6 1.8 collective-permute-start.7
  66.4 1.6 collective-permute-start.8
  68.0 9.4 %attend_forward.3 = (bf16[1024,768]{1,0:T(8,128)(2,1)S(1)}, f32[6,8,1024]{2,1,0:T(8,128)S(1)}) custom-call(s32[4]{0:T(128)S(1)} %compare_convert_fusion.flags_ref, bf16[1024,768]{1,0:T(8,128)(2,1)S(1)} %get-tuple-element.202.q_ref, bf16[1024,768]{1,0:T(8,128)(2,1)S(1)} %get-tuple-element.198.k_ref, ...), custom_call_target="tpu_custom_call", output_to_operand_aliasing={{0}: (4, {}), {1}: (5, {})} | custom-call | flops 4560000000 | bytes 4559999 | tf_op jit(solution)/shard_map/attend_forward/pallas_call | solution.py:88
  77.5 2.4 collective-permute-done.7.refs_13_
  80.5 3.1 %collective-permute-done.12.refs_16_ = bf16[384,768]{1,0:T(8,128)(2,1)S(1)} collective-permute-done((bf16[384,768]{1,0:T(8,128)(2,1)}, bf16[384,768]{1,0:T(8,128)(2,1)S(1)}, u32[]{:S(2)}, u32[]{:S(2)}) %collective-permute-start.12) | collective-permute-done | bytes 589856 | tf_op jit(solution)/shard_map/ppermute | solution.py:689
  83.8 35.2 %middle_stage.1 = (bf16[1024,768]{1,0:T(8,128)(2,1)S(1)}, bf16[1024,3072]{1,0:T(8,128)(2,1)}, bf16[1024,3072]{1,0:T(8,128)(2,1)}, bf16[512,768]{1,0:T(8,128)(2,1...) custom-call(s32[3]{0:T(128)S(1)} %pad_add_fusion.place_ref, ...), custom_call_target="tpu_custom_call" | custom-call | flops 15200000000 | bytes 15200000 | tf_op jit(solution)/shard_map/middle_stage/pallas_call | solution.py:427
  119.1 1.1 collective-permute-start.14
  120.2 2.8 copy-done.16
  123.0 8.4 %proj_grad.1 = (bf16[2,2,480,768]{3,2,1,0:T(8,128)(2,1)S(1)}, bf16[2,2,480,768]{3,2,1,0:T(8,128)(2,1)S(1)}) custom-call(s32[3]{0:T(128)S(1)} %pad_add_fusion.place_ref, bf16[1024,3072]{1,0:T(8,128)(2,1)S(1)} %copy-done.16, bf16[1024,3072]{1,0:T(8,128)(2,1)S(1)} %copy-done.16, bf16[512,768]{1,0:T(8,128)(2,1)S(1)} %copy-done.18, ...), custom_call_target="tpu_custom_call" | custom-call | flops 5200000000 | bytes 5200000 | tf_op jit(solution)/shard_map/proj_grad/pallas_call | solution.py:568
  132.5 7.2 %fc_grad.1 = (bf16[2,2,192,1536]{3,2,1,0:T(8,128)(2,1)S(1)}, bf16[2,2,192,1536]{3,2,1,0:T(8,128)(2,1)S(1)}) custom-call(s32[3]{0:T(128)S(1)} %pad_add_fusion.place_ref, bf16[1024,768]{1,0:T(8,128)(2,1)S(1)} %get-tuple-element.227.left_ref, bf16[1024,3072]{1,0:T(8,128)(2,1)S(1)} %copy-done.19), custom_call_target="tpu_custom_call" | custom-call | flops 4800000000 | bytes 4800000 | tf_op jit(solution)/shard_map/fc_grad/pallas_call | solution.py:468
  139.7 3.3 %collective-permute-done.16.second_ref = bf16[256,768]{1,0:T(8,128)(2,1)S(1)} collective-permute-done((bf16[256,768]{1,0:T(8,128)(2,1)S(1)}, bf16[256,768]{1,0:T(8,128)(2,1)S(1)}, u32[]{:S(2)}, u32[]{:S(2)}) %collective-permute-start.16) | collective-permute-done | bytes 393248 | tf_op jit(solution)/shard_map/ppermute | solution.py:689
  143.2 1.6 collective-permute-start.18
  145.5 2.0 collective-permute-done.17
  148.9 17.2 %attend_backward.3 = (bf16[3,1024,384]{2,1,0:T(8,128)(2,1)S(1)}, f32[8,384]{1,0:T(8,128)S(1)}) custom-call(s32[4]{0:T(128)S(1)} %compare_convert_fusion.flags_ref, bf16[1024,768]{1,0:T(8,128)(2,1)S(1)} %get-tuple-element.202.q_ref, bf16[1024,768]{1,0:T(8,128)(2,1)S(1)} %get-tuple-element.198.k_ref, bf16[1024,768]{1,0:T(8,128)(2,1)S(1)} %get-tuple-element.199.v_ref, ...), custom_call_target="tpu_custom_call" | custom-call | flops 7600000000 | bytes 7600000 | tf_op jit(solution)/shard_map/attend_backward/pallas_call | solution.py:155
  166.4 1.1 collective-permute-start.20
  167.5 4.8 %qkv_grad.2 = (bf16[2,3,192,384]{3,2,1,0:T(8,128)(2,1)S(1)}, bf16[2,3,192,384]{3,2,1,0:T(8,128)(2,1)S(1)}, f32[8,768]{1,0:T(8,128)S(1)}) custom-call(s32[3]{0:T(128)S(1)} %pad_add_fusion.place_ref, bf16[1024,768]{1,0:T(8,128)(2,1)S(1)} %get-tuple-element.249.left_ref, bf16[3,1024,384]{2,1,0:T(8,128)(2,1)S(1)} %get-tuple-element.250.refs_0_.refs_2_, ...), custom_call_target="tpu_custom_call" | custom-call | flops 2600000000 | bytes 2600000 | tf_op jit(solution)/shard_map/qkv_grad/pallas_call | solution.py:526
  172.3 4.4 %collective-permute-done.19 = bf16[2,192,1536]{2,1,0:T(8,128)(2,1)S(1)} collective-permute-done((bf16[2,192,1536]{2,1,0:T(8,128)(2,1)S(1)}, bf16[2,192,1536]{2,1,0:T(8,128)(2,1)S(1)}, u32[]{:S(2)}, u32[]{:S(2)}) %collective-permute-start.19) | collective-permute-done | bytes 1179680 | tf_op jit(solution)/shard_map/ppermute | solution.py:689
  176.9 1.6 collective-permute-start.22
  178.5 11.4 %attend_backward.4 = (bf16[3,1024,256]{2,1,0:T(8,128)(2,1)S(1)}, f32[8,256]{1,0:T(8,128)S(1)}) custom-call(s32[4]{0:T(128)S(1)} %compare_convert_fusion.flags_ref, bf16[1024,768]{1,0:T(8,128)(2,1)S(1)} %get-tuple-element.202.q_ref, bf16[1024,768]{1,0:T(8,128)(2,1)S(1)} %get-tuple-element.198.k_ref, bf16[1024,768]{1,0:T(8,128)(2,1)S(1)} %get-tuple-element.199.v_ref, ...), custom_call_target="tpu_custom_call" | custom-call | flops 5200000000 | bytes 5200000 | tf_op jit(solution)/shard_map/attend_backward/pallas_call | solution.py:155
  189.9 1.8 collective-permute-done.20
  193.4 3.5 %collective-permute-start.25 = (bf16[480,768]{1,0:T(8,128)(2,1)S(1)}, bf16[480,768]{1,0:T(8,128)(2,1)S(1)}, u32[]{:S(2)}, u32[]{:S(2)}) collective-permute-start(bf16[480,768]{1,0:T(8,128)(2,1)S(1)} %fusion.1), channel_id=1, source_target_pairs={{0,2},{6,4},{1,3},{7,5},{8,10},{14,12},{9,11},{15,13},{16,18},{22,... | collective-permute-start | bytes 2211848 | tf_op jit(solution)/shard_map/ppermute | solution.py:704
  197.1 1.6 collective-permute-start.24
  198.6 1.5 collective-permute-start.30
  200.1 5.7 %attend_backward.5 = (bf16[3,1024,128]{2,1,0:T(8,128)(2,1)S(1)}, f32[8,128]{1,0:T(8,128)S(1)}) custom-call(s32[4]{0:T(128)S(1)} %compare_convert_fusion.flags_ref, bf16[1024,768]{1,0:T(8,128)(2,1)S(1)} %get-tuple-element.202.q_ref, bf16[1024,768]{1,0:T(8,128)(2,1)S(1)} %get-tuple-element.198.k_ref, bf16[1024,768]{1,0:T(8,128)(2,1)S(1)} %get-tuple-element.199.v_ref, ...), custom_call_target="tpu_custom_call" | custom-call | flops 2800000000 | bytes 2800000 | tf_op jit(solution)/shard_map/attend_backward/pallas_call | solution.py:155
  205.8 3.0 %qkv_grad.3 = (bf16[2,3,192,384]{3,2,1,0:T(8,128)(2,1)S(1)}, bf16[2,3,192,384]{3,2,1,0:T(8,128)(2,1)S(1)}, f32[8,768]{1,0:T(8,128)S(1)}) custom-call(s32[3]{0:T(128)S(1)} %pad_add_fusion.place_ref, bf16[1024,768]{1,0:T(8,128)(2,1)S(1)} %get-tuple-element.249.left_ref, bf16[3,1024,256]{2,1,0:T(8,128)(2,1)S(1)} %get-tuple-element.271.refs_0_, ...), custom_call_target="tpu_custom_call" | custom-call | flops 2600000000 | bytes 2600000 | tf_op jit(solution)/shard_map/qkv_grad/pallas_call | solution.py:526
  208.9 4.9 %collective-permute-done.25 = bf16[480,768]{1,0:T(8,128)(2,1)S(1)} collective-permute-done((bf16[480,768]{1,0:T(8,128)(2,1)S(1)}, bf16[480,768]{1,0:T(8,128)(2,1)S(1)}, u32[]{:S(2)}, u32[]{:S(2)}) %collective-permute-start.25) | collective-permute-done | bytes 737312 | tf_op jit(solution)/shard_map/ppermute | solution.py:704
  216.3 1.6 collective-permute-start.27
  217.9 4.9 %collective-permute-start.31 = (f32[8,5376]{1,0:T(8,128)S(1)}, f32[8,5376]{1,0:T(8,128)S(1)}, u32[]{:S(2)}, u32[]{:S(2)}) collective-permute-start(f32[8,5376]{1,0:T(8,128)S(1)} %constant_dynamic-update-slice_fusion), channel_id=1, source_target_pairs={{0,2},{2,0},{4,6},{6,4},{1,3},{3,1},{5,7},{7,5},{8,10},{10,8},{12,... | collective-permute-start | bytes 516104 | tf_op jit(solution)/shard_map/ppermute | solution.py:689
  222.8 9.2 %input_grad.1 = (bf16[512,768]{1,0:T(8,128)(2,1)S(1)}, bf16[512,768]{1,0:T(8,128)(2,1)S(1)}) custom-call(s32[3]{0:T(128)S(1)} %pad_add_fusion.place_ref, bf16[3,1024,256]{2,1,0:T(8,128)(2,1)S(1)} %get-tuple-element.271.refs_0_, bf16[3,1024,128]{2,1,0:T(8,128)(2,1)S(1)} %get-tuple-element.269.refs_1_, ...), custom_call_target="tpu_custom_call" | custom-call | flops 3600000000 | bytes 3600000 | tf_op jit(solution)/shard_map/input_grad/pallas_call | solution.py:642
  233.1 1.5 collective-permute-start.34
  235.6 10.1 %collective-permute-start.32 = (bf16[3,192,384]{2,1,0:T(8,128)(2,1)}, bf16[3,192,384]{2,1,0:T(8,128)(2,1)}, u32[]{:S(2)}, u32[]{:S(2)}) collective-permute-start(bf16[3,192,384]{2,1,0:T(8,128)(2,1)} %fusion.9), channel_id=1, source_target_pairs={{0,2},{6,4},{1,3},{7,5},{8,10},{14,12},{9,11},{15,13},{16,18},{22,... | collective-permute-start | bytes 1327112 | tf_op jit(solution)/shard_map/ppermute | solution.py:704
  245.8 1.5 add_convert_fusion.1
  247.4 1.3 collective-permute-start.36
  249.3 4.7 %pack_rows.2 = bf16[767,2,512]{2,1,0:T(2,128)(2,1)} custom-call(s32[3]{0:T(128)S(1)} %pad_add_fusion.place_ref, bf16[512,768]{1,0:T(8,128)(2,1)S(1)} %get-tuple-element.305.own_ref, bf16[256,768]{1,0:T(8,128)(2,1)S(1)} %collective-permute-done.14.first_ref, bf16[256,768]{1,0:T(8,128)(2,1)S(1)} %collective-permute-done.16.second_ref), custom_call_target="tpu_custom_call" | custom-call | flops 40000000 | bytes 40000 | tf_op jit(solution)/shard_map/pack_rows/pallas_call | solution.py:673
  254.0 8.6 %collective-permute-done.33 = f32[8,5376]{1,0:T(8,128)S(1)} collective-permute-done((f32[8,5376]{1,0:T(8,128)S(1)}, f32[8,5376]{1,0:T(8,128)S(1)}, u32[]{:S(2)}, u32[]{:S(2)}) %collective-permute-start.33) | collective-permute-done | bytes 172064 | tf_op jit(solution)/shard_map/ppermute | solution.py:689
  262.7 1.3 add_convert_fusion.8
  264.6 1.4 add_convert_fusion.5
  266.0 1.3 collective-permute-start.42
  267.3 3.2 %collective-permute-done.36 = bf16[480,768]{1,0:T(8,128)(2,1)S(1)} collective-permute-done((bf16[480,768]{1,0:T(8,128)(2,1)S(1)}, bf16[480,768]{1,0:T(8,128)(2,1)S(1)}, u32[]{:S(2)}, u32[]{:S(2)}) %collective-permute-start.36) | collective-permute-done | bytes 737312 | tf_op jit(solution)/shard_map/ppermute | solution.py:712
  270.5 1.6 collective-permute-start.37
  274.0 2.0 collective-permute-done.37
  276.8 1.3 collective-permute-start.40
  278.1 4.7 %pack_rows.3 = bf16[767,2,512]{2,1,0:T(2,128)(2,1)} custom-call(s32[3]{0:T(128)S(1)} %pad_add_fusion.place_ref, bf16[512,768]{1,0:T(8,128)(2,1)S(1)} %get-tuple-element.326.own_ref, bf16[512,768]{1,0:T(8,128)(2,1)S(1)} %collective-permute-done.38.first_ref.second_ref, bf16[512,768]{1,0:T(8,128)(2,1)S(1)} %collective-permute-done.38.first_ref.second_ref), custom_call_target="tpu_custom_call" | custom-call | flops 40000000 | bytes 40000 | tf_op jit(solution)/shard_map/pack_rows/pallas_call | solution.py:673
  282.8 1.2 collective-permute-done.42
  286.5 1.1 select_convert_fusion
  287.6 5.5 %collective-permute-done.40 = bf16[3,192,384]{2,1,0:T(8,128)(2,1)S(1)} collective-permute-done((bf16[3,192,384]{2,1,0:T(8,128)(2,1)S(1)}, bf16[3,192,384]{2,1,0:T(8,128)(2,1)S(1)}, u32[]{:S(2)}, u32[]{:S(2)}) %collective-permute-start.40) | collective-permute-done | bytes 442400 | tf_op jit(solution)/shard_map/ppermute | solution.py:712
  (166 shorter events, 28.6 us)
Async XLA Ops:
  0.6 5.6 %copy-start = (s32[2,1024]{1,0:T(2,128)S(1)}, s32[2,1024]{1,0:T(2,128)}, u32[]{:S(2)}) copy-start(s32[2,1024]{1,0:T(2,128)} %param.12) | copy-start | bytes 24580
  1.7 13.3 %collective-permute-start = (bf16[3,192,384]{2,1,0:T(8,128)(2,1)S(1)}, bf16[3,192,384]{2,1,0:T(8,128)(2,1)}, u32[]{:S(2)}, u32[]{:S(2)}) collective-permute-start(bf16[3,192,384]{2,1,0:T(8,128)(2,1)S(1)} %constant_dynamic-slice_fusion.5), channel_id=1, source_target_pairs={{0,1},{1,0},{2,3},{3,2},{4,5},{5,4},{6,7},{7,6},{8,9},{9,8},{10,11... | collective-permute-start | bytes 1327112 | tf_op jit(solution)/shard_map/ppermute | solution.py:689
  7.2 1.4 copy-start.7
  8.6 3.3 %copy-start.24 = (bf16[2,768]{1,0:T(2,128)(2,1)S(1)}, bf16[2,768]{1,0:T(2,128)(2,1)}, u32[]{:S(2)}) copy-start(bf16[2,768]{1,0:T(2,128)(2,1)} %param.13) | copy-start | bytes 9220
  8.6 9.7 %copy-start.20 = (bf16[1536,767]{1,0:T(8,128)(2,1)S(1)}, bf16[1536,767]{1,0:T(8,128)(2,1)}, u32[]{:S(2)}) copy-start(bf16[1536,767]{1,0:T(8,128)(2,1)} %param.19) | copy-start | bytes 7068676
  11.9 8.0 %copy-start.13 = (bf16[512,768]{1,0:T(8,128)(2,1)}, bf16[512,768]{1,0:T(8,128)(2,1)S(1)}, u32[]{:S(2)}) copy-start(bf16[512,768]{1,0:T(8,128)(2,1)S(1)} %get-tuple-element.182.own_ref.refs_1_.refs_3_) | copy-start | bytes 2359300
  15.0 21.0 %collective-permute-start.2 = (bf16[528,768]{1,0:T(8,128)(2,1)S(1)}, bf16[528,768]{1,0:T(8,128)(2,1)S(1)}, u32[]{:S(2)}, u32[]{:S(2)}) collective-permute-start(bf16[528,768]{1,0:T(8,128)(2,1)S(1)} %get-tuple-element.184), channel_id=1, source_target_pairs={{0,1},{1,0},{2,3},{3,2},{4,5},{5,4},{6,7},{7,6},{8,9},{9,8},{10,11... | collective-permute-start | bytes 2433032 | tf_op jit(solution)/shard_map/ppermute | solution.py:689
  16.8 6.6 %collective-permute-start.3 = (bf16[3,192,384]{2,1,0:T(8,128)(2,1)}, bf16[3,192,384]{2,1,0:T(8,128)(2,1)S(1)}, u32[]{:S(2)}, u32[]{:S(2)}) collective-permute-start(bf16[3,192,384]{2,1,0:T(8,128)(2,1)} %collective-permute-done.a.refs_1_.refs_8_), channel_id=1, source_target_pairs={{0,8},{8,0},{16,24},{24,16},{1,9},{9,1},{17,25},{25,17},{2,10},{10... | collective-permute-start | bytes 1327112 | tf_op jit(solution)/shard_map/ppermute | solution.py:689
  16.8 13.6 %collective-permute-start.1 = (bf16[3,192,384]{2,1,0:T(8,128)(2,1)}, bf16[3,192,384]{2,1,0:T(8,128)(2,1)}, u32[]{:S(2)}, u32[]{:S(2)}) collective-permute-start(bf16[3,192,384]{2,1,0:T(8,128)(2,1)} %collective-permute-done.a.refs_1_.refs_8_), channel_id=1, source_target_pairs={{0,16},{8,24},{16,0},{24,8},{1,17},{9,25},{17,1},{25,9},{2,18},{10... | collective-permute-start | bytes 1327112 | tf_op jit(solution)/shard_map/ppermute | solution.py:689
  20.0 1.2 copy-start.22
  21.2 5.0 %copy-start.8 = (bf16[2,512,767]{1,0,2:T(2,128)(2,1)S(1)}, bf16[2,512,767]{1,0,2:T(2,128)(2,1)}, u32[]{:S(2)}) copy-start(bf16[2,512,767]{1,0,2:T(2,128)(2,1)} %param.21) | copy-start | bytes 4712452
  24.2 40.4 %collective-permute-start.5 = (bf16[480,768]{1,0:T(8,128)(2,1)}, bf16[480,768]{1,0:T(8,128)(2,1)}, u32[]{:S(2)}, u32[]{:S(2)}) collective-permute-start(bf16[480,768]{1,0:T(8,128)(2,1)} %fusion.12), channel_id=1, source_target_pairs={{0,1},{1,0},{2,3},{3,2},{4,5},{5,4},{6,7},{7,6},{8,9},{9,8},{10,11... | collective-permute-start | bytes 2211848 | tf_op jit(solution)/shard_map/ppermute | solution.py:689
  24.7 39.9 %collective-permute-start.6 = (bf16[384,768]{1,0:T(8,128)(2,1)}, bf16[384,768]{1,0:T(8,128)(2,1)}, u32[]{:S(2)}, u32[]{:S(2)}) collective-permute-start(bf16[384,768]{1,0:T(8,128)(2,1)} %pad.22), channel_id=1, source_target_pairs={{0,1},{1,0},{2,3},{3,2},{4,5},{5,4},{6,7},{7,6},{8,9},{9,8},{10,11... | collective-permute-start | bytes 1769480 | tf_op jit(solution)/shard_map/ppermute | solution.py:689
  26.2 12.0 %copy-start.2 = (bf16[3,768,384]{2,1,0:T(8,128)(2,1)S(1)}, bf16[3,768,384]{2,1,0:T(8,128)(2,1)}, u32[]{:S(2)}) copy-start(bf16[3,768,384]{2,1,0:T(8,128)(2,1)} %refs_7_.1) | copy-start | bytes 5308420
  36.0 2.1 collective-permute-start.4
  49.3 30.6 %collective-permute-start.9 = (bf16[512,768]{1,0:T(8,128)(2,1)S(1)}, bf16[512,768]{1,0:T(8,128)(2,1)S(1)}, u32[]{:S(2)}, u32[]{:S(2)}) collective-permute-start(bf16[512,768]{1,0:T(8,128)(2,1)S(1)} %get-tuple-element.209), channel_id=1, source_target_pairs={{0,1},{1,0},{2,3},{3,2},{4,5},{5,4},{6,7},{7,6},{8,9},{9,8},{10,11... | collective-permute-start | bytes 2359304 | tf_op jit(solution)/shard_map/ppermute | solution.py:689
  64.6 15.8 %copy-start.26 = (bf16[2,767]{1,0:T(2,128)(2,1)S(1)}, bf16[2,767]{1,0:T(2,128)(2,1)}, u32[]{:S(2)}) copy-start(bf16[2,767]{1,0:T(2,128)(2,1)} %param.20) | copy-start | bytes 9208
  64.6 15.8 %copy-start.25 = (bf16[1536]{0:T(1024)(128)(2,1)S(1)}, bf16[1536]{0:T(1024)(128)(2,1)}, u32[]{:S(2)}) copy-start(bf16[1536]{0:T(1024)(128)(2,1)} %param.18) | copy-start | bytes 9220
  64.6 19.2 %copy-start.6 = (bf16[528,768]{1,0:T(8,128)(2,1)S(1)}, bf16[528,768]{1,0:T(8,128)(2,1)}, u32[]{:S(2)}) copy-start(bf16[528,768]{1,0:T(8,128)(2,1)} %copy-done.4) | copy-start | bytes 2433028
  64.6 19.2 %copy-start.15 = (bf16[512,768]{1,0:T(8,128)(2,1)S(1)}, bf16[512,768]{1,0:T(8,128)(2,1)}, u32[]{:S(2)}) copy-start(bf16[512,768]{1,0:T(8,128)(2,1)} %copy-done.13) | copy-start | bytes 2359300
  64.6 19.2 %copy-start.18 = (bf16[512,768]{1,0:T(8,128)(2,1)S(1)}, bf16[512,768]{1,0:T(8,128)(2,1)}, u32[]{:S(2)}) copy-start(bf16[512,768]{1,0:T(8,128)(2,1)} %copy-done.17) | copy-start | bytes 2359300
  64.6 15.3 %collective-permute-start.7 = (bf16[480,768]{1,0:T(8,128)(2,1)}, bf16[480,768]{1,0:T(8,128)(2,1)S(1)}, u32[]{:S(2)}, u32[]{:S(2)}) collective-permute-start(bf16[480,768]{1,0:T(8,128)(2,1)} %collective-permute-done.5.refs_11_), channel_id=1, source_target_pairs={{0,16},{8,24},{16,0},{24,8},{1,17},{9,25},{17,1},{25,9},{2,18},{10... | collective-permute-start | bytes 2211848 | tf_op jit(solution)/shard_map/ppermute | solution.py:689
  66.4 11.1 %collective-permute-start.8 = (bf16[384,768]{1,0:T(8,128)(2,1)}, bf16[384,768]{1,0:T(8,128)(2,1)S(1)}, u32[]{:S(2)}, u32[]{:S(2)}) collective-permute-start(bf16[384,768]{1,0:T(8,128)(2,1)} %collective-permute-done.6.refs_15_), channel_id=1, source_target_pairs={{0,2},{2,0},{4,6},{6,4},{1,3},{3,1},{5,7},{7,5},{8,10},{10,8},{12,... | collective-permute-start | bytes 1769480 | tf_op jit(solution)/shard_map/ppermute | solution.py:689
  68.0 15.7 %collective-permute-start.10 = (bf16[480,768]{1,0:T(8,128)(2,1)}, bf16[480,768]{1,0:T(8,128)(2,1)S(1)}, u32[]{:S(2)}, u32[]{:S(2)}) collective-permute-start(bf16[480,768]{1,0:T(8,128)(2,1)} %collective-permute-done.5.refs_11_), channel_id=1, source_target_pairs={{0,8},{8,0},{16,24},{24,16},{1,9},{9,1},{17,25},{25,17},{2,10},{10... | collective-permute-start | bytes 2211848 | tf_op jit(solution)/shard_map/ppermute | solution.py:689
  79.9 3.9 %collective-permute-start.11 = (bf16[480,768]{1,0:T(8,128)(2,1)S(1)}, bf16[480,768]{1,0:T(8,128)(2,1)S(1)}, u32[]{:S(2)}, u32[]{:S(2)}) collective-permute-start(bf16[480,768]{1,0:T(8,128)(2,1)S(1)} %collective-permute-done.7.refs_13_), channel_id=1, source_target_pairs={{0,8},{8,0},{16,24},{24,16},{1,9},{9,1},{17,25},{25,17},{2,10},{10... | collective-permute-start | bytes 2211848 | tf_op jit(solution)/shard_map/ppermute | solution.py:689
  79.9 3.7 %collective-permute-start.12 = (bf16[384,768]{1,0:T(8,128)(2,1)}, bf16[384,768]{1,0:T(8,128)(2,1)S(1)}, u32[]{:S(2)}, u32[]{:S(2)}) collective-permute-start(bf16[384,768]{1,0:T(8,128)(2,1)} %collective-permute-done.6.refs_15_), channel_id=1, source_target_pairs={{0,8},{8,0},{16,24},{24,16},{1,9},{9,1},{17,25},{25,17},{2,10},{10... | collective-permute-start | bytes 1769480 | tf_op jit(solution)/shard_map/ppermute | solution.py:689
  80.4 3.4 %collective-permute-start.13 = (bf16[384,768]{1,0:T(8,128)(2,1)S(1)}, bf16[384,768]{1,0:T(8,128)(2,1)S(1)}, u32[]{:S(2)}, u32[]{:S(2)}) collective-permute-start(bf16[384,768]{1,0:T(8,128)(2,1)S(1)} %collective-permute-done.8.refs_17_), channel_id=1, source_target_pairs={{0,8},{8,0},{16,24},{24,16},{1,9},{9,1},{17,25},{25,17},{2,10},{10... | collective-permute-start | bytes 1769480 | tf_op jit(solution)/shard_map/ppermute | solution.py:689
  119.1 12.3 %collective-permute-start.14 = (bf16[256,768]{1,0:T(8,128)(2,1)S(1)}, bf16[256,768]{1,0:T(8,128)(2,1)S(1)}, u32[]{:S(2)}, u32[]{:S(2)}) collective-permute-start(bf16[256,768]{1,0:T(8,128)(2,1)S(1)} %get-tuple-element.224), channel_id=1, source_target_pairs={{0,1},{1,0},{2,3},{3,2},{4,5},{5,4},{6,7},{7,6},{8,9},{9,8},{10,11... | collective-permute-start | bytes 1179656 | tf_op jit(solution)/shard_map/ppermute | solution.py:689
  120.2 2.8 copy-start.16
  123.0 9.5 %copy-start.19 = (bf16[1024,3072]{1,0:T(8,128)(2,1)S(1)}, bf16[1024,3072]{1,0:T(8,128)(2,1)}, u32[]{:S(2)}) copy-start(bf16[1024,3072]{1,0:T(8,128)(2,1)} %get-tuple-element.228.right_ref) | copy-start | bytes 18874372
  131.4 11.6 %collective-permute-start.15 = (bf16[2,2,480,768]{3,2,1,0:T(8,128)(2,1)S(1)}, bf16[2,2,480,768]{3,2,1,0:T(8,128)(2,1)S(1)}, u32[]{:S(2)}, u32[]{:S(2)}) collective-permute-start(bf16[2,2,480,768]{3,2,1,0:T(8,128)(2,1)S(1)} %get-tuple-element.231), channel_id=1, source_target_pairs={{0,8},{8,0},{16,24},{24,16},{1,9},{9,1},{17,25},{25,17},{2,10},{10... | collective-permute-start | bytes 8847368 | tf_op jit(solution)/shard_map/ppermute | solution.py:689
  131.4 11.5 %collective-permute-start.16 = (bf16[256,768]{1,0:T(8,128)(2,1)S(1)}, bf16[256,768]{1,0:T(8,128)(2,1)S(1)}, u32[]{:S(2)}, u32[]{:S(2)}) collective-permute-start(bf16[256,768]{1,0:T(8,128)(2,1)S(1)} %get-tuple-element.233), channel_id=1, source_target_pairs={{0,1},{1,0},{2,3},{3,2},{4,5},{5,4},{6,7},{7,6},{8,9},{9,8},{10,11... | collective-permute-start | bytes 1179656 | tf_op jit(solution)/shard_map/ppermute | solution.py:689
  143.0 4.5 %collective-permute-start.17 = (bf16[2,2,192,1536]{3,2,1,0:T(8,128)(2,1)S(1)}, bf16[2,2,192,1536]{3,2,1,0:T(8,128)(2,1)S(1)}, u32[]{:S(2)}, u32[]{:S(2)}) collective-permute-start(bf16[2,2,192,1536]{3,2,1,0:T(8,128)(2,1)S(1)} %get-tuple-element.235), channel_id=1, source_target_pairs={{0,8},{8,0},{16,24},{24,16},{1,9},{9,1},{17,25},{25,17},{2,10},{10... | collective-permute-start | bytes 7077896 | tf_op jit(solution)/shard_map/ppermute | solution.py:689
  143.2 22.9 %collective-permute-start.18 = (bf16[480,768]{1,0:T(8,128)(2,1)S(1)}, bf16[480,768]{1,0:T(8,128)(2,1)S(1)}, u32[]{:S(2)}, u32[]{:S(2)}) collective-permute-start(bf16[480,768]{1,0:T(8,128)(2,1)S(1)} %fusion.13), channel_id=1, source_target_pairs={{0,16},{8,24},{16,0},{24,8},{1,17},{9,25},{17,1},{25,9},{2,18},{10... | collective-permute-start | bytes 2211848 | tf_op jit(solution)/shard_map/ppermute | solution.py:689
  144.9 45.0 %collective-permute-start.21 = (bf16[480,768]{1,0:T(8,128)(2,1)S(1)}, bf16[480,768]{1,0:T(8,128)(2,1)S(1)}, u32[]{:S(2)}, u32[]{:S(2)}) collective-permute-start(bf16[480,768]{1,0:T(8,128)(2,1)S(1)} %fusion.14), channel_id=1, source_target_pairs={{0,16},{8,24},{16,0},{24,8},{1,17},{9,25},{17,1},{25,9},{2,18},{10... | collective-permute-start | bytes 2211848 | tf_op jit(solution)/shard_map/ppermute | solution.py:689
  147.8 28.9 %collective-permute-start.19 = (bf16[2,192,1536]{2,1,0:T(8,128)(2,1)S(1)}, bf16[2,192,1536]{2,1,0:T(8,128)(2,1)S(1)}, u32[]{:S(2)}, u32[]{:S(2)}) collective-permute-start(bf16[2,192,1536]{2,1,0:T(8,128)(2,1)S(1)} %fusion.4), channel_id=1, source_target_pairs={{0,1},{1,0},{2,3},{3,2},{4,5},{5,4},{6,7},{7,6},{8,9},{9,8},{10,11... | collective-permute-start | bytes 3538952 | tf_op jit(solution)/shard_map/ppermute | solution.py:689
  166.1 1.4 copy-start.11
  166.4 25.3 %collective-permute-start.20 = (bf16[480,768]{1,0:T(8,128)(2,1)S(1)}, bf16[480,768]{1,0:T(8,128)(2,1)S(1)}, u32[]{:S(2)}, u32[]{:S(2)}) collective-permute-start(bf16[480,768]{1,0:T(8,128)(2,1)S(1)} %fusion.2), channel_id=1, source_target_pairs={{0,1},{1,0},{2,3},{3,2},{4,5},{5,4},{6,7},{7,6},{8,9},{9,8},{10,11... | collective-permute-start | bytes 2211848 | tf_op jit(solution)/shard_map/ppermute | solution.py:689
  176.7 16.0 %collective-permute-start.23 = (bf16[2,3,192,384]{3,2,1,0:T(8,128)(2,1)S(1)}, bf16[2,3,192,384]{3,2,1,0:T(8,128)(2,1)S(1)}, u32[]{:S(2)}, u32[]{:S(2)}) collective-permute-start(bf16[2,3,192,384]{3,2,1,0:T(8,128)(2,1)S(1)} %get-tuple-element.260), channel_id=1, source_target_pairs={{0,8},{8,0},{16,24},{24,16},{1,9},{9,1},{17,25},{25,17},{2,10},{10... | collective-permute-start | bytes 2654216 | tf_op jit(solution)/shard_map/ppermute | solution.py:689
  176.9 15.8 %collective-permute-start.22 = (bf16[192,1536]{1,0:T(8,128)(2,1)S(1)}, bf16[192,1536]{1,0:T(8,128)(2,1)S(1)}, u32[]{:S(2)}, u32[]{:S(2)}) collective-permute-start(bf16[192,1536]{1,0:T(8,128)(2,1)S(1)} %fusion.7), channel_id=1, source_target_pairs={{0,16},{8,24},{16,0},{24,8},{1,17},{9,25},{17,1},{25,9},{2,18},{10... | collective-permute-start | bytes 1769480 | tf_op jit(solution)/shard_map/ppermute | solution.py:689
  193.4 20.4 %collective-permute-start.25 = (bf16[480,768]{1,0:T(8,128)(2,1)S(1)}, bf16[480,768]{1,0:T(8,128)(2,1)S(1)}, u32[]{:S(2)}, u32[]{:S(2)}) collective-permute-start(bf16[480,768]{1,0:T(8,128)(2,1)S(1)} %fusion.1), channel_id=1, source_target_pairs={{0,2},{6,4},{1,3},{7,5},{8,10},{14,12},{9,11},{15,13},{16,18},{22,... | collective-permute-start | bytes 2211848 | tf_op jit(solution)/shard_map/ppermute | solution.py:704
  197.0 8.8 %copy-start.3 = (bf16[3,768,384]{2,1,0:T(8,128)(2,1)S(1)}, bf16[3,768,384]{2,1,0:T(8,128)(2,1)}, u32[]{:S(2)}) copy-start(bf16[3,768,384]{2,1,0:T(8,128)(2,1)} %refs_7_.1) | copy-start | bytes 5308420
  197.1 11.8 %collective-permute-start.24 = (bf16[3,192,384]{2,1,0:T(8,128)(2,1)S(1)}, bf16[3,192,384]{2,1,0:T(8,128)(2,1)S(1)}, u32[]{:S(2)}, u32[]{:S(2)}) collective-permute-start(bf16[3,192,384]{2,1,0:T(8,128)(2,1)S(1)} %fusion.15), channel_id=1, source_target_pairs={{0,16},{8,24},{16,0},{24,8},{1,17},{9,25},{17,1},{25,9},{2,18},{10... | collective-permute-start | bytes 1327112 | tf_op jit(solution)/shard_map/ppermute | solution.py:689
  198.6 33.4 %collective-permute-start.30 = (bf16[192,1536]{1,0:T(8,128)(2,1)S(1)}, bf16[192,1536]{1,0:T(8,128)(2,1)S(1)}, u32[]{:S(2)}, u32[]{:S(2)}) collective-permute-start(bf16[192,1536]{1,0:T(8,128)(2,1)S(1)} %fusion.6), channel_id=1, source_target_pairs={{0,2},{6,4},{1,3},{7,5},{8,10},{14,12},{9,11},{15,13},{16,18},{22,... | collective-permute-start | bytes 1769480 | tf_op jit(solution)/shard_map/ppermute | solution.py:704
  213.8 2.4 collective-permute-start.26
  214.0 2.4 copy-start.21
  214.0 8.8 %copy-start.12 = (f32[1024,768]{1,0:T(8,128)S(1)}, f32[1024,768]{1,0:T(8,128)}, u32[]{:S(2)}) copy-start(f32[1024,768]{1,0:T(8,128)} %get-tuple-element.285.refs_5_) | copy-start | bytes 9437188
  214.0 18.1 %collective-permute-start.29 = (bf16[480,768]{1,0:T(8,128)(2,1)S(1)}, bf16[480,768]{1,0:T(8,128)(2,1)S(1)}, u32[]{:S(2)}, u32[]{:S(2)}) collective-permute-start(bf16[480,768]{1,0:T(8,128)(2,1)S(1)} %add_convert_fusion.2), channel_id=1, source_target_pairs={{2,4},{4,2},{3,5},{5,3},{10,12},{12,10},{11,13},{13,11},{18,20},{2... | collective-permute-start | bytes 2211848 | tf_op jit(solution)/shard_map/ppermute | solution.py:708
  215.0 17.1 %collective-permute-start.28 = (bf16[3,192,384]{2,1,0:T(8,128)(2,1)S(1)}, bf16[3,192,384]{2,1,0:T(8,128)(2,1)S(1)}, u32[]{:S(2)}, u32[]{:S(2)}) collective-permute-start(bf16[3,192,384]{2,1,0:T(8,128)(2,1)S(1)} %fusion.10), channel_id=1, source_target_pairs={{0,1},{1,0},{2,3},{3,2},{4,5},{5,4},{6,7},{7,6},{8,9},{9,8},{10,11... | collective-permute-start | bytes 1327112 | tf_op jit(solution)/shard_map/ppermute | solution.py:689
  216.3 15.8 %collective-permute-start.27 = (bf16[3,192,384]{2,1,0:T(8,128)(2,1)S(1)}, bf16[3,192,384]{2,1,0:T(8,128)(2,1)S(1)}, u32[]{:S(2)}, u32[]{:S(2)}) collective-permute-start(bf16[3,192,384]{2,1,0:T(8,128)(2,1)S(1)} %fusion.16), channel_id=1, source_target_pairs={{0,16},{8,24},{16,0},{24,8},{1,17},{9,25},{17,1},{25,9},{2,18},{10... | collective-permute-start | bytes 1327112 | tf_op jit(solution)/shard_map/ppermute | solution.py:689
  217.9 14.2 %collective-permute-start.31 = (f32[8,5376]{1,0:T(8,128)S(1)}, f32[8,5376]{1,0:T(8,128)S(1)}, u32[]{:S(2)}, u32[]{:S(2)}) collective-permute-start(f32[8,5376]{1,0:T(8,128)S(1)} %constant_dynamic-update-slice_fusion), channel_id=1, source_target_pairs={{0,2},{2,0},{4,6},{6,4},{1,3},{3,1},{5,7},{7,5},{8,10},{10,8},{12,... | collective-permute-start | bytes 516104 | tf_op jit(solution)/shard_map/ppermute | solution.py:689
  232.1 3.6 %copy-start.23 = (bf16[480,768]{1,0:T(8,128)(2,1)}, bf16[480,768]{1,0:T(8,128)(2,1)S(1)}, u32[]{:S(2)}) copy-start(bf16[480,768]{1,0:T(8,128)(2,1)S(1)} %collective-permute-done.29) | copy-start | bytes 2211844
  233.1 29.4 %collective-permute-start.34 = (bf16[192,1536]{1,0:T(8,128)(2,1)}, bf16[192,1536]{1,0:T(8,128)(2,1)}, u32[]{:S(2)}, u32[]{:S(2)}) collective-permute-start(bf16[192,1536]{1,0:T(8,128)(2,1)} %add_convert_fusion.6), channel_id=1, source_target_pairs={{2,4},{4,2},{3,5},{5,3},{10,12},{12,10},{11,13},{13,11},{18,20},{2... | collective-permute-start | bytes 1769480 | tf_op jit(solution)/shard_map/ppermute | solution.py:708
  235.6 26.9 %collective-permute-start.32 = (bf16[3,192,384]{2,1,0:T(8,128)(2,1)}, bf16[3,192,384]{2,1,0:T(8,128)(2,1)}, u32[]{:S(2)}, u32[]{:S(2)}) collective-permute-start(bf16[3,192,384]{2,1,0:T(8,128)(2,1)} %fusion.9), channel_id=1, source_target_pairs={{0,2},{6,4},{1,3},{7,5},{8,10},{14,12},{9,11},{15,13},{16,18},{22,... | collective-permute-start | bytes 1327112 | tf_op jit(solution)/shard_map/ppermute | solution.py:704
  245.8 16.8 %collective-permute-start.33 = (f32[8,5376]{1,0:T(8,128)S(1)}, f32[8,5376]{1,0:T(8,128)S(1)}, u32[]{:S(2)}, u32[]{:S(2)}) collective-permute-start(f32[8,5376]{1,0:T(8,128)S(1)} %add.190), channel_id=1, source_target_pairs={{0,4},{2,6},{4,0},{6,2},{1,5},{3,7},{5,1},{7,3},{8,12},{10,14},{12... | collective-permute-start | bytes 516104 | tf_op jit(solution)/shard_map/ppermute | solution.py:689
  247.4 23.1 %collective-permute-start.36 = (bf16[480,768]{1,0:T(8,128)(2,1)S(1)}, bf16[480,768]{1,0:T(8,128)(2,1)S(1)}, u32[]{:S(2)}, u32[]{:S(2)}) collective-permute-start(bf16[480,768]{1,0:T(8,128)(2,1)S(1)} %add_convert_fusion.1), channel_id=1, source_target_pairs={{2,0},{4,6},{3,1},{5,7},{10,8},{12,14},{11,9},{13,15},{18,16},{20,... | collective-permute-start | bytes 2211848 | tf_op jit(solution)/shard_map/ppermute | solution.py:712
  248.7 25.3 %collective-permute-start.38 = (bf16[512,768]{1,0:T(8,128)(2,1)S(1)}, bf16[512,768]{1,0:T(8,128)(2,1)S(1)}, u32[]{:S(2)}, u32[]{:S(2)}) collective-permute-start(bf16[512,768]{1,0:T(8,128)(2,1)S(1)} %get-tuple-element.318), channel_id=1, source_target_pairs={{0,1},{1,0},{2,3},{3,2},{4,5},{5,4},{6,7},{7,6},{8,9},{9,8},{10,11... | collective-permute-start | bytes 2359304 | tf_op jit(solution)/shard_map/ppermute | solution.py:689
  262.6 7.9 %collective-permute-start.35 = (f32[8,5376]{1,0:T(8,128)S(1)}, f32[8,5376]{1,0:T(8,128)S(1)}, u32[]{:S(2)}, u32[]{:S(2)}) collective-permute-start(f32[8,5376]{1,0:T(8,128)S(1)} %add.191), channel_id=1, source_target_pairs={{0,8},{8,0},{16,24},{24,16},{1,9},{9,1},{17,25},{25,17},{2,10},{10... | collective-permute-start | bytes 516104 | tf_op jit(solution)/shard_map/ppermute | solution.py:689
  263.9 12.1 %collective-permute-start.39 = (bf16[3,192,384]{2,1,0:T(8,128)(2,1)S(1)}, bf16[3,192,384]{2,1,0:T(8,128)(2,1)S(1)}, u32[]{:S(2)}, u32[]{:S(2)}) collective-permute-start(bf16[3,192,384]{2,1,0:T(8,128)(2,1)S(1)} %add_convert_fusion.8), channel_id=1, source_target_pairs={{2,4},{4,2},{3,5},{5,3},{10,12},{12,10},{11,13},{13,11},{18,20},{2... | collective-permute-start | bytes 1327112 | tf_op jit(solution)/shard_map/ppermute | solution.py:708
  266.0 18.0 %collective-permute-start.42 = (bf16[192,1536]{1,0:T(8,128)(2,1)S(1)}, bf16[192,1536]{1,0:T(8,128)(2,1)S(1)}, u32[]{:S(2)}, u32[]{:S(2)}) collective-permute-start(bf16[192,1536]{1,0:T(8,128)(2,1)S(1)} %add_convert_fusion.5), channel_id=1, source_target_pairs={{2,0},{4,6},{3,1},{5,7},{10,8},{12,14},{11,9},{13,15},{18,16},{20,... | collective-permute-start | bytes 1769480 | tf_op jit(solution)/shard_map/ppermute | solution.py:712
  270.5 5.5 %collective-permute-start.37 = (f32[8,5376]{1,0:T(8,128)S(1)}, f32[8,5376]{1,0:T(8,128)S(1)}, u32[]{:S(2)}, u32[]{:S(2)}) collective-permute-start(f32[8,5376]{1,0:T(8,128)S(1)} %add.194), channel_id=1, source_target_pairs={{0,16},{8,24},{16,0},{24,8},{1,17},{9,25},{17,1},{25,9},{2,18},{10... | collective-permute-start | bytes 516104 | tf_op jit(solution)/shard_map/ppermute | solution.py:689
  276.1 6.8 %collective-permute-start.41 = (f32[8,3456]{1,0:T(8,128)S(1)}, f32[8,3456]{1,0:T(8,128)S(1)}, u32[]{:S(2)}, u32[]{:S(2)}) collective-permute-start(f32[8,3456]{1,0:T(8,128)S(1)} %pad_maximum_fusion.1), channel_id=1, source_target_pairs={{0,1},{1,0},{2,3},{3,2},{4,5},{5,4},{6,7},{7,6},{8,9},{9,8},{10,11... | collective-permute-start | bytes 331784 | tf_op jit(solution)/shard_map/ppermute | solution.py:689
  276.8 16.3 %collective-permute-start.40 = (bf16[3,192,384]{2,1,0:T(8,128)(2,1)S(1)}, bf16[3,192,384]{2,1,0:T(8,128)(2,1)S(1)}, u32[]{:S(2)}, u32[]{:S(2)}) collective-permute-start(bf16[3,192,384]{2,1,0:T(8,128)(2,1)S(1)} %add_convert_fusion.7), channel_id=1, source_target_pairs={{2,0},{4,6},{3,1},{5,7},{10,8},{12,14},{11,9},{13,15},{18,16},{20,... | collective-permute-start | bytes 1327112 | tf_op jit(solution)/shard_map/ppermute | solution.py:712
  286.5 7.6 %copy-start.1 = (s32[2,1024]{1,0:T(2,128)S(1)}, s32[2,1024]{1,0:T(2,128)}, u32[]{:S(2)}) copy-start(s32[2,1024]{1,0:T(2,128)} %param.12) | copy-start | bytes 24580
  (6 other events, 5.8 us)

commit v6 on v5

--- a/solution.py
+++ b/solution.py
@@ -829,62 +829,67 @@
         qo_x = x_swap(qo_f)
         own_b, sums_b = backward(after(attended_grad, qo_f, proj_shard, fc_shard), log_sums, pairs - 1, 1)
         qm_k, qm_s, qm_sum = qkv_grad(after(place, own_b), normed_one, [own_a, own_b], [qkv_weight])
-        qm_k, qm_s, qm_sum, qo_k, qo_c, qo_x, proj_shard, proj_z = meet(
-            qm_k, qm_s, qm_sum, qo_k, qo_c, qo_x, proj_shard, proj_z)
+        qm_k, qm_s, qm_sum, qo_k, qo_c, qo_x = meet(qm_k, qm_s, qm_sum, qo_k, qo_c, qo_x)
         qm_c = c_swap(qm_s)
         in_sums = (qm_sum + qo_sum) / gains[0:1]
         small = jnp.concatenate([in_sums, middle_sums, own_sums, other_sums, sums_a, sums_b, first_sums], 1)
-        small_z = z_swap(small)
+        small_c = c_swap(small)
         qo_r = add_low(qo_k[0], qo_c[0], qo_x)
         qo_y = y_swap(qo_r)
+        qm_k, qm_c, qo_r, small, small_c = meet(qm_k, qm_c, qo_r, small, small_c)
+        small = small + small_c
+        small_x = x_swap(small)
+        qm_f = add_low(after(qm_k, small)[1], qm_c[1])
+        qm_x = x_swap(qm_f)
+        qm_f, proj_shard, proj_z = meet(qm_f, proj_shard, proj_z)
         proj_shard = add_low(proj_shard, proj_z)
         proj_z = chain_across(proj_shard)
-        qm_k, qm_c, qo_r, proj_shard = meet(qm_k, qm_c, qo_r, proj_shard)
-        qm_f = add_low(qm_k[1], qm_c[1])
-        qm_x = x_swap(qm_f)
-        in_mine, in_send = input_grad(
-            after(place, qm_f), [own_a, own_b], [first], res_own, res_other, middle_grad, gains[0:1],
-            qkv_weight, qkv_others)
-        in_mine, in_send, qm_x, qo_y, proj_shard, proj_z, fc_shard, fc_z, small, small_z = meet(
-            in_mine, in_send, qm_x, qo_y, proj_shard, proj_z, fc_shard, fc_z, small, small_z)
-        small = small + small_z
-        small_z = swap(small, "group", 2, n_group)
-        last = add_low(qm_k[0], qm_c[0], qm_x, qo_y)
-        last_z = chain_in(last)
+        block_out = restore(after(out_mine, proj_shard), *out_got)
+        block_out, fc_shard, fc_z, small, small_x = meet(block_out, fc_shard, fc_z, small, small_x)
         fc_shard = add_low(fc_shard, fc_z)
         fc_z = chain_across(fc_shard)
-        proj_shard = add_low(proj_shard, proj_z)
-        proj_z = chain_out(proj_shard)
-        in_got = y_swap(in_send)
-        block_out = restore(after(out_mine, last, proj_shard, fc_shard, small), *out_got)
-        last, last_z, block_out, small, small_z, fc_shard, fc_z = meet(
-            last, last_z, block_out, small, small_z, fc_shard, fc_z)
-        small = small + small_z
-        small_c = c_swap(small)
-        last = add_low(last, last_z)
-        last_z = chain_across(last)
-        fc_shard = add_low(fc_shard, fc_z)
-        fc_z = chain_out(fc_shard)
-        middle_one = (group_at == 1) | (group_at == 2)
-        small, small_c, last, fc_shard, proj_shard, proj_z = meet(small, small_c, last, fc_shard, proj_shard, proj_z)
-        small = small + small_c
-        small_x = x_swap(small)
-        proj_shard = jnp.where(middle_one, proj_shard, proj_z)
-        out_shard = proj_shard[hid // 4 :, : D - 1].astype(F32)
-        proj_shard = proj_shard[: hid // 4, : D - 1].astype(F32)
-        small, small_x, in_mine, in_got, last, last_z, fc_shard, proj_shard, out_shard = meet(
-            small, small_x, in_mine, in_got, last, last_z, fc_shard, proj_shard, out_shard)
-        last = add_low(last, last_z)
-        last_z = chain_out(last)
         small = small + small_x
         split = 2 * D + hid
         mine = jnp.concatenate([small[:, :split], small[:, split + hid : split + hid + half]], 1)
         other = jnp.concatenate([small[:, : 2 * D], small[:, split : split + hid], small[:, split + hid + half :]], 1)
         small_y = y_swap(other)
-        in_out = restore(after(in_mine, last), in_got, in_got)
-        in_out, mine, small_y, fc_shard, fc_z = meet(in_out, mine, small_y, fc_shard, fc_z)
-        small = small_outputs(mine + small_y)
+        qm_k, qm_c, qm_x, qo_y, fc_shard, mine, small_y, proj_shard, proj_z = meet(
+            qm_k, qm_c, qm_x, qo_y, fc_shard, mine, small_y, proj_shard, proj_z)
+        last = add_low(qm_k[0], qm_c[0], qm_x, qo_y)
+        last_z = chain_in(last)
+        small = mine + small_y
+        small_z = chain_in(small)
+        proj_shard = add_low(after(proj_shard, last, small), proj_z)
+        proj_z = chain_out(proj_shard)
+        in_mine, in_send = input_grad(
+            after(place, last, proj_shard, small), [own_a, own_b], [first], res_own, res_other, middle_grad,
+            gains[0:1], qkv_weight, qkv_others)
+        in_mine, in_send, last, last_z, fc_shard, fc_z, small, small_z = meet(
+            in_mine, in_send, last, last_z, fc_shard, fc_z, small, small_z)
+        last = add_low(last, last_z)
+        last_z = chain_across(last)
+        small = small + small_z
+        small_z = chain_across(small)
+        fc_shard = add_low(after(fc_shard, last, small), fc_z)
+        fc_z = chain_out(fc_shard)
+        in_got = y_swap(in_send)
+        middle_one = (group_at == 1) | (group_at == 2)
+        small, last, fc_shard, proj_shard, proj_z = meet(small, last, fc_shard, proj_shard, proj_z)
+        proj_shard = jnp.where(middle_one, proj_shard, proj_z)
+        out_shard = proj_shard[hid // 4 :, : D - 1].astype(F32)
+        proj_shard = proj_shard[: hid // 4, : D - 1].astype(F32)
+        small, small_z, last, last_z, proj_shard, out_shard = meet(
+            small, small_z, last, last_z, proj_shard, out_shard)
+        last = add_low(last, last_z)
+        last_z = chain_out(last)
+        small = small + small_z
+        small_z = chain_out(small)
+        in_mine, in_got, last, small = meet(in_mine, in_got, last, small)
+        in_out = restore(in_mine, in_got, in_got)
+        in_out, fc_shard, fc_z = meet(in_out, fc_shard, fc_z)
         fc_shard = jnp.where(middle_one, fc_shard, fc_z).astype(F32)
+        fc_shard, small, small_z = meet(fc_shard, small, small_z)
+        small = small_outputs(jnp.where(middle_one, small, small_z))
         last, last_z, in_out, proj_shard, out_shard, fc_shard, *small = meet(
             last, last_z, in_out, proj_shard, out_shard, fc_shard, *small)
         qkv_shard = jnp.where(middle_one, last, last_z)

time: 300 us -> 295 us (0.983)
  waiting for transfers between devices: 58.2 us -> 49.7 us
  starting transfers between devices: 55.7 us -> 50.5 us
  local copies, waits for them, and re-layouts: 18.8 us -> 24 us
  other arithmetic: 15.2 us -> 18.5 us
    ppermute x34 -> x32, waiting for transfers between devices: 43.4 us -> 36.2 us  [swap(): return lax.ppermute(value, axis, [(n, n ^ bit) for n in range(size)])]
    ppermute x34 -> x32, starting transfers between devices: 33.6 us -> 27.1 us  [swap(): return lax.ppermute(value, axis, [(n, n ^ bit) for n in range(size)])]
    unnamed x62 -> x100, local copies, waits for them, and re-layouts: 11.1 us -> 16.3 us
    ppermute x3 -> x4, waiting for transfers between devices: 9.89 us -> 6.43 us  [chain_out(): return lax.ppermute(value, 'group', [(1, 0), (2, 3)])]
    convert_element_type x17, other arithmetic: 8.65 us -> 12 us  [add_low(): return total.astype(BF16)]
    ppermute x3 -> x4, waiting for transfers between devices: 4.91 us -> 6.99 us  [chain_in(): return lax.ppermute(value, 'group', [(0, 1), (3, 2)])]
    ppermute x3 -> x4, starting transfers between devices: 15.1 us -> 15.3 us  [chain_in(): return lax.ppermute(value, 'group', [(0, 1), (3, 2)])]
  transfers between devices with their start and end apart: 43 -> 44, of which waited for: 20 -> 19; matrix products, arithmetic and copies ran while one was open for 7% -> 8% of each run, Pallas kernels for 37% -> 38%
where the time goes in v6:
time: 295 us; the launch traced here: 290 us
  Pallas kernels  145 us (49%)
  starting transfers between devices  50.5 us (17%)
  waiting for transfers between devices  49.7 us (17%)
  local copies, waits for them, and re-layouts  24 us (8%)
  other arithmetic  18.5 us (6%)
    ppermute x32, waiting for transfers between devices, swap(): return lax.ppermute(value, axis, [(n, n ^ bit) for n in range(size)])  36.2 us
    pallas_call x1, Pallas kernels, middle_stage(): pl.pallas_call(body, grid_spec=pltpu.PrefetchScalarGridSpec(num_scalar_pr...  35.2 us
    pallas_call x3, Pallas kernels, attend_backward(): pl.pallas_call(functools.partial(attend_backward_kernel, block=length //...  34.3 us
    ppermute x32, starting transfers between devices, swap(): return lax.ppermute(value, axis, [(n, n ^ bit) for n in range(size)])  27.1 us
    pallas_call x2, Pallas kernels, attend_forward(): pl.pallas_call(body, grid_spec=pltpu.PrefetchScalarGridSpec(num_scalar_pr...  18.8 us
    unnamed x100, local copies, waits for them, and re-layouts  16.3 us
    ppermute x4, starting transfers between devices, chain_in(): return lax.ppermute(value, 'group', [(0, 1), (3, 2)])  15.3 us
    convert_element_type x17, other arithmetic, add_low(): return total.astype(BF16)  12 us
  transfers between devices with their start and end apart: 44, of which 19 were waited for; matrix products, arithmetic and copies ran while one was open for 8% of the time, Pallas kernels for 38%

profile of v6, /device:TPU:0, one launch (start us, length us, event | category | flops | bytes accessed | tf_op | source)
XLA Modules:
  0.0 289.9 jit_solution(8601162766615246239)
XLA Ops:
  1.7 3.0 %collective-permute-start = (bf16[3,192,384]{2,1,0:T(8,128)(2,1)S(1)}, bf16[3,192,384]{2,1,0:T(8,128)(2,1)}, u32[]{:S(2)}, u32[]{:S(2)}) collective-permute-start(bf16[3,192,384]{2,1,0:T(8,128)(2,1)S(1)} %constant_dynamic-slice_fusion.5), channel_id=1, source_target_pairs={{0,1},{1,0},{2,3},{3,2},{4,5},{5,4},{6,7},{7,6},{8,9},{9,8},{10,11... | collective-permute-start | bytes 1327112 | tf_op jit(solution)/shard_map/ppermute | solution.py:689
  7.2 1.4 copy-done.12
  8.6 3.3 %unpack_rows.2 = (bf16[512,768]{1,0:T(8,128)(2,1)S(1)}, bf16[528,768]{1,0:T(8,128)(2,1)S(1)}) custom-call(s32[3]{0:T(128)S(1)} %pad_add_fusion.place_ref, bf16[767,2,512]{2,1,0:T(2,128)(2,1)S(1)} %bitcast.55, bf16[16,768]{1,0:T(8,128)(2,1)S(1)} %maximum_maximum_fusion.refs_0_), custom_call_target="tpu_custom_call" | custom-call | flops 2000000000 | bytes 2000000 | tf_op jit(solution)/shard_map/unpack_rows/pallas_call | solution.py:192
  12.8 2.2 collective-permute-done.a.refs_1_.refs_8_
  15.0 1.7 collective-permute-start.2
  16.8 1.5 collective-permute-start.1
  18.3 1.7 pad.20.refs_10_
  21.2 1.2 constant_dynamic-slice_fusion
  24.7 1.5 collective-permute-start.6
  26.2 3.3 %unpack_rows.3 = (bf16[512,768]{1,0:T(8,128)(2,1)S(1)}, bf16[512,768]{1,0:T(8,128)(2,1)S(1)}) custom-call(s32[3]{0:T(128)S(1)} %pad_add_fusion.place_ref, bf16[767,2,512]{2,1,0:T(2,128)(2,1)S(1)} %bitcast.56), custom_call_target="tpu_custom_call" | custom-call | flops 2000000000 | bytes 2000000 | tf_op jit(solution)/shard_map/unpack_rows/pallas_call | solution.py:192
  31.3 4.8 %collective-permute-done.2.other_ref.refs_2_.refs_4_ = bf16[528,768]{1,0:T(8,128)(2,1)S(1)} collective-permute-done((bf16[528,768]{1,0:T(8,128)(2,1)S(1)}, bf16[528,768]{1,0:T(8,128)(2,1)S(1)}, u32[]{:S(2)}, u32[]{:S(2)}) %collective-permute-start.2) | collective-permute-done | bytes 811040 | tf_op jit(solution)/shard_map/ppermute | solution.py:689
  36.1 2.1 collective-permute-done.4.d.refs_4_.refs_11_
  40.3 7.9 %norm_project.1 = (bf16[1024,768]{1,0:T(8,128)(2,1)S(1)}, bf16[1024,768]{1,0:T(8,128)(2,1)S(1)}, bf16[1024,768]{1,0:T(8,128)(2,1)S(1)}, bf16[1024,768]{1,0:T(8,128)(2,1)S(1)}) custom-call(s32[3]{0:T(128)S(1)} %pad_add_fusion.place_ref, bf16[512,768]{1,0:T(8,128)(2,1)S(1)} %copy-done.21, ...), custom_call_target="tpu_custom_call" | custom-call | flops 4000000000 | bytes 4000000 | tf_op jit(solution)/shard_map/norm_project/pallas_call | solution.py:283
  48.3 1.8 collective-permute-start.9
  50.1 9.4 %attend_forward.2 = (bf16[1024,768]{1,0:T(8,128)(2,1)S(1)}, f32[6,8,1024]{2,1,0:T(8,128)S(1)}) custom-call(s32[4]{0:T(128)S(1)} %compare_convert_fusion.flags_ref, bf16[1024,768]{1,0:T(8,128)(2,1)S(1)} %get-tuple-element.211.q_ref, bf16[1024,768]{1,0:T(8,128)(2,1)S(1)} %get-tuple-element.207.k_ref, bf16[1024,768]{1,0:T(8,128)(2,1)S(1)} %get-tuple-element.208.v_ref), custom_call_target="tpu_custom_call" | custom-call | flops 4560000000 | bytes 4559999 | tf_op jit(solution)/shard_map/attend_forward/pallas_call | solution.py:88
  59.5 5.1 %collective-permute-done.6.refs_15_ = bf16[384,768]{1,0:T(8,128)(2,1)} collective-permute-done((bf16[384,768]{1,0:T(8,128)(2,1)}, bf16[384,768]{1,0:T(8,128)(2,1)}, u32[]{:S(2)}, u32[]{:S(2)}) %collective-permute-start.6) | collective-permute-done | bytes 589856 | tf_op jit(solution)/shard_map/ppermute | solution.py:689
  64.6 1.8 collective-permute-start.7
  66.4 1.6 collective-permute-start.8
  68.0 9.4 %attend_forward.3 = (bf16[1024,768]{1,0:T(8,128)(2,1)S(1)}, f32[6,8,1024]{2,1,0:T(8,128)S(1)}) custom-call(s32[4]{0:T(128)S(1)} %compare_convert_fusion.flags_ref, bf16[1024,768]{1,0:T(8,128)(2,1)S(1)} %get-tuple-element.211.q_ref, bf16[1024,768]{1,0:T(8,128)(2,1)S(1)} %get-tuple-element.207.k_ref, ...), custom_call_target="tpu_custom_call", output_to_operand_aliasing={{0}: (4, {}), {1}: (5, {})} | custom-call | flops 4560000000 | bytes 4559999 | tf_op jit(solution)/shard_map/attend_forward/pallas_call | solution.py:88
  78.1 1.8 collective-permute-done.7.refs_13_
  80.5 3.1 %collective-permute-done.12.refs_16_ = bf16[384,768]{1,0:T(8,128)(2,1)S(1)} collective-permute-done((bf16[384,768]{1,0:T(8,128)(2,1)}, bf16[384,768]{1,0:T(8,128)(2,1)S(1)}, u32[]{:S(2)}, u32[]{:S(2)}) %collective-permute-start.12) | collective-permute-done | bytes 589856 | tf_op jit(solution)/shard_map/ppermute | solution.py:689
  83.8 35.2 %middle_stage.1 = (bf16[1024,768]{1,0:T(8,128)(2,1)S(1)}, bf16[1024,3072]{1,0:T(8,128)(2,1)}, bf16[1024,3072]{1,0:T(8,128)(2,1)}, bf16[512,768]{1,0:T(8,128)(2,1...) custom-call(s32[3]{0:T(128)S(1)} %pad_add_fusion.place_ref, ...), custom_call_target="tpu_custom_call" | custom-call | flops 15200000000 | bytes 15200000 | tf_op jit(solution)/shard_map/middle_stage/pallas_call | solution.py:427
  121.2 2.8 copy-done.24
  124.0 8.3 %proj_grad.1 = (bf16[2,2,480,768]{3,2,1,0:T(8,128)(2,1)S(1)}, bf16[2,2,480,768]{3,2,1,0:T(8,128)(2,1)S(1)}) custom-call(s32[3]{0:T(128)S(1)} %pad_add_fusion.place_ref, bf16[1024,3072]{1,0:T(8,128)(2,1)S(1)} %copy-done.24, bf16[1024,3072]{1,0:T(8,128)(2,1)S(1)} %copy-done.24, bf16[512,768]{1,0:T(8,128)(2,1)S(1)} %copy-done.26, ...), custom_call_target="tpu_custom_call" | custom-call | flops 5200000000 | bytes 5200000 | tf_op jit(solution)/shard_map/proj_grad/pallas_call | solution.py:568
  133.5 8.0 %fc_grad.1 = (bf16[2,2,192,1536]{3,2,1,0:T(8,128)(2,1)S(1)}, bf16[2,2,192,1536]{3,2,1,0:T(8,128)(2,1)}) custom-call(s32[3]{0:T(128)S(1)} %pad_add_fusion.place_ref, bf16[1024,768]{1,0:T(8,128)(2,1)S(1)} %get-tuple-element.237.left_ref, bf16[1024,3072]{1,0:T(8,128)(2,1)S(1)} %copy-done.38), custom_call_target="tpu_custom_call" | custom-call | flops 4800000000 | bytes 4800000 | tf_op jit(solution)/shard_map/fc_grad/pallas_call | solution.py:468
  141.5 1.4 copy-done.2
  144.7 1.4 fusion.13
  146.2 1.6 collective-permute-start.18
  147.7 1.4 fusion.14
  149.8 1.9 fusion.4
  152.4 1.4 copy-done.34
  153.8 16.8 %attend_backward.3 = (bf16[3,1024,384]{2,1,0:T(8,128)(2,1)S(1)}, f32[8,384]{1,0:T(8,128)S(1)}) custom-call(s32[4]{0:T(128)S(1)} %compare_convert_fusion.flags_ref, bf16[1024,768]{1,0:T(8,128)(2,1)S(1)} %copy-done.28, bf16[1024,768]{1,0:T(8,128)(2,1)S(1)} %copy-done.30, bf16[1024,768]{1,0:T(8,128)(2,1)S(1)} %copy-done.32, bf16[1024,768]{1,0:T(8,128)(2,1)S(1)} %copy-done.34, ...), custom_call_target="tpu_custom_call" | custom-call | flops 7600000000 | bytes 7600000 | tf_op jit(solution)/shard_map/attend_backward/pallas_call | solution.py:155
  170.7 1.6 fusion.2
  172.3 1.4 collective-permute-start.20
  173.7 4.7 %qkv_grad.2 = (bf16[2,3,192,384]{3,2,1,0:T(8,128)(2,1)S(1)}, bf16[2,3,192,384]{3,2,1,0:T(8,128)(2,1)S(1)}, f32[8,768]{1,0:T(8,128)S(1)}) custom-call(s32[3]{0:T(128)S(1)} %pad_add_fusion.place_ref, bf16[1024,768]{1,0:T(8,128)(2,1)S(1)} %copy-done.37, bf16[3,1024,384]{2,1,0:T(8,128)(2,1)S(1)} %get-tuple-element.260.refs_0_.refs_2_, ...), custom_call_target="tpu_custom_call" | custom-call | flops 2600000000 | bytes 2600000 | tf_op jit(solution)/shard_map/qkv_grad/pallas_call | solution.py:526
  178.4 2.2 collective-permute-done.19
  180.6 1.3 fusion.7
  181.9 1.2 collective-permute-start.22
  183.1 11.8 %attend_backward.4 = (bf16[3,1024,256]{2,1,0:T(8,128)(2,1)S(1)}, f32[8,256]{1,0:T(8,128)S(1)}) custom-call(s32[4]{0:T(128)S(1)} %compare_convert_fusion.flags_ref, bf16[1024,768]{1,0:T(8,128)(2,1)S(1)} %copy-done.28, bf16[1024,768]{1,0:T(8,128)(2,1)S(1)} %copy-done.30, bf16[1024,768]{1,0:T(8,128)(2,1)S(1)} %copy-done.32, bf16[1024,768]{1,0:T(8,128)(2,1)S(1)} %copy-done.35, ...), custom_call_target="tpu_custom_call" | custom-call | flops 5200000000 | bytes 5200000 | tf_op jit(solution)/shard_map/attend_backward/pallas_call | solution.py:155
  195.2 2.5 collective-permute-done.22
  197.7 1.4 fusion.6
  199.1 1.2 collective-permute-start.24
  200.4 1.5 fusion.1
  201.9 3.7 %collective-permute-start.27 = (bf16[480,768]{1,0:T(8,128)(2,1)S(1)}, bf16[480,768]{1,0:T(8,128)(2,1)S(1)}, u32[]{:S(2)}, u32[]{:S(2)}) collective-permute-start(bf16[480,768]{1,0:T(8,128)(2,1)S(1)} %fusion.1), channel_id=1, source_target_pairs={{0,2},{6,4},{1,3},{7,5},{8,10},{14,12},{9,11},{15,13},{16,18},{22,... | collective-permute-start | bytes 2211848 | tf_op jit(solution)/shard_map/ppermute | solution.py:704
  205.6 1.5 collective-permute-start.28
  207.1 5.7 %attend_backward.5 = (bf16[3,1024,128]{2,1,0:T(8,128)(2,1)S(1)}, f32[8,128]{1,0:T(8,128)S(1)}) custom-call(s32[4]{0:T(128)S(1)} %compare_convert_fusion.flags_ref, bf16[1024,768]{1,0:T(8,128)(2,1)S(1)} %copy-done.28, bf16[1024,768]{1,0:T(8,128)(2,1)S(1)} %copy-done.30, bf16[1024,768]{1,0:T(8,128)(2,1)S(1)} %copy-done.32, bf16[1024,768]{1,0:T(8,128)(2,1)S(1)} %copy-done.35, ...), custom_call_target="tpu_custom_call" | custom-call | flops 2800000000 | bytes 2800000 | tf_op jit(solution)/shard_map/attend_backward/pallas_call | solution.py:155
  212.8 3.0 %qkv_grad.3 = (bf16[2,3,192,384]{3,2,1,0:T(8,128)(2,1)S(1)}, bf16[2,3,192,384]{3,2,1,0:T(8,128)(2,1)S(1)}, f32[8,768]{1,0:T(8,128)S(1)}) custom-call(s32[3]{0:T(128)S(1)} %pad_add_fusion.place_ref, bf16[1024,768]{1,0:T(8,128)(2,1)S(1)} %copy-done.37, bf16[3,1024,256]{2,1,0:T(8,128)(2,1)S(1)} %get-tuple-element.281.refs_0_, ...), custom_call_target="tpu_custom_call" | custom-call | flops 2600000000 | bytes 2600000 | tf_op jit(solution)/shard_map/qkv_grad/pallas_call | solution.py:526
  217.3 1.2 collective-permute-done.26
  219.6 1.2 collective-permute-start.30
  220.9 1.6 collective-permute-done.27
  223.4 4.7 %pack_rows.2 = bf16[767,2,512]{2,1,0:T(2,128)(2,1)} custom-call(s32[3]{0:T(128)S(1)} %pad_add_fusion.place_ref, bf16[512,768]{1,0:T(8,128)(2,1)S(1)} %copy-done.5, bf16[256,768]{1,0:T(8,128)(2,1)S(1)} %collective-permute-done.14.first_ref, bf16[256,768]{1,0:T(8,128)(2,1)S(1)} %copy-done.7), custom_call_target="tpu_custom_call" | custom-call | flops 40000000 | bytes 40000 | tf_op jit(solution)/shard_map/pack_rows/pallas_call | solution.py:673
  228.1 5.4 %collective-permute-done.28 = bf16[192,1536]{1,0:T(8,128)(2,1)S(1)} collective-permute-done((bf16[192,1536]{1,0:T(8,128)(2,1)S(1)}, bf16[192,1536]{1,0:T(8,128)(2,1)S(1)}, u32[]{:S(2)}, u32[]{:S(2)}) %collective-permute-start.28) | collective-permute-done | bytes 589856 | tf_op jit(solution)/shard_map/ppermute | solution.py:704
  235.1 3.3 %collective-permute-done.32 = f32[8,3456]{1,0:T(8,128)S(1)} collective-permute-done((f32[8,3456]{1,0:T(8,128)S(1)}, f32[8,3456]{1,0:T(8,128)S(1)}, u32[]{:S(2)}, u32[]{:S(2)}) %collective-permute-start.32) | collective-permute-done | bytes 110624 | tf_op jit(solution)/shard_map/ppermute | solution.py:689
  238.7 8.8 %collective-permute-start.34 = (bf16[3,192,384]{2,1,0:T(8,128)(2,1)S(1)}, bf16[3,192,384]{2,1,0:T(8,128)(2,1)S(1)}, u32[]{:S(2)}, u32[]{:S(2)}) collective-permute-start(bf16[3,192,384]{2,1,0:T(8,128)(2,1)S(1)} %fusion.9), channel_id=1, source_target_pairs={{0,2},{6,4},{1,3},{7,5},{8,10},{14,12},{9,11},{15,13},{16,18},{22,... | collective-permute-start | bytes 1327112 | tf_op jit(solution)/shard_map/ppermute | solution.py:704
  247.5 1.3 collective-permute-start.36
  249.0 1.5 collective-permute-start.38
  250.5 9.1 %input_grad.1 = (bf16[512,768]{1,0:T(8,128)(2,1)S(1)}, bf16[512,768]{1,0:T(8,128)(2,1)S(1)}) custom-call(s32[3]{0:T(128)S(1)} %pad_add_fusion.place_ref, bf16[3,1024,256]{2,1,0:T(8,128)(2,1)S(1)} %get-tuple-element.281.refs_0_, bf16[3,1024,128]{2,1,0:T(8,128)(2,1)S(1)} %get-tuple-element.279.refs_1_, ...), custom_call_target="tpu_custom_call" | custom-call | flops 3600000000 | bytes 3600000 | tf_op jit(solution)/shard_map/input_grad/pallas_call | solution.py:642
  261.5 1.3 collective-permute-start.42
  264.8 1.3 collective-permute-start.43
  266.2 1.3 collective-permute-start.41
  267.5 6.5 %collective-permute-done.37.first_ref.second_ref = bf16[512,768]{1,0:T(8,128)(2,1)S(1)} collective-permute-done((bf16[512,768]{1,0:T(8,128)(2,1)S(1)}, bf16[512,768]{1,0:T(8,128)(2,1)S(1)}, u32[]{:S(2)}, u32[]{:S(2)}) %collective-permute-start.37) | collective-permute-done | bytes 786464 | tf_op jit(solution)/shard_map/ppermute | solution.py:689
  274.0 4.7 %pack_rows.3 = bf16[767,2,512]{2,1,0:T(2,128)(2,1)} custom-call(s32[3]{0:T(128)S(1)} %pad_add_fusion.place_ref, bf16[512,768]{1,0:T(8,128)(2,1)S(1)} %get-tuple-element.344.own_ref, bf16[512,768]{1,0:T(8,128)(2,1)S(1)} %collective-permute-done.37.first_ref.second_ref, bf16[512,768]{1,0:T(8,128)(2,1)S(1)} %collective-permute-done.37.first_ref.second_ref), custom_call_target="tpu_custom_call" | custom-call | flops 40000000 | bytes 40000 | tf_op jit(solution)/shard_map/pack_rows/pallas_call | solution.py:673
  278.7 4.1 %collective-permute-done.42 = bf16[192,1536]{1,0:T(8,128)(2,1)S(1)} collective-permute-done((bf16[192,1536]{1,0:T(8,128)(2,1)S(1)}, bf16[192,1536]{1,0:T(8,128)(2,1)S(1)}, u32[]{:S(2)}, u32[]{:S(2)}) %collective-permute-start.42) | collective-permute-done | bytes 589856 | tf_op jit(solution)/shard_map/ppermute | solution.py:712
  286.4 2.3 collective-permute-done.41
  (207 shorter events, 34.0 us)
Async XLA Ops:
  0.6 5.6 %copy-start = (s32[2,1024]{1,0:T(2,128)S(1)}, s32[2,1024]{1,0:T(2,128)}, u32[]{:S(2)}) copy-start(s32[2,1024]{1,0:T(2,128)} %param.12) | copy-start | bytes 24580
  1.7 13.3 %collective-permute-start = (bf16[3,192,384]{2,1,0:T(8,128)(2,1)S(1)}, bf16[3,192,384]{2,1,0:T(8,128)(2,1)}, u32[]{:S(2)}, u32[]{:S(2)}) collective-permute-start(bf16[3,192,384]{2,1,0:T(8,128)(2,1)S(1)} %constant_dynamic-slice_fusion.5), channel_id=1, source_target_pairs={{0,1},{1,0},{2,3},{3,2},{4,5},{5,4},{6,7},{7,6},{8,9},{9,8},{10,11... | collective-permute-start | bytes 1327112 | tf_op jit(solution)/shard_map/ppermute | solution.py:689
  8.6 9.7 %copy-start.41 = (bf16[1536,767]{1,0:T(8,128)(2,1)S(1)}, bf16[1536,767]{1,0:T(8,128)(2,1)}, u32[]{:S(2)}) copy-start(bf16[1536,767]{1,0:T(8,128)(2,1)} %param.19) | copy-start | bytes 7068676
  15.0 21.0 %collective-permute-start.2 = (bf16[528,768]{1,0:T(8,128)(2,1)S(1)}, bf16[528,768]{1,0:T(8,128)(2,1)S(1)}, u32[]{:S(2)}, u32[]{:S(2)}) collective-permute-start(bf16[528,768]{1,0:T(8,128)(2,1)S(1)} %get-tuple-element.193), channel_id=1, source_target_pairs={{0,1},{1,0},{2,3},{3,2},{4,5},{5,4},{6,7},{7,6},{8,9},{9,8},{10,11... | collective-permute-start | bytes 2433032 | tf_op jit(solution)/shard_map/ppermute | solution.py:689
  16.8 6.6 %collective-permute-start.3 = (bf16[3,192,384]{2,1,0:T(8,128)(2,1)}, bf16[3,192,384]{2,1,0:T(8,128)(2,1)S(1)}, u32[]{:S(2)}, u32[]{:S(2)}) collective-permute-start(bf16[3,192,384]{2,1,0:T(8,128)(2,1)} %collective-permute-done.a.refs_1_.refs_8_), channel_id=1, source_target_pairs={{0,8},{8,0},{16,24},{24,16},{1,9},{9,1},{17,25},{25,17},{2,10},{10... | collective-permute-start | bytes 1327112 | tf_op jit(solution)/shard_map/ppermute | solution.py:689
  16.8 14.5 %collective-permute-start.1 = (bf16[3,192,384]{2,1,0:T(8,128)(2,1)}, bf16[3,192,384]{2,1,0:T(8,128)(2,1)}, u32[]{:S(2)}, u32[]{:S(2)}) collective-permute-start(bf16[3,192,384]{2,1,0:T(8,128)(2,1)} %collective-permute-done.a.refs_1_.refs_8_), channel_id=1, source_target_pairs={{0,16},{8,24},{16,0},{24,8},{1,17},{9,25},{17,1},{25,9},{2,18},{10... | collective-permute-start | bytes 1327112 | tf_op jit(solution)/shard_map/ppermute | solution.py:689
  24.1 40.4 %collective-permute-start.5 = (bf16[480,768]{1,0:T(8,128)(2,1)}, bf16[480,768]{1,0:T(8,128)(2,1)}, u32[]{:S(2)}, u32[]{:S(2)}) collective-permute-start(bf16[480,768]{1,0:T(8,128)(2,1)} %fusion.12), channel_id=1, source_target_pairs={{0,1},{1,0},{2,3},{3,2},{4,5},{5,4},{6,7},{7,6},{8,9},{9,8},{10,11... | collective-permute-start | bytes 2211848 | tf_op jit(solution)/shard_map/ppermute | solution.py:689
  24.7 39.9 %collective-permute-start.6 = (bf16[384,768]{1,0:T(8,128)(2,1)}, bf16[384,768]{1,0:T(8,128)(2,1)}, u32[]{:S(2)}, u32[]{:S(2)}) collective-permute-start(bf16[384,768]{1,0:T(8,128)(2,1)} %pad.22), channel_id=1, source_target_pairs={{0,1},{1,0},{2,3},{3,2},{4,5},{5,4},{6,7},{7,6},{8,9},{9,8},{10,11... | collective-permute-start | bytes 1769480 | tf_op jit(solution)/shard_map/ppermute | solution.py:689
  26.2 12.0 %copy-start.8 = (bf16[3,768,384]{2,1,0:T(8,128)(2,1)S(1)}, bf16[3,768,384]{2,1,0:T(8,128)(2,1)}, u32[]{:S(2)}) copy-start(bf16[3,768,384]{2,1,0:T(8,128)(2,1)} %refs_7_.1) | copy-start | bytes 5308420
  36.0 47.8 %copy-start.10 = (bf16[528,768]{1,0:T(8,128)(2,1)}, bf16[528,768]{1,0:T(8,128)(2,1)S(1)}, u32[]{:S(2)}) copy-start(bf16[528,768]{1,0:T(8,128)(2,1)S(1)} %collective-permute-done.2.other_ref.refs_2_.refs_4_) | copy-start | bytes 2433028
  36.0 2.1 collective-permute-start.4
  40.3 7.9 %copy-start.15 = (bf16[512,768]{1,0:T(8,128)(2,1)S(1)}, bf16[512,768]{1,0:T(8,128)(2,1)}, u32[]{:S(2)}) copy-start(bf16[512,768]{1,0:T(8,128)(2,1)} %copy-done.14) | copy-start | bytes 2359300
  48.2 11.3 %copy-start.36 = (bf16[1024,768]{1,0:T(8,128)(2,1)}, bf16[1024,768]{1,0:T(8,128)(2,1)S(1)}, u32[]{:S(2)}) copy-start(bf16[1024,768]{1,0:T(8,128)(2,1)S(1)} %get-tuple-element.259.left_ref) | copy-start | bytes 4718596
  48.2 19.7 %copy-start.27 = (bf16[1024,768]{1,0:T(8,128)(2,1)}, bf16[1024,768]{1,0:T(8,128)(2,1)S(1)}, u32[]{:S(2)}) copy-start(bf16[1024,768]{1,0:T(8,128)(2,1)S(1)} %get-tuple-element.211.q_ref) | copy-start | bytes 4718596
  48.2 19.7 %copy-start.29 = (bf16[1024,768]{1,0:T(8,128)(2,1)}, bf16[1024,768]{1,0:T(8,128)(2,1)S(1)}, u32[]{:S(2)}) copy-start(bf16[1024,768]{1,0:T(8,128)(2,1)S(1)} %get-tuple-element.207.k_ref) | copy-start | bytes 4718596
  48.3 19.7 %copy-start.31 = (bf16[1024,768]{1,0:T(8,128)(2,1)}, bf16[1024,768]{1,0:T(8,128)(2,1)S(1)}, u32[]{:S(2)}) copy-start(bf16[1024,768]{1,0:T(8,128)(2,1)S(1)} %get-tuple-element.208.v_ref) | copy-start | bytes 4718596
  48.3 31.6 %collective-permute-start.9 = (bf16[512,768]{1,0:T(8,128)(2,1)S(1)}, bf16[512,768]{1,0:T(8,128)(2,1)S(1)}, u32[]{:S(2)}, u32[]{:S(2)}) collective-permute-start(bf16[512,768]{1,0:T(8,128)(2,1)S(1)} %copy-done.15), channel_id=1, source_target_pairs={{0,1},{1,0},{2,3},{3,2},{4,5},{5,4},{6,7},{7,6},{8,9},{9,8},{10,11... | collective-permute-start | bytes 2359304 | tf_op jit(solution)/shard_map/ppermute | solution.py:689
  64.6 15.8 %copy-start.45 = (bf16[2,767]{1,0:T(2,128)(2,1)S(1)}, bf16[2,767]{1,0:T(2,128)(2,1)}, u32[]{:S(2)}) copy-start(bf16[2,767]{1,0:T(2,128)(2,1)} %param.20) | copy-start | bytes 9208
  64.6 15.8 %copy-start.44 = (bf16[1536]{0:T(1024)(128)(2,1)S(1)}, bf16[1536]{0:T(1024)(128)(2,1)}, u32[]{:S(2)}) copy-start(bf16[1536]{0:T(1024)(128)(2,1)} %param.18) | copy-start | bytes 9220
  64.6 19.2 %copy-start.22 = (bf16[512,768]{1,0:T(8,128)(2,1)S(1)}, bf16[512,768]{1,0:T(8,128)(2,1)}, u32[]{:S(2)}) copy-start(bf16[512,768]{1,0:T(8,128)(2,1)} %copy-done.20) | copy-start | bytes 2359300
  64.6 19.2 %copy-start.26 = (bf16[512,768]{1,0:T(8,128)(2,1)S(1)}, bf16[512,768]{1,0:T(8,128)(2,1)}, u32[]{:S(2)}) copy-start(bf16[512,768]{1,0:T(8,128)(2,1)} %copy-done.25) | copy-start | bytes 2359300
  64.6 15.3 %collective-permute-start.7 = (bf16[480,768]{1,0:T(8,128)(2,1)}, bf16[480,768]{1,0:T(8,128)(2,1)S(1)}, u32[]{:S(2)}, u32[]{:S(2)}) collective-permute-start(bf16[480,768]{1,0:T(8,128)(2,1)} %collective-permute-done.5.refs_11_), channel_id=1, source_target_pairs={{0,16},{8,24},{16,0},{24,8},{1,17},{9,25},{17,1},{25,9},{2,18},{10... | collective-permute-start | bytes 2211848 | tf_op jit(solution)/shard_map/ppermute | solution.py:689
  66.4 11.7 %collective-permute-start.8 = (bf16[384,768]{1,0:T(8,128)(2,1)}, bf16[384,768]{1,0:T(8,128)(2,1)S(1)}, u32[]{:S(2)}, u32[]{:S(2)}) collective-permute-start(bf16[384,768]{1,0:T(8,128)(2,1)} %collective-permute-done.6.refs_15_), channel_id=1, source_target_pairs={{0,2},{2,0},{4,6},{6,4},{1,3},{3,1},{5,7},{7,5},{8,10},{10,8},{12,... | collective-permute-start | bytes 1769480 | tf_op jit(solution)/shard_map/ppermute | solution.py:689
  68.0 15.7 %collective-permute-start.10 = (bf16[480,768]{1,0:T(8,128)(2,1)}, bf16[480,768]{1,0:T(8,128)(2,1)S(1)}, u32[]{:S(2)}, u32[]{:S(2)}) collective-permute-start(bf16[480,768]{1,0:T(8,128)(2,1)} %collective-permute-done.5.refs_11_), channel_id=1, source_target_pairs={{0,8},{8,0},{16,24},{24,16},{1,9},{9,1},{17,25},{25,17},{2,10},{10... | collective-permute-start | bytes 2211848 | tf_op jit(solution)/shard_map/ppermute | solution.py:689
  79.9 3.9 %collective-permute-start.11 = (bf16[480,768]{1,0:T(8,128)(2,1)S(1)}, bf16[480,768]{1,0:T(8,128)(2,1)S(1)}, u32[]{:S(2)}, u32[]{:S(2)}) collective-permute-start(bf16[480,768]{1,0:T(8,128)(2,1)S(1)} %collective-permute-done.7.refs_13_), channel_id=1, source_target_pairs={{0,8},{8,0},{16,24},{24,16},{1,9},{9,1},{17,25},{25,17},{2,10},{10... | collective-permute-start | bytes 2211848 | tf_op jit(solution)/shard_map/ppermute | solution.py:689
  79.9 3.7 %collective-permute-start.12 = (bf16[384,768]{1,0:T(8,128)(2,1)}, bf16[384,768]{1,0:T(8,128)(2,1)S(1)}, u32[]{:S(2)}, u32[]{:S(2)}) collective-permute-start(bf16[384,768]{1,0:T(8,128)(2,1)} %collective-permute-done.6.refs_15_), channel_id=1, source_target_pairs={{0,8},{8,0},{16,24},{24,16},{1,9},{9,1},{17,25},{25,17},{2,10},{10... | collective-permute-start | bytes 1769480 | tf_op jit(solution)/shard_map/ppermute | solution.py:689
  80.4 3.4 %collective-permute-start.13 = (bf16[384,768]{1,0:T(8,128)(2,1)S(1)}, bf16[384,768]{1,0:T(8,128)(2,1)S(1)}, u32[]{:S(2)}, u32[]{:S(2)}) collective-permute-start(bf16[384,768]{1,0:T(8,128)(2,1)S(1)} %collective-permute-done.8.refs_17_), channel_id=1, source_target_pairs={{0,8},{8,0},{16,24},{24,16},{1,9},{9,1},{17,25},{25,17},{2,10},{10... | collective-permute-start | bytes 1769480 | tf_op jit(solution)/shard_map/ppermute | solution.py:689
  120.2 12.1 %copy-start.4 = (bf16[512,768]{1,0:T(8,128)(2,1)}, bf16[512,768]{1,0:T(8,128)(2,1)S(1)}, u32[]{:S(2)}) copy-start(bf16[512,768]{1,0:T(8,128)(2,1)S(1)} %get-tuple-element.304.own_ref) | copy-start | bytes 2359300
  120.2 12.1 %collective-permute-start.14 = (bf16[256,768]{1,0:T(8,128)(2,1)S(1)}, bf16[256,768]{1,0:T(8,128)(2,1)S(1)}, u32[]{:S(2)}, u32[]{:S(2)}) collective-permute-start(bf16[256,768]{1,0:T(8,128)(2,1)S(1)} %get-tuple-element.234), channel_id=1, source_target_pairs={{0,1},{1,0},{2,3},{3,2},{4,5},{5,4},{6,7},{7,6},{8,9},{9,8},{10,11... | collective-permute-start | bytes 1179656 | tf_op jit(solution)/shard_map/ppermute | solution.py:689
  124.0 9.5 %copy-start.38 = (bf16[1024,3072]{1,0:T(8,128)(2,1)S(1)}, bf16[1024,3072]{1,0:T(8,128)(2,1)}, u32[]{:S(2)}) copy-start(bf16[1024,3072]{1,0:T(8,128)(2,1)} %get-tuple-element.238.right_ref) | copy-start | bytes 18874372
  132.3 12.4 %collective-permute-start.15 = (bf16[2,2,480,768]{3,2,1,0:T(8,128)(2,1)S(1)}, bf16[2,2,480,768]{3,2,1,0:T(8,128)(2,1)}, u32[]{:S(2)}, u32[]{:S(2)}) collective-permute-start(bf16[2,2,480,768]{3,2,1,0:T(8,128)(2,1)S(1)} %get-tuple-element.241), channel_id=1, source_target_pairs={{0,8},{8,0},{16,24},{24,16},{1,9},{9,1},{17,25},{25,17},{2,10},{10... | collective-permute-start | bytes 8847368 | tf_op jit(solution)/shard_map/ppermute | solution.py:689
  132.4 11.5 %collective-permute-start.16 = (bf16[256,768]{1,0:T(8,128)(2,1)S(1)}, bf16[256,768]{1,0:T(8,128)(2,1)S(1)}, u32[]{:S(2)}, u32[]{:S(2)}) collective-permute-start(bf16[256,768]{1,0:T(8,128)(2,1)S(1)} %get-tuple-element.243), channel_id=1, source_target_pairs={{0,1},{1,0},{2,3},{3,2},{4,5},{5,4},{6,7},{7,6},{8,9},{9,8},{10,11... | collective-permute-start | bytes 1179656 | tf_op jit(solution)/shard_map/ppermute | solution.py:689
  144.7 5.1 %collective-permute-start.17 = (bf16[2,2,192,1536]{3,2,1,0:T(8,128)(2,1)}, bf16[2,2,192,1536]{3,2,1,0:T(8,128)(2,1)}, u32[]{:S(2)}, u32[]{:S(2)}) collective-permute-start(bf16[2,2,192,1536]{3,2,1,0:T(8,128)(2,1)} %get-tuple-element.245), channel_id=1, source_target_pairs={{0,8},{8,0},{16,24},{24,16},{1,9},{9,1},{17,25},{25,17},{2,10},{10... | collective-permute-start | bytes 7077896 | tf_op jit(solution)/shard_map/ppermute | solution.py:689
  146.2 24.5 %collective-permute-start.18 = (bf16[480,768]{1,0:T(8,128)(2,1)S(1)}, bf16[480,768]{1,0:T(8,128)(2,1)S(1)}, u32[]{:S(2)}, u32[]{:S(2)}) collective-permute-start(bf16[480,768]{1,0:T(8,128)(2,1)S(1)} %fusion.13), channel_id=1, source_target_pairs={{0,16},{8,24},{16,0},{24,8},{1,17},{9,25},{17,1},{25,9},{2,18},{10... | collective-permute-start | bytes 2211848 | tf_op jit(solution)/shard_map/ppermute | solution.py:689
  149.2 45.8 %collective-permute-start.21 = (bf16[480,768]{1,0:T(8,128)(2,1)S(1)}, bf16[480,768]{1,0:T(8,128)(2,1)S(1)}, u32[]{:S(2)}, u32[]{:S(2)}) collective-permute-start(bf16[480,768]{1,0:T(8,128)(2,1)S(1)} %fusion.14), channel_id=1, source_target_pairs={{0,16},{8,24},{16,0},{24,8},{1,17},{9,25},{17,1},{25,9},{2,18},{10... | collective-permute-start | bytes 2211848 | tf_op jit(solution)/shard_map/ppermute | solution.py:689
  151.6 28.9 %collective-permute-start.19 = (bf16[2,192,1536]{2,1,0:T(8,128)(2,1)S(1)}, bf16[2,192,1536]{2,1,0:T(8,128)(2,1)S(1)}, u32[]{:S(2)}, u32[]{:S(2)}) collective-permute-start(bf16[2,192,1536]{2,1,0:T(8,128)(2,1)S(1)} %fusion.4), channel_id=1, source_target_pairs={{0,1},{1,0},{2,3},{3,2},{4,5},{5,4},{6,7},{7,6},{8,9},{9,8},{10,11... | collective-permute-start | bytes 3538952 | tf_op jit(solution)/shard_map/ppermute | solution.py:689
  172.3 22.9 %collective-permute-start.20 = (bf16[480,768]{1,0:T(8,128)(2,1)S(1)}, bf16[480,768]{1,0:T(8,128)(2,1)S(1)}, u32[]{:S(2)}, u32[]{:S(2)}) collective-permute-start(bf16[480,768]{1,0:T(8,128)(2,1)S(1)} %fusion.2), channel_id=1, source_target_pairs={{0,1},{1,0},{2,3},{3,2},{4,5},{5,4},{6,7},{7,6},{8,9},{9,8},{10,11... | collective-permute-start | bytes 2211848 | tf_op jit(solution)/shard_map/ppermute | solution.py:689
  180.6 17.1 %collective-permute-start.23 = (bf16[2,3,192,384]{3,2,1,0:T(8,128)(2,1)S(1)}, bf16[2,3,192,384]{3,2,1,0:T(8,128)(2,1)S(1)}, u32[]{:S(2)}, u32[]{:S(2)}) collective-permute-start(bf16[2,3,192,384]{3,2,1,0:T(8,128)(2,1)S(1)} %get-tuple-element.270), channel_id=1, source_target_pairs={{0,8},{8,0},{16,24},{24,16},{1,9},{9,1},{17,25},{25,17},{2,10},{10... | collective-permute-start | bytes 2654216 | tf_op jit(solution)/shard_map/ppermute | solution.py:689
  181.9 15.8 %collective-permute-start.22 = (bf16[192,1536]{1,0:T(8,128)(2,1)S(1)}, bf16[192,1536]{1,0:T(8,128)(2,1)S(1)}, u32[]{:S(2)}, u32[]{:S(2)}) collective-permute-start(bf16[192,1536]{1,0:T(8,128)(2,1)S(1)} %fusion.7), channel_id=1, source_target_pairs={{0,16},{8,24},{16,0},{24,8},{1,17},{9,25},{17,1},{25,9},{2,18},{10... | collective-permute-start | bytes 1769480 | tf_op jit(solution)/shard_map/ppermute | solution.py:689
  199.1 16.6 %collective-permute-start.24 = (bf16[3,192,384]{2,1,0:T(8,128)(2,1)S(1)}, bf16[3,192,384]{2,1,0:T(8,128)(2,1)S(1)}, u32[]{:S(2)}, u32[]{:S(2)}) collective-permute-start(bf16[3,192,384]{2,1,0:T(8,128)(2,1)S(1)} %fusion.15), channel_id=1, source_target_pairs={{0,16},{8,24},{16,0},{24,8},{1,17},{9,25},{17,1},{25,9},{2,18},{10... | collective-permute-start | bytes 1327112 | tf_op jit(solution)/shard_map/ppermute | solution.py:689
  201.9 10.9 %copy-start.9 = (bf16[3,768,384]{2,1,0:T(8,128)(2,1)S(1)}, bf16[3,768,384]{2,1,0:T(8,128)(2,1)}, u32[]{:S(2)}) copy-start(bf16[3,768,384]{2,1,0:T(8,128)(2,1)} %refs_7_.1) | copy-start | bytes 5308420
  201.9 20.5 %collective-permute-start.27 = (bf16[480,768]{1,0:T(8,128)(2,1)S(1)}, bf16[480,768]{1,0:T(8,128)(2,1)S(1)}, u32[]{:S(2)}, u32[]{:S(2)}) collective-permute-start(bf16[480,768]{1,0:T(8,128)(2,1)S(1)} %fusion.1), channel_id=1, source_target_pairs={{0,2},{6,4},{1,3},{7,5},{8,10},{14,12},{9,11},{15,13},{16,18},{22,... | collective-permute-start | bytes 2211848 | tf_op jit(solution)/shard_map/ppermute | solution.py:704
  205.6 27.9 %collective-permute-start.28 = (bf16[192,1536]{1,0:T(8,128)(2,1)S(1)}, bf16[192,1536]{1,0:T(8,128)(2,1)S(1)}, u32[]{:S(2)}, u32[]{:S(2)}) collective-permute-start(bf16[192,1536]{1,0:T(8,128)(2,1)S(1)} %fusion.6), channel_id=1, source_target_pairs={{0,2},{6,4},{1,3},{7,5},{8,10},{14,12},{9,11},{15,13},{16,18},{22,... | collective-permute-start | bytes 1769480 | tf_op jit(solution)/shard_map/ppermute | solution.py:704
  215.8 2.7 collective-permute-start.25
  215.9 2.6 collective-permute-start.26
  216.6 18.5 %collective-permute-start.31 = (bf16[3,192,384]{2,1,0:T(8,128)(2,1)S(1)}, bf16[3,192,384]{2,1,0:T(8,128)(2,1)S(1)}, u32[]{:S(2)}, u32[]{:S(2)}) collective-permute-start(bf16[3,192,384]{2,1,0:T(8,128)(2,1)S(1)} %fusion.10), channel_id=1, source_target_pairs={{0,1},{1,0},{2,3},{3,2},{4,5},{5,4},{6,7},{7,6},{8,9},{9,8},{10,11... | collective-permute-start | bytes 1327112 | tf_op jit(solution)/shard_map/ppermute | solution.py:689
  218.6 14.9 %collective-permute-start.29 = (f32[8,5376]{1,0:T(8,128)S(1)}, f32[8,5376]{1,0:T(8,128)S(1)}, u32[]{:S(2)}, u32[]{:S(2)}) collective-permute-start(f32[8,5376]{1,0:T(8,128)S(1)} %add.182), channel_id=1, source_target_pairs={{0,16},{8,24},{16,0},{24,8},{1,17},{9,25},{17,1},{25,9},{2,18},{10... | collective-permute-start | bytes 516104 | tf_op jit(solution)/shard_map/ppermute | solution.py:689
  219.6 18.8 %collective-permute-start.30 = (bf16[3,192,384]{2,1,0:T(8,128)(2,1)S(1)}, bf16[3,192,384]{2,1,0:T(8,128)(2,1)S(1)}, u32[]{:S(2)}, u32[]{:S(2)}) collective-permute-start(bf16[3,192,384]{2,1,0:T(8,128)(2,1)S(1)} %fusion.16), channel_id=1, source_target_pairs={{0,16},{8,24},{16,0},{24,8},{1,17},{9,25},{17,1},{25,9},{2,18},{10... | collective-permute-start | bytes 1327112 | tf_op jit(solution)/shard_map/ppermute | solution.py:689
  222.6 15.8 %collective-permute-start.33 = (bf16[480,768]{1,0:T(8,128)(2,1)S(1)}, bf16[480,768]{1,0:T(8,128)(2,1)S(1)}, u32[]{:S(2)}, u32[]{:S(2)}) collective-permute-start(bf16[480,768]{1,0:T(8,128)(2,1)S(1)} %add_convert_fusion.2), channel_id=1, source_target_pairs={{2,4},{4,2},{3,5},{5,3},{10,12},{12,10},{11,13},{13,11},{18,20},{2... | collective-permute-start | bytes 2211848 | tf_op jit(solution)/shard_map/ppermute | solution.py:708
  233.6 4.8 %collective-permute-start.32 = (f32[8,3456]{1,0:T(8,128)S(1)}, f32[8,3456]{1,0:T(8,128)S(1)}, u32[]{:S(2)}, u32[]{:S(2)}) collective-permute-start(f32[8,3456]{1,0:T(8,128)S(1)} %pad_maximum_fusion.1), channel_id=1, source_target_pairs={{0,1},{1,0},{2,3},{3,2},{4,5},{5,4},{6,7},{7,6},{8,9},{9,8},{10,11... | collective-permute-start | bytes 331784 | tf_op jit(solution)/shard_map/ppermute | solution.py:689
  234.4 25.3 %collective-permute-start.35 = (bf16[192,1536]{1,0:T(8,128)(2,1)S(1)}, bf16[192,1536]{1,0:T(8,128)(2,1)S(1)}, u32[]{:S(2)}, u32[]{:S(2)}) collective-permute-start(bf16[192,1536]{1,0:T(8,128)(2,1)S(1)} %add_convert_fusion.6), channel_id=1, source_target_pairs={{2,4},{4,2},{3,5},{5,3},{10,12},{12,10},{11,13},{13,11},{18,20},{2... | collective-permute-start | bytes 1769480 | tf_op jit(solution)/shard_map/ppermute | solution.py:708
  238.4 12.1 %copy-start.19 = (f32[1024,768]{1,0:T(8,128)S(1)}, f32[1024,768]{1,0:T(8,128)}, u32[]{:S(2)}) copy-start(f32[1024,768]{1,0:T(8,128)} %get-tuple-element.322.refs_5_) | copy-start | bytes 9437188
  238.6 11.9 %copy-start.11 = (bf16[528,768]{1,0:T(8,128)(2,1)S(1)}, bf16[528,768]{1,0:T(8,128)(2,1)}, u32[]{:S(2)}) copy-start(bf16[528,768]{1,0:T(8,128)(2,1)} %copy-done.10) | copy-start | bytes 2433028
  238.7 11.9 %copy-start.23 = (bf16[512,768]{1,0:T(8,128)(2,1)S(1)}, bf16[512,768]{1,0:T(8,128)(2,1)}, u32[]{:S(2)}) copy-start(bf16[512,768]{1,0:T(8,128)(2,1)} %copy-done.20) | copy-start | bytes 2359300
  238.7 21.1 %collective-permute-start.34 = (bf16[3,192,384]{2,1,0:T(8,128)(2,1)S(1)}, bf16[3,192,384]{2,1,0:T(8,128)(2,1)S(1)}, u32[]{:S(2)}, u32[]{:S(2)}) collective-permute-start(bf16[3,192,384]{2,1,0:T(8,128)(2,1)S(1)} %fusion.9), channel_id=1, source_target_pairs={{0,2},{6,4},{1,3},{7,5},{8,10},{14,12},{9,11},{15,13},{16,18},{22,... | collective-permute-start | bytes 1327112 | tf_op jit(solution)/shard_map/ppermute | solution.py:704
  247.5 12.2 %collective-permute-start.36 = (f32[8,3456]{1,0:T(8,128)S(1)}, f32[8,3456]{1,0:T(8,128)S(1)}, u32[]{:S(2)}, u32[]{:S(2)}) collective-permute-start(f32[8,3456]{1,0:T(8,128)S(1)} %add.191), channel_id=1, source_target_pairs={{0,2},{6,4},{1,3},{7,5},{8,10},{14,12},{9,11},{15,13},{16,18},{22,... | collective-permute-start | bytes 331784 | tf_op jit(solution)/shard_map/ppermute | solution.py:704
  249.0 13.8 %collective-permute-start.38 = (bf16[480,768]{1,0:T(8,128)(2,1)S(1)}, bf16[480,768]{1,0:T(8,128)(2,1)S(1)}, u32[]{:S(2)}, u32[]{:S(2)}) collective-permute-start(bf16[480,768]{1,0:T(8,128)(2,1)S(1)} %add_convert_fusion.1), channel_id=1, source_target_pairs={{2,0},{4,6},{3,1},{5,7},{10,8},{12,14},{11,9},{13,15},{18,16},{20,... | collective-permute-start | bytes 2211848 | tf_op jit(solution)/shard_map/ppermute | solution.py:712
  259.8 4.9 %collective-permute-start.40 = (bf16[3,192,384]{2,1,0:T(8,128)(2,1)S(1)}, bf16[3,192,384]{2,1,0:T(8,128)(2,1)S(1)}, u32[]{:S(2)}, u32[]{:S(2)}) collective-permute-start(bf16[3,192,384]{2,1,0:T(8,128)(2,1)S(1)} %add_convert_fusion.8), channel_id=1, source_target_pairs={{2,4},{4,2},{3,5},{5,3},{10,12},{12,10},{11,13},{13,11},{18,20},{2... | collective-permute-start | bytes 1327112 | tf_op jit(solution)/shard_map/ppermute | solution.py:708
  260.6 4.2 %collective-permute-start.39 = (f32[8,3456]{1,0:T(8,128)S(1)}, f32[8,3456]{1,0:T(8,128)S(1)}, u32[]{:S(2)}, u32[]{:S(2)}) collective-permute-start(f32[8,3456]{1,0:T(8,128)S(1)} %add.193), channel_id=1, source_target_pairs={{2,4},{4,2},{3,5},{5,3},{10,12},{12,10},{11,13},{13,11},{18,20},{2... | collective-permute-start | bytes 331784 | tf_op jit(solution)/shard_map/ppermute | solution.py:708
  261.2 12.8 %collective-permute-start.37 = (bf16[512,768]{1,0:T(8,128)(2,1)S(1)}, bf16[512,768]{1,0:T(8,128)(2,1)S(1)}, u32[]{:S(2)}, u32[]{:S(2)}) collective-permute-start(bf16[512,768]{1,0:T(8,128)(2,1)S(1)} %get-tuple-element.327), channel_id=1, source_target_pairs={{0,1},{1,0},{2,3},{3,2},{4,5},{5,4},{6,7},{7,6},{8,9},{9,8},{10,11... | collective-permute-start | bytes 2359304 | tf_op jit(solution)/shard_map/ppermute | solution.py:689
  261.5 21.3 %collective-permute-start.42 = (bf16[192,1536]{1,0:T(8,128)(2,1)S(1)}, bf16[192,1536]{1,0:T(8,128)(2,1)S(1)}, u32[]{:S(2)}, u32[]{:S(2)}) collective-permute-start(bf16[192,1536]{1,0:T(8,128)(2,1)S(1)} %add_convert_fusion.5), channel_id=1, source_target_pairs={{2,0},{4,6},{3,1},{5,7},{10,8},{12,14},{11,9},{13,15},{18,16},{20,... | collective-permute-start | bytes 1769480 | tf_op jit(solution)/shard_map/ppermute | solution.py:712
  264.8 19.2 %collective-permute-start.43 = (f32[8,3456]{1,0:T(8,128)S(1)}, f32[8,3456]{1,0:T(8,128)S(1)}, u32[]{:S(2)}, u32[]{:S(2)}) collective-permute-start(f32[8,3456]{1,0:T(8,128)S(1)} %add.197), channel_id=1, source_target_pairs={{2,0},{4,6},{3,1},{5,7},{10,8},{12,14},{11,9},{13,15},{18,16},{20,... | collective-permute-start | bytes 331784 | tf_op jit(solution)/shard_map/ppermute | solution.py:712
  266.2 22.5 %collective-permute-start.41 = (bf16[3,192,384]{2,1,0:T(8,128)(2,1)S(1)}, bf16[3,192,384]{2,1,0:T(8,128)(2,1)S(1)}, u32[]{:S(2)}, u32[]{:S(2)}) collective-permute-start(bf16[3,192,384]{2,1,0:T(8,128)(2,1)S(1)} %add_convert_fusion.7), channel_id=1, source_target_pairs={{2,0},{4,6},{3,1},{5,7},{10,8},{12,14},{11,9},{13,15},{18,16},{20,... | collective-permute-start | bytes 1327112 | tf_op jit(solution)/shard_map/ppermute | solution.py:712
  282.8 6.9 %copy-start.1 = (s32[2,1024]{1,0:T(2,128)S(1)}, s32[2,1024]{1,0:T(2,128)}, u32[]{:S(2)}) copy-start(s32[2,1024]{1,0:T(2,128)} %param.12) | copy-start | bytes 24580
  (26 other events, 65.4 us)

commit v7 on v6

--- a/solution.py
+++ b/solution.py
@@ -738,9 +738,8 @@
     qkv_y = y_swap(qkv_piece)
     bias_rows = jnp.concatenate([fc_bias.reshape(-1, D), qv_bias.reshape(1, D), jnp.zeros((13, D), BF16)], 0)
     res_own, res_send = unpack_rows(after(place, qkv_piece), residual_in, bias_rows)
-    qkv_y, res_own, res_send, out_gated, fc_gated, proj_gated = meet(
-        qkv_y, res_own, res_send, out_weight, fc_weight, proj_weight)
     res_other = y_swap(res_send)
+    qkv_y, res_own, out_gated, fc_gated, proj_gated = meet(qkv_y, res_own, out_weight, fc_weight, proj_weight)
     qkv_x = x_swap(qkv_y)
     qkv_c = c_swap(qkv_y)
     fc_piece = piece_of(fc_gated, 0, quarter_at)
@@ -819,10 +818,10 @@
         fc_far = add_low(fc_k[0, 1], fc_c[0, 1], fc_y[1])
         fc_x = x_swap(fc_far)
         own_a, sums_a = backward(after(attended_grad, fc_far), log_sums, 0, pairs - 1)
-        own_a, sums_a, proj_y, proj_xm, proj_k, proj_c, fc_x, qo_k, qo_c = meet(
-            own_a, sums_a, proj_y, proj_xm, proj_k, proj_c, fc_x, qo_k, qo_c)
+        own_a, sums_a, proj_y, proj_xm, proj_k, proj_c = meet(own_a, sums_a, proj_y, proj_xm, proj_k, proj_c)
         proj_shard = add_low(proj_k[0, 0], proj_c[0, 0], proj_xm, proj_y)
         proj_z = chain_in(proj_shard)
+        proj_shard, fc_x, qo_k, qo_c = meet(proj_shard, fc_x, qo_k, qo_c)
         fc_shard = add_low(fc_k[0, 0], fc_c[0, 0], fc_y[0], fc_x)
         fc_z = chain_in(fc_shard)
         qo_f = add_low(qo_k[1], qo_c[1])
@@ -832,7 +831,8 @@
         qm_k, qm_s, qm_sum, qo_k, qo_c, qo_x = meet(qm_k, qm_s, qm_sum, qo_k, qo_c, qo_x)
         qm_c = c_swap(qm_s)
         in_sums = (qm_sum + qo_sum) / gains[0:1]
-        small = jnp.concatenate([in_sums, middle_sums, own_sums, other_sums, sums_a, sums_b, first_sums], 1)
+        small = jnp.concatenate(
+            [value[:4] for value in (in_sums, middle_sums, own_sums, other_sums, sums_a, sums_b, first_sums)], 1)
         small_c = c_swap(small)
         qo_r = add_low(qo_k[0], qo_c[0], qo_x)
         qo_y = y_swap(qo_r)
@@ -845,24 +845,24 @@
         proj_shard = add_low(proj_shard, proj_z)
         proj_z = chain_across(proj_shard)
         block_out = restore(after(out_mine, proj_shard), *out_got)
-        block_out, fc_shard, fc_z, small, small_x = meet(block_out, fc_shard, fc_z, small, small_x)
-        fc_shard = add_low(fc_shard, fc_z)
-        fc_z = chain_across(fc_shard)
+        block_out, small, small_x = meet(block_out, small, small_x)
         small = small + small_x
         split = 2 * D + hid
         mine = jnp.concatenate([small[:, :split], small[:, split + hid : split + hid + half]], 1)
         other = jnp.concatenate([small[:, : 2 * D], small[:, split : split + hid], small[:, split + hid + half :]], 1)
         small_y = y_swap(other)
-        qm_k, qm_c, qm_x, qo_y, fc_shard, mine, small_y, proj_shard, proj_z = meet(
-            qm_k, qm_c, qm_x, qo_y, fc_shard, mine, small_y, proj_shard, proj_z)
+        qm_k, qm_c, qm_x, qo_y, mine, small_y = meet(qm_k, qm_c, qm_x, qo_y, mine, small_y)
         last = add_low(qm_k[0], qm_c[0], qm_x, qo_y)
         last_z = chain_in(last)
         small = mine + small_y
         small_z = chain_in(small)
-        proj_shard = add_low(after(proj_shard, last, small), proj_z)
+        fc_shard, fc_z, proj_shard, proj_z, last, small = meet(fc_shard, fc_z, proj_shard, proj_z, last, small)
+        fc_shard = add_low(fc_shard, fc_z)
+        fc_z = chain_across(fc_shard)
+        proj_shard = add_low(proj_shard, proj_z)
         proj_z = chain_out(proj_shard)
         in_mine, in_send = input_grad(
-            after(place, last, proj_shard, small), [own_a, own_b], [first], res_own, res_other, middle_grad,
+            after(place, last, proj_shard, fc_shard, small), [own_a, own_b], [first], res_own, res_other, middle_grad,
             gains[0:1], qkv_weight, qkv_others)
         in_mine, in_send, last, last_z, fc_shard, fc_z, small, small_z = meet(
             in_mine, in_send, last, last_z, fc_shard, fc_z, small, small_z)

time: 295 us -> 288 us (0.976)
  starting transfers between devices: 50.5 us -> 43.9 us
  waiting for transfers between devices: 49.7 us -> 45.8 us
    ppermute x4, waiting for transfers between devices: 6.43 us -> 13.7 us  [chain_out(): return lax.ppermute(value, 'group', [(1, 0), (2, 3)])]
    ppermute x4, waiting for transfers between devices: 6.99 us -> 0.01 us  [chain_in(): return lax.ppermute(value, 'group', [(0, 1), (3, 2)])]
    ppermute x4, starting transfers between devices: 15.3 us -> 10.3 us  [chain_in(): return lax.ppermute(value, 'group', [(0, 1), (3, 2)])]
    ppermute x32, waiting for transfers between devices: 36.2 us -> 32.1 us  [swap(): return lax.ppermute(value, axis, [(n, n ^ bit) for n in range(size)])]
  transfers between devices with their start and end apart: 44 -> 44, of which waited for: 19 -> 20; matrix products, arithmetic and copies ran while one was open for 8% -> 10% of each run, Pallas kernels for 38% -> 39%
where the time goes in v7:
time: 288 us; the launch traced here: 282 us
  Pallas kernels  146 us (51%)
  waiting for transfers between devices  45.8 us (16%)
  starting transfers between devices  43.9 us (15%)
  local copies, waits for them, and re-layouts  26.5 us (9%)
  other arithmetic  17.7 us (6%)
    pallas_call x1, Pallas kernels, middle_stage(): pl.pallas_call(body, grid_spec=pltpu.PrefetchScalarGridSpec(num_scalar_pr...  35.2 us
    pallas_call x3, Pallas kernels, attend_backward(): pl.pallas_call(functools.partial(attend_backward_kernel, block=length //...  34.3 us
    ppermute x32, waiting for transfers between devices, swap(): return lax.ppermute(value, axis, [(n, n ^ bit) for n in range(size)])  32.1 us
    ppermute x32, starting transfers between devices, swap(): return lax.ppermute(value, axis, [(n, n ^ bit) for n in range(size)])  25.3 us
    pallas_call x2, Pallas kernels, attend_forward(): pl.pallas_call(body, grid_spec=pltpu.PrefetchScalarGridSpec(num_scalar_pr...  18.8 us
    unnamed x100, local copies, waits for them, and re-layouts  16 us
    ppermute x4, waiting for transfers between devices, chain_out(): return lax.ppermute(value, 'group', [(1, 0), (2, 3)])  13.7 us
    convert_element_type x17, other arithmetic, add_low(): return total.astype(BF16)  11.8 us
  transfers between devices with their start and end apart: 44, of which 20 were waited for; matrix products, arithmetic and copies ran while one was open for 10% of the time, Pallas kernels for 39%

profile of v7, /device:TPU:0, one launch (start us, length us, event | category | flops | bytes accessed | tf_op | source)
XLA Modules:
  0.0 282.0 jit_solution(11902085986713371257)
XLA Ops:
  1.7 3.0 %collective-permute-start = (bf16[3,192,384]{2,1,0:T(8,128)(2,1)S(1)}, bf16[3,192,384]{2,1,0:T(8,128)(2,1)}, u32[]{:S(2)}, u32[]{:S(2)}) collective-permute-start(bf16[3,192,384]{2,1,0:T(8,128)(2,1)S(1)} %constant_dynamic-slice_fusion.5), channel_id=1, source_target_pairs={{0,1},{1,0},{2,3},{3,2},{4,5},{5,4},{6,7},{7,6},{8,9},{9,8},{10,11... | collective-permute-start | bytes 1327112 | tf_op jit(solution)/shard_map/ppermute | solution.py:689
  6.4 1.4 copy-done.12
  7.8 4.1 %unpack_rows.2 = (bf16[512,768]{1,0:T(8,128)(2,1)S(1)}, bf16[528,768]{1,0:T(8,128)(2,1)}) custom-call(s32[3]{0:T(128)S(1)} %pad_add_fusion.place_ref, bf16[767,2,512]{2,1,0:T(2,128)(2,1)S(1)} %bitcast.55, bf16[16,768]{1,0:T(8,128)(2,1)S(1)} %maximum_maximum_fusion.refs_0_), custom_call_target="tpu_custom_call" | custom-call | flops 2000000000 | bytes 2000000 | tf_op jit(solution)/shard_map/unpack_rows/pallas_call | solution.py:192
  13.0 2.3 collective-permute-done.a.refs_1_.refs_8_
  15.3 1.4 collective-permute-start.1
  16.8 3.3 %pad.20.refs_10_ = bf16[1536,768]{1,0:T(8,128)(2,1)} pad(bf16[1536,767]{1,0:T(8,128)(2,1)} %param.19, bf16[]{:T(256)} %constant.14.clone.1), padding=0_0x0_1 | pad | bytes 4715522 | tf_op jit(solution)/shard_map/jit(_pad)/pad | solution.py:753
  25.1 2.4 collective-permute-start.5
  27.6 3.3 %unpack_rows.3 = (bf16[512,768]{1,0:T(8,128)(2,1)S(1)}, bf16[512,768]{1,0:T(8,128)(2,1)S(1)}) custom-call(s32[3]{0:T(128)S(1)} %pad_add_fusion.place_ref, bf16[767,2,512]{2,1,0:T(2,128)(2,1)S(1)} %bitcast.56), custom_call_target="tpu_custom_call" | custom-call | flops 2000000000 | bytes 2000000 | tf_op jit(solution)/shard_map/unpack_rows/pallas_call | solution.py:192
  32.7 1.3 collective-permute-done.2.other_ref.refs_2_.refs_4_
  34.1 2.1 collective-permute-done.4.d.refs_4_.refs_11_
  38.3 7.9 %norm_project.1 = (bf16[1024,768]{1,0:T(8,128)(2,1)S(1)}, bf16[1024,768]{1,0:T(8,128)(2,1)S(1)}, bf16[1024,768]{1,0:T(8,128)(2,1)S(1)}, bf16[1024,768]{1,0:T(8,128)(2,1)S(1)}) custom-call(s32[3]{0:T(128)S(1)} %pad_add_fusion.place_ref, bf16[512,768]{1,0:T(8,128)(2,1)S(1)} %copy-done.21, ...), custom_call_target="tpu_custom_call" | custom-call | flops 4000000000 | bytes 4000000 | tf_op jit(solution)/shard_map/norm_project/pallas_call | solution.py:283
  46.3 1.2 collective-permute-start.9
  47.5 9.4 %attend_forward.2 = (bf16[1024,768]{1,0:T(8,128)(2,1)S(1)}, f32[6,8,1024]{2,1,0:T(8,128)S(1)}) custom-call(s32[4]{0:T(128)S(1)} %compare_convert_fusion.flags_ref, bf16[1024,768]{1,0:T(8,128)(2,1)S(1)} %get-tuple-element.210.q_ref, bf16[1024,768]{1,0:T(8,128)(2,1)S(1)} %get-tuple-element.206.k_ref, bf16[1024,768]{1,0:T(8,128)(2,1)S(1)} %get-tuple-element.207.v_ref), custom_call_target="tpu_custom_call" | custom-call | flops 4560000000 | bytes 4559999 | tf_op jit(solution)/shard_map/attend_forward/pallas_call | solution.py:88
  56.9 5.7 %collective-permute-done.6.refs_15_ = bf16[384,768]{1,0:T(8,128)(2,1)} collective-permute-done((bf16[384,768]{1,0:T(8,128)(2,1)}, bf16[384,768]{1,0:T(8,128)(2,1)}, u32[]{:S(2)}, u32[]{:S(2)}) %collective-permute-start.6) | collective-permute-done | bytes 589856 | tf_op jit(solution)/shard_map/ppermute | solution.py:689
  62.6 1.6 collective-permute-start.7
  64.2 1.6 collective-permute-start.8
  65.8 9.4 %attend_forward.3 = (bf16[1024,768]{1,0:T(8,128)(2,1)S(1)}, f32[6,8,1024]{2,1,0:T(8,128)S(1)}) custom-call(s32[4]{0:T(128)S(1)} %compare_convert_fusion.flags_ref, bf16[1024,768]{1,0:T(8,128)(2,1)S(1)} %get-tuple-element.210.q_ref, bf16[1024,768]{1,0:T(8,128)(2,1)S(1)} %get-tuple-element.206.k_ref, ...), custom_call_target="tpu_custom_call", output_to_operand_aliasing={{0}: (4, {}), {1}: (5, {})} | custom-call | flops 4560000000 | bytes 4559999 | tf_op jit(solution)/shard_map/attend_forward/pallas_call | solution.py:88
  75.8 2.0 collective-permute-done.9.refs_4_.other_cot
  79.1 3.1 %collective-permute-done.12.refs_16_ = bf16[384,768]{1,0:T(8,128)(2,1)S(1)} collective-permute-done((bf16[384,768]{1,0:T(8,128)(2,1)}, bf16[384,768]{1,0:T(8,128)(2,1)S(1)}, u32[]{:S(2)}, u32[]{:S(2)}) %collective-permute-start.12) | collective-permute-done | bytes 589856 | tf_op jit(solution)/shard_map/ppermute | solution.py:689
  82.4 35.2 %middle_stage.1 = (bf16[1024,768]{1,0:T(8,128)(2,1)S(1)}, bf16[1024,3072]{1,0:T(8,128)(2,1)}, bf16[1024,3072]{1,0:T(8,128)(2,1)}, bf16[512,768]{1,0:T(8,128)(2,1...) custom-call(s32[3]{0:T(128)S(1)} %pad_add_fusion.place_ref, ...), custom_call_target="tpu_custom_call" | custom-call | flops 15200000000 | bytes 15200000 | tf_op jit(solution)/shard_map/middle_stage/pallas_call | solution.py:427
  118.8 1.7 collective-permute-start.14
  120.5 2.8 copy-done.24
  123.2 8.3 %proj_grad.1 = (bf16[2,2,480,768]{3,2,1,0:T(8,128)(2,1)S(1)}, bf16[2,2,480,768]{3,2,1,0:T(8,128)(2,1)S(1)}) custom-call(s32[3]{0:T(128)S(1)} %pad_add_fusion.place_ref, bf16[1024,3072]{1,0:T(8,128)(2,1)S(1)} %copy-done.24, bf16[1024,3072]{1,0:T(8,128)(2,1)S(1)} %copy-done.24, bf16[512,768]{1,0:T(8,128)(2,1)S(1)} %copy-done.26, ...), custom_call_target="tpu_custom_call" | custom-call | flops 5200000000 | bytes 5200000 | tf_op jit(solution)/shard_map/proj_grad/pallas_call | solution.py:568
  132.2 8.0 %fc_grad.1 = (bf16[2,2,192,1536]{3,2,1,0:T(8,128)(2,1)S(1)}, bf16[2,2,192,1536]{3,2,1,0:T(8,128)(2,1)}) custom-call(s32[3]{0:T(128)S(1)} %pad_add_fusion.place_ref, bf16[1024,768]{1,0:T(8,128)(2,1)S(1)} %get-tuple-element.236.left_ref, bf16[1024,3072]{1,0:T(8,128)(2,1)S(1)} %copy-done.38), custom_call_target="tpu_custom_call" | custom-call | flops 4800000000 | bytes 4800000 | tf_op jit(solution)/shard_map/fc_grad/pallas_call | solution.py:468
  140.2 1.4 copy-done.2
  141.6 1.6 collective-permute-done.16.second_ref
  144.0 1.4 fusion.13
  145.4 1.8 collective-permute-start.18
  147.2 1.4 fusion.14
  149.0 1.8 fusion.4
  151.2 1.4 copy-done.34
  152.6 16.8 %attend_backward.3 = (bf16[3,1024,384]{2,1,0:T(8,128)(2,1)S(1)}, f32[8,384]{1,0:T(8,128)S(1)}) custom-call(s32[4]{0:T(128)S(1)} %compare_convert_fusion.flags_ref, bf16[1024,768]{1,0:T(8,128)(2,1)S(1)} %copy-done.28, bf16[1024,768]{1,0:T(8,128)(2,1)S(1)} %copy-done.30, bf16[1024,768]{1,0:T(8,128)(2,1)S(1)} %copy-done.32, bf16[1024,768]{1,0:T(8,128)(2,1)S(1)} %copy-done.34, ...), custom_call_target="tpu_custom_call" | custom-call | flops 7600000000 | bytes 7600000 | tf_op jit(solution)/shard_map/attend_backward/pallas_call | solution.py:155
  169.5 1.6 fusion.2
  171.0 1.8 collective-permute-start.20
  172.8 4.7 %qkv_grad.2 = (bf16[2,3,192,384]{3,2,1,0:T(8,128)(2,1)S(1)}, bf16[2,3,192,384]{3,2,1,0:T(8,128)(2,1)S(1)}, f32[8,768]{1,0:T(8,128)S(1)}) custom-call(s32[3]{0:T(128)S(1)} %pad_add_fusion.place_ref, bf16[1024,768]{1,0:T(8,128)(2,1)S(1)} %copy-done.37, bf16[3,1024,384]{2,1,0:T(8,128)(2,1)S(1)} %get-tuple-element.259.refs_0_.refs_2_, ...), custom_call_target="tpu_custom_call" | custom-call | flops 2600000000 | bytes 2600000 | tf_op jit(solution)/shard_map/qkv_grad/pallas_call | solution.py:526
  177.5 2.2 collective-permute-done.19
  179.7 1.3 fusion.7
  181.0 1.6 collective-permute-start.22
  182.6 11.8 %attend_backward.4 = (bf16[3,1024,256]{2,1,0:T(8,128)(2,1)S(1)}, f32[8,256]{1,0:T(8,128)S(1)}) custom-call(s32[4]{0:T(128)S(1)} %compare_convert_fusion.flags_ref, bf16[1024,768]{1,0:T(8,128)(2,1)S(1)} %copy-done.28, bf16[1024,768]{1,0:T(8,128)(2,1)S(1)} %copy-done.30, bf16[1024,768]{1,0:T(8,128)(2,1)S(1)} %copy-done.32, bf16[1024,768]{1,0:T(8,128)(2,1)S(1)} %copy-done.35, ...), custom_call_target="tpu_custom_call" | custom-call | flops 5200000000 | bytes 5200000 | tf_op jit(solution)/shard_map/attend_backward/pallas_call | solution.py:155
  194.4 1.5 fusion.1
  195.9 3.7 %collective-permute-start.27 = (bf16[480,768]{1,0:T(8,128)(2,1)S(1)}, bf16[480,768]{1,0:T(8,128)(2,1)S(1)}, u32[]{:S(2)}, u32[]{:S(2)}) collective-permute-start(bf16[480,768]{1,0:T(8,128)(2,1)S(1)} %fusion.1), channel_id=1, source_target_pairs={{0,2},{6,4},{1,3},{7,5},{8,10},{14,12},{9,11},{15,13},{16,18},{22,... | collective-permute-start | bytes 2211848 | tf_op jit(solution)/shard_map/ppermute | solution.py:704
  199.7 1.4 fusion.6
  201.2 1.4 collective-permute-start.24
  202.6 1.5 collective-permute-start.29
  204.1 5.7 %attend_backward.5 = (bf16[3,1024,128]{2,1,0:T(8,128)(2,1)S(1)}, f32[8,128]{1,0:T(8,128)S(1)}) custom-call(s32[4]{0:T(128)S(1)} %compare_convert_fusion.flags_ref, bf16[1024,768]{1,0:T(8,128)(2,1)S(1)} %copy-done.28, bf16[1024,768]{1,0:T(8,128)(2,1)S(1)} %copy-done.30, bf16[1024,768]{1,0:T(8,128)(2,1)S(1)} %copy-done.32, bf16[1024,768]{1,0:T(8,128)(2,1)S(1)} %copy-done.35, ...), custom_call_target="tpu_custom_call" | custom-call | flops 2800000000 | bytes 2800000 | tf_op jit(solution)/shard_map/attend_backward/pallas_call | solution.py:155
  209.8 3.0 %qkv_grad.3 = (bf16[2,3,192,384]{3,2,1,0:T(8,128)(2,1)S(1)}, bf16[2,3,192,384]{3,2,1,0:T(8,128)(2,1)S(1)}, f32[8,768]{1,0:T(8,128)S(1)}) custom-call(s32[3]{0:T(128)S(1)} %pad_add_fusion.place_ref, bf16[1024,768]{1,0:T(8,128)(2,1)S(1)} %copy-done.37, bf16[3,1024,256]{2,1,0:T(8,128)(2,1)S(1)} %get-tuple-element.281.refs_0_, ...), custom_call_target="tpu_custom_call" | custom-call | flops 2600000000 | bytes 2600000 | tf_op jit(solution)/shard_map/qkv_grad/pallas_call | solution.py:526
  214.3 1.4 collective-permute-done.26
  216.8 1.2 collective-permute-start.31
  219.0 4.7 %pack_rows.2 = bf16[767,2,512]{2,1,0:T(2,128)(2,1)} custom-call(s32[3]{0:T(128)S(1)} %pad_add_fusion.place_ref, bf16[512,768]{1,0:T(8,128)(2,1)S(1)} %copy-done.5, bf16[256,768]{1,0:T(8,128)(2,1)S(1)} %collective-permute-done.14.first_ref, bf16[256,768]{1,0:T(8,128)(2,1)S(1)} %copy-done.7), custom_call_target="tpu_custom_call" | custom-call | flops 40000000 | bytes 40000 | tf_op jit(solution)/shard_map/pack_rows/pallas_call | solution.py:673
  224.2 2.0 collective-permute-done.32
  226.2 1.8 collective-permute-done.33
  228.0 1.9 collective-permute-done.31
  230.1 3.8 %collective-permute-start.34 = (bf16[3,192,384]{2,1,0:T(8,128)(2,1)S(1)}, bf16[3,192,384]{2,1,0:T(8,128)(2,1)S(1)}, u32[]{:S(2)}, u32[]{:S(2)}) collective-permute-start(bf16[3,192,384]{2,1,0:T(8,128)(2,1)S(1)} %fusion.9), channel_id=1, source_target_pairs={{0,2},{6,4},{1,3},{7,5},{8,10},{14,12},{9,11},{15,13},{16,18},{22,... | collective-permute-start | bytes 1327112 | tf_op jit(solution)/shard_map/ppermute | solution.py:704
  233.9 1.3 collective-permute-start.36
  236.5 1.5 collective-permute-start.38
  238.0 9.1 %input_grad.1 = (bf16[512,768]{1,0:T(8,128)(2,1)S(1)}, bf16[512,768]{1,0:T(8,128)(2,1)S(1)}) custom-call(s32[3]{0:T(128)S(1)} %pad_add_fusion.place_ref, bf16[3,1024,256]{2,1,0:T(8,128)(2,1)S(1)} %get-tuple-element.281.refs_0_, bf16[3,1024,128]{2,1,0:T(8,128)(2,1)S(1)} %get-tuple-element.279.refs_1_, ...), custom_call_target="tpu_custom_call" | custom-call | flops 3600000000 | bytes 3600000 | tf_op jit(solution)/shard_map/input_grad/pallas_call | solution.py:642
  249.2 1.3 collective-permute-start.42
  250.5 6.3 %collective-permute-done.38 = bf16[480,768]{1,0:T(8,128)(2,1)S(1)} collective-permute-done((bf16[480,768]{1,0:T(8,128)(2,1)S(1)}, bf16[480,768]{1,0:T(8,128)(2,1)S(1)}, u32[]{:S(2)}, u32[]{:S(2)}) %collective-permute-start.38) | collective-permute-done | bytes 737312 | tf_op jit(solution)/shard_map/ppermute | solution.py:712
  258.7 1.3 collective-permute-start.43
  260.2 1.3 collective-permute-start.41
  261.5 3.6 %collective-permute-done.37.first_ref.second_ref = bf16[512,768]{1,0:T(8,128)(2,1)S(1)} collective-permute-done((bf16[512,768]{1,0:T(8,128)(2,1)S(1)}, bf16[512,768]{1,0:T(8,128)(2,1)S(1)}, u32[]{:S(2)}, u32[]{:S(2)}) %collective-permute-start.37) | collective-permute-done | bytes 786464 | tf_op jit(solution)/shard_map/ppermute | solution.py:689
  265.1 4.7 %pack_rows.3 = bf16[767,2,512]{2,1,0:T(2,128)(2,1)} custom-call(s32[3]{0:T(128)S(1)} %pad_add_fusion.place_ref, bf16[512,768]{1,0:T(8,128)(2,1)S(1)} %get-tuple-element.344.own_ref, bf16[512,768]{1,0:T(8,128)(2,1)S(1)} %collective-permute-done.37.first_ref.second_ref, bf16[512,768]{1,0:T(8,128)(2,1)S(1)} %collective-permute-done.37.first_ref.second_ref), custom_call_target="tpu_custom_call" | custom-call | flops 40000000 | bytes 40000 | tf_op jit(solution)/shard_map/pack_rows/pallas_call | solution.py:673
  269.8 4.9 %collective-permute-done.42 = bf16[192,1536]{1,0:T(8,128)(2,1)S(1)} collective-permute-done((bf16[192,1536]{1,0:T(8,128)(2,1)S(1)}, bf16[192,1536]{1,0:T(8,128)(2,1)S(1)}, u32[]{:S(2)}, u32[]{:S(2)}) %collective-permute-start.42) | collective-permute-done | bytes 589856 | tf_op jit(solution)/shard_map/ppermute | solution.py:712
  278.3 2.5 collective-permute-done.41
  (207 shorter events, 32.3 us)
Async XLA Ops:
  0.6 12.2 %copy-start = (s32[2,1024]{1,0:T(2,128)S(1)}, s32[2,1024]{1,0:T(2,128)}, u32[]{:S(2)}) copy-start(s32[2,1024]{1,0:T(2,128)} %param.12) | copy-start | bytes 24580
  1.7 13.6 %collective-permute-start = (bf16[3,192,384]{2,1,0:T(8,128)(2,1)S(1)}, bf16[3,192,384]{2,1,0:T(8,128)(2,1)}, u32[]{:S(2)}, u32[]{:S(2)}) collective-permute-start(bf16[3,192,384]{2,1,0:T(8,128)(2,1)S(1)} %constant_dynamic-slice_fusion.5), channel_id=1, source_target_pairs={{0,1},{1,0},{2,3},{3,2},{4,5},{5,4},{6,7},{7,6},{8,9},{9,8},{10,11... | collective-permute-start | bytes 1327112 | tf_op jit(solution)/shard_map/ppermute | solution.py:689
  7.8 5.2 %copy-start.42 = (bf16[2,768]{1,0:T(2,128)(2,1)S(1)}, bf16[2,768]{1,0:T(2,128)(2,1)}, u32[]{:S(2)}) copy-start(bf16[2,768]{1,0:T(2,128)(2,1)} %param.13) | copy-start | bytes 9220
  12.8 21.2 %collective-permute-start.2 = (bf16[528,768]{1,0:T(8,128)(2,1)}, bf16[528,768]{1,0:T(8,128)(2,1)S(1)}, u32[]{:S(2)}, u32[]{:S(2)}) collective-permute-start(bf16[528,768]{1,0:T(8,128)(2,1)} %get-tuple-element.192), channel_id=1, source_target_pairs={{0,1},{1,0},{2,3},{3,2},{4,5},{5,4},{6,7},{7,6},{8,9},{9,8},{10,11... | collective-permute-start | bytes 2433032 | tf_op jit(solution)/shard_map/ppermute | solution.py:689
  15.3 9.0 %collective-permute-start.3 = (bf16[3,192,384]{2,1,0:T(8,128)(2,1)}, bf16[3,192,384]{2,1,0:T(8,128)(2,1)S(1)}, u32[]{:S(2)}, u32[]{:S(2)}) collective-permute-start(bf16[3,192,384]{2,1,0:T(8,128)(2,1)} %collective-permute-done.a.refs_1_.refs_8_), channel_id=1, source_target_pairs={{0,8},{8,0},{16,24},{24,16},{1,9},{9,1},{17,25},{25,17},{2,10},{10... | collective-permute-start | bytes 1327112 | tf_op jit(solution)/shard_map/ppermute | solution.py:689
  15.3 18.7 %collective-permute-start.1 = (bf16[3,192,384]{2,1,0:T(8,128)(2,1)}, bf16[3,192,384]{2,1,0:T(8,128)(2,1)}, u32[]{:S(2)}, u32[]{:S(2)}) collective-permute-start(bf16[3,192,384]{2,1,0:T(8,128)(2,1)} %collective-permute-done.a.refs_1_.refs_8_), channel_id=1, source_target_pairs={{0,16},{8,24},{16,0},{24,8},{1,17},{9,25},{17,1},{25,9},{2,18},{10... | collective-permute-start | bytes 1327112 | tf_op jit(solution)/shard_map/ppermute | solution.py:689
  22.2 5.4 %copy-start.13 = (bf16[2,512,767]{1,0,2:T(2,128)(2,1)S(1)}, bf16[2,512,767]{1,0,2:T(2,128)(2,1)}, u32[]{:S(2)}) copy-start(bf16[2,512,767]{1,0,2:T(2,128)(2,1)} %param.21) | copy-start | bytes 4712452
  25.1 37.5 %collective-permute-start.5 = (bf16[480,768]{1,0:T(8,128)(2,1)}, bf16[480,768]{1,0:T(8,128)(2,1)}, u32[]{:S(2)}, u32[]{:S(2)}) collective-permute-start(bf16[480,768]{1,0:T(8,128)(2,1)} %fusion.12), channel_id=1, source_target_pairs={{0,1},{1,0},{2,3},{3,2},{4,5},{5,4},{6,7},{7,6},{8,9},{9,8},{10,11... | collective-permute-start | bytes 2211848 | tf_op jit(solution)/shard_map/ppermute | solution.py:689
  27.5 35.0 %collective-permute-start.6 = (bf16[384,768]{1,0:T(8,128)(2,1)}, bf16[384,768]{1,0:T(8,128)(2,1)}, u32[]{:S(2)}, u32[]{:S(2)}) collective-permute-start(bf16[384,768]{1,0:T(8,128)(2,1)} %pad.22), channel_id=1, source_target_pairs={{0,1},{1,0},{2,3},{3,2},{4,5},{5,4},{6,7},{7,6},{8,9},{9,8},{10,11... | collective-permute-start | bytes 1769480 | tf_op jit(solution)/shard_map/ppermute | solution.py:689
  27.6 8.6 %copy-start.8 = (bf16[3,768,384]{2,1,0:T(8,128)(2,1)S(1)}, bf16[3,768,384]{2,1,0:T(8,128)(2,1)}, u32[]{:S(2)}) copy-start(bf16[3,768,384]{2,1,0:T(8,128)(2,1)} %refs_7_.1) | copy-start | bytes 5308420
  34.0 48.3 %copy-start.10 = (bf16[528,768]{1,0:T(8,128)(2,1)}, bf16[528,768]{1,0:T(8,128)(2,1)S(1)}, u32[]{:S(2)}) copy-start(bf16[528,768]{1,0:T(8,128)(2,1)S(1)} %collective-permute-done.2.other_ref.refs_2_.refs_4_) | copy-start | bytes 2433028
  34.0 2.1 collective-permute-start.4
  38.3 7.9 %copy-start.15 = (bf16[512,768]{1,0:T(8,128)(2,1)S(1)}, bf16[512,768]{1,0:T(8,128)(2,1)}, u32[]{:S(2)}) copy-start(bf16[512,768]{1,0:T(8,128)(2,1)} %copy-done.14) | copy-start | bytes 2359300
  46.2 10.7 %copy-start.36 = (bf16[1024,768]{1,0:T(8,128)(2,1)}, bf16[1024,768]{1,0:T(8,128)(2,1)S(1)}, u32[]{:S(2)}) copy-start(bf16[1024,768]{1,0:T(8,128)(2,1)S(1)} %get-tuple-element.258.left_ref) | copy-start | bytes 4718596
  46.2 19.5 %copy-start.27 = (bf16[1024,768]{1,0:T(8,128)(2,1)}, bf16[1024,768]{1,0:T(8,128)(2,1)S(1)}, u32[]{:S(2)}) copy-start(bf16[1024,768]{1,0:T(8,128)(2,1)S(1)} %get-tuple-element.210.q_ref) | copy-start | bytes 4718596
  46.2 19.5 %copy-start.29 = (bf16[1024,768]{1,0:T(8,128)(2,1)}, bf16[1024,768]{1,0:T(8,128)(2,1)S(1)}, u32[]{:S(2)}) copy-start(bf16[1024,768]{1,0:T(8,128)(2,1)S(1)} %get-tuple-element.206.k_ref) | copy-start | bytes 4718596
  46.2 19.5 %copy-start.31 = (bf16[1024,768]{1,0:T(8,128)(2,1)}, bf16[1024,768]{1,0:T(8,128)(2,1)S(1)}, u32[]{:S(2)}) copy-start(bf16[1024,768]{1,0:T(8,128)(2,1)S(1)} %get-tuple-element.207.v_ref) | copy-start | bytes 4718596
  46.3 31.6 %collective-permute-start.9 = (bf16[512,768]{1,0:T(8,128)(2,1)S(1)}, bf16[512,768]{1,0:T(8,128)(2,1)S(1)}, u32[]{:S(2)}, u32[]{:S(2)}) collective-permute-start(bf16[512,768]{1,0:T(8,128)(2,1)S(1)} %copy-done.15), channel_id=1, source_target_pairs={{0,1},{1,0},{2,3},{3,2},{4,5},{5,4},{6,7},{7,6},{8,9},{9,8},{10,11... | collective-permute-start | bytes 2359304 | tf_op jit(solution)/shard_map/ppermute | solution.py:689
  62.6 16.4 %copy-start.45 = (bf16[2,767]{1,0:T(2,128)(2,1)S(1)}, bf16[2,767]{1,0:T(2,128)(2,1)}, u32[]{:S(2)}) copy-start(bf16[2,767]{1,0:T(2,128)(2,1)} %param.20) | copy-start | bytes 9208
  62.6 16.4 %copy-start.43 = (bf16[1536]{0:T(1024)(128)(2,1)S(1)}, bf16[1536]{0:T(1024)(128)(2,1)}, u32[]{:S(2)}) copy-start(bf16[1536]{0:T(1024)(128)(2,1)} %param.18) | copy-start | bytes 9220
  62.6 19.8 %copy-start.22 = (bf16[512,768]{1,0:T(8,128)(2,1)S(1)}, bf16[512,768]{1,0:T(8,128)(2,1)}, u32[]{:S(2)}) copy-start(bf16[512,768]{1,0:T(8,128)(2,1)} %copy-done.20) | copy-start | bytes 2359300
  62.6 19.8 %copy-start.26 = (bf16[512,768]{1,0:T(8,128)(2,1)S(1)}, bf16[512,768]{1,0:T(8,128)(2,1)}, u32[]{:S(2)}) copy-start(bf16[512,768]{1,0:T(8,128)(2,1)} %copy-done.25) | copy-start | bytes 2359300
  62.6 15.9 %collective-permute-start.7 = (bf16[480,768]{1,0:T(8,128)(2,1)}, bf16[480,768]{1,0:T(8,128)(2,1)S(1)}, u32[]{:S(2)}, u32[]{:S(2)}) collective-permute-start(bf16[480,768]{1,0:T(8,128)(2,1)} %collective-permute-done.5.refs_11_), channel_id=1, source_target_pairs={{0,16},{8,24},{16,0},{24,8},{1,17},{9,25},{17,1},{25,9},{2,18},{10... | collective-permute-start | bytes 2211848 | tf_op jit(solution)/shard_map/ppermute | solution.py:689
  64.2 13.7 %collective-permute-start.8 = (bf16[384,768]{1,0:T(8,128)(2,1)}, bf16[384,768]{1,0:T(8,128)(2,1)S(1)}, u32[]{:S(2)}, u32[]{:S(2)}) collective-permute-start(bf16[384,768]{1,0:T(8,128)(2,1)} %collective-permute-done.6.refs_15_), channel_id=1, source_target_pairs={{0,2},{2,0},{4,6},{6,4},{1,3},{3,1},{5,7},{7,5},{8,10},{10,8},{12,... | collective-permute-start | bytes 1769480 | tf_op jit(solution)/shard_map/ppermute | solution.py:689
  65.7 16.5 %collective-permute-start.10 = (bf16[480,768]{1,0:T(8,128)(2,1)}, bf16[480,768]{1,0:T(8,128)(2,1)S(1)}, u32[]{:S(2)}, u32[]{:S(2)}) collective-permute-start(bf16[480,768]{1,0:T(8,128)(2,1)} %collective-permute-done.5.refs_11_), channel_id=1, source_target_pairs={{0,8},{8,0},{16,24},{24,16},{1,9},{9,1},{17,25},{25,17},{2,10},{10... | collective-permute-start | bytes 2211848 | tf_op jit(solution)/shard_map/ppermute | solution.py:689
  78.5 3.9 %collective-permute-start.11 = (bf16[480,768]{1,0:T(8,128)(2,1)S(1)}, bf16[480,768]{1,0:T(8,128)(2,1)S(1)}, u32[]{:S(2)}, u32[]{:S(2)}) collective-permute-start(bf16[480,768]{1,0:T(8,128)(2,1)S(1)} %collective-permute-done.7.refs_13_), channel_id=1, source_target_pairs={{0,8},{8,0},{16,24},{24,16},{1,9},{9,1},{17,25},{25,17},{2,10},{10... | collective-permute-start | bytes 2211848 | tf_op jit(solution)/shard_map/ppermute | solution.py:689
  78.5 3.7 %collective-permute-start.12 = (bf16[384,768]{1,0:T(8,128)(2,1)}, bf16[384,768]{1,0:T(8,128)(2,1)S(1)}, u32[]{:S(2)}, u32[]{:S(2)}) collective-permute-start(bf16[384,768]{1,0:T(8,128)(2,1)} %collective-permute-done.6.refs_15_), channel_id=1, source_target_pairs={{0,8},{8,0},{16,24},{24,16},{1,9},{9,1},{17,25},{25,17},{2,10},{10... | collective-permute-start | bytes 1769480 | tf_op jit(solution)/shard_map/ppermute | solution.py:689
  79.0 3.4 %collective-permute-start.13 = (bf16[384,768]{1,0:T(8,128)(2,1)S(1)}, bf16[384,768]{1,0:T(8,128)(2,1)S(1)}, u32[]{:S(2)}, u32[]{:S(2)}) collective-permute-start(bf16[384,768]{1,0:T(8,128)(2,1)S(1)} %collective-permute-done.8.refs_17_), channel_id=1, source_target_pairs={{0,8},{8,0},{16,24},{24,16},{1,9},{9,1},{17,25},{25,17},{2,10},{10... | collective-permute-start | bytes 1769480 | tf_op jit(solution)/shard_map/ppermute | solution.py:689
  118.8 12.8 %copy-start.4 = (bf16[512,768]{1,0:T(8,128)(2,1)}, bf16[512,768]{1,0:T(8,128)(2,1)S(1)}, u32[]{:S(2)}) copy-start(bf16[512,768]{1,0:T(8,128)(2,1)S(1)} %get-tuple-element.304.own_ref) | copy-start | bytes 2359300
  118.8 12.8 %collective-permute-start.14 = (bf16[256,768]{1,0:T(8,128)(2,1)S(1)}, bf16[256,768]{1,0:T(8,128)(2,1)S(1)}, u32[]{:S(2)}, u32[]{:S(2)}) collective-permute-start(bf16[256,768]{1,0:T(8,128)(2,1)S(1)} %get-tuple-element.233), channel_id=1, source_target_pairs={{0,1},{1,0},{2,3},{3,2},{4,5},{5,4},{6,7},{7,6},{8,9},{9,8},{10,11... | collective-permute-start | bytes 1179656 | tf_op jit(solution)/shard_map/ppermute | solution.py:689
  123.2 8.9 %copy-start.38 = (bf16[1024,3072]{1,0:T(8,128)(2,1)S(1)}, bf16[1024,3072]{1,0:T(8,128)(2,1)}, u32[]{:S(2)}) copy-start(bf16[1024,3072]{1,0:T(8,128)(2,1)} %get-tuple-element.237.right_ref) | copy-start | bytes 18874372
  131.6 12.4 %collective-permute-start.15 = (bf16[2,2,480,768]{3,2,1,0:T(8,128)(2,1)S(1)}, bf16[2,2,480,768]{3,2,1,0:T(8,128)(2,1)}, u32[]{:S(2)}, u32[]{:S(2)}) collective-permute-start(bf16[2,2,480,768]{3,2,1,0:T(8,128)(2,1)S(1)} %get-tuple-element.240), channel_id=1, source_target_pairs={{0,8},{8,0},{16,24},{24,16},{1,9},{9,1},{17,25},{25,17},{2,10},{10... | collective-permute-start | bytes 8847368 | tf_op jit(solution)/shard_map/ppermute | solution.py:689
  131.7 11.5 %collective-permute-start.16 = (bf16[256,768]{1,0:T(8,128)(2,1)S(1)}, bf16[256,768]{1,0:T(8,128)(2,1)S(1)}, u32[]{:S(2)}, u32[]{:S(2)}) collective-permute-start(bf16[256,768]{1,0:T(8,128)(2,1)S(1)} %get-tuple-element.242), channel_id=1, source_target_pairs={{0,1},{1,0},{2,3},{3,2},{4,5},{5,4},{6,7},{7,6},{8,9},{9,8},{10,11... | collective-permute-start | bytes 1179656 | tf_op jit(solution)/shard_map/ppermute | solution.py:689
  143.9 5.1 %collective-permute-start.17 = (bf16[2,2,192,1536]{3,2,1,0:T(8,128)(2,1)}, bf16[2,2,192,1536]{3,2,1,0:T(8,128)(2,1)}, u32[]{:S(2)}, u32[]{:S(2)}) collective-permute-start(bf16[2,2,192,1536]{3,2,1,0:T(8,128)(2,1)} %get-tuple-element.244), channel_id=1, source_target_pairs={{0,8},{8,0},{16,24},{24,16},{1,9},{9,1},{17,25},{25,17},{2,10},{10... | collective-permute-start | bytes 7077896 | tf_op jit(solution)/shard_map/ppermute | solution.py:689
  145.4 24.0 %collective-permute-start.18 = (bf16[480,768]{1,0:T(8,128)(2,1)S(1)}, bf16[480,768]{1,0:T(8,128)(2,1)S(1)}, u32[]{:S(2)}, u32[]{:S(2)}) collective-permute-start(bf16[480,768]{1,0:T(8,128)(2,1)S(1)} %fusion.13), channel_id=1, source_target_pairs={{0,16},{8,24},{16,0},{24,8},{1,17},{9,25},{17,1},{25,9},{2,18},{10... | collective-permute-start | bytes 2211848 | tf_op jit(solution)/shard_map/ppermute | solution.py:689
  148.7 45.8 %collective-permute-start.21 = (bf16[480,768]{1,0:T(8,128)(2,1)S(1)}, bf16[480,768]{1,0:T(8,128)(2,1)S(1)}, u32[]{:S(2)}, u32[]{:S(2)}) collective-permute-start(bf16[480,768]{1,0:T(8,128)(2,1)S(1)} %fusion.14), channel_id=1, source_target_pairs={{0,16},{8,24},{16,0},{24,8},{1,17},{9,25},{17,1},{25,9},{2,18},{10... | collective-permute-start | bytes 2211848 | tf_op jit(solution)/shard_map/ppermute | solution.py:689
  150.8 28.9 %collective-permute-start.19 = (bf16[2,192,1536]{2,1,0:T(8,128)(2,1)S(1)}, bf16[2,192,1536]{2,1,0:T(8,128)(2,1)S(1)}, u32[]{:S(2)}, u32[]{:S(2)}) collective-permute-start(bf16[2,192,1536]{2,1,0:T(8,128)(2,1)S(1)} %fusion.4), channel_id=1, source_target_pairs={{0,1},{1,0},{2,3},{3,2},{4,5},{5,4},{6,7},{7,6},{8,9},{9,8},{10,11... | collective-permute-start | bytes 3538952 | tf_op jit(solution)/shard_map/ppermute | solution.py:689
  171.0 23.4 %collective-permute-start.20 = (bf16[480,768]{1,0:T(8,128)(2,1)S(1)}, bf16[480,768]{1,0:T(8,128)(2,1)S(1)}, u32[]{:S(2)}, u32[]{:S(2)}) collective-permute-start(bf16[480,768]{1,0:T(8,128)(2,1)S(1)} %fusion.2), channel_id=1, source_target_pairs={{0,1},{1,0},{2,3},{3,2},{4,5},{5,4},{6,7},{7,6},{8,9},{9,8},{10,11... | collective-permute-start | bytes 2211848 | tf_op jit(solution)/shard_map/ppermute | solution.py:689
  177.5 5.1 %copy-start.35 = (bf16[1024,768]{1,0:T(8,128)(2,1)S(1)}, bf16[1024,768]{1,0:T(8,128)(2,1)}, u32[]{:S(2)}) copy-start(bf16[1024,768]{1,0:T(8,128)(2,1)} %copy-done.33) | copy-start | bytes 4718596
  179.7 20.0 %collective-permute-start.23 = (bf16[2,3,192,384]{3,2,1,0:T(8,128)(2,1)S(1)}, bf16[2,3,192,384]{3,2,1,0:T(8,128)(2,1)S(1)}, u32[]{:S(2)}, u32[]{:S(2)}) collective-permute-start(bf16[2,3,192,384]{3,2,1,0:T(8,128)(2,1)S(1)} %get-tuple-element.273), channel_id=1, source_target_pairs={{0,8},{8,0},{16,24},{24,16},{1,9},{9,1},{17,25},{25,17},{2,10},{10... | collective-permute-start | bytes 2654216 | tf_op jit(solution)/shard_map/ppermute | solution.py:689
  181.0 18.7 %collective-permute-start.22 = (bf16[192,1536]{1,0:T(8,128)(2,1)S(1)}, bf16[192,1536]{1,0:T(8,128)(2,1)S(1)}, u32[]{:S(2)}, u32[]{:S(2)}) collective-permute-start(bf16[192,1536]{1,0:T(8,128)(2,1)S(1)} %fusion.7), channel_id=1, source_target_pairs={{0,16},{8,24},{16,0},{24,8},{1,17},{9,25},{17,1},{25,9},{2,18},{10... | collective-permute-start | bytes 1769480 | tf_op jit(solution)/shard_map/ppermute | solution.py:689
  195.9 22.1 %collective-permute-start.27 = (bf16[480,768]{1,0:T(8,128)(2,1)S(1)}, bf16[480,768]{1,0:T(8,128)(2,1)S(1)}, u32[]{:S(2)}, u32[]{:S(2)}) collective-permute-start(bf16[480,768]{1,0:T(8,128)(2,1)S(1)} %fusion.1), channel_id=1, source_target_pairs={{0,2},{6,4},{1,3},{7,5},{8,10},{14,12},{9,11},{15,13},{16,18},{22,... | collective-permute-start | bytes 2211848 | tf_op jit(solution)/shard_map/ppermute | solution.py:704
  201.2 8.6 %copy-start.9 = (bf16[3,768,384]{2,1,0:T(8,128)(2,1)S(1)}, bf16[3,768,384]{2,1,0:T(8,128)(2,1)}, u32[]{:S(2)}) copy-start(bf16[3,768,384]{2,1,0:T(8,128)(2,1)} %refs_7_.1) | copy-start | bytes 5308420
  201.2 11.9 %collective-permute-start.24 = (bf16[3,192,384]{2,1,0:T(8,128)(2,1)S(1)}, bf16[3,192,384]{2,1,0:T(8,128)(2,1)S(1)}, u32[]{:S(2)}, u32[]{:S(2)}) collective-permute-start(bf16[3,192,384]{2,1,0:T(8,128)(2,1)S(1)} %fusion.15), channel_id=1, source_target_pairs={{0,16},{8,24},{16,0},{24,8},{1,17},{9,25},{17,1},{25,9},{2,18},{10... | collective-permute-start | bytes 1327112 | tf_op jit(solution)/shard_map/ppermute | solution.py:689
  202.6 32.6 %collective-permute-start.29 = (bf16[192,1536]{1,0:T(8,128)(2,1)S(1)}, bf16[192,1536]{1,0:T(8,128)(2,1)S(1)}, u32[]{:S(2)}, u32[]{:S(2)}) collective-permute-start(bf16[192,1536]{1,0:T(8,128)(2,1)S(1)} %fusion.6), channel_id=1, source_target_pairs={{0,2},{6,4},{1,3},{7,5},{8,10},{14,12},{9,11},{15,13},{16,18},{22,... | collective-permute-start | bytes 1769480 | tf_op jit(solution)/shard_map/ppermute | solution.py:704
  213.1 2.6 collective-permute-start.25
  213.3 2.5 collective-permute-start.26
  214.0 12.2 %collective-permute-start.32 = (bf16[3,192,384]{2,1,0:T(8,128)(2,1)S(1)}, bf16[3,192,384]{2,1,0:T(8,128)(2,1)S(1)}, u32[]{:S(2)}, u32[]{:S(2)}) collective-permute-start(bf16[3,192,384]{2,1,0:T(8,128)(2,1)S(1)} %fusion.10), channel_id=1, source_target_pairs={{0,1},{1,0},{2,3},{3,2},{4,5},{5,4},{6,7},{7,6},{8,9},{9,8},{10,11... | collective-permute-start | bytes 1327112 | tf_op jit(solution)/shard_map/ppermute | solution.py:689
  215.8 7.9 %collective-permute-start.28 = (f32[4,5376]{1,0:T(4,128)S(1)}, f32[4,5376]{1,0:T(4,128)S(1)}, u32[]{:S(2)}, u32[]{:S(2)}) collective-permute-start(f32[4,5376]{1,0:T(4,128)S(1)} %add.182), channel_id=1, source_target_pairs={{0,16},{8,24},{16,0},{24,8},{1,17},{9,25},{17,1},{25,9},{2,18},{10... | collective-permute-start | bytes 258056 | tf_op jit(solution)/shard_map/ppermute | solution.py:689
  216.8 13.1 %collective-permute-start.31 = (bf16[3,192,384]{2,1,0:T(8,128)(2,1)S(1)}, bf16[3,192,384]{2,1,0:T(8,128)(2,1)S(1)}, u32[]{:S(2)}, u32[]{:S(2)}) collective-permute-start(bf16[3,192,384]{2,1,0:T(8,128)(2,1)S(1)} %fusion.16), channel_id=1, source_target_pairs={{0,16},{8,24},{16,0},{24,8},{1,17},{9,25},{17,1},{25,9},{2,18},{10... | collective-permute-start | bytes 1327112 | tf_op jit(solution)/shard_map/ppermute | solution.py:689
  218.3 17.0 %collective-permute-start.30 = (bf16[480,768]{1,0:T(8,128)(2,1)S(1)}, bf16[480,768]{1,0:T(8,128)(2,1)S(1)}, u32[]{:S(2)}, u32[]{:S(2)}) collective-permute-start(bf16[480,768]{1,0:T(8,128)(2,1)S(1)} %add_convert_fusion.2), channel_id=1, source_target_pairs={{2,4},{4,2},{3,5},{5,3},{10,12},{12,10},{11,13},{13,11},{18,20},{2... | collective-permute-start | bytes 2211848 | tf_op jit(solution)/shard_map/ppermute | solution.py:708
  223.8 4.2 %collective-permute-start.33 = (f32[4,3456]{1,0:T(4,128)S(1)}, f32[4,3456]{1,0:T(4,128)S(1)}, u32[]{:S(2)}, u32[]{:S(2)}) collective-permute-start(f32[4,3456]{1,0:T(4,128)S(1)} %pad_maximum_fusion.1), channel_id=1, source_target_pairs={{0,1},{1,0},{2,3},{3,2},{4,5},{5,4},{6,7},{7,6},{8,9},{9,8},{10,11... | collective-permute-start | bytes 165896 | tf_op jit(solution)/shard_map/ppermute | solution.py:689
  229.9 8.1 %copy-start.23 = (bf16[512,768]{1,0:T(8,128)(2,1)S(1)}, bf16[512,768]{1,0:T(8,128)(2,1)}, u32[]{:S(2)}) copy-start(bf16[512,768]{1,0:T(8,128)(2,1)} %copy-done.20) | copy-start | bytes 2359300
  230.1 17.0 %collective-permute-start.34 = (bf16[3,192,384]{2,1,0:T(8,128)(2,1)S(1)}, bf16[3,192,384]{2,1,0:T(8,128)(2,1)S(1)}, u32[]{:S(2)}, u32[]{:S(2)}) collective-permute-start(bf16[3,192,384]{2,1,0:T(8,128)(2,1)S(1)} %fusion.9), channel_id=1, source_target_pairs={{0,2},{6,4},{1,3},{7,5},{8,10},{14,12},{9,11},{15,13},{16,18},{22,... | collective-permute-start | bytes 1327112 | tf_op jit(solution)/shard_map/ppermute | solution.py:704
  233.9 13.2 %collective-permute-start.36 = (f32[4,3456]{1,0:T(4,128)S(1)}, f32[4,3456]{1,0:T(4,128)S(1)}, u32[]{:S(2)}, u32[]{:S(2)}) collective-permute-start(f32[4,3456]{1,0:T(4,128)S(1)} %add.190), channel_id=1, source_target_pairs={{0,2},{6,4},{1,3},{7,5},{8,10},{14,12},{9,11},{15,13},{16,18},{22,... | collective-permute-start | bytes 165896 | tf_op jit(solution)/shard_map/ppermute | solution.py:704
  235.4 11.8 %collective-permute-start.35 = (bf16[192,1536]{1,0:T(8,128)(2,1)S(1)}, bf16[192,1536]{1,0:T(8,128)(2,1)S(1)}, u32[]{:S(2)}, u32[]{:S(2)}) collective-permute-start(bf16[192,1536]{1,0:T(8,128)(2,1)S(1)} %add_convert_fusion.6), channel_id=1, source_target_pairs={{2,4},{4,2},{3,5},{5,3},{10,12},{12,10},{11,13},{13,11},{18,20},{2... | collective-permute-start | bytes 1769480 | tf_op jit(solution)/shard_map/ppermute | solution.py:708
  236.5 20.3 %collective-permute-start.38 = (bf16[480,768]{1,0:T(8,128)(2,1)S(1)}, bf16[480,768]{1,0:T(8,128)(2,1)S(1)}, u32[]{:S(2)}, u32[]{:S(2)}) collective-permute-start(bf16[480,768]{1,0:T(8,128)(2,1)S(1)} %add_convert_fusion.1), channel_id=1, source_target_pairs={{2,0},{4,6},{3,1},{5,7},{10,8},{12,14},{11,9},{13,15},{18,16},{20,... | collective-permute-start | bytes 2211848 | tf_op jit(solution)/shard_map/ppermute | solution.py:712
  247.3 11.4 %collective-permute-start.40 = (bf16[3,192,384]{2,1,0:T(8,128)(2,1)S(1)}, bf16[3,192,384]{2,1,0:T(8,128)(2,1)S(1)}, u32[]{:S(2)}, u32[]{:S(2)}) collective-permute-start(bf16[3,192,384]{2,1,0:T(8,128)(2,1)S(1)} %add_convert_fusion.8), channel_id=1, source_target_pairs={{2,4},{4,2},{3,5},{5,3},{10,12},{12,10},{11,13},{13,11},{18,20},{2... | collective-permute-start | bytes 1327112 | tf_op jit(solution)/shard_map/ppermute | solution.py:708
  248.0 10.7 %collective-permute-start.39 = (f32[4,3456]{1,0:T(4,128)S(1)}, f32[4,3456]{1,0:T(4,128)S(1)}, u32[]{:S(2)}, u32[]{:S(2)}) collective-permute-start(f32[4,3456]{1,0:T(4,128)S(1)} %add.193), channel_id=1, source_target_pairs={{2,4},{4,2},{3,5},{5,3},{10,12},{12,10},{11,13},{13,11},{18,20},{2... | collective-permute-start | bytes 165896 | tf_op jit(solution)/shard_map/ppermute | solution.py:708
  248.7 16.4 %collective-permute-start.37 = (bf16[512,768]{1,0:T(8,128)(2,1)S(1)}, bf16[512,768]{1,0:T(8,128)(2,1)S(1)}, u32[]{:S(2)}, u32[]{:S(2)}) collective-permute-start(bf16[512,768]{1,0:T(8,128)(2,1)S(1)} %get-tuple-element.327), channel_id=1, source_target_pairs={{0,1},{1,0},{2,3},{3,2},{4,5},{5,4},{6,7},{7,6},{8,9},{9,8},{10,11... | collective-permute-start | bytes 2359304 | tf_op jit(solution)/shard_map/ppermute | solution.py:689
  249.2 25.4 %collective-permute-start.42 = (bf16[192,1536]{1,0:T(8,128)(2,1)S(1)}, bf16[192,1536]{1,0:T(8,128)(2,1)S(1)}, u32[]{:S(2)}, u32[]{:S(2)}) collective-permute-start(bf16[192,1536]{1,0:T(8,128)(2,1)S(1)} %add_convert_fusion.5), channel_id=1, source_target_pairs={{2,0},{4,6},{3,1},{5,7},{10,8},{12,14},{11,9},{13,15},{18,16},{20,... | collective-permute-start | bytes 1769480 | tf_op jit(solution)/shard_map/ppermute | solution.py:712
  258.7 17.1 %collective-permute-start.43 = (f32[4,3456]{1,0:T(4,128)S(1)}, f32[4,3456]{1,0:T(4,128)S(1)}, u32[]{:S(2)}, u32[]{:S(2)}) collective-permute-start(f32[4,3456]{1,0:T(4,128)S(1)} %add.197), channel_id=1, source_target_pairs={{2,0},{4,6},{3,1},{5,7},{10,8},{12,14},{11,9},{13,15},{18,16},{20,... | collective-permute-start | bytes 165896 | tf_op jit(solution)/shard_map/ppermute | solution.py:712
  260.2 20.6 %collective-permute-start.41 = (bf16[3,192,384]{2,1,0:T(8,128)(2,1)S(1)}, bf16[3,192,384]{2,1,0:T(8,128)(2,1)S(1)}, u32[]{:S(2)}, u32[]{:S(2)}) collective-permute-start(bf16[3,192,384]{2,1,0:T(8,128)(2,1)S(1)} %add_convert_fusion.7), channel_id=1, source_target_pairs={{2,0},{4,6},{3,1},{5,7},{10,8},{12,14},{11,9},{13,15},{18,16},{20,... | collective-permute-start | bytes 1327112 | tf_op jit(solution)/shard_map/ppermute | solution.py:712
  274.6 7.1 %copy-start.1 = (s32[2,1024]{1,0:T(2,128)S(1)}, s32[2,1024]{1,0:T(2,128)}, u32[]{:S(2)}) copy-start(s32[2,1024]{1,0:T(2,128)} %param.12) | copy-start | bytes 24580
  (26 other events, 57.4 us)

commit v8 on v7

--- a/solution.py
+++ b/solution.py
@@ -473,7 +473,7 @@
                       pl.BlockSpec((length, chunk), lambda n, s: (0, n))],
             out_specs=[out_spec, out_spec]),
         out_shape=[out, out],
-        compiler_params=pltpu.CompilerParams(vmem_limit_bytes=12 * MIB),
+        compiler_params=pltpu.CompilerParams(vmem_limit_bytes=52 * MIB),
         cost_estimate=cost(12),
         name="fc_grad",
     )(place, left, right)
@@ -575,7 +575,7 @@
             out_specs=[out_spec, out_spec],
             scratch_shapes=[pltpu.VMEM((attended.shape[1], D), BF16)]),
         out_shape=[out, out],
-        compiler_params=pltpu.CompilerParams(vmem_limit_bytes=19 * MIB),
+        compiler_params=pltpu.CompilerParams(vmem_limit_bytes=40 * MIB),
         cost_estimate=cost(13),
         name="proj_grad",
     )(place, active, active, cot_own, cot_other, attended, branch)

time: 288 us -> 286 us (level)
  local copies, waits for them, and re-layouts: 26.5 us -> 20.6 us
  starting transfers between devices: 43.9 us -> 49.6 us
  waiting for transfers between devices: 45.8 us -> 42.2 us
  Pallas kernels: 146 us -> 149 us
    unnamed x100 -> x92, local copies, waits for them, and re-layouts: 16 us -> 10.1 us
    ppermute x32, starting transfers between devices: 25.3 us -> 30.6 us  [swap(): return lax.ppermute(value, axis, [(n, n ^ bit) for n in range(size)])]
  transfers between devices with their start and end apart: 44 -> 44, of which waited for: 20 -> 19; matrix products, arithmetic and copies ran while one was open for 10% -> 10% of each run, Pallas kernels for 39% -> 40%
where the time goes in v8:
time: 286 us; the launch traced here: 281 us
  Pallas kernels  149 us (52%)
  starting transfers between devices  49.6 us (17%)
  waiting for transfers between devices  42.2 us (15%)
  local copies, waits for them, and re-layouts  20.6 us (7%)
  other arithmetic  18 us (6%)
    pallas_call x1, Pallas kernels, middle_stage(): pl.pallas_call(body, grid_spec=pltpu.PrefetchScalarGridSpec(num_scalar_pr...  35.1 us
    pallas_call x3, Pallas kernels, attend_backward(): pl.pallas_call(functools.partial(attend_backward_kernel, block=length //...  34.3 us
    ppermute x32, starting transfers between devices, swap(): return lax.ppermute(value, axis, [(n, n ^ bit) for n in range(size)])  30.6 us
    ppermute x32, waiting for transfers between devices, swap(): return lax.ppermute(value, axis, [(n, n ^ bit) for n in range(size)])  30.2 us
    pallas_call x2, Pallas kernels, attend_forward(): pl.pallas_call(body, grid_spec=pltpu.PrefetchScalarGridSpec(num_scalar_pr...  18.8 us
    convert_element_type x17, other arithmetic, add_low(): return total.astype(BF16)  12.2 us
    ppermute x4, waiting for transfers between devices, chain_out(): return lax.ppermute(value, 'group', [(1, 0), (2, 3)])  12 us
    ppermute x4, starting transfers between devices, chain_in(): return lax.ppermute(value, 'group', [(0, 1), (3, 2)])  10.7 us
  transfers between devices with their start and end apart: 44, of which 19 were waited for; matrix products, arithmetic and copies ran while one was open for 10% of the time, Pallas kernels for 40%

profile of v8, /device:TPU:0, one launch (start us, length us, event | category | flops | bytes accessed | tf_op | source)
XLA Modules:
  0.0 280.8 jit_solution(3636658629730431210)
XLA Ops:
  1.7 3.0 %collective-permute-start = (bf16[3,192,384]{2,1,0:T(8,128)(2,1)S(1)}, bf16[3,192,384]{2,1,0:T(8,128)(2,1)}, u32[]{:S(2)}, u32[]{:S(2)}) collective-permute-start(bf16[3,192,384]{2,1,0:T(8,128)(2,1)S(1)} %constant_dynamic-slice_fusion.5), channel_id=1, source_target_pairs={{0,1},{1,0},{2,3},{3,2},{4,5},{5,4},{6,7},{7,6},{8,9},{9,8},{10,11... | collective-permute-start | bytes 1327112 | tf_op jit(solution)/shard_map/ppermute | solution.py:689
  6.4 1.4 copy-done.10
  7.8 4.1 %unpack_rows.2 = (bf16[512,768]{1,0:T(8,128)(2,1)S(1)}, bf16[528,768]{1,0:T(8,128)(2,1)}) custom-call(s32[3]{0:T(128)S(1)} %pad_add_fusion.place_ref, bf16[767,2,512]{2,1,0:T(2,128)(2,1)S(1)} %bitcast.55, bf16[16,768]{1,0:T(8,128)(2,1)S(1)} %maximum_maximum_fusion.refs_0_), custom_call_target="tpu_custom_call" | custom-call | flops 2000000000 | bytes 2000000 | tf_op jit(solution)/shard_map/unpack_rows/pallas_call | solution.py:192
  13.0 2.3 collective-permute-done.a.refs_1_.refs_8_
  15.3 1.4 collective-permute-start.1
  16.8 3.3 %pad.20.refs_10_ = bf16[1536,768]{1,0:T(8,128)(2,1)} pad(bf16[1536,767]{1,0:T(8,128)(2,1)} %param.19, bf16[]{:T(256)} %constant.14.clone.1), padding=0_0x0_1 | pad | bytes 4715522 | tf_op jit(solution)/shard_map/jit(_pad)/pad | solution.py:753
  20.1 1.2 constant_dynamic-slice_fusion.3
  22.2 1.2 constant_dynamic-slice_fusion
  25.1 2.4 collective-permute-start.5
  27.6 3.3 %unpack_rows.3 = (bf16[512,768]{1,0:T(8,128)(2,1)S(1)}, bf16[512,768]{1,0:T(8,128)(2,1)S(1)}) custom-call(s32[3]{0:T(128)S(1)} %pad_add_fusion.place_ref, bf16[767,2,512]{2,1,0:T(2,128)(2,1)S(1)} %bitcast.56), custom_call_target="tpu_custom_call" | custom-call | flops 2000000000 | bytes 2000000 | tf_op jit(solution)/shard_map/unpack_rows/pallas_call | solution.py:192
  32.7 1.3 collective-permute-done.2.other_ref.refs_2_.refs_4_
  34.1 2.1 collective-permute-done.4.d.refs_4_.refs_11_
  38.3 7.9 %norm_project.1 = (bf16[1024,768]{1,0:T(8,128)(2,1)S(1)}, bf16[1024,768]{1,0:T(8,128)(2,1)S(1)}, bf16[1024,768]{1,0:T(8,128)(2,1)S(1)}, bf16[1024,768]{1,0:T(8,128)(2,1)S(1)}) custom-call(s32[3]{0:T(128)S(1)} %pad_add_fusion.place_ref, bf16[512,768]{1,0:T(8,128)(2,1)S(1)} %copy-done.19, ...), custom_call_target="tpu_custom_call" | custom-call | flops 4000000000 | bytes 4000000 | tf_op jit(solution)/shard_map/norm_project/pallas_call | solution.py:283
  46.3 1.2 collective-permute-start.9
  47.5 9.4 %attend_forward.2 = (bf16[1024,768]{1,0:T(8,128)(2,1)S(1)}, f32[6,8,1024]{2,1,0:T(8,128)S(1)}) custom-call(s32[4]{0:T(128)S(1)} %compare_convert_fusion.flags_ref, bf16[1024,768]{1,0:T(8,128)(2,1)S(1)} %get-tuple-element.210.q_ref, bf16[1024,768]{1,0:T(8,128)(2,1)S(1)} %get-tuple-element.206.k_ref, bf16[1024,768]{1,0:T(8,128)(2,1)S(1)} %get-tuple-element.207.v_ref), custom_call_target="tpu_custom_call" | custom-call | flops 4560000000 | bytes 4559999 | tf_op jit(solution)/shard_map/attend_forward/pallas_call | solution.py:88
  56.9 5.7 %collective-permute-done.6.refs_15_ = bf16[384,768]{1,0:T(8,128)(2,1)} collective-permute-done((bf16[384,768]{1,0:T(8,128)(2,1)}, bf16[384,768]{1,0:T(8,128)(2,1)}, u32[]{:S(2)}, u32[]{:S(2)}) %collective-permute-start.6) | collective-permute-done | bytes 589856 | tf_op jit(solution)/shard_map/ppermute | solution.py:689
  62.6 1.6 collective-permute-start.7
  64.2 1.6 collective-permute-start.8
  65.8 9.4 %attend_forward.3 = (bf16[1024,768]{1,0:T(8,128)(2,1)S(1)}, f32[6,8,1024]{2,1,0:T(8,128)S(1)}) custom-call(s32[4]{0:T(128)S(1)} %compare_convert_fusion.flags_ref, bf16[1024,768]{1,0:T(8,128)(2,1)S(1)} %get-tuple-element.210.q_ref, bf16[1024,768]{1,0:T(8,128)(2,1)S(1)} %get-tuple-element.206.k_ref, ...), custom_call_target="tpu_custom_call", output_to_operand_aliasing={{0}: (4, {}), {1}: (5, {})} | custom-call | flops 4560000000 | bytes 4559999 | tf_op jit(solution)/shard_map/attend_forward/pallas_call | solution.py:88
  75.8 2.0 collective-permute-done.9.refs_4_.other_cot
  79.1 3.1 %collective-permute-done.12.refs_16_ = bf16[384,768]{1,0:T(8,128)(2,1)S(1)} collective-permute-done((bf16[384,768]{1,0:T(8,128)(2,1)}, bf16[384,768]{1,0:T(8,128)(2,1)S(1)}, u32[]{:S(2)}, u32[]{:S(2)}) %collective-permute-start.12) | collective-permute-done | bytes 589856 | tf_op jit(solution)/shard_map/ppermute | solution.py:689
  82.4 35.1 %middle_stage.1 = (bf16[1024,768]{1,0:T(8,128)(2,1)S(1)}, bf16[1024,3072]{1,0:T(8,128)(2,1)}, bf16[1024,3072]{1,0:T(8,128)(2,1)}, bf16[512,768]{1,0:T(8,128)(2,1...) custom-call(s32[3]{0:T(128)S(1)} %pad_add_fusion.place_ref, ...), custom_call_target="tpu_custom_call" | custom-call | flops 15200000000 | bytes 15200000 | tf_op jit(solution)/shard_map/middle_stage/pallas_call | solution.py:427
  118.4 1.7 collective-permute-start.14
  120.1 9.3 %proj_grad.1 = (bf16[2,2,480,768]{3,2,1,0:T(8,128)(2,1)S(1)}, bf16[2,2,480,768]{3,2,1,0:T(8,128)(2,1)S(1)}) custom-call(s32[3]{0:T(128)S(1)} %pad_add_fusion.place_ref, bf16[1024,3072]{1,0:T(8,128)(2,1)} %get-tuple-element.229.own_act.other_act, bf16[1024,3072]{1,0:T(8,128)(2,1)} %get-tuple-element.229.own_act.other_act, bf16[512,768]{1,0:T(8,128)(2,1)S(1)} %copy-done.23, ...), custom_call_target="tpu_custom_call" | custom-call | flops 5200000000 | bytes 5200000 | tf_op jit(solution)/shard_map/proj_grad/pallas_call | solution.py:568
  129.7 1.7 collective-permute-start.16
  131.4 9.3 %fc_grad.1 = (bf16[2,2,192,1536]{3,2,1,0:T(8,128)(2,1)}, bf16[2,2,192,1536]{3,2,1,0:T(8,128)(2,1)}) custom-call(s32[3]{0:T(128)S(1)} %pad_add_fusion.place_ref, bf16[1024,768]{1,0:T(8,128)(2,1)S(1)} %get-tuple-element.236.left_ref, bf16[1024,3072]{1,0:T(8,128)(2,1)} %get-tuple-element.237.right_ref), custom_call_target="tpu_custom_call" | custom-call | flops 4800000000 | bytes 4800000 | tf_op jit(solution)/shard_map/fc_grad/pallas_call | solution.py:468
  142.0 1.4 fusion.13
  143.4 1.8 collective-permute-start.18
  145.2 1.4 fusion.14
  147.0 2.1 fusion.4
  149.1 1.8 collective-permute-start.19
  150.9 17.2 %attend_backward.3 = (bf16[3,1024,384]{2,1,0:T(8,128)(2,1)S(1)}, f32[8,384]{1,0:T(8,128)S(1)}) custom-call(s32[4]{0:T(128)S(1)} %compare_convert_fusion.flags_ref, bf16[1024,768]{1,0:T(8,128)(2,1)S(1)} %copy-done.25, bf16[1024,768]{1,0:T(8,128)(2,1)S(1)} %copy-done.27, bf16[1024,768]{1,0:T(8,128)(2,1)S(1)} %copy-done.29, bf16[1024,768]{1,0:T(8,128)(2,1)S(1)} %copy-done.31, ...), custom_call_target="tpu_custom_call" | custom-call | flops 7600000000 | bytes 7600000 | tf_op jit(solution)/shard_map/attend_backward/pallas_call | solution.py:155
  168.2 1.5 fusion.2
  170.1 4.9 %qkv_grad.2 = (bf16[2,3,192,384]{3,2,1,0:T(8,128)(2,1)S(1)}, bf16[2,3,192,384]{3,2,1,0:T(8,128)(2,1)S(1)}, f32[8,768]{1,0:T(8,128)S(1)}) custom-call(s32[3]{0:T(128)S(1)} %pad_add_fusion.place_ref, bf16[1024,768]{1,0:T(8,128)(2,1)S(1)} %copy-done.33, bf16[3,1024,384]{2,1,0:T(8,128)(2,1)S(1)} %get-tuple-element.259.refs_0_.refs_2_, ...), custom_call_target="tpu_custom_call" | custom-call | flops 2600000000 | bytes 2600000 | tf_op jit(solution)/shard_map/qkv_grad/pallas_call | solution.py:526
  175.0 3.1 %collective-permute-done.19 = bf16[2,192,1536]{2,1,0:T(8,128)(2,1)S(1)} collective-permute-done((bf16[2,192,1536]{2,1,0:T(8,128)(2,1)S(1)}, bf16[2,192,1536]{2,1,0:T(8,128)(2,1)S(1)}, u32[]{:S(2)}, u32[]{:S(2)}) %collective-permute-start.19) | collective-permute-done | bytes 1179680 | tf_op jit(solution)/shard_map/ppermute | solution.py:689
  178.1 1.3 fusion.7
  179.3 1.5 collective-permute-start.22
  180.9 11.4 %attend_backward.4 = (bf16[3,1024,256]{2,1,0:T(8,128)(2,1)S(1)}, f32[8,256]{1,0:T(8,128)S(1)}) custom-call(s32[4]{0:T(128)S(1)} %compare_convert_fusion.flags_ref, bf16[1024,768]{1,0:T(8,128)(2,1)S(1)} %copy-done.25, bf16[1024,768]{1,0:T(8,128)(2,1)S(1)} %copy-done.27, bf16[1024,768]{1,0:T(8,128)(2,1)S(1)} %copy-done.29, bf16[1024,768]{1,0:T(8,128)(2,1)S(1)} %copy-done.31, ...), custom_call_target="tpu_custom_call" | custom-call | flops 5200000000 | bytes 5200000 | tf_op jit(solution)/shard_map/attend_backward/pallas_call | solution.py:155
  192.8 1.5 fusion.1
  194.3 3.7 %collective-permute-start.27 = (bf16[480,768]{1,0:T(8,128)(2,1)S(1)}, bf16[480,768]{1,0:T(8,128)(2,1)S(1)}, u32[]{:S(2)}, u32[]{:S(2)}) collective-permute-start(bf16[480,768]{1,0:T(8,128)(2,1)S(1)} %fusion.1), channel_id=1, source_target_pairs={{0,2},{6,4},{1,3},{7,5},{8,10},{14,12},{9,11},{15,13},{16,18},{22,... | collective-permute-start | bytes 2211848 | tf_op jit(solution)/shard_map/ppermute | solution.py:704
  198.1 1.4 fusion.6
  199.6 1.4 collective-permute-start.24
  200.9 1.5 collective-permute-start.29
  202.4 5.7 %attend_backward.5 = (bf16[3,1024,128]{2,1,0:T(8,128)(2,1)S(1)}, f32[8,128]{1,0:T(8,128)S(1)}) custom-call(s32[4]{0:T(128)S(1)} %compare_convert_fusion.flags_ref, bf16[1024,768]{1,0:T(8,128)(2,1)S(1)} %copy-done.25, bf16[1024,768]{1,0:T(8,128)(2,1)S(1)} %copy-done.27, bf16[1024,768]{1,0:T(8,128)(2,1)S(1)} %copy-done.29, bf16[1024,768]{1,0:T(8,128)(2,1)S(1)} %copy-done.31, ...), custom_call_target="tpu_custom_call" | custom-call | flops 2800000000 | bytes 2800000 | tf_op jit(solution)/shard_map/attend_backward/pallas_call | solution.py:155
  208.1 3.0 %qkv_grad.3 = (bf16[2,3,192,384]{3,2,1,0:T(8,128)(2,1)S(1)}, bf16[2,3,192,384]{3,2,1,0:T(8,128)(2,1)S(1)}, f32[8,768]{1,0:T(8,128)S(1)}) custom-call(s32[3]{0:T(128)S(1)} %pad_add_fusion.place_ref, bf16[1024,768]{1,0:T(8,128)(2,1)S(1)} %copy-done.33, bf16[3,1024,256]{2,1,0:T(8,128)(2,1)S(1)} %get-tuple-element.281.refs_0_, ...), custom_call_target="tpu_custom_call" | custom-call | flops 2600000000 | bytes 2600000 | tf_op jit(solution)/shard_map/qkv_grad/pallas_call | solution.py:526
  212.0 1.8 collective-permute-start.32
  214.8 1.4 collective-permute-start.31
  217.1 4.7 %pack_rows.2 = bf16[767,2,512]{2,1,0:T(2,128)(2,1)} custom-call(s32[3]{0:T(128)S(1)} %pad_add_fusion.place_ref, bf16[512,768]{1,0:T(8,128)(2,1)S(1)} %copy-done.3, bf16[256,768]{1,0:T(8,128)(2,1)S(1)} %collective-permute-done.14.first_ref, bf16[256,768]{1,0:T(8,128)(2,1)S(1)} %copy-done.5), custom_call_target="tpu_custom_call" | custom-call | flops 40000000 | bytes 40000 | tf_op jit(solution)/shard_map/pack_rows/pallas_call | solution.py:673
  221.9 1.7 collective-permute-start.33
  224.2 1.9 collective-permute-done.33
  226.1 1.8 collective-permute-done.31
  228.2 4.1 %collective-permute-start.34 = (bf16[3,192,384]{2,1,0:T(8,128)(2,1)S(1)}, bf16[3,192,384]{2,1,0:T(8,128)(2,1)S(1)}, u32[]{:S(2)}, u32[]{:S(2)}) collective-permute-start(bf16[3,192,384]{2,1,0:T(8,128)(2,1)S(1)} %fusion.9), channel_id=1, source_target_pairs={{0,2},{6,4},{1,3},{7,5},{8,10},{14,12},{9,11},{15,13},{16,18},{22,... | collective-permute-start | bytes 1327112 | tf_op jit(solution)/shard_map/ppermute | solution.py:704
  232.3 1.3 collective-permute-start.36
  234.9 1.5 collective-permute-start.38
  236.4 9.1 %input_grad.1 = (bf16[512,768]{1,0:T(8,128)(2,1)S(1)}, bf16[512,768]{1,0:T(8,128)(2,1)S(1)}) custom-call(s32[3]{0:T(128)S(1)} %pad_add_fusion.place_ref, bf16[3,1024,256]{2,1,0:T(8,128)(2,1)S(1)} %get-tuple-element.281.refs_0_, bf16[3,1024,128]{2,1,0:T(8,128)(2,1)S(1)} %get-tuple-element.279.refs_1_, ...), custom_call_target="tpu_custom_call" | custom-call | flops 3600000000 | bytes 3600000 | tf_op jit(solution)/shard_map/input_grad/pallas_call | solution.py:642
  247.1 1.8 collective-permute-start.37
  249.1 1.3 collective-permute-start.42
  250.4 3.8 %collective-permute-done.38 = bf16[480,768]{1,0:T(8,128)(2,1)S(1)} collective-permute-done((bf16[480,768]{1,0:T(8,128)(2,1)S(1)}, bf16[480,768]{1,0:T(8,128)(2,1)S(1)}, u32[]{:S(2)}, u32[]{:S(2)}) %collective-permute-start.38) | collective-permute-done | bytes 737312 | tf_op jit(solution)/shard_map/ppermute | solution.py:712
  256.1 1.3 collective-permute-start.43
  257.6 1.3 collective-permute-start.41
  258.9 4.3 %collective-permute-done.37.first_ref.second_ref = bf16[512,768]{1,0:T(8,128)(2,1)S(1)} collective-permute-done((bf16[512,768]{1,0:T(8,128)(2,1)S(1)}, bf16[512,768]{1,0:T(8,128)(2,1)S(1)}, u32[]{:S(2)}, u32[]{:S(2)}) %collective-permute-start.37) | collective-permute-done | bytes 786464 | tf_op jit(solution)/shard_map/ppermute | solution.py:689
  263.2 4.7 %pack_rows.3 = bf16[767,2,512]{2,1,0:T(2,128)(2,1)} custom-call(s32[3]{0:T(128)S(1)} %pad_add_fusion.place_ref, bf16[512,768]{1,0:T(8,128)(2,1)S(1)} %get-tuple-element.344.own_ref, bf16[512,768]{1,0:T(8,128)(2,1)S(1)} %collective-permute-done.37.first_ref.second_ref, bf16[512,768]{1,0:T(8,128)(2,1)S(1)} %collective-permute-done.37.first_ref.second_ref), custom_call_target="tpu_custom_call" | custom-call | flops 40000000 | bytes 40000 | tf_op jit(solution)/shard_map/pack_rows/pallas_call | solution.py:673
  267.9 6.2 %collective-permute-done.42 = bf16[192,1536]{1,0:T(8,128)(2,1)S(1)} collective-permute-done((bf16[192,1536]{1,0:T(8,128)(2,1)S(1)}, bf16[192,1536]{1,0:T(8,128)(2,1)S(1)}, u32[]{:S(2)}, u32[]{:S(2)}) %collective-permute-start.42) | collective-permute-done | bytes 589856 | tf_op jit(solution)/shard_map/ppermute | solution.py:712
  277.6 2.0 collective-permute-done.41
  (199 shorter events, 29.2 us)
Async XLA Ops:
  0.6 12.2 %copy-start = (s32[2,1024]{1,0:T(2,128)S(1)}, s32[2,1024]{1,0:T(2,128)}, u32[]{:S(2)}) copy-start(s32[2,1024]{1,0:T(2,128)} %param.12) | copy-start | bytes 24580
  1.7 13.6 %collective-permute-start = (bf16[3,192,384]{2,1,0:T(8,128)(2,1)S(1)}, bf16[3,192,384]{2,1,0:T(8,128)(2,1)}, u32[]{:S(2)}, u32[]{:S(2)}) collective-permute-start(bf16[3,192,384]{2,1,0:T(8,128)(2,1)S(1)} %constant_dynamic-slice_fusion.5), channel_id=1, source_target_pairs={{0,1},{1,0},{2,3},{3,2},{4,5},{5,4},{6,7},{7,6},{8,9},{9,8},{10,11... | collective-permute-start | bytes 1327112 | tf_op jit(solution)/shard_map/ppermute | solution.py:689
  12.8 21.2 %collective-permute-start.2 = (bf16[528,768]{1,0:T(8,128)(2,1)}, bf16[528,768]{1,0:T(8,128)(2,1)S(1)}, u32[]{:S(2)}, u32[]{:S(2)}) collective-permute-start(bf16[528,768]{1,0:T(8,128)(2,1)} %get-tuple-element.192), channel_id=1, source_target_pairs={{0,1},{1,0},{2,3},{3,2},{4,5},{5,4},{6,7},{7,6},{8,9},{9,8},{10,11... | collective-permute-start | bytes 2433032 | tf_op jit(solution)/shard_map/ppermute | solution.py:689
  15.3 9.0 %collective-permute-start.3 = (bf16[3,192,384]{2,1,0:T(8,128)(2,1)}, bf16[3,192,384]{2,1,0:T(8,128)(2,1)S(1)}, u32[]{:S(2)}, u32[]{:S(2)}) collective-permute-start(bf16[3,192,384]{2,1,0:T(8,128)(2,1)} %collective-permute-done.a.refs_1_.refs_8_), channel_id=1, source_target_pairs={{0,8},{8,0},{16,24},{24,16},{1,9},{9,1},{17,25},{25,17},{2,10},{10... | collective-permute-start | bytes 1327112 | tf_op jit(solution)/shard_map/ppermute | solution.py:689
  15.3 18.7 %collective-permute-start.1 = (bf16[3,192,384]{2,1,0:T(8,128)(2,1)}, bf16[3,192,384]{2,1,0:T(8,128)(2,1)}, u32[]{:S(2)}, u32[]{:S(2)}) collective-permute-start(bf16[3,192,384]{2,1,0:T(8,128)(2,1)} %collective-permute-done.a.refs_1_.refs_8_), channel_id=1, source_target_pairs={{0,16},{8,24},{16,0},{24,8},{1,17},{9,25},{17,1},{25,9},{2,18},{10... | collective-permute-start | bytes 1327112 | tf_op jit(solution)/shard_map/ppermute | solution.py:689
  22.2 5.4 %copy-start.11 = (bf16[2,512,767]{1,0,2:T(2,128)(2,1)S(1)}, bf16[2,512,767]{1,0,2:T(2,128)(2,1)}, u32[]{:S(2)}) copy-start(bf16[2,512,767]{1,0,2:T(2,128)(2,1)} %param.21) | copy-start | bytes 4712452
  25.1 37.5 %collective-permute-start.5 = (bf16[480,768]{1,0:T(8,128)(2,1)}, bf16[480,768]{1,0:T(8,128)(2,1)}, u32[]{:S(2)}, u32[]{:S(2)}) collective-permute-start(bf16[480,768]{1,0:T(8,128)(2,1)} %fusion.12), channel_id=1, source_target_pairs={{0,1},{1,0},{2,3},{3,2},{4,5},{5,4},{6,7},{7,6},{8,9},{9,8},{10,11... | collective-permute-start | bytes 2211848 | tf_op jit(solution)/shard_map/ppermute | solution.py:689
  27.5 35.0 %collective-permute-start.6 = (bf16[384,768]{1,0:T(8,128)(2,1)}, bf16[384,768]{1,0:T(8,128)(2,1)}, u32[]{:S(2)}, u32[]{:S(2)}) collective-permute-start(bf16[384,768]{1,0:T(8,128)(2,1)} %pad.22), channel_id=1, source_target_pairs={{0,1},{1,0},{2,3},{3,2},{4,5},{5,4},{6,7},{7,6},{8,9},{9,8},{10,11... | collective-permute-start | bytes 1769480 | tf_op jit(solution)/shard_map/ppermute | solution.py:689
  27.6 8.6 %copy-start.6 = (bf16[3,768,384]{2,1,0:T(8,128)(2,1)S(1)}, bf16[3,768,384]{2,1,0:T(8,128)(2,1)}, u32[]{:S(2)}) copy-start(bf16[3,768,384]{2,1,0:T(8,128)(2,1)} %refs_7_.1) | copy-start | bytes 5308420
  34.0 48.3 %copy-start.8 = (bf16[528,768]{1,0:T(8,128)(2,1)}, bf16[528,768]{1,0:T(8,128)(2,1)S(1)}, u32[]{:S(2)}) copy-start(bf16[528,768]{1,0:T(8,128)(2,1)S(1)} %collective-permute-done.2.other_ref.refs_2_.refs_4_) | copy-start | bytes 2433028
  34.0 2.1 collective-permute-start.4
  38.3 7.9 %copy-start.13 = (bf16[512,768]{1,0:T(8,128)(2,1)S(1)}, bf16[512,768]{1,0:T(8,128)(2,1)}, u32[]{:S(2)}) copy-start(bf16[512,768]{1,0:T(8,128)(2,1)} %copy-done.12) | copy-start | bytes 2359300
  46.2 10.7 %copy-start.32 = (bf16[1024,768]{1,0:T(8,128)(2,1)}, bf16[1024,768]{1,0:T(8,128)(2,1)S(1)}, u32[]{:S(2)}) copy-start(bf16[1024,768]{1,0:T(8,128)(2,1)S(1)} %get-tuple-element.258.left_ref) | copy-start | bytes 4718596
  46.2 19.5 %copy-start.24 = (bf16[1024,768]{1,0:T(8,128)(2,1)}, bf16[1024,768]{1,0:T(8,128)(2,1)S(1)}, u32[]{:S(2)}) copy-start(bf16[1024,768]{1,0:T(8,128)(2,1)S(1)} %get-tuple-element.210.q_ref) | copy-start | bytes 4718596
  46.2 19.5 %copy-start.26 = (bf16[1024,768]{1,0:T(8,128)(2,1)}, bf16[1024,768]{1,0:T(8,128)(2,1)S(1)}, u32[]{:S(2)}) copy-start(bf16[1024,768]{1,0:T(8,128)(2,1)S(1)} %get-tuple-element.206.k_ref) | copy-start | bytes 4718596
  46.2 19.5 %copy-start.28 = (bf16[1024,768]{1,0:T(8,128)(2,1)}, bf16[1024,768]{1,0:T(8,128)(2,1)S(1)}, u32[]{:S(2)}) copy-start(bf16[1024,768]{1,0:T(8,128)(2,1)S(1)} %get-tuple-element.207.v_ref) | copy-start | bytes 4718596
  46.3 31.6 %collective-permute-start.9 = (bf16[512,768]{1,0:T(8,128)(2,1)S(1)}, bf16[512,768]{1,0:T(8,128)(2,1)S(1)}, u32[]{:S(2)}, u32[]{:S(2)}) collective-permute-start(bf16[512,768]{1,0:T(8,128)(2,1)S(1)} %copy-done.13), channel_id=1, source_target_pairs={{0,1},{1,0},{2,3},{3,2},{4,5},{5,4},{6,7},{7,6},{8,9},{9,8},{10,11... | collective-permute-start | bytes 2359304 | tf_op jit(solution)/shard_map/ppermute | solution.py:689
  62.6 16.4 %copy-start.41 = (bf16[2,767]{1,0:T(2,128)(2,1)S(1)}, bf16[2,767]{1,0:T(2,128)(2,1)}, u32[]{:S(2)}) copy-start(bf16[2,767]{1,0:T(2,128)(2,1)} %param.20) | copy-start | bytes 9208
  62.6 16.4 %copy-start.39 = (bf16[1536]{0:T(1024)(128)(2,1)S(1)}, bf16[1536]{0:T(1024)(128)(2,1)}, u32[]{:S(2)}) copy-start(bf16[1536]{0:T(1024)(128)(2,1)} %param.18) | copy-start | bytes 9220
  62.6 19.8 %copy-start.20 = (bf16[512,768]{1,0:T(8,128)(2,1)S(1)}, bf16[512,768]{1,0:T(8,128)(2,1)}, u32[]{:S(2)}) copy-start(bf16[512,768]{1,0:T(8,128)(2,1)} %copy-done.18) | copy-start | bytes 2359300
  62.6 19.8 %copy-start.23 = (bf16[512,768]{1,0:T(8,128)(2,1)S(1)}, bf16[512,768]{1,0:T(8,128)(2,1)}, u32[]{:S(2)}) copy-start(bf16[512,768]{1,0:T(8,128)(2,1)} %copy-done.22) | copy-start | bytes 2359300
  62.6 15.9 %collective-permute-start.7 = (bf16[480,768]{1,0:T(8,128)(2,1)}, bf16[480,768]{1,0:T(8,128)(2,1)S(1)}, u32[]{:S(2)}, u32[]{:S(2)}) collective-permute-start(bf16[480,768]{1,0:T(8,128)(2,1)} %collective-permute-done.5.refs_11_), channel_id=1, source_target_pairs={{0,16},{8,24},{16,0},{24,8},{1,17},{9,25},{17,1},{25,9},{2,18},{10... | collective-permute-start | bytes 2211848 | tf_op jit(solution)/shard_map/ppermute | solution.py:689
  64.2 13.7 %collective-permute-start.8 = (bf16[384,768]{1,0:T(8,128)(2,1)}, bf16[384,768]{1,0:T(8,128)(2,1)S(1)}, u32[]{:S(2)}, u32[]{:S(2)}) collective-permute-start(bf16[384,768]{1,0:T(8,128)(2,1)} %collective-permute-done.6.refs_15_), channel_id=1, source_target_pairs={{0,2},{2,0},{4,6},{6,4},{1,3},{3,1},{5,7},{7,5},{8,10},{10,8},{12,... | collective-permute-start | bytes 1769480 | tf_op jit(solution)/shard_map/ppermute | solution.py:689
  65.7 16.5 %collective-permute-start.10 = (bf16[480,768]{1,0:T(8,128)(2,1)}, bf16[480,768]{1,0:T(8,128)(2,1)S(1)}, u32[]{:S(2)}, u32[]{:S(2)}) collective-permute-start(bf16[480,768]{1,0:T(8,128)(2,1)} %collective-permute-done.5.refs_11_), channel_id=1, source_target_pairs={{0,8},{8,0},{16,24},{24,16},{1,9},{9,1},{17,25},{25,17},{2,10},{10... | collective-permute-start | bytes 2211848 | tf_op jit(solution)/shard_map/ppermute | solution.py:689
  78.5 3.9 %collective-permute-start.11 = (bf16[480,768]{1,0:T(8,128)(2,1)S(1)}, bf16[480,768]{1,0:T(8,128)(2,1)S(1)}, u32[]{:S(2)}, u32[]{:S(2)}) collective-permute-start(bf16[480,768]{1,0:T(8,128)(2,1)S(1)} %collective-permute-done.7.refs_13_), channel_id=1, source_target_pairs={{0,8},{8,0},{16,24},{24,16},{1,9},{9,1},{17,25},{25,17},{2,10},{10... | collective-permute-start | bytes 2211848 | tf_op jit(solution)/shard_map/ppermute | solution.py:689
  78.5 3.7 %collective-permute-start.12 = (bf16[384,768]{1,0:T(8,128)(2,1)}, bf16[384,768]{1,0:T(8,128)(2,1)S(1)}, u32[]{:S(2)}, u32[]{:S(2)}) collective-permute-start(bf16[384,768]{1,0:T(8,128)(2,1)} %collective-permute-done.6.refs_15_), channel_id=1, source_target_pairs={{0,8},{8,0},{16,24},{24,16},{1,9},{9,1},{17,25},{25,17},{2,10},{10... | collective-permute-start | bytes 1769480 | tf_op jit(solution)/shard_map/ppermute | solution.py:689
  79.0 3.4 %collective-permute-start.13 = (bf16[384,768]{1,0:T(8,128)(2,1)S(1)}, bf16[384,768]{1,0:T(8,128)(2,1)S(1)}, u32[]{:S(2)}, u32[]{:S(2)}) collective-permute-start(bf16[384,768]{1,0:T(8,128)(2,1)S(1)} %collective-permute-done.8.refs_17_), channel_id=1, source_target_pairs={{0,8},{8,0},{16,24},{24,16},{1,9},{9,1},{17,25},{25,17},{2,10},{10... | collective-permute-start | bytes 1769480 | tf_op jit(solution)/shard_map/ppermute | solution.py:689
  118.4 11.0 %copy-start.30 = (bf16[1024,768]{1,0:T(8,128)(2,1)}, bf16[1024,768]{1,0:T(8,128)(2,1)S(1)}, u32[]{:S(2)}) copy-start(bf16[1024,768]{1,0:T(8,128)(2,1)S(1)} %get-tuple-element.278.up_ref) | copy-start | bytes 4718596
  118.4 11.3 %collective-permute-start.14 = (bf16[256,768]{1,0:T(8,128)(2,1)S(1)}, bf16[256,768]{1,0:T(8,128)(2,1)S(1)}, u32[]{:S(2)}, u32[]{:S(2)}) collective-permute-start(bf16[256,768]{1,0:T(8,128)(2,1)S(1)} %get-tuple-element.233), channel_id=1, source_target_pairs={{0,1},{1,0},{2,3},{3,2},{4,5},{5,4},{6,7},{7,6},{8,9},{9,8},{10,11... | collective-permute-start | bytes 1179656 | tf_op jit(solution)/shard_map/ppermute | solution.py:689
  129.7 12.3 %collective-permute-start.15 = (bf16[2,2,480,768]{3,2,1,0:T(8,128)(2,1)S(1)}, bf16[2,2,480,768]{3,2,1,0:T(8,128)(2,1)}, u32[]{:S(2)}, u32[]{:S(2)}) collective-permute-start(bf16[2,2,480,768]{3,2,1,0:T(8,128)(2,1)S(1)} %get-tuple-element.240), channel_id=1, source_target_pairs={{0,8},{8,0},{16,24},{24,16},{1,9},{9,1},{17,25},{25,17},{2,10},{10... | collective-permute-start | bytes 8847368 | tf_op jit(solution)/shard_map/ppermute | solution.py:689
  129.7 11.5 %collective-permute-start.16 = (bf16[256,768]{1,0:T(8,128)(2,1)S(1)}, bf16[256,768]{1,0:T(8,128)(2,1)S(1)}, u32[]{:S(2)}, u32[]{:S(2)}) collective-permute-start(bf16[256,768]{1,0:T(8,128)(2,1)S(1)} %get-tuple-element.242), channel_id=1, source_target_pairs={{0,1},{1,0},{2,3},{3,2},{4,5},{5,4},{6,7},{7,6},{8,9},{9,8},{10,11... | collective-permute-start | bytes 1179656 | tf_op jit(solution)/shard_map/ppermute | solution.py:689
  141.9 5.1 %collective-permute-start.17 = (bf16[2,2,192,1536]{3,2,1,0:T(8,128)(2,1)}, bf16[2,2,192,1536]{3,2,1,0:T(8,128)(2,1)}, u32[]{:S(2)}, u32[]{:S(2)}) collective-permute-start(bf16[2,2,192,1536]{3,2,1,0:T(8,128)(2,1)} %get-tuple-element.244), channel_id=1, source_target_pairs={{0,8},{8,0},{16,24},{24,16},{1,9},{9,1},{17,25},{25,17},{2,10},{10... | collective-permute-start | bytes 7077896 | tf_op jit(solution)/shard_map/ppermute | solution.py:689
  142.0 8.9 %copy-start.31 = (bf16[1024,768]{1,0:T(8,128)(2,1)S(1)}, bf16[1024,768]{1,0:T(8,128)(2,1)}, u32[]{:S(2)}) copy-start(bf16[1024,768]{1,0:T(8,128)(2,1)} %copy-done.30) | copy-start | bytes 4718596
  143.4 24.7 %collective-permute-start.18 = (bf16[480,768]{1,0:T(8,128)(2,1)S(1)}, bf16[480,768]{1,0:T(8,128)(2,1)S(1)}, u32[]{:S(2)}, u32[]{:S(2)}) collective-permute-start(bf16[480,768]{1,0:T(8,128)(2,1)S(1)} %fusion.13), channel_id=1, source_target_pairs={{0,16},{8,24},{16,0},{24,8},{1,17},{9,25},{17,1},{25,9},{2,18},{10... | collective-permute-start | bytes 2211848 | tf_op jit(solution)/shard_map/ppermute | solution.py:689
  145.2 5.7 %copy-start.29 = (bf16[1024,768]{1,0:T(8,128)(2,1)S(1)}, bf16[1024,768]{1,0:T(8,128)(2,1)}, u32[]{:S(2)}) copy-start(bf16[1024,768]{1,0:T(8,128)(2,1)} %copy-done.28) | copy-start | bytes 4718596
  146.6 45.7 %collective-permute-start.21 = (bf16[480,768]{1,0:T(8,128)(2,1)S(1)}, bf16[480,768]{1,0:T(8,128)(2,1)S(1)}, u32[]{:S(2)}, u32[]{:S(2)}) collective-permute-start(bf16[480,768]{1,0:T(8,128)(2,1)S(1)} %fusion.14), channel_id=1, source_target_pairs={{0,16},{8,24},{16,0},{24,8},{1,17},{9,25},{17,1},{25,9},{2,18},{10... | collective-permute-start | bytes 2211848 | tf_op jit(solution)/shard_map/ppermute | solution.py:689
  149.1 28.9 %collective-permute-start.19 = (bf16[2,192,1536]{2,1,0:T(8,128)(2,1)S(1)}, bf16[2,192,1536]{2,1,0:T(8,128)(2,1)S(1)}, u32[]{:S(2)}, u32[]{:S(2)}) collective-permute-start(bf16[2,192,1536]{2,1,0:T(8,128)(2,1)S(1)} %fusion.4), channel_id=1, source_target_pairs={{0,1},{1,0},{2,3},{3,2},{4,5},{5,4},{6,7},{7,6},{8,9},{9,8},{10,11... | collective-permute-start | bytes 3538952 | tf_op jit(solution)/shard_map/ppermute | solution.py:689
  169.7 23.0 %collective-permute-start.20 = (bf16[480,768]{1,0:T(8,128)(2,1)S(1)}, bf16[480,768]{1,0:T(8,128)(2,1)S(1)}, u32[]{:S(2)}, u32[]{:S(2)}) collective-permute-start(bf16[480,768]{1,0:T(8,128)(2,1)S(1)} %fusion.2), channel_id=1, source_target_pairs={{0,1},{1,0},{2,3},{3,2},{4,5},{5,4},{6,7},{7,6},{8,9},{9,8},{10,11... | collective-permute-start | bytes 2211848 | tf_op jit(solution)/shard_map/ppermute | solution.py:689
  170.1 8.0 %copy-start.36 = (bf16[2,2,192,1536]{3,2,1,0:T(8,128)(2,1)S(1)}, bf16[2,2,192,1536]{3,2,1,0:T(8,128)(2,1)}, u32[]{:S(2)}) copy-start(bf16[2,2,192,1536]{3,2,1,0:T(8,128)(2,1)} %get-tuple-element.262) | copy-start | bytes 7077892
  178.0 20.0 %collective-permute-start.23 = (bf16[2,3,192,384]{3,2,1,0:T(8,128)(2,1)S(1)}, bf16[2,3,192,384]{3,2,1,0:T(8,128)(2,1)S(1)}, u32[]{:S(2)}, u32[]{:S(2)}) collective-permute-start(bf16[2,3,192,384]{3,2,1,0:T(8,128)(2,1)S(1)} %get-tuple-element.273), channel_id=1, source_target_pairs={{0,8},{8,0},{16,24},{24,16},{1,9},{9,1},{17,25},{25,17},{2,10},{10... | collective-permute-start | bytes 2654216 | tf_op jit(solution)/shard_map/ppermute | solution.py:689
  179.3 18.7 %collective-permute-start.22 = (bf16[192,1536]{1,0:T(8,128)(2,1)S(1)}, bf16[192,1536]{1,0:T(8,128)(2,1)S(1)}, u32[]{:S(2)}, u32[]{:S(2)}) collective-permute-start(bf16[192,1536]{1,0:T(8,128)(2,1)S(1)} %fusion.7), channel_id=1, source_target_pairs={{0,16},{8,24},{16,0},{24,8},{1,17},{9,25},{17,1},{25,9},{2,18},{10... | collective-permute-start | bytes 1769480 | tf_op jit(solution)/shard_map/ppermute | solution.py:689
  194.3 21.9 %collective-permute-start.27 = (bf16[480,768]{1,0:T(8,128)(2,1)S(1)}, bf16[480,768]{1,0:T(8,128)(2,1)S(1)}, u32[]{:S(2)}, u32[]{:S(2)}) collective-permute-start(bf16[480,768]{1,0:T(8,128)(2,1)S(1)} %fusion.1), channel_id=1, source_target_pairs={{0,2},{6,4},{1,3},{7,5},{8,10},{14,12},{9,11},{15,13},{16,18},{22,... | collective-permute-start | bytes 2211848 | tf_op jit(solution)/shard_map/ppermute | solution.py:704
  199.5 8.6 %copy-start.7 = (bf16[3,768,384]{2,1,0:T(8,128)(2,1)S(1)}, bf16[3,768,384]{2,1,0:T(8,128)(2,1)}, u32[]{:S(2)}) copy-start(bf16[3,768,384]{2,1,0:T(8,128)(2,1)} %refs_7_.1) | copy-start | bytes 5308420
  199.6 11.6 %collective-permute-start.24 = (bf16[3,192,384]{2,1,0:T(8,128)(2,1)S(1)}, bf16[3,192,384]{2,1,0:T(8,128)(2,1)S(1)}, u32[]{:S(2)}, u32[]{:S(2)}) collective-permute-start(bf16[3,192,384]{2,1,0:T(8,128)(2,1)S(1)} %fusion.15), channel_id=1, source_target_pairs={{0,16},{8,24},{16,0},{24,8},{1,17},{9,25},{17,1},{25,9},{2,18},{10... | collective-permute-start | bytes 1327112 | tf_op jit(solution)/shard_map/ppermute | solution.py:689
  200.9 32.7 %collective-permute-start.29 = (bf16[192,1536]{1,0:T(8,128)(2,1)S(1)}, bf16[192,1536]{1,0:T(8,128)(2,1)S(1)}, u32[]{:S(2)}, u32[]{:S(2)}) collective-permute-start(bf16[192,1536]{1,0:T(8,128)(2,1)S(1)} %fusion.6), channel_id=1, source_target_pairs={{0,2},{6,4},{1,3},{7,5},{8,10},{14,12},{9,11},{15,13},{16,18},{22,... | collective-permute-start | bytes 1769480 | tf_op jit(solution)/shard_map/ppermute | solution.py:704
  211.2 2.7 collective-permute-start.25
  211.3 2.5 collective-permute-start.26
  212.0 12.2 %collective-permute-start.32 = (bf16[3,192,384]{2,1,0:T(8,128)(2,1)S(1)}, bf16[3,192,384]{2,1,0:T(8,128)(2,1)S(1)}, u32[]{:S(2)}, u32[]{:S(2)}) collective-permute-start(bf16[3,192,384]{2,1,0:T(8,128)(2,1)S(1)} %fusion.10), channel_id=1, source_target_pairs={{0,1},{1,0},{2,3},{3,2},{4,5},{5,4},{6,7},{7,6},{8,9},{9,8},{10,11... | collective-permute-start | bytes 1327112 | tf_op jit(solution)/shard_map/ppermute | solution.py:689
  213.9 7.9 %collective-permute-start.28 = (f32[4,5376]{1,0:T(4,128)S(1)}, f32[4,5376]{1,0:T(4,128)S(1)}, u32[]{:S(2)}, u32[]{:S(2)}) collective-permute-start(f32[4,5376]{1,0:T(4,128)S(1)} %add.182), channel_id=1, source_target_pairs={{0,16},{8,24},{16,0},{24,8},{1,17},{9,25},{17,1},{25,9},{2,18},{10... | collective-permute-start | bytes 258056 | tf_op jit(solution)/shard_map/ppermute | solution.py:689
  214.8 13.2 %collective-permute-start.31 = (bf16[3,192,384]{2,1,0:T(8,128)(2,1)S(1)}, bf16[3,192,384]{2,1,0:T(8,128)(2,1)S(1)}, u32[]{:S(2)}, u32[]{:S(2)}) collective-permute-start(bf16[3,192,384]{2,1,0:T(8,128)(2,1)S(1)} %fusion.16), channel_id=1, source_target_pairs={{0,16},{8,24},{16,0},{24,8},{1,17},{9,25},{17,1},{25,9},{2,18},{10... | collective-permute-start | bytes 1327112 | tf_op jit(solution)/shard_map/ppermute | solution.py:689
  216.4 17.3 %collective-permute-start.30 = (bf16[480,768]{1,0:T(8,128)(2,1)S(1)}, bf16[480,768]{1,0:T(8,128)(2,1)S(1)}, u32[]{:S(2)}, u32[]{:S(2)}) collective-permute-start(bf16[480,768]{1,0:T(8,128)(2,1)S(1)} %add_convert_fusion.2), channel_id=1, source_target_pairs={{2,4},{4,2},{3,5},{5,3},{10,12},{12,10},{11,13},{13,11},{18,20},{2... | collective-permute-start | bytes 2211848 | tf_op jit(solution)/shard_map/ppermute | solution.py:708
  221.9 4.2 %collective-permute-start.33 = (f32[4,3456]{1,0:T(4,128)S(1)}, f32[4,3456]{1,0:T(4,128)S(1)}, u32[]{:S(2)}, u32[]{:S(2)}) collective-permute-start(f32[4,3456]{1,0:T(4,128)S(1)} %pad_maximum_fusion.1), channel_id=1, source_target_pairs={{0,1},{1,0},{2,3},{3,2},{4,5},{5,4},{6,7},{7,6},{8,9},{9,8},{10,11... | collective-permute-start | bytes 165896 | tf_op jit(solution)/shard_map/ppermute | solution.py:689
  227.9 8.5 %copy-start.21 = (bf16[512,768]{1,0:T(8,128)(2,1)S(1)}, bf16[512,768]{1,0:T(8,128)(2,1)}, u32[]{:S(2)}) copy-start(bf16[512,768]{1,0:T(8,128)(2,1)} %copy-done.18) | copy-start | bytes 2359300
  228.2 17.4 %collective-permute-start.34 = (bf16[3,192,384]{2,1,0:T(8,128)(2,1)S(1)}, bf16[3,192,384]{2,1,0:T(8,128)(2,1)S(1)}, u32[]{:S(2)}, u32[]{:S(2)}) collective-permute-start(bf16[3,192,384]{2,1,0:T(8,128)(2,1)S(1)} %fusion.9), channel_id=1, source_target_pairs={{0,2},{6,4},{1,3},{7,5},{8,10},{14,12},{9,11},{15,13},{16,18},{22,... | collective-permute-start | bytes 1327112 | tf_op jit(solution)/shard_map/ppermute | solution.py:704
  232.3 13.2 %collective-permute-start.36 = (f32[4,3456]{1,0:T(4,128)S(1)}, f32[4,3456]{1,0:T(4,128)S(1)}, u32[]{:S(2)}, u32[]{:S(2)}) collective-permute-start(f32[4,3456]{1,0:T(4,128)S(1)} %add.190), channel_id=1, source_target_pairs={{0,2},{6,4},{1,3},{7,5},{8,10},{14,12},{9,11},{15,13},{16,18},{22,... | collective-permute-start | bytes 165896 | tf_op jit(solution)/shard_map/ppermute | solution.py:704
  233.9 11.7 %collective-permute-start.35 = (bf16[192,1536]{1,0:T(8,128)(2,1)S(1)}, bf16[192,1536]{1,0:T(8,128)(2,1)S(1)}, u32[]{:S(2)}, u32[]{:S(2)}) collective-permute-start(bf16[192,1536]{1,0:T(8,128)(2,1)S(1)} %add_convert_fusion.6), channel_id=1, source_target_pairs={{2,4},{4,2},{3,5},{5,3},{10,12},{12,10},{11,13},{13,11},{18,20},{2... | collective-permute-start | bytes 1769480 | tf_op jit(solution)/shard_map/ppermute | solution.py:708
  234.9 19.3 %collective-permute-start.38 = (bf16[480,768]{1,0:T(8,128)(2,1)S(1)}, bf16[480,768]{1,0:T(8,128)(2,1)S(1)}, u32[]{:S(2)}, u32[]{:S(2)}) collective-permute-start(bf16[480,768]{1,0:T(8,128)(2,1)S(1)} %add_convert_fusion.1), channel_id=1, source_target_pairs={{2,0},{4,6},{3,1},{5,7},{10,8},{12,14},{11,9},{13,15},{18,16},{20,... | collective-permute-start | bytes 2211848 | tf_op jit(solution)/shard_map/ppermute | solution.py:712
  245.7 10.4 %collective-permute-start.40 = (bf16[3,192,384]{2,1,0:T(8,128)(2,1)S(1)}, bf16[3,192,384]{2,1,0:T(8,128)(2,1)S(1)}, u32[]{:S(2)}, u32[]{:S(2)}) collective-permute-start(bf16[3,192,384]{2,1,0:T(8,128)(2,1)S(1)} %add_convert_fusion.8), channel_id=1, source_target_pairs={{2,4},{4,2},{3,5},{5,3},{10,12},{12,10},{11,13},{13,11},{18,20},{2... | collective-permute-start | bytes 1327112 | tf_op jit(solution)/shard_map/ppermute | solution.py:708
  246.5 9.7 %collective-permute-start.39 = (f32[4,3456]{1,0:T(4,128)S(1)}, f32[4,3456]{1,0:T(4,128)S(1)}, u32[]{:S(2)}, u32[]{:S(2)}) collective-permute-start(f32[4,3456]{1,0:T(4,128)S(1)} %add.193), channel_id=1, source_target_pairs={{2,4},{4,2},{3,5},{5,3},{10,12},{12,10},{11,13},{13,11},{18,20},{2... | collective-permute-start | bytes 165896 | tf_op jit(solution)/shard_map/ppermute | solution.py:708
  247.1 16.0 %collective-permute-start.37 = (bf16[512,768]{1,0:T(8,128)(2,1)S(1)}, bf16[512,768]{1,0:T(8,128)(2,1)S(1)}, u32[]{:S(2)}, u32[]{:S(2)}) collective-permute-start(bf16[512,768]{1,0:T(8,128)(2,1)S(1)} %get-tuple-element.327), channel_id=1, source_target_pairs={{0,1},{1,0},{2,3},{3,2},{4,5},{5,4},{6,7},{7,6},{8,9},{9,8},{10,11... | collective-permute-start | bytes 2359304 | tf_op jit(solution)/shard_map/ppermute | solution.py:689
  249.1 24.9 %collective-permute-start.42 = (bf16[192,1536]{1,0:T(8,128)(2,1)S(1)}, bf16[192,1536]{1,0:T(8,128)(2,1)S(1)}, u32[]{:S(2)}, u32[]{:S(2)}) collective-permute-start(bf16[192,1536]{1,0:T(8,128)(2,1)S(1)} %add_convert_fusion.5), channel_id=1, source_target_pairs={{2,0},{4,6},{3,1},{5,7},{10,8},{12,14},{11,9},{13,15},{18,16},{20,... | collective-permute-start | bytes 1769480 | tf_op jit(solution)/shard_map/ppermute | solution.py:712
  256.1 19.0 %collective-permute-start.43 = (f32[4,3456]{1,0:T(4,128)S(1)}, f32[4,3456]{1,0:T(4,128)S(1)}, u32[]{:S(2)}, u32[]{:S(2)}) collective-permute-start(f32[4,3456]{1,0:T(4,128)S(1)} %add.197), channel_id=1, source_target_pairs={{2,0},{4,6},{3,1},{5,7},{10,8},{12,14},{11,9},{13,15},{18,16},{20,... | collective-permute-start | bytes 165896 | tf_op jit(solution)/shard_map/ppermute | solution.py:712
  257.6 22.0 %collective-permute-start.41 = (bf16[3,192,384]{2,1,0:T(8,128)(2,1)S(1)}, bf16[3,192,384]{2,1,0:T(8,128)(2,1)S(1)}, u32[]{:S(2)}, u32[]{:S(2)}) collective-permute-start(bf16[3,192,384]{2,1,0:T(8,128)(2,1)S(1)} %add_convert_fusion.7), channel_id=1, source_target_pairs={{2,0},{4,6},{3,1},{5,7},{10,8},{12,14},{11,9},{13,15},{18,16},{20,... | collective-permute-start | bytes 1327112 | tf_op jit(solution)/shard_map/ppermute | solution.py:712
  274.0 6.6 %copy-start.1 = (s32[2,1024]{1,0:T(2,128)S(1)}, s32[2,1024]{1,0:T(2,128)}, u32[]{:S(2)}) copy-start(s32[2,1024]{1,0:T(2,128)} %param.12) | copy-start | bytes 24580
  (22 other events, 50.1 us)
